TPU v7x, 32 devices: a whole 2x2x4 slice. The times are simulated.
32 devices in a mesh: cfg: 2 (over y), slab: 4 (over z), energy: 4 (over x, core).
Axes of the slice: x: 2, y: 2, z: 4, core: 2. Of those that a mesh axis runs over, the one named last changes fastest.
Arguments:
- energy_index: int32 [4], P('energy'), may hold values from 0 to 8190, as said below
- diag_blocks: float32 [16, 192, 192], P(('cfg', 'slab')), parts along dimension 0, may hold values from -3 to 7, as said below
- couple: float32 [16, 192, 192], P(('cfg', 'slab')), parts along dimension 0, may hold values from -4 to 4, as said below
- probes: float32 [1536, 128], P('slab'), may hold values from -12 to 12
- orbital_cell: int32 [1536], P('slab'), may hold values from 0 to 262143, as said below
- dopant_cells: int32 [2048], P('cfg'), parts along dimension 0, may hold values from 0 to 262143
- initial_potential: float32 [64, 64, 128], P(('cfg', 'slab'), 'energy'), parts along dimension 0, may hold values from -4 to 4
Outputs:
- potential: float32 [64, 64, 128], P(('cfg', 'slab'), 'energy'), parts along dimension 0
- density: float32 [3072], P(('cfg', 'slab')), parts along dimension 0
There are 2 independent parts, one for each index of `cfg`. A program takes and returns all parts, laid end to end along the dimension named above; an argument that names none is the same for every part. Nothing has to cross between parts.
Inputs may be any that keep to these rules, and one draw needn't show every extreme that they name: `energy_index`: one energy point has index 0 and another has index 8190. Each placement has its own operator: diag_blocks and couple are the diagonal and below-diagonal blocks of a symmetric positive semidefinite block-tridiagonal matrix; each diagonal block is symmetric. couple[i] is the block of that same matrix in block row i and block column i - 1. `orbital_cell`: orbital o lies in a cell whose z index is at least (o // 384) * 8 and below that plus 8.
All inputs are finite; a program needn't handle non-finite values.
Results may differ from a plain program's by a relative error of at most 0.0003.
Values sent between devices are 32-bit elements; how exact they have to be, the bound alone decides.
No kernel may reach another device: no remote copies, remote signals or barrier semaphores. Data moves between devices by JAX's collectives and lax.ppermute only.
A program may use at most 64 MiB of HBM per device.

v0:
```python
import jax
import jax.numpy as jnp
from jax import lax
from jax.sharding import PartitionSpec as P

SWEEPS = 2


sigma_base = 0.02
sigma_step = 0.01
coupling_beta = 0.5
dopant_charge = 4.0


def from_behind(value, axis, steps):
    count = lax.axis_size(axis)
    leading, last = (max(0, -steps), min(count, count - steps))
    return lax.ppermute(value, axis, [(source, source + steps) for source in range(leading, last)])


def entering(shard, axis, combine, identity, reverse):
    peers, mine = (lax.axis_size(axis), lax.axis_index(axis))
    everything = jax.tree.map(lambda part: lax.all_gather(part, axis), shard)
    start = jax.tree.map(
        lambda part, zero: jnp.broadcast_to(jnp.asarray(zero, part.dtype), part.shape),
        shard,
        identity,
    )

    def step(k, before):
        at = peers - 1 - k if reverse else k
        reached = at > mine if reverse else at < mine
        new = combine(before, jax.tree.map(lambda part: part[at], everything))
        return jax.tree.map(lambda a, b: jnp.where(reached, a, b), new, before)

    return lax.fori_loop(0, peers, step, start)


def padded_2(block, sides, width):
    for axis, dim in sides:
        count = lax.axis_size(axis)
        forward = [(i, i + 1) for i in range(count - 1)]
        backward = [(target, source) for source, target in forward]
        low = lax.ppermute(
            lax.slice_in_dim(block, block.shape[dim] - width, None, axis=dim), axis, forward
        )
        high = lax.ppermute(lax.slice_in_dim(block, 0, width, axis=dim), axis, backward)
        block = jnp.concatenate([low, block, high], axis=dim)
    return block


def product(left, right):
    return jnp.dot(left, right, precision=lax.Precision.HIGHEST, preferred_element_type=jnp.float32)


def solve_definite(matrix, right_side):
    factor = jnp.linalg.cholesky(matrix)
    return jax.scipy.linalg.cho_solve((factor, True), right_side)


def single_part(diagonal, link, source):
    return (
        jnp.zeros_like(diagonal),
        link,
        diagonal,
        jnp.zeros_like(source),
        source,
        jnp.zeros((), jnp.float32),
    )


def merge_parts(first, second):
    width = first[0].shape[0]
    pivot = first[2] + second[0]
    stacked = jnp.concatenate([first[1].T, second[1], first[4] + second[3]], axis=1)
    solved = solve_definite(pivot, stacked)
    toward_first = solved[:, :width]
    toward_second = solved[:, width : 2 * width]
    toward_source = solved[:, 2 * width :]
    merged = (
        first[0] - product(first[1], toward_first),
        -product(first[1], toward_second),
        second[2] - product(second[1].T, toward_second),
        first[3] - product(first[1], toward_source),
        second[4] - product(second[1].T, toward_source),
        first[5] * second[5],
    )
    first_empty = first[5] > 0.5
    second_empty = second[5] > 0.5
    return tuple(
        (
            jnp.where(first_empty, later, jnp.where(second_empty, earlier, joined))
            for earlier, later, joined in zip(first, second, merged)
        )
    )


def compose_maps(earlier, later):
    return (later[0] - product(later[1], earlier[0]), -product(later[1], earlier[1]))


def body(energy_index, diag_blocks, couple, probes, orbital_cell, dopant_cells, initial_potential):
    blocks = diag_blocks.shape[0]
    width = diag_blocks.shape[1]
    probe_count = probes.shape[1]
    slab_place = lax.axis_index("slab")
    first_lower = jnp.where(slab_place == 0, jnp.zeros_like(couple[0]), couple[0])
    lowers = [first_lower] + [couple[1]]
    next_lower = from_behind(couple[0], "slab", -1)
    sources = [probes[block * width : (block + 1) * width] for block in range(blocks)]
    unit = jnp.eye(width, dtype=jnp.float32)
    empty_source = jnp.zeros((width, probe_count), jnp.float32)
    identity = (
        jnp.zeros_like(unit),
        jnp.zeros_like(unit),
        unit,
        empty_source,
        empty_source,
        jnp.ones((), jnp.float32),
    )
    energies = lax.axis_size("energy") * energy_index.shape[0]
    density = jnp.zeros((blocks * width,), jnp.float32)
    shift_value = sigma_base + sigma_step * energy_index[0].astype(jnp.float32)
    diagonals = [diag_blocks[block] + shift_value * unit for block in range(blocks)]
    segment = single_part(diagonals[0], lowers[0].T, sources[0])
    block = 1
    segment = merge_parts(segment, single_part(diagonals[block], lowers[block].T, sources[block]))
    left_part = entering(segment, "slab", merge_parts, identity, False)
    left_solved = solve_definite(left_part[2], jnp.concatenate([lowers[0].T, left_part[4]], axis=1))
    carry_couple = left_solved[:, :width]
    carry_value = left_solved[:, width:]
    factors = []
    values = []
    for block in range(blocks):
        pivot = diagonals[block] - product(lowers[block], carry_couple)
        reduced = sources[block] - product(lowers[block], carry_value)
        if block + 1 < blocks:
            solved = solve_definite(pivot, jnp.concatenate([lowers[block + 1].T, reduced], axis=1))
            carry_couple = solved[:, :width]
            carry_value = solved[:, width:]
            factors.append(carry_couple)
            values.append(carry_value)
        else:
            last_pivot = pivot
            last_reduced = reduced
    solved = solve_definite(last_pivot, jnp.concatenate([next_lower.T, last_reduced], axis=1))
    factors.append(solved[:, :width])
    values.append(solved[:, width:])
    offset = values[-1]
    gain = factors[-1]
    block = 0
    offset = values[block] - product(factors[block], offset)
    gain = -product(factors[block], gain)
    beyond = entering((offset, gain), "slab", compose_maps, (jnp.zeros_like(offset), -unit), True)[
        0
    ]
    solution = values[-1] - product(factors[-1], beyond)
    pieces = [solution]
    block = 0
    solution = values[block] - product(factors[block], solution)
    pieces.append(solution)
    block_solution = jnp.concatenate(pieces[::-1], axis=0)
    density = density + jnp.sum(probes * block_solution, axis=1)
    density = lax.psum(density / (probe_count * energies), "energy")
    depth = initial_potential.shape[0]
    rows_here = initial_potential.shape[1]
    across = initial_potential.shape[2]
    total_rows = rows_here * lax.axis_size("energy")
    plane = total_rows * across
    energy_place = lax.axis_index("energy")
    start = lax.all_gather(initial_potential, "energy", axis=1, tiled=True)

    def deposit(indices, weights):
        layer = indices // plane - slab_place * depth
        row = indices // across % total_rows
        column = indices % across
        inside = (layer >= 0) & (layer < depth) & (row >= 0) & (row < total_rows)
        count = depth * total_rows * across
        flat = jnp.where(inside, (layer * total_rows + row) * across + column, count)
        summed = jax.ops.segment_sum(jnp.where(inside, weights, 0.0), flat, num_segments=count + 1)
        return summed[:count].reshape(depth, total_rows, across)

    electrons = deposit(orbital_cell, density)
    dopants = dopant_charge * deposit(dopant_cells, jnp.ones(dopant_cells.shape, jnp.float32))
    potential = start
    for sweep in range(SWEEPS):
        padded = padded_2(potential, (("slab", 0),), 1)
        padded = jnp.pad(padded, ((0, 0), (1, 1), (0, 0)))
        padded = jnp.pad(padded, ((0, 0), (0, 0), (1, 1)))
        beside_all = padded[2:, 1:-1, 1:-1] + padded[:-2, 1:-1, 1:-1]
        beside_all = beside_all + padded[1:-1, 2:, 1:-1] + padded[1:-1, :-2, 1:-1]
        beside_all = beside_all + padded[1:-1, 1:-1, 2:] + padded[1:-1, 1:-1, :-2]
        growth = jnp.exp(potential - start)
        residual = beside_all - 6.0 * potential + coupling_beta * (dopants - electrons * growth)
        potential = potential + residual / (6.0 + coupling_beta * jnp.abs(electrons) * growth)
    potential = lax.dynamic_slice_in_dim(potential, energy_place * rows_here, rows_here, 1)
    return (potential, density)


def solution(mesh):
    placed = (
        P("energy"),
        P(("cfg", "slab"), None, None),
        P(("cfg", "slab"), None, None),
        P("slab", None),
        P("slab"),
        P("cfg"),
        P(("cfg", "slab"), "energy", None),
    )
    return jax.shard_map(
        body,
        mesh=mesh,
        in_specs=placed,
        out_specs=(P(("cfg", "slab"), "energy", None), P(("cfg", "slab"))),
        check_vma=False,
    )
```

profile of v0, /device:TPU:0, one launch (start us, length us, event | category | flops | bytes accessed | tf_op | source)
XLA Modules:
  0.0 642.3 jit_solution(10217847360849363682)
XLA Ops:
  20.4 11.7 %cholesky.312 = f32[128,128]{1,0:T(8,128)S(1)} custom-call(f32[128,128]{1,0:T(8,128)S(1)} %cholesky.463), custom_call_target="Cholesky" | custom-call | tf_op jit(solution)/shard_map/jit(cholesky)/cholesky | solution.py:57
  32.1 9.8 %custom-call.30 = f32[1,128,128]{1,2,0:T(8,128)S(1)} custom-call(f32[1,128,128]{2,1,0:T(8,128)S(1)} %get-tuple-element.599), custom_call_target="InvertDiagBlocksLowerTriangular" | custom-call | tf_op jit(solution)/shard_map/jit(cholesky)/cholesky | solution.py:57
  50.9 20.2 %custom-call.31 = f32[2,128,128]{1,2,0:T(8,128)S(1)} custom-call(f32[2,128,128]{2,1,0:T(8,128)S(1)} %pad_maximum_fusion.14), custom_call_target="InvertDiagBlocksLowerTriangular" | custom-call | tf_op jit(solution)/shard_map/jit(_cho_solve)/triangular_solve | solution.py:58
  79.6 18.6 %all-gather.3 = f32[768,192]{1,0:T(8,128)S(1)} all-gather(f32[192,192]{1,0:T(8,128)S(1)} %copy.108), channel_id=5, replica_groups=mesh['cfg'=2,'slab'=4,'energy'=4] {'slab'}, dimensions={0}, use_global_device_ids=true | all-gather | bytes 737280 | tf_op jit(solution)/shard_map/all_gather | solution.py:23
  98.2 14.7 %all-gather.2 = f32[768,128]{1,0:T(8,128)S(1)} all-gather(f32[192,128]{1,0:T(8,128)S(1)} %convolution_subtract_fusion.19), channel_id=4, replica_groups=mesh['cfg'=2,'slab'=4,'energy'=4] {'slab'}, dimensions={0}, use_global_device_ids=true | all-gather | bytes 491520 | tf_op jit(solution)/shard_map/all_gather | solution.py:23
  112.9 16.0 %all-gather.4 = f32[768,128]{1,0:T(8,128)} all-gather(f32[192,128]{1,0:T(8,128)S(1)} %fusion.43), channel_id=6, replica_groups=mesh['cfg'=2,'slab'=4,'energy'=4] {'slab'}, dimensions={0}, use_global_device_ids=true | all-gather | bytes 491520 | tf_op jit(solution)/shard_map/all_gather | solution.py:23
  129.0 19.5 %all-gather.1 = f32[768,192]{1,0:T(8,128)} all-gather(f32[192,192]{1,0:T(8,128)S(1)} %copy.106), channel_id=3, replica_groups=mesh['cfg'=2,'slab'=4,'energy'=4] {'slab'}, dimensions={0}, use_global_device_ids=true | all-gather | bytes 737280 | tf_op jit(solution)/shard_map/all_gather | solution.py:23
  148.5 15.8 %all-gather = f32[768,192]{1,0:T(8,128)S(1)} all-gather(f32[192,192]{1,0:T(8,128)S(1)} %convolution_negate_fusion.2), channel_id=2, replica_groups=mesh['cfg'=2,'slab'=4,'energy'=4] {'slab'}, dimensions={0}, use_global_device_ids=true | all-gather | bytes 737280 | tf_op jit(solution)/shard_map/all_gather | solution.py:23
  166.3 10.9 %all-reduce.9 = f32[4]{0:T(128)S(1)} all-reduce(f32[4]{0:T(128)S(1)} %dynamic-update-slice.8), channel_id=1, replica_groups=mesh['cfg'=2,'slab'=4,'energy'=4] {'slab'}, use_global_device_ids=true, to_apply=%add.9 | all-reduce | flops 4 | bytes 32
  177.2 239.0 %while.43 = (s32[]{:T(128)}, f32[192,192]{0,1:T(8,128)S(1)}, f32[192,192]{0,1:T(8,128)S(1)}, f32[192,128]{1,0:T(8,128)S(1)}, f32[]{:T(128)}, /*index=5*/s32[]{:T...) while((s32[]{:T(128)}, f32[192,192]{0,1:T(8,128)S(1)}, ...), condition=%wide.region_6.9_spmd.clone, body=%wide.region_5.8_spmd.clone.sunk | while | flops 599175360 | bytes 16085591 | solution.py:36
  178.8 11.7 %cholesky.770 = f32[128,128]{1,0:T(8,128)S(1)} custom-call(f32[128,128]{1,0:T(8,128)S(1)} %cholesky.769), custom_call_target="Cholesky" | custom-call | tf_op jit(solution)/shard_map/while/body/eval_jaxpr/jit(cholesky)/cholesky | solution.py:57
  190.5 9.8 %custom-call.40 = f32[1,128,128]{1,2,0:T(8,128)S(1)} custom-call(f32[1,128,128]{2,1,0:T(8,128)S(1)} %get-tuple-element.725), custom_call_target="InvertDiagBlocksLowerTriangular" | custom-call | tf_op jit(solution)/shard_map/while/body/eval_jaxpr/jit(cholesky)/cholesky | solution.py:57
  209.4 19.7 %custom-call.41 = f32[2,128,128]{1,2,0:T(8,128)S(1)} custom-call(f32[2,128,128]{2,1,0:T(8,128)S(1)} %pad_maximum_fusion.35), custom_call_target="InvertDiagBlocksLowerTriangular" | custom-call | tf_op jit(solution)/shard_map/while/body/eval_jaxpr/jit(_cho_solve)/triangular_solve | solution.py:58
  238.4 11.7 %cholesky.770 = f32[128,128]{1,0:T(8,128)S(1)} custom-call(f32[128,128]{1,0:T(8,128)S(1)} %cholesky.769), custom_call_target="Cholesky" | custom-call | tf_op jit(solution)/shard_map/while/body/eval_jaxpr/jit(cholesky)/cholesky | solution.py:57
  250.2 9.8 %custom-call.40 = f32[1,128,128]{1,2,0:T(8,128)S(1)} custom-call(f32[1,128,128]{2,1,0:T(8,128)S(1)} %get-tuple-element.725), custom_call_target="InvertDiagBlocksLowerTriangular" | custom-call | tf_op jit(solution)/shard_map/while/body/eval_jaxpr/jit(cholesky)/cholesky | solution.py:57
  269.1 19.7 %custom-call.41 = f32[2,128,128]{1,2,0:T(8,128)S(1)} custom-call(f32[2,128,128]{2,1,0:T(8,128)S(1)} %pad_maximum_fusion.35), custom_call_target="InvertDiagBlocksLowerTriangular" | custom-call | tf_op jit(solution)/shard_map/while/body/eval_jaxpr/jit(_cho_solve)/triangular_solve | solution.py:58
  298.1 11.7 %cholesky.770 = f32[128,128]{1,0:T(8,128)S(1)} custom-call(f32[128,128]{1,0:T(8,128)S(1)} %cholesky.769), custom_call_target="Cholesky" | custom-call | tf_op jit(solution)/shard_map/while/body/eval_jaxpr/jit(cholesky)/cholesky | solution.py:57
  309.8 9.8 %custom-call.40 = f32[1,128,128]{1,2,0:T(8,128)S(1)} custom-call(f32[1,128,128]{2,1,0:T(8,128)S(1)} %get-tuple-element.725), custom_call_target="InvertDiagBlocksLowerTriangular" | custom-call | tf_op jit(solution)/shard_map/while/body/eval_jaxpr/jit(cholesky)/cholesky | solution.py:57
  328.7 19.7 %custom-call.41 = f32[2,128,128]{1,2,0:T(8,128)S(1)} custom-call(f32[2,128,128]{2,1,0:T(8,128)S(1)} %pad_maximum_fusion.35), custom_call_target="InvertDiagBlocksLowerTriangular" | custom-call | tf_op jit(solution)/shard_map/while/body/eval_jaxpr/jit(_cho_solve)/triangular_solve | solution.py:58
  357.7 11.7 %cholesky.770 = f32[128,128]{1,0:T(8,128)S(1)} custom-call(f32[128,128]{1,0:T(8,128)S(1)} %cholesky.769), custom_call_target="Cholesky" | custom-call | tf_op jit(solution)/shard_map/while/body/eval_jaxpr/jit(cholesky)/cholesky | solution.py:57
  369.5 9.8 %custom-call.40 = f32[1,128,128]{1,2,0:T(8,128)S(1)} custom-call(f32[1,128,128]{2,1,0:T(8,128)S(1)} %get-tuple-element.725), custom_call_target="InvertDiagBlocksLowerTriangular" | custom-call | tf_op jit(solution)/shard_map/while/body/eval_jaxpr/jit(cholesky)/cholesky | solution.py:57
  388.4 19.7 %custom-call.41 = f32[2,128,128]{1,2,0:T(8,128)S(1)} custom-call(f32[2,128,128]{2,1,0:T(8,128)S(1)} %pad_maximum_fusion.35), custom_call_target="InvertDiagBlocksLowerTriangular" | custom-call | tf_op jit(solution)/shard_map/while/body/eval_jaxpr/jit(_cho_solve)/triangular_solve | solution.py:58
  416.3 11.7 %cholesky.350 = f32[128,128]{1,0:T(8,128)S(1)} custom-call(f32[128,128]{1,0:T(8,128)S(1)} %cholesky.466), custom_call_target="Cholesky" | custom-call | tf_op jit(solution)/shard_map/jit(cholesky)/cholesky | solution.py:57
  428.1 9.8 %custom-call.32 = f32[1,128,128]{1,2,0:T(8,128)S(1)} custom-call(f32[1,128,128]{2,1,0:T(8,128)S(1)} %get-tuple-element.597), custom_call_target="InvertDiagBlocksLowerTriangular" | custom-call | tf_op jit(solution)/shard_map/jit(cholesky)/cholesky | solution.py:57
  448.0 20.1 %custom-call.33 = f32[2,128,128]{1,2,0:T(8,128)S(1)} custom-call(f32[2,128,128]{2,1,0:T(8,128)S(1)} %pad_maximum_fusion.15), custom_call_target="InvertDiagBlocksLowerTriangular" | custom-call | tf_op jit(solution)/shard_map/jit(_cho_solve)/triangular_solve | solution.py:58
  471.5 11.7 %cholesky.388 = f32[128,128]{1,0:T(8,128)S(1)} custom-call(f32[128,128]{1,0:T(8,128)S(1)} %cholesky.469), custom_call_target="Cholesky" | custom-call | tf_op jit(solution)/shard_map/jit(cholesky)/cholesky | solution.py:57
  483.3 9.8 %custom-call.34 = f32[1,128,128]{1,2,0:T(8,128)S(1)} custom-call(f32[1,128,128]{2,1,0:T(8,128)S(1)} %get-tuple-element.595), custom_call_target="InvertDiagBlocksLowerTriangular" | custom-call | tf_op jit(solution)/shard_map/jit(cholesky)/cholesky | solution.py:57
  503.4 19.8 %custom-call.35 = f32[2,128,128]{1,2,0:T(8,128)S(1)} custom-call(f32[2,128,128]{2,1,0:T(8,128)S(1)} %pad_maximum_fusion.16), custom_call_target="InvertDiagBlocksLowerTriangular" | custom-call | tf_op jit(solution)/shard_map/jit(_cho_solve)/triangular_solve | solution.py:58
  526.6 11.7 %cholesky.426 = f32[128,128]{1,0:T(8,128)S(1)} custom-call(f32[128,128]{1,0:T(8,128)S(1)} %cholesky.472), custom_call_target="Cholesky" | custom-call | tf_op jit(solution)/shard_map/jit(cholesky)/cholesky | solution.py:57
  564.8 19.9 %custom-call.37 = f32[2,128,128]{1,2,0:T(8,128)S(1)} custom-call(f32[2,128,128]{2,1,0:T(8,128)S(1)} %pad_maximum_fusion.17), custom_call_target="InvertDiagBlocksLowerTriangular" | custom-call | tf_op jit(solution)/shard_map/jit(_cho_solve)/triangular_solve | solution.py:58
  590.2 16.2 %all-gather.6 = f32[768,192]{1,0:T(8,128)S(1)} all-gather(f32[192,192]{1,0:T(8,128)S(1)} %convolution_negate_fusion.1), channel_id=8, replica_groups=mesh['cfg'=2,'slab'=4,'energy'=4] {'slab'}, dimensions={0}, use_global_device_ids=true | all-gather | bytes 737280 | tf_op jit(solution)/shard_map/all_gather | solution.py:23
  606.4 14.2 %all-gather.5 = f32[768,128]{1,0:T(8,128)S(1)} all-gather(f32[192,128]{1,0:T(8,128)S(1)} %convolution_subtract_fusion.18), channel_id=7, replica_groups=mesh['cfg'=2,'slab'=4,'energy'=4] {'slab'}, dimensions={0}, use_global_device_ids=true | all-gather | bytes 491520 | tf_op jit(solution)/shard_map/all_gather | solution.py:23
  (377 shorter events, 175.0 us)
Async XLA Ops:
  0.6 3.2 copy-start.17
  1.7 71.3 %copy-start.2 = (f32[192,192]{0,1:T(8,128)}, f32[192,192]{0,1:T(8,128)S(1)}, u32[]{:S(2)}) copy-start(f32[192,192]{0,1:T(8,128)S(1)} %get-tuple-element.583) | copy-start | bytes 442372
  1.7 17.7 %copy-start.16 = (f32[2,192,192]{2,1,0:T(8,128)S(1)}, f32[2,192,192]{2,1,0:T(8,128)}, u32[]{:S(2)}) copy-start(f32[2,192,192]{2,1,0:T(8,128)} %param.17) | copy-start | bytes 884740
  2.5 583.0 %collective-permute-start.2 = (f32[192,192]{0,1:T(8,128)}, f32[192,192]{0,1:T(8,128)}, u32[]{:S(2)}, u32[]{:S(2)}) collective-permute-start(f32[192,192]{0,1:T(8,128)} %bitcast.3), channel_id=1, source_target_pairs={{4,0},{8,4},{12,8},{5,1},{9,5},{13,9},{6,2},{10,6},{14,10},{7,3},{... | collective-permute-start | bytes 442376 | tf_op jit(solution)/shard_map/ppermute | solution.py:18
  11.1 8.4 %copy-start.4 = (f32[8,64,128]{2,1,0:T(8,128)}, f32[8,64,128]{2,1,0:T(8,128)S(1)}, u32[]{:S(2)}) copy-start(f32[8,64,128]{2,1,0:T(8,128)S(1)} %all_gather.49) | copy-start | bytes 786436
  11.7 572.9 %collective-permute-start = (f32[1,64,128]{2,1,0:T(8,128)}, f32[1,64,128]{2,1,0:T(8,128)}, u32[]{:S(2)}, u32[]{:S(2)}) collective-permute-start(f32[1,64,128]{2,1,0:T(8,128)} %get-tuple-element.591), channel_id=1, source_target_pairs={{4,0},{8,4},{12,8},{5,1},{9,5},{13,9},{6,2},{10,6},{14,10},{7,3},{... | collective-permute-start | bytes 98312 | tf_op jit(solution)/shard_map/ppermute | solution.py:47
  13.0 571.7 %collective-permute-start.1 = (f32[1,64,128]{2,1,0:T(8,128)}, f32[1,64,128]{2,1,0:T(8,128)}, u32[]{:S(2)}, u32[]{:S(2)}) collective-permute-start(f32[1,64,128]{2,1,0:T(8,128)} %get-tuple-element.590), channel_id=1, source_target_pairs={{0,4},{4,8},{8,12},{1,5},{5,9},{9,13},{2,6},{6,10},{10,14},{3,7},{... | collective-permute-start | bytes 98312 | tf_op jit(solution)/shard_map/ppermute | solution.py:44
  19.7 0.7 copy-start.8
  72.0 0.9 slice-start
  76.3 1.0 copy-start
  76.3 1.0 copy-start.12
  78.8 0.7 copy-start.10
  164.3 0.7 copy-start.21
  177.3 51.8 %copy-start.6 = (f32[4,192,128]{2,1,0:T(8,128)}, f32[4,192,128]{2,1,0:T(8,128)S(1)}, u32[]{:S(2)}) copy-start(f32[4,192,128]{2,1,0:T(8,128)S(1)} %get-tuple-element.779) | copy-start | bytes 1179652 | tf_op jit(solution)/shard_map/while
  235.7 1.3 copy-start.7
  237.0 51.8 %copy-start.6 = (f32[4,192,128]{2,1,0:T(8,128)}, f32[4,192,128]{2,1,0:T(8,128)S(1)}, u32[]{:S(2)}) copy-start(f32[4,192,128]{2,1,0:T(8,128)S(1)} %get-tuple-element.779) | copy-start | bytes 1179652 | tf_op jit(solution)/shard_map/while
  295.3 1.3 copy-start.7
  296.7 51.8 %copy-start.6 = (f32[4,192,128]{2,1,0:T(8,128)}, f32[4,192,128]{2,1,0:T(8,128)S(1)}, u32[]{:S(2)}) copy-start(f32[4,192,128]{2,1,0:T(8,128)S(1)} %get-tuple-element.779) | copy-start | bytes 1179652 | tf_op jit(solution)/shard_map/while
  355.0 1.3 copy-start.7
  356.3 51.8 %copy-start.6 = (f32[4,192,128]{2,1,0:T(8,128)}, f32[4,192,128]{2,1,0:T(8,128)S(1)}, u32[]{:S(2)}) copy-start(f32[4,192,128]{2,1,0:T(8,128)S(1)} %get-tuple-element.779) | copy-start | bytes 1179652 | tf_op jit(solution)/shard_map/while
  414.6 1.3 copy-start.7
  470.1 0.9 copy-start.9
  502.1 0.9 copy-start.15
  503.3 20.0 %copy-start.3 = (f32[192,192]{0,1:T(8,128)S(1)}, f32[192,192]{0,1:T(8,128)}, u32[]{:S(2)}) copy-start(f32[192,192]{0,1:T(8,128)} %copy-done.2) | copy-start | bytes 442372
  524.4 1.0 copy-start.1
  524.9 1.0 copy-start.11
  557.1 1.3 copy-start.18
  557.2 0.9 copy-start.13
  564.7 20.0 %copy-start.5 = (f32[8,64,128]{2,1,0:T(8,128)S(1)}, f32[8,64,128]{2,1,0:T(8,128)}, u32[]{:S(2)}) copy-start(f32[8,64,128]{2,1,0:T(8,128)} %copy-done.4) | copy-start | bytes 786436
  622.9 5.7 copy-start.19
  633.7 5.9 collective-permute-start.3
  635.0 6.1 collective-permute-start.4
  (2 other events, 1.2 us)
where the time goes:
time: 649 us; the launch traced here: 642 us
  other arithmetic  406 us (63%)
  blocking collectives  139 us (21%)
  matrix products  38.2 us (6%)
  local copies, waits for them, and re-layouts  22.1 us (3%)
  starting transfers between devices  14.2 us (2%)
  loops' own time  13.8 us (2%)
  between operations  7.93 us (1%)
    another operation x56, other arithmetic, solve_definite(): factor = jnp.linalg.cholesky(matrix)  230 us
    another operation x43, other arithmetic, solve_definite(): return jax.scipy.linalg.cho_solve((factor, True), right_side)  160 us
    all_gather x7, blocking collectives, entering(): everything = jax.tree.map(lambda part: lax.all_gather(part, axis), shard)  115 us
    another operation x48, matrix products, solve_definite(): return jax.scipy.linalg.cho_solve((factor, True), right_side)  18.7 us
    dot_general x29, matrix products, product(): jnp.dot(left, right, precision=lax.Precision.HIGHEST, preferred_element_t...  16.6 us
    another operation x2, loops' own time, entering(): return lax.fori_loop(0, peers, step, start)  13.8 us
  transfers between devices with their start and end apart: 5, of which 1 were waited for; matrix products, arithmetic and copies ran while one was open for 69% of the time, Pallas kernels for 0%

commit v1 on v0

v1 whole, which is shorter than its diff:
```python
import functools

import jax
import jax.numpy as jnp
from jax import lax
from jax.experimental import pallas as pl
from jax.experimental.pallas import tpu as pltpu
from jax.sharding import PartitionSpec as P

SWEEPS = 2

sigma_base = 0.02
sigma_step = 0.01
coupling_beta = 0.5
dopant_charge = 4.0

F32 = jnp.float32
BF16 = jnp.bfloat16
NT = (((1,), (1,)), ((), ()))
NN = (((1,), (0,)), ((), ()))


def split2(a):
    high = a.astype(BF16)
    return high, (a - high.astype(F32)).astype(BF16)


def one_pass(a, b, dims=NN):
    return lax.dot_general(a, b, dims, preferred_element_type=F32)


def dot3(a, b):
    ah, al = split2(a)
    bh, bl = split2(b)
    return one_pass(ah, bh) + (one_pass(ah, bl) + one_pass(al, bh))


def dot6(a, b, dims=NN):
    return lax.dot_general(
        a, b, dims, precision=lax.Precision.HIGHEST, preferred_element_type=F32
    )


def eye(n):
    return (
        lax.broadcasted_iota(jnp.int32, (n, n), 0) == lax.broadcasted_iota(jnp.int32, (n, n), 1)
    ).astype(F32)


def invert(matrix, hold, ratio, doublings):
    unit = eye(matrix.shape[0])
    sums = jnp.sum(jnp.abs(matrix), axis=0, keepdims=True)
    bound = jnp.max(sums, axis=1, keepdims=True)
    first = 2.0 / (bound * (1.0 + ratio))
    error = unit - first * matrix
    guess = first * unit
    tau = (1.0 + ratio) / (1.0 - ratio)
    for k in range(doublings):
        after = 2.0 * tau * tau - 1.0
        scale = (after + 1.0) / after
        if k == 0:
            grown = guess + first * error
        else:
            grown = guess + dot3(guess, error)
        if k + 1 < doublings:
            error = scale * dot3(error, error) - (scale - 1.0) * unit
        guess = scale * grown
        tau = after
    residual = unit - dot6(matrix, guess)
    size = jnp.sum(residual * residual)
    hold[...] = guess + dot3(guess, residual)

    @pl.when(jnp.logical_not(size < 0.9))
    def _():
        hold[...] = first * unit

    def go_on(state):
        count, last = state
        return jnp.logical_and(count < 64, jnp.logical_not(last < 1e-5))

    def newton(state):
        count, _ = state
        now = hold[...]
        left = unit - dot6(matrix, now)
        hold[...] = now + dot6(now, left)
        return count + 1, jnp.sum(left * left)

    lax.while_loop(go_on, newton, (jnp.int32(0), size))
    return hold[...]


def pack_symmetric(matrix, out):
    half = matrix.shape[0] // 3
    out[0:half, :] = matrix[half : 2 * half, 0 : 2 * half]
    out[half : 2 * half, :] = matrix[2 * half :, 0 : 2 * half]
    out[2 * half : 3 * half, :] = jnp.concatenate(
        [matrix[0:half, 0:half], matrix[2 * half :, 2 * half :]], axis=1
    )


def unpack_symmetric(packed):
    third = packed.shape[0] // 3
    row1 = packed[0:third]
    row2 = packed[third : 2 * third]
    ends = packed[2 * third :]
    b10, b11 = row1[:, :third], row1[:, third:]
    b20, b21 = row2[:, :third], row2[:, third:]
    b00, b22 = ends[:, :third], ends[:, third:]
    return jnp.concatenate(
        [
            jnp.concatenate([b00, b10.T, b20.T], axis=1),
            jnp.concatenate([b10, b11, b21.T], axis=1),
            jnp.concatenate([b20, b21, b22], axis=1),
        ],
        axis=0,
    )


def stage_kernel(has_message, ratios, doublings, place, energy, diag, couple, probes, message,
                 factor_p, value_p, matrix_q, source_q, inverse_q, value_q, out, hold):
    left = place[0] > 0
    right_index = 1 - place[0]
    width = diag.shape[1]
    unit = eye(width)
    shift = sigma_base + sigma_step * jnp.full((1, 1), energy[0], jnp.int32).astype(F32)
    shifted = shift * unit
    sp = diag[right_index] + shifted
    rp = probes[pl.ds(pl.multiple_of(right_index * width, width), width), :]
    rq = probes[pl.ds(pl.multiple_of((1 - right_index) * width, width), width), :]
    if has_message:
        taken = place[1] > 0
        block = jnp.where(taken, unpack_symmetric(message[0:width, :]), 0.0)
        column = jnp.where(taken, message[width : 2 * width, :], 0.0)
        outer = couple[0]
        matrix_q[...] = block
        source_q[...] = column

        @pl.when(left)
        def _():
            matrix_q[...] = dot3(outer, dot3(block, outer.T))
            source_q[...] = dot3(outer, column)

        sp = sp - matrix_q[...]
        rp = rp - source_q[...]
    inner = couple[1]
    inner_t = inner.T
    apq = jnp.where(left, inner_t, inner)
    aqp = jnp.where(left, inner, inner_t)
    xp = invert(sp, hold, ratios[0], doublings[0])
    fp = dot3(xp, apq)
    yp = dot3(xp, rp)
    factor_p[...] = fp
    value_p[...] = yp
    sq = diag[1 - right_index] + shifted - dot3(aqp, fp)
    rq = rq - dot3(aqp, yp)
    matrix_q[...] = sq
    source_q[...] = rq
    xq = invert(sq, hold, ratios[1], doublings[1])
    yq = dot3(xq, rq)
    inverse_q[...] = xq
    value_q[...] = yq

    @pl.when(left)
    def _():
        pack_symmetric(xq, out)
        out[width : 2 * width, :] = yq

    @pl.when(jnp.logical_not(left))
    def _():
        own = couple[0]
        own_t = own.T
        pack_symmetric(dot3(own_t, dot3(xq, own)), out)
        out[width : 2 * width, :] = dot3(own_t, yq)


def join_kernel(ratio, doublings, place, couple, message, factor_p, value_p, matrix_q, source_q,
                out_p, out_q, out, hold, hold_r):
    left = place[0] > 0
    width = couple.shape[1]
    block = unpack_symmetric(message[0:width, :])
    column = message[width : 2 * width, :]
    hold[...] = block
    hold_r[...] = column

    @pl.when(jnp.logical_not(left))
    def _():
        own = couple[0]
        hold[...] = dot3(own, dot3(block, own.T))
        hold_r[...] = dot3(own, column)

    sq = matrix_q[...] - hold[...]
    rq = source_q[...] - hold_r[...]
    xq = dot3(invert(sq, hold, ratio, doublings), rq)
    xp = value_p[...] - dot3(factor_p[...], xq)
    out_p[...] = xp
    out_q[...] = xq
    out[...] = xp

    @pl.when(left)
    def _():
        out[...] = dot3(couple[0].T, xp)


def back_kernel(place, couple, probes, message, known_p, known_q, factor_p, value_p, inverse_q,
                value_q, out_p, out_q, out, dens):
    left = place[0] > 0
    width = couple.shape[1]
    out_p[...] = known_p[...]
    out_q[...] = known_q[...]

    @pl.when(place[1] > 0)
    def _():
        out_q[...] = message[...]

        @pl.when(jnp.logical_not(left))
        def _():
            out_q[...] = dot3(couple[0], message[...])

        xq = value_q[...] - dot3(inverse_q[...], out_q[...])
        out_q[...] = xq
        out_p[...] = value_p[...] - dot3(factor_p[...], xq)

    xp = out_p[...]
    xq = out_q[...]
    out[...] = xp

    @pl.when(left)
    def _():
        out[...] = dot3(couple[0].T, xp)

    xa = jnp.where(left, xp, xq)
    xb = jnp.where(left, xq, xp)
    terms = jnp.concatenate([probes[0:width, :] * xa, probes[width:, :] * xb], axis=0)
    dens[...] = dot6(jnp.ones((8, terms.shape[1]), F32), terms, NT)


def poisson_kernel(rows_all, cells, place, weights, orbitals, dopants, around, out, fine):
    depth, pitch, across = around.shape
    total = depth * pitch
    first_z, first_x, planes = place[0], place[1], place[2]
    plane = rows_all * across

    def spots(index):
        z = index // plane - first_z
        x = index // across % rows_all - first_x
        y = index % across
        inside = (z >= 0) & (z < depth) & (x >= 0) & (x < pitch)
        row = jnp.where(inside, z * pitch + x, -1)
        n = index.shape[1]
        pick_row = lax.broadcasted_iota(jnp.int32, (total, n), 0) == row
        pick_y = lax.broadcasted_iota(jnp.int32, (across, n), 0) == y
        return pick_row.astype(F32).astype(BF16), pick_y.astype(F32)

    rows, ys = spots(dopants[...])
    dopant = dopant_charge * one_pass(rows, ys.astype(BF16), NT)
    rows, ys = spots(orbitals[...])
    spread = ys * weights[...]
    h = spread.astype(BF16)
    rest = spread - h.astype(F32)
    m = rest.astype(BF16)
    low = (rest - m.astype(F32)).astype(BF16)
    electron = one_pass(rows, h, NT) + (one_pass(rows, m, NT) + one_pass(rows, low, NT))
    electron = electron.reshape(depth, pitch, across)
    dopant = dopant.reshape(depth, pitch, across)
    start = around[...]
    zs = lax.broadcasted_iota(jnp.int32, start.shape, 0) + first_z
    xs = lax.broadcasted_iota(jnp.int32, start.shape, 1) + first_x
    ys = lax.broadcasted_iota(jnp.int32, start.shape, 2)
    exists = (zs >= 0) & (zs < planes) & (xs >= 0) & (xs < rows_all)
    potential = jnp.where(exists, start, 0.0)
    start = potential
    strength = coupling_beta * jnp.abs(electron)
    for _ in range(SWEEPS):
        blank = jnp.zeros((1, pitch, across), F32)
        beside = jnp.concatenate([potential[1:], blank], axis=0)
        beside = beside + jnp.concatenate([blank, potential[:-1]], axis=0)
        beside = beside + pltpu.roll(potential, 1, 1) + pltpu.roll(potential, pitch - 1, 1)
        beside = beside + jnp.where(ys > 0, pltpu.roll(potential, 1, 2), 0.0)
        beside = beside + jnp.where(ys < across - 1, pltpu.roll(potential, across - 1, 2), 0.0)
        growth = jnp.exp(potential - start)
        residual = beside - 6.0 * potential + coupling_beta * (dopant - electron * growth)
        potential = potential + residual / (6.0 + strength * growth)
        potential = jnp.where(exists, potential, 0.0)
    halo = SWEEPS
    out[...] = potential[halo : halo + out.shape[0], halo : halo + out.shape[1], :]


VM = pl.BlockSpec(memory_space=pltpu.VMEM)
SM = pl.BlockSpec(memory_space=pltpu.SMEM)


def like(*shape, dtype=F32):
    return jax.ShapeDtypeStruct(shape, dtype)


def pairs_of(count, odd):
    found = []
    for first in range(1 if odd else 0, count - 1, 2):
        found += [(first, first + 1), (first + 1, first)]
    return found


def slab_exchange(value, odd):
    slabs, energies = lax.axis_size("slab"), lax.axis_size("energy")
    pairs = pairs_of(slabs, odd)
    busy = {a for a, _ in pairs}
    whole = [(a * energies + e, b * energies + e) for a, b in pairs for e in range(energies)]
    for a in range(slabs):
        if a not in busy:
            whole += [(a * energies + e, a * energies + (e ^ 1)) for e in range(energies)]
    return lax.ppermute(value, ("slab", "energy"), whole)


def energy_exchange(value, odd):
    energies = lax.axis_size("energy")
    pairs = pairs_of(energies, odd)
    if odd:
        pairs += [(energies - 1, 0), (0, energies - 1)]
    return lax.ppermute(value, "energy", pairs)


def body(energy_index, diag_blocks, couple, probes, orbital_cell, dopant_cells, initial_potential):
    width = diag_blocks.shape[1]
    probe_count = probes.shape[1]
    slab, slabs = lax.axis_index("slab"), lax.axis_size("slab")
    energy, energies = lax.axis_index("energy"), lax.axis_size("energy")
    half = slabs // 2
    left = slab < half
    distance = jnp.where(left, slab, slabs - 1 - slab)
    left_flag = left.astype(jnp.int32)
    square, column = like(width, width), like(width, probe_count)
    letter = like(2 * width, probe_count)

    def flags(second):
        return jnp.stack([left_flag, second.astype(jnp.int32)])

    message = None
    for t in range(half):
        if t == 0:
            inbound = jnp.zeros((8, 128), F32)
        elif t == 1:
            inbound = message
        else:
            inbound = jnp.where(distance == t, message, kept)
        kept = inbound
        if t == 1:
            kept = jnp.where(distance == t, message, 0.0) if half > 2 else inbound
        accept = (distance >= 1) & (distance <= t)
        state = pl.pallas_call(
            functools.partial(stage_kernel, t > 0, (1 / 16, 1 / 16), (4, 4)),
            out_shape=(square, column, square, column, square, column, letter),
            in_specs=[SM, SM, VM, VM, VM, VM],
            out_specs=(VM,) * 7,
            scratch_shapes=[pltpu.VMEM((width, width), F32)],
            name=f"stage{t}",
        )(flags(accept), energy_index, diag_blocks, couple, probes, inbound)
        factor_p, value_p, matrix_q, source_q, inverse_q, value_q, sent = state
        message = slab_exchange(sent, t % 2 == 1)
    out_p, out_q, sent = pl.pallas_call(
        functools.partial(join_kernel, 1 / 128, 6),
        out_shape=(column, column, column),
        in_specs=[SM] + [VM] * 6,
        out_specs=(VM,) * 3,
        scratch_shapes=[pltpu.VMEM((width, width), F32), pltpu.VMEM((width, probe_count), F32)],
        name="join",
    )(flags(left), couple, message, factor_p, value_p, matrix_q, source_q)
    for t in range(half - 2, -1, -1):
        message = slab_exchange(sent, t % 2 == 1)
        out_p, out_q, sent, dens = pl.pallas_call(
            back_kernel,
            out_shape=(column, column, column, like(8, 2 * width)),
            in_specs=[SM] + [VM] * 9,
            out_specs=(VM,) * 4,
            name=f"back{t}",
        )(flags(distance == t), couple, probes, message, out_p, out_q, factor_p, value_p,
          inverse_q, value_q)
    total = dens
    for k in range(1, energies):
        total = total + lax.ppermute(
            dens, "energy", [(e, e ^ k) for e in range(energies)]
        )
    total = total[0:1] * (1.0 / (probe_count * energies))
    density = total.reshape(-1)

    cells_here = orbital_cell.reshape(1, -1)
    packet = jnp.concatenate([total, cells_here.astype(F32)], axis=0)
    near = slab_exchange(packet, False)
    far = slab_exchange(packet, True)
    weights = jnp.concatenate([total, near[0:1], far[0:1]], axis=1)
    alone = (slab == 0) | (slab == slabs - 1)
    nobody = jnp.int32(-(2**30))
    orbitals = jnp.concatenate(
        [cells_here, near[1:2].astype(jnp.int32),
         jnp.where(alone, nobody, far[1:2].astype(jnp.int32))],
        axis=1,
    )

    depth, rows_here, across = initial_potential.shape
    halo = SWEEPS
    odd_e = energy % 2 == 1
    low, high = initial_potential[:, :halo], initial_potential[:, rows_here - halo :]
    got_even = energy_exchange(jnp.where(odd_e, low, high), False)
    got_odd = energy_exchange(jnp.where(odd_e, high, low), True)
    below = jnp.where(odd_e, got_even, got_odd)
    above = jnp.where(odd_e, got_odd, got_even)
    wide = jnp.concatenate([below, initial_potential, above], axis=1)
    odd_s = slab % 2 == 1
    low, high = wide[:halo], wide[depth - halo :]
    got_even = slab_exchange(jnp.where(odd_s, low, high), False)
    got_odd = slab_exchange(jnp.where(odd_s, high, low), True)
    below = jnp.where(odd_s, got_even, got_odd)
    above = jnp.where(odd_s, got_odd, got_even)
    region = jnp.concatenate([below, wide, above], axis=0)
    pitch = -(-region.shape[1] // 8) * 8
    region = jnp.pad(region, ((0, 0), (0, pitch - region.shape[1]), (0, 0)))
    rows_all = rows_here * energies
    place = jnp.stack([slab * depth - halo, energy * rows_here - halo, jnp.int32(depth * slabs)])
    potential = pl.pallas_call(
        functools.partial(poisson_kernel, rows_all, None),
        out_shape=like(depth, rows_here, across),
        in_specs=[SM] + [VM] * 4,
        out_specs=VM,
        scratch_shapes=[pltpu.VMEM((8, 128), F32)],
        name="poisson",
    )(place, weights, orbitals, dopant_cells.reshape(1, -1), region)
    return (potential, density)


def solution(mesh):
    placed = (
        P("energy"),
        P(("cfg", "slab"), None, None),
        P(("cfg", "slab"), None, None),
        P("slab", None),
        P("slab"),
        P("cfg"),
        P(("cfg", "slab"), "energy", None),
    )
    return jax.shard_map(
        body,
        mesh=mesh,
        in_specs=placed,
        out_specs=(P(("cfg", "slab"), "energy", None), P(("cfg", "slab"))),
        check_vma=False,
    )
```

time: 649 us -> 118 us (0.18)
  other arithmetic: 406 us -> 6.4 us
  blocking collectives: 139 us -> 0 us
  starting transfers between devices: 14.2 us -> 68.9 us
  matrix products: 38.2 us -> 0 us
  Pallas kernels: 0 us -> 30 us
  local copies, waits for them, and re-layouts: 22.1 us -> 4.65 us
  loops' own time: 13.8 us -> 0 us
  between operations: 7.93 us -> 1.36 us
    another operation x99 -> x5, other arithmetic: 390 us -> 3.16 us  [the longest x4 2.49 us: flags(): return jnp.stack([left_flag, second.astype(jnp.int32)])]
    all_gather x8 -> x0, blocking collectives: 122 us -> none  [the longest x7 115 us: entering(): everything = jax.tree.map(lambda part: lax.all_gather(part, axis), shard)]
    ppermute x5 -> x12, starting transfers between devices: 14.2 us -> 68.9 us  [the longest x7 65.4 us: slab_exchange(): return lax.ppermute(value, ('slab', 'energy'), whole)]
    pallas_call x0 -> x5, Pallas kernels: none -> 30 us  [the longest x2 18.4 us: body(): pl.pallas_call(functools.partial(stage_kernel, t > 0, (1 / 16, 1 / 16), (...]
    another operation x64 -> x0, matrix products: 21.6 us -> none  [the longest x48 18.7 us: solve_definite(): return jax.scipy.linalg.cho_solve((factor, True), right_side)]
    dot_general x29 -> x0, matrix products: 16.6 us -> none  [product(): jnp.dot(left, right, precision=lax.Precision.HIGHEST, preferred_element_t...]
    another operation x2 -> x0, loops' own time: 13.8 us -> none  [entering(): return lax.fori_loop(0, peers, step, start)]
    unnamed x1 -> x0, blocking collectives: 10.9 us -> none
  transfers between devices with their start and end apart: 5 -> 12, of which waited for: 1 -> 6; matrix products, arithmetic and copies ran while one was open for 69% -> 3% of each run, Pallas kernels for 0% -> 16%
where the time goes in v1:
time: 118 us; the launch traced here: 117 us
  starting transfers between devices  68.9 us (58%)
  Pallas kernels  30 us (25%)
  other arithmetic  6.4 us (5%)
  waiting for transfers between devices  5.91 us (5%)
  local copies, waits for them, and re-layouts  4.65 us (4%)
  between operations  1.36 us (1%)
    ppermute x7, starting transfers between devices, slab_exchange(): return lax.ppermute(value, ('slab', 'energy'), whole)  65.4 us
    pallas_call x2, Pallas kernels, body(): pl.pallas_call(functools.partial(stage_kernel, t > 0, (1 / 16, 1 / 16), (...  18.4 us
    pallas_call x1, Pallas kernels, body(): pl.pallas_call(functools.partial(join_kernel, 1 / 128, 6), out_shape=(col...  5.75 us
    ppermute x7, waiting for transfers between devices, slab_exchange(): return lax.ppermute(value, ('slab', 'energy'), whole)  3.87 us
    unnamed x14, local copies, waits for them, and re-layouts  3.37 us
    pallas_call x1, Pallas kernels, body(): pl.pallas_call(back_kernel, out_shape=(column, column, column, like(8, 2...  3.26 us
    pallas_call x1, Pallas kernels, body(): pl.pallas_call(functools.partial(poisson_kernel, rows_all, None), out_sha...  2.68 us
    another operation x4, other arithmetic, flags(): return jnp.stack([left_flag, second.astype(jnp.int32)])  2.49 us
  transfers between devices with their start and end apart: 12, of which 6 were waited for; matrix products, arithmetic and copies ran while one was open for 3% of the time, Pallas kernels for 16%

profile of v1, /device:TPU:0, one launch (start us, length us, event | category | flops | bytes accessed | tf_op | source)
XLA Modules:
  0.0 117.2 jit_solution(17591338774410545508)
XLA Ops:
  1.3 0.6 pad_add_fusion.5.place
  1.9 0.6 broadcast_in_dim.7.message
  2.5 8.8 %stage0.1 = (f32[192,192]{1,0:T(8,128)}, f32[192,128]{1,0:T(8,128)}, f32[192,192]{1,0:T(8,128)}, f32[192,128]{1,0:T(8,128)}, f32[192,192]{1,0:T(8,128)}, /*index=5*/f32[192,128]{1,0:T(8,128)}, f32[384,128]{1,0:T(8,128)}) custom-call(s32[2]{0:T(128)} %pad_add_fusion.5.place, s32[1]{0:T(128)S(6)} %copy.9.energy, f32[2,192,192]{2,1,0:T(8,128)} %diag.3, ...), custom_call_target="tpu_custom_call" | custom-call | tf_op jit(solution)/shard_map/stage0/pallas_call | solution.py:349
  11.3 3.1 %collective-permute-start = (f32[384,128]{1,0:T(8,128)}, f32[384,128]{1,0:T(8,128)S(1)}, u32[]{:S(2)}, u32[]{:S(2)}) collective-permute-start(f32[384,128]{1,0:T(8,128)} %get-tuple-element.14), channel_id=1, source_target_pairs={{0,4},{1,5},{2,6},{3,7},{4,0},{5,1},{6,2},{7,3},{8,12},{9,13},{10,... | collective-permute-start | bytes 589832 | tf_op jit(solution)/shard_map/ppermute | solution.py:311
  14.4 1.6 %collective-permute-start.9 = (f32[8,2,128]{2,1,0:T(2,128)S(1)}, f32[8,2,128]{2,1,0:T(2,128)S(1)}, u32[]{:S(2)}, u32[]{:S(2)}) collective-permute-start(f32[8,2,128]{2,1,0:T(2,128)S(1)} %get-tuple-element.32), channel_id=1, source_target_pairs={{1,2},{2,1},{3,0},{0,3},{5,6},{6,5},{7,4},{4,7},{9,10},{10,9},{11,... | collective-permute-start | bytes 24584 | tf_op jit(solution)/shard_map/ppermute | solution.py:319
  16.0 0.7 pad_add_fusion.3.place
  16.7 0.7 pad_add_fusion.2.place
  17.3 0.6 pad_add_fusion.4.place
  17.9 0.5 collective-permute-start.10
  18.4 1.0 collective-permute-done.message
  19.4 0.7 copy-done.1
  20.1 9.6 %stage1.1 = (f32[192,192]{1,0:T(8,128)}, f32[192,128]{1,0:T(8,128)}, f32[192,192]{1,0:T(8,128)}, f32[192,128]{1,0:T(8,128)}, f32[192,192]{1,0:T(8,128)}, /*index=5*/f32[192,128]{1,0:T(8,128)}, f32[384,128]{1,0:T(8,128)}) custom-call(s32[2]{0:T(128)} %pad_add_fusion.4.place, s32[1]{0:T(128)S(6)} %copy.9.energy, f32[2,192,192]{2,1,0:T(8,128)} %diag.3, ...), custom_call_target="tpu_custom_call" | custom-call | tf_op jit(solution)/shard_map/stage1/pallas_call | solution.py:349
  29.7 0.5 collective-permute-start.11
  30.2 1.1 collective-permute-done.1.message
  31.4 0.7 copy-done.2
  32.0 5.7 %join.1 = (f32[192,128]{1,0:T(8,128)}, f32[192,128]{1,0:T(8,128)}, f32[192,128]{1,0:T(8,128)}) custom-call(s32[2]{0:T(128)} %pad_add_fusion.3.place, f32[2,192,192]{2,1,0:T(8,128)} %couple.7, f32[384,128]{1,0:T(8,128)} %copy-done.2, f32[192,192]{1,0:T(8,128)} %get-tuple-element.16.factor_p, f32[192,128]{1,0:T(8,128)} %get-tuple-element.17.value_p, ...), custom_call_target="tpu_custom_call" | custom-call | tf_op jit(solution)/shard_map/join/pallas_call | solution.py:359
  37.8 6.6 %collective-permute-start.2 = (f32[192,128]{1,0:T(8,128)}, f32[192,128]{1,0:T(8,128)S(1)}, u32[]{:S(2)}, u32[]{:S(2)}) collective-permute-start(f32[192,128]{1,0:T(8,128)} %get-tuple-element.20), channel_id=1, source_target_pairs={{0,4},{1,5},{2,6},{3,7},{4,0},{5,1},{6,2},{7,3},{8,12},{9,13},{10,... | collective-permute-start | bytes 294920 | tf_op jit(solution)/shard_map/ppermute | solution.py:311
  44.4 0.7 pad_add_fusion.1.place
  45.1 0.7 copy-done.4
  45.8 1.4 %collective-permute-done.2.message = f32[192,128]{1,0:T(8,128)S(1)} collective-permute-done((f32[192,128]{1,0:T(8,128)}, f32[192,128]{1,0:T(8,128)S(1)}, u32[]{:S(2)}, u32[]{:S(2)}) %collective-permute-start.2) | collective-permute-done | bytes 98336 | tf_op jit(solution)/shard_map/ppermute | solution.py:311
  47.2 0.6 copy-done.3
  47.9 3.3 %back0.1 = (f32[192,128]{1,0:T(8,128)}, f32[192,128]{1,0:T(8,128)}, f32[192,128]{1,0:T(8,128)}, f32[8,384]{1,0:T(8,128)}) custom-call(s32[2]{0:T(128)} %pad_add_fusion.2.place, f32[2,192,192]{2,1,0:T(8,128)} %couple.7, f32[384,128]{1,0:T(8,128)} %probes.5, f32[192,128]{1,0:T(8,128)} %copy-done.3, f32[192,128]{1,0:T(8,128)} %get-tuple-element.21.known_p, ...), custom_call_target="tpu_custom_call" | custom-call | tf_op jit(solution)/shard_map/back0/pallas_call | solution.py:369
  51.1 1.5 %collective-permute-start.4 = (f32[8,384]{1,0:T(8,128)}, f32[8,384]{1,0:T(8,128)S(1)}, u32[]{:S(2)}, u32[]{:S(2)}) collective-permute-start(f32[8,384]{1,0:T(8,128)} %get-tuple-element.25), channel_id=1, source_target_pairs={{0,2},{1,3},{2,0},{3,1},{4,6},{5,7},{6,4},{7,5},{8,10},{9,11},{10,... | collective-permute-start | bytes 36872 | tf_op jit(solution)/shard_map/ppermute | solution.py:379
  53.0 1.6 %collective-permute-done.5 = f32[8,384]{1,0:T(8,128)S(1)} collective-permute-done((f32[8,384]{1,0:T(8,128)}, f32[8,384]{1,0:T(8,128)S(1)}, u32[]{:S(2)}, u32[]{:S(2)}) %collective-permute-start.5) | collective-permute-done | bytes 12320 | tf_op jit(solution)/shard_map/ppermute | solution.py:379
  55.0 1.3 %fusion.6 = (f32[384]{0:T(512)}, f32[1,384]{1,0:T(1,128)S(1)}) fusion(f32[8,384]{1,0:T(8,128)S(1)} %collective-permute-done.5, f32[8,384]{1,0:T(8,128)S(1)} %collective-permute-done.4, f32[8,384]{1,0:T(8,128)S(1)} %collective-permute-done.3, f32[8,384]{1,0:T(8,128)} %get-tuple-element.25), kind=kLoop, calls=%fused_computation.34 | loop fusion | flops 1536 | bytes 9216 | tf_op jit(solution)/shard_map/mul | solution.py:382
  56.8 54.2 %collective-permute-start.6 = (f32[2,384]{1,0:T(2,128)S(1)}, f32[2,384]{1,0:T(2,128)S(1)}, u32[]{:S(2)}, u32[]{:S(2)}) collective-permute-start(f32[2,384]{1,0:T(2,128)S(1)} %pad_maximum_fusion.4), channel_id=1, source_target_pairs={{0,4},{1,5},{2,6},{3,7},{4,0},{5,1},{6,2},{7,3},{8,12},{9,13},{10,... | collective-permute-start | bytes 9224 | tf_op jit(solution)/shard_map/ppermute | solution.py:311
  111.0 0.7 select_maximum_fusion.around
  111.7 0.6 copy-done.5
  112.6 0.7 slice-done
  113.3 0.6 pad_maximum_fusion.3.weights
  114.0 0.6 pad_add_fusion.orbitals
  114.6 2.7 %poisson.1 = f32[8,16,128]{2,1,0:T(8,128)} custom-call(s32[3]{0:T(128)} %pad_add_fusion.1.place, f32[1,1152]{1,0:T(1,128)} %pad_maximum_fusion.3.weights, s32[1,1152]{1,0:T(1,128)} %pad_add_fusion.orbitals, s32[1,1024]{1,0:T(1,128)} %bitcast.17, f32[12,24,128]{2,1,0:T(8,128)} %select_maximum_fusion.around), custom_call_target="tpu_custom_call" | custom-call | tf_op jit(solution)/shard_map/poisson/pallas_call | solution.py:418
  (34 shorter events, 1.8 us)
Async XLA Ops:
  2.5 11.8 %copy-start = (f32[8,16,128]{2,1,0:T(8,128)S(1)}, f32[8,16,128]{2,1,0:T(8,128)}, u32[]{:S(2)}) copy-start(f32[8,16,128]{2,1,0:T(8,128)} %param.13) | copy-start | bytes 196612
  11.3 8.2 %collective-permute-start = (f32[384,128]{1,0:T(8,128)}, f32[384,128]{1,0:T(8,128)S(1)}, u32[]{:S(2)}, u32[]{:S(2)}) collective-permute-start(f32[384,128]{1,0:T(8,128)} %get-tuple-element.14), channel_id=1, source_target_pairs={{0,4},{1,5},{2,6},{3,7},{4,0},{5,1},{6,2},{7,3},{8,12},{9,13},{10,... | collective-permute-start | bytes 589832 | tf_op jit(solution)/shard_map/ppermute | solution.py:311
  14.3 3.6 %collective-permute-start.8 = (f32[8,2,128]{2,1,0:T(2,128)S(1)}, f32[8,2,128]{2,1,0:T(2,128)S(1)}, u32[]{:S(2)}, u32[]{:S(2)}) collective-permute-start(f32[8,2,128]{2,1,0:T(2,128)S(1)} %get-tuple-element.31), channel_id=1, source_target_pairs={{0,1},{1,0},{2,3},{3,2},{4,5},{5,4},{6,7},{7,6},{8,9},{9,8},{10,11... | collective-permute-start | bytes 24584 | tf_op jit(solution)/shard_map/ppermute | solution.py:319
  14.4 3.5 %collective-permute-start.9 = (f32[8,2,128]{2,1,0:T(2,128)S(1)}, f32[8,2,128]{2,1,0:T(2,128)S(1)}, u32[]{:S(2)}, u32[]{:S(2)}) collective-permute-start(f32[8,2,128]{2,1,0:T(2,128)S(1)} %get-tuple-element.32), channel_id=1, source_target_pairs={{1,2},{2,1},{3,0},{0,3},{5,6},{6,5},{7,4},{4,7},{9,10},{10,9},{11,... | collective-permute-start | bytes 24584 | tf_op jit(solution)/shard_map/ppermute | solution.py:319
  17.9 35.1 %collective-permute-start.10 = (f32[2,20,128]{2,1,0:T(8,128)S(1)}, f32[2,20,128]{2,1,0:T(8,128)S(1)}, u32[]{:S(2)}, u32[]{:S(2)}) collective-permute-start(f32[2,20,128]{2,1,0:T(8,128)S(1)} %get-tuple-element.28), channel_id=1, source_target_pairs={{0,4},{1,5},{2,6},{3,7},{4,0},{5,1},{6,2},{7,3},{8,12},{9,13},{10,... | collective-permute-start | bytes 61448 | tf_op jit(solution)/shard_map/ppermute | solution.py:311
  19.4 0.7 copy-start.1
  29.7 1.7 %collective-permute-start.1 = (f32[384,128]{1,0:T(8,128)}, f32[384,128]{1,0:T(8,128)S(1)}, u32[]{:S(2)}, u32[]{:S(2)}) collective-permute-start(f32[384,128]{1,0:T(8,128)} %get-tuple-element.15), channel_id=1, source_target_pairs={{4,8},{5,9},{6,10},{7,11},{8,4},{9,5},{10,6},{11,7},{0,1},{1,0},{2... | collective-permute-start | bytes 589832 | tf_op jit(solution)/shard_map/ppermute | solution.py:311
  29.7 23.3 %collective-permute-start.11 = (f32[2,20,128]{2,1,0:T(8,128)S(1)}, f32[2,20,128]{2,1,0:T(8,128)S(1)}, u32[]{:S(2)}, u32[]{:S(2)}) collective-permute-start(f32[2,20,128]{2,1,0:T(8,128)S(1)} %broadcast_select_fusion.2), channel_id=1, source_target_pairs={{4,8},{5,9},{6,10},{7,11},{8,4},{9,5},{10,6},{11,7},{0,1},{1,0},{2... | collective-permute-start | bytes 61448 | tf_op jit(solution)/shard_map/ppermute | solution.py:311
  31.3 0.7 copy-start.2
  37.8 9.4 %collective-permute-start.2 = (f32[192,128]{1,0:T(8,128)}, f32[192,128]{1,0:T(8,128)S(1)}, u32[]{:S(2)}, u32[]{:S(2)}) collective-permute-start(f32[192,128]{1,0:T(8,128)} %get-tuple-element.20), channel_id=1, source_target_pairs={{0,4},{1,5},{2,6},{3,7},{4,0},{5,1},{6,2},{7,3},{8,12},{9,13},{10,... | collective-permute-start | bytes 294920 | tf_op jit(solution)/shard_map/ppermute | solution.py:311
  45.1 0.7 copy-start.4
  47.2 0.6 copy-start.3
  51.1 3.5 %collective-permute-start.5 = (f32[8,384]{1,0:T(8,128)}, f32[8,384]{1,0:T(8,128)S(1)}, u32[]{:S(2)}, u32[]{:S(2)}) collective-permute-start(f32[8,384]{1,0:T(8,128)} %get-tuple-element.25), channel_id=1, source_target_pairs={{0,3},{1,2},{2,1},{3,0},{4,7},{5,6},{6,5},{7,4},{8,11},{9,10},{10,... | collective-permute-start | bytes 36872 | tf_op jit(solution)/shard_map/ppermute | solution.py:379
  51.1 3.9 %collective-permute-start.4 = (f32[8,384]{1,0:T(8,128)}, f32[8,384]{1,0:T(8,128)S(1)}, u32[]{:S(2)}, u32[]{:S(2)}) collective-permute-start(f32[8,384]{1,0:T(8,128)} %get-tuple-element.25), channel_id=1, source_target_pairs={{0,2},{1,3},{2,0},{3,1},{4,6},{5,7},{6,4},{7,5},{8,10},{9,11},{10,... | collective-permute-start | bytes 36872 | tf_op jit(solution)/shard_map/ppermute | solution.py:379
  52.6 2.5 %collective-permute-start.3 = (f32[8,384]{1,0:T(8,128)}, f32[8,384]{1,0:T(8,128)S(1)}, u32[]{:S(2)}, u32[]{:S(2)}) collective-permute-start(f32[8,384]{1,0:T(8,128)} %get-tuple-element.25), channel_id=1, source_target_pairs={{0,1},{1,0},{2,3},{3,2},{4,5},{5,4},{6,7},{7,6},{8,9},{9,8},{10,11... | collective-permute-start | bytes 36872 | tf_op jit(solution)/shard_map/ppermute | solution.py:379
  56.4 55.3 %collective-permute-start.7 = (f32[2,384]{1,0:T(2,128)S(1)}, f32[2,384]{1,0:T(2,128)S(1)}, u32[]{:S(2)}, u32[]{:S(2)}) collective-permute-start(f32[2,384]{1,0:T(2,128)S(1)} %pad_maximum_fusion.4), channel_id=1, source_target_pairs={{4,8},{5,9},{6,10},{7,11},{8,4},{9,5},{10,6},{11,7},{0,1},{1,0},{2... | collective-permute-start | bytes 9224 | tf_op jit(solution)/shard_map/ppermute | solution.py:311
  56.8 55.8 %collective-permute-start.6 = (f32[2,384]{1,0:T(2,128)S(1)}, f32[2,384]{1,0:T(2,128)S(1)}, u32[]{:S(2)}, u32[]{:S(2)}) collective-permute-start(f32[2,384]{1,0:T(2,128)S(1)} %pad_maximum_fusion.4), channel_id=1, source_target_pairs={{0,4},{1,5},{2,6},{3,7},{4,0},{5,1},{6,2},{7,3},{8,12},{9,13},{10,... | collective-permute-start | bytes 9224 | tf_op jit(solution)/shard_map/ppermute | solution.py:311
  111.7 0.6 copy-start.5
  112.6 0.7 slice-start
  113.3 0.7 copy-start.6

commit v2 on v1

--- a/solution.py
+++ b/solution.py
@@ -116,99 +116,167 @@
     )
 
 
-def stage_kernel(has_message, ratios, doublings, place, energy, diag, couple, probes, message,
-                 factor_p, value_p, matrix_q, source_q, inverse_q, value_q, out, hold):
-    left = place[0] > 0
-    right_index = 1 - place[0]
+def place():
+    slab, slabs = lax.axis_index("slab"), lax.axis_size("slab")
+    left = slab < slabs // 2
+    return slab, left, jnp.where(left, slab, slabs - 1 - slab)
+
+
+def take_message(message, couple, left, transform_left, block, column):
+    width = block.shape[0]
+    block[...] = unpack_symmetric(message[0:width, :])
+    column[...] = message[width : 2 * width, :]
+
+    @pl.when(left if transform_left else jnp.logical_not(left))
+    def _():
+        own = couple[0]
+        term = dot3(own, dot3(block[...], own.T))
+        column[...] = dot3(own, column[...])
+        block[...] = term
+
+
+def stage_kernel(step, energy, diag, couple, probes, *rest):
+    if step > 0:
+        message, rest = rest[0], rest[1:]
+    factor_p, value_p, inverse_p, matrix_q, source_q, inverse_q, value_q, out, hold, column = rest
+    _, left, distance = place()
+    centre = lax.axis_size("slab") // 2 - 1
+    forward = jnp.logical_and(left, distance < centre)
+    first = jnp.where(forward, 0, 1)
     width = diag.shape[1]
-    unit = eye(width)
     shift = sigma_base + sigma_step * jnp.full((1, 1), energy[0], jnp.int32).astype(F32)
-    shifted = shift * unit
-    sp = diag[right_index] + shifted
-    rp = probes[pl.ds(pl.multiple_of(right_index * width, width), width), :]
-    rq = probes[pl.ds(pl.multiple_of((1 - right_index) * width, width), width), :]
-    if has_message:
-        taken = place[1] > 0
-        block = jnp.where(taken, unpack_symmetric(message[0:width, :]), 0.0)
-        column = jnp.where(taken, message[width : 2 * width, :], 0.0)
-        outer = couple[0]
-        matrix_q[...] = block
-        source_q[...] = column
-
-        @pl.when(left)
-        def _():
-            matrix_q[...] = dot3(outer, dot3(block, outer.T))
-            source_q[...] = dot3(outer, column)
-
-        sp = sp - matrix_q[...]
-        rp = rp - source_q[...]
+    shifted = shift * eye(width)
+    sp = diag[first] + shifted
+    rp = probes[pl.ds(pl.multiple_of(first * width, width), width), :]
+    rq = probes[pl.ds(pl.multiple_of((1 - first) * width, width), width), :]
+    if step > 0:
+        taken = jnp.logical_and(distance >= 1, distance <= step)
+        take_message(message, couple, left, True, matrix_q, source_q)
+        sp = sp - jnp.where(taken, matrix_q[...], 0.0)
+        rp = rp - jnp.where(taken, source_q[...], 0.0)
     inner = couple[1]
     inner_t = inner.T
-    apq = jnp.where(left, inner_t, inner)
-    aqp = jnp.where(left, inner, inner_t)
-    xp = invert(sp, hold, ratios[0], doublings[0])
+    apq = jnp.where(forward, inner_t, inner)
+    aqp = jnp.where(forward, inner, inner_t)
+    xp = invert(sp, hold, 1 / 16, 4)
+    inverse_p[...] = xp
     fp = dot3(xp, apq)
     yp = dot3(xp, rp)
     factor_p[...] = fp
     value_p[...] = yp
-    sq = diag[1 - right_index] + shifted - dot3(aqp, fp)
+    sq = diag[1 - first] + shifted - dot3(aqp, fp)
     rq = rq - dot3(aqp, yp)
     matrix_q[...] = sq
     source_q[...] = rq
-    xq = invert(sq, hold, ratios[1], doublings[1])
-    yq = dot3(xq, rq)
-    inverse_q[...] = xq
-    value_q[...] = yq
-
-    @pl.when(left)
-    def _():
-        pack_symmetric(xq, out)
-        out[width : 2 * width, :] = yq
-
-    @pl.when(jnp.logical_not(left))
-    def _():
-        own = couple[0]
-        own_t = own.T
-        pack_symmetric(dot3(own_t, dot3(xq, own)), out)
-        out[width : 2 * width, :] = dot3(own_t, yq)
-
-
-def join_kernel(ratio, doublings, place, couple, message, factor_p, value_p, matrix_q, source_q,
-                out_p, out_q, out, hold, hold_r):
-    left = place[0] > 0
+
+    @pl.when(distance < centre)
+    def _():
+        xq = invert(sq, hold, 1 / 16, 4)
+        yq = dot3(xq, rq)
+        inverse_q[...] = xq
+        value_q[...] = yq
+
+        @pl.when(left)
+        def _():
+            pack_symmetric(xq, out)
+            out[width : 2 * width, :] = yq
+
+        @pl.when(jnp.logical_not(left))
+        def _():
+            own = couple[0]
+            own_t = own.T
+            pack_symmetric(dot3(own_t, dot3(xq, own)), out)
+            out[width : 2 * width, :] = dot3(own_t, yq)
+
+
+def ready_kernel(energy, diag, couple, probes, following, factor_p, value_p, inverse_p, matrix_q,
+                 source_q, matrix, source, link, base, base_source, reach):
+    slab, left, distance = place()
+    half = lax.axis_size("slab") // 2
+    width = diag.shape[1]
+
+    @pl.when(slab == half - 1)
+    def _():
+        ahead = following[...]
+        across = dot3(inverse_p[...], ahead.T)
+        reach[...] = across
+        matrix[...] = matrix_q[...]
+        source[...] = source_q[...]
+        link[...] = dot3(couple[1].T, across)
+        base[...] = dot3(ahead, across)
+        base_source[...] = dot3(ahead, value_p[...])
+
+    @pl.when(slab == half)
+    def _():
+        shift = sigma_base + sigma_step * jnp.full((1, 1), energy[0], jnp.int32).astype(F32)
+        shifted = shift * eye(width)
+        matrix[...] = diag[1] + shifted
+        source[...] = probes[width : 2 * width, :]
+        link[...] = couple[1]
+        base[...] = diag[0] + shifted
+        base_source[...] = probes[0:width, :]
+
+
+def centre_kernel(couple, message, matrix, source, link, base, base_source, factor, value,
+                  total, total_source, out, hold, block, column):
+    slab, left, distance = place()
+    half = lax.axis_size("slab") // 2
+    width = matrix.shape[0]
+
+    @pl.when(jnp.logical_or(slab == half - 1, slab == half))
+    def _():
+        take_message(message, couple, left, True, block, column)
+        solved = invert(matrix[...] - block[...], hold, 1 / 16, 4)
+        right_side = source[...] - column[...]
+        near = link[...]
+        near_t = near.T
+        reach = dot3(solved, near)
+        found = dot3(solved, right_side)
+        factor[...] = reach
+        value[...] = found
+        sign = jnp.where(left, 1.0, -1.0)
+        both = base[...] + sign * dot3(near_t, reach)
+        both_source = base_source[...] - dot3(near_t, found)
+        total[...] = both
+        total_source[...] = both_source
+        pack_symmetric(both, out)
+        out[width : 2 * width, :] = both_source
+
+
+def join_kernel(couple, message, total, total_source, factor, value, out_first, out_middle, out,
+                hold):
+    slab, left, distance = place()
+    half = lax.axis_size("slab") // 2
+    width = total.shape[0]
+
+    @pl.when(jnp.logical_or(slab == half - 1, slab == half))
+    def _():
+        sign = jnp.where(left, 1.0, -1.0)
+        matrix = sign * (unpack_symmetric(message[0:width, :]) - total[...])
+        right_side = sign * (message[width : 2 * width, :] - total_source[...])
+        middle = dot3(invert(matrix, hold, 1 / 64, 5), right_side)
+        first = value[...] + sign * dot3(factor[...], middle)
+        out_first[...] = first
+        out_middle[...] = middle
+        out[...] = first
+
+        @pl.when(left)
+        def _():
+            out[...] = dot3(couple[0].T, first)
+
+
+def back_kernel(step, cells, couple, probes, message, first, middle, known_p, known_q, factor_p,
+                value_p, inverse_q, value_q, reach, out_p, out_q, out, dens):
+    slab, left, distance = place()
+    centre = lax.axis_size("slab") // 2 - 1
     width = couple.shape[1]
-    block = unpack_symmetric(message[0:width, :])
-    column = message[width : 2 * width, :]
-    hold[...] = block
-    hold_r[...] = column
-
-    @pl.when(jnp.logical_not(left))
-    def _():
-        own = couple[0]
-        hold[...] = dot3(own, dot3(block, own.T))
-        hold_r[...] = dot3(own, column)
-
-    sq = matrix_q[...] - hold[...]
-    rq = source_q[...] - hold_r[...]
-    xq = dot3(invert(sq, hold, ratio, doublings), rq)
-    xp = value_p[...] - dot3(factor_p[...], xq)
-    out_p[...] = xp
-    out_q[...] = xq
-    out[...] = xp
-
-    @pl.when(left)
-    def _():
-        out[...] = dot3(couple[0].T, xp)
-
-
-def back_kernel(place, couple, probes, message, known_p, known_q, factor_p, value_p, inverse_q,
-                value_q, out_p, out_q, out, dens):
-    left = place[0] > 0
-    width = couple.shape[1]
-    out_p[...] = known_p[...]
-    out_q[...] = known_q[...]
-
-    @pl.when(place[1] > 0)
+
+    @pl.when(jnp.logical_and(distance < centre, distance != step))
+    def _():
+        out_p[...] = known_p[...]
+        out_q[...] = known_q[...]
+
+    @pl.when(distance == step)
     def _():
         out_q[...] = message[...]
 
@@ -220,13 +288,26 @@
         out_q[...] = xq
         out_p[...] = value_p[...] - dot3(factor_p[...], xq)
 
+    @pl.when(jnp.logical_and(distance == centre, left))
+    def _():
+        xa = first[...]
+        out_p[...] = xa
+        out_q[...] = value_p[...] - dot3(factor_p[...], xa) - dot3(reach[...], middle[...])
+
+    @pl.when(jnp.logical_and(distance == centre, jnp.logical_not(left)))
+    def _():
+        out_p[...] = first[...]
+        out_q[...] = middle[...]
+
     xp = out_p[...]
     xq = out_q[...]
     out[...] = xp
 
-    @pl.when(left)
-    def _():
-        out[...] = dot3(couple[0].T, xp)
+    if step > 0:
+
+        @pl.when(left)
+        def _():
+            out[...] = dot3(couple[0].T, xp)
 
     xa = jnp.where(left, xp, xq)
     xb = jnp.where(left, xq, xp)
@@ -234,10 +315,21 @@
     dens[...] = dot6(jnp.ones((8, terms.shape[1]), F32), terms, NT)
 
 
-def poisson_kernel(rows_all, cells, place, weights, orbitals, dopants, around, out, fine):
+def total_kernel(scale, cells, *rest):
+    parts, out = rest[:-1], rest[-1]
+    total = parts[0][0:1, :]
+    for part in parts[1:]:
+        total = total + part[0:1, :]
+    out[0:1, :] = total * scale
+    out[1:2, :] = cells[...].astype(F32)
+
+
+def poisson_kernel(rows_all, planes, packet, near, far, dopants, around, out):
+    slab, slabs = lax.axis_index("slab"), lax.axis_size("slab")
     depth, pitch, across = around.shape
     total = depth * pitch
-    first_z, first_x, planes = place[0], place[1], place[2]
+    first_z = slab * out.shape[0] - SWEEPS
+    first_x = lax.axis_index("energy") * out.shape[1] - SWEEPS
     plane = rows_all * across
 
     def spots(index):
@@ -253,8 +345,12 @@
 
     rows, ys = spots(dopants[...])
     dopant = dopant_charge * one_pass(rows, ys.astype(BF16), NT)
-    rows, ys = spots(orbitals[...])
-    spread = ys * weights[...]
+    alone = jnp.logical_or(slab == 0, slab == slabs - 1)
+    lonely = jnp.where(alone, 0.0, far[0:1, :])
+    weights = jnp.concatenate([packet[0:1, :], near[0:1, :], lonely], axis=1)
+    orbitals = jnp.concatenate([packet[1:2, :], near[1:2, :], far[1:2, :]], axis=1)
+    rows, ys = spots(orbitals.astype(jnp.int32))
+    spread = ys * weights
     h = spread.astype(BF16)
     rest = spread - h.astype(F32)
     m = rest.astype(BF16)
@@ -287,10 +383,24 @@
 
 VM = pl.BlockSpec(memory_space=pltpu.VMEM)
 SM = pl.BlockSpec(memory_space=pltpu.SMEM)
+GRANT = 16 << 20
 
 
 def like(*shape, dtype=F32):
     return jax.ShapeDtypeStruct(shape, dtype)
+
+
+def call(kernel, name, outs, args, scratch=(), scalars=0, flops=10**8):
+    return pl.pallas_call(
+        kernel,
+        out_shape=outs,
+        in_specs=[SM] * scalars + [VM] * (len(args) - scalars),
+        out_specs=jax.tree.map(lambda _: VM, outs),
+        scratch_shapes=[pltpu.VMEM(shape, F32) for shape in scratch],
+        compiler_params=pltpu.CompilerParams(vmem_limit_bytes=GRANT),
+        cost_estimate=pl.CostEstimate(flops=flops, bytes_accessed=10**6, transcendentals=0),
+        name=name,
+    )(*args)
 
 
 def pairs_of(count, odd):
@@ -325,75 +435,68 @@
     slab, slabs = lax.axis_index("slab"), lax.axis_size("slab")
     energy, energies = lax.axis_index("energy"), lax.axis_size("energy")
     half = slabs // 2
-    left = slab < half
-    distance = jnp.where(left, slab, slabs - 1 - slab)
-    left_flag = left.astype(jnp.int32)
     square, column = like(width, width), like(width, probe_count)
     letter = like(2 * width, probe_count)
-
-    def flags(second):
-        return jnp.stack([left_flag, second.astype(jnp.int32)])
+    sq, col = (width, width), (width, probe_count)
+
+    following = lax.ppermute(couple[0], "slab", [(s + 1, s) for s in range(half - 1, half)])
 
     message = None
-    for t in range(half):
+    for t in range(half - 1):
+        args = [energy_index, diag_blocks, couple, probes]
+        if t > 0:
+            if t > 1:
+                _, _, distance = place()
+                message = jnp.where(distance == t, message, kept)
+            kept = message
+            args.append(message)
+        state = call(
+            functools.partial(stage_kernel, t), f"stage{t}",
+            (square, column, square, square, column, square, column, letter),
+            args, (sq, col), 1,
+        )
         if t == 0:
-            inbound = jnp.zeros((8, 128), F32)
-        elif t == 1:
-            inbound = message
-        else:
-            inbound = jnp.where(distance == t, message, kept)
-        kept = inbound
-        if t == 1:
-            kept = jnp.where(distance == t, message, 0.0) if half > 2 else inbound
-        accept = (distance >= 1) & (distance <= t)
-        state = pl.pallas_call(
-            functools.partial(stage_kernel, t > 0, (1 / 16, 1 / 16), (4, 4)),
-            out_shape=(square, column, square, column, square, column, letter),
-            in_specs=[SM, SM, VM, VM, VM, VM],
-            out_specs=(VM,) * 7,
-            scratch_shapes=[pltpu.VMEM((width, width), F32)],
-            name=f"stage{t}",
-        )(flags(accept), energy_index, diag_blocks, couple, probes, inbound)
-        factor_p, value_p, matrix_q, source_q, inverse_q, value_q, sent = state
-        message = slab_exchange(sent, t % 2 == 1)
-    out_p, out_q, sent = pl.pallas_call(
-        functools.partial(join_kernel, 1 / 128, 6),
-        out_shape=(column, column, column),
-        in_specs=[SM] + [VM] * 6,
-        out_specs=(VM,) * 3,
-        scratch_shapes=[pltpu.VMEM((width, width), F32), pltpu.VMEM((width, probe_count), F32)],
-        name="join",
-    )(flags(left), couple, message, factor_p, value_p, matrix_q, source_q)
+            prepared = state
+        message = slab_exchange(state[-1], t % 2 == 1)
+    factor_p, value_p, _, _, _, inverse_q, value_q, _ = state
+    matrix, source, link, base, base_source, reach = call(
+        ready_kernel, "ready", (square, column, square, square, column, square),
+        [energy_index, diag_blocks, couple, probes, following, *prepared[:5]], (), 1,
+    )
+    factor, value, total, total_source, sent = call(
+        centre_kernel, "centre", (square, column, square, column, letter),
+        [couple, message, matrix, source, link, base, base_source], (sq, sq, col),
+    )
+    message = slab_exchange(sent, half % 2 == 0)
+    first, middle, sent = call(
+        join_kernel, "join", (column, column, column),
+        [couple, message, total, total_source, factor, value], (sq,),
+    )
+    cells_here = orbital_cell.reshape(1, -1)
+    centred = lax.axis_index("slab") == half - 1
+    if half > 2:
+        factor_p = jnp.where(centred, prepared[0], factor_p)
+        value_p = jnp.where(centred, prepared[1], value_p)
+    known_p, known_q = first, middle
     for t in range(half - 2, -1, -1):
         message = slab_exchange(sent, t % 2 == 1)
-        out_p, out_q, sent, dens = pl.pallas_call(
-            back_kernel,
-            out_shape=(column, column, column, like(8, 2 * width)),
-            in_specs=[SM] + [VM] * 9,
-            out_specs=(VM,) * 4,
-            name=f"back{t}",
-        )(flags(distance == t), couple, probes, message, out_p, out_q, factor_p, value_p,
-          inverse_q, value_q)
-    total = dens
-    for k in range(1, energies):
-        total = total + lax.ppermute(
-            dens, "energy", [(e, e ^ k) for e in range(energies)]
+        known_p, known_q, sent, dens = call(
+            functools.partial(back_kernel, t), f"back{t}",
+            (column, column, column, like(8, 2 * width)),
+            [cells_here, couple, probes, message, first, middle, known_p, known_q, factor_p,
+             value_p, inverse_q, value_q, reach],
         )
-    total = total[0:1] * (1.0 / (probe_count * energies))
-    density = total.reshape(-1)
-
-    cells_here = orbital_cell.reshape(1, -1)
-    packet = jnp.concatenate([total, cells_here.astype(F32)], axis=0)
+    parts = [dens] + [
+        lax.ppermute(dens, "energy", [(e, e ^ k) for e in range(energies)])
+        for k in range(1, energies)
+    ]
+    packet = call(
+        functools.partial(total_kernel, 1.0 / (probe_count * energies)), "total",
+        like(8, 2 * width), [cells_here, *parts],
+    )
+    density = packet[0]
     near = slab_exchange(packet, False)
     far = slab_exchange(packet, True)
-    weights = jnp.concatenate([total, near[0:1], far[0:1]], axis=1)
-    alone = (slab == 0) | (slab == slabs - 1)
-    nobody = jnp.int32(-(2**30))
-    orbitals = jnp.concatenate(
-        [cells_here, near[1:2].astype(jnp.int32),
-         jnp.where(alone, nobody, far[1:2].astype(jnp.int32))],
-        axis=1,
-    )
 
     depth, rows_here, across = initial_potential.shape
     halo = SWEEPS
@@ -414,15 +517,11 @@
     pitch = -(-region.shape[1] // 8) * 8
     region = jnp.pad(region, ((0, 0), (0, pitch - region.shape[1]), (0, 0)))
     rows_all = rows_here * energies
-    place = jnp.stack([slab * depth - halo, energy * rows_here - halo, jnp.int32(depth * slabs)])
-    potential = pl.pallas_call(
-        functools.partial(poisson_kernel, rows_all, None),
-        out_shape=like(depth, rows_here, across),
-        in_specs=[SM] + [VM] * 4,
-        out_specs=VM,
-        scratch_shapes=[pltpu.VMEM((8, 128), F32)],
-        name="poisson",
-    )(place, weights, orbitals, dopant_cells.reshape(1, -1), region)
+    potential = call(
+        functools.partial(poisson_kernel, rows_all, depth * slabs), "poisson",
+        like(depth, rows_here, across),
+        [packet, near, far, dopant_cells.reshape(1, -1), region],
+    )
     return (potential, density)
 
 

time: 118 us -> 55.5 us (0.47)
  starting transfers between devices: 68.9 us -> 32.7 us
  Pallas kernels: 30 us -> 9.74 us
  other arithmetic: 6.4 us -> 0.07 us
  waiting for transfers between devices: 5.91 us -> 7.52 us
    ppermute x7, starting transfers between devices: 65.4 us -> 26.9 us  [slab_exchange(): return lax.ppermute(value, ('slab', 'energy'), whole)]
    pallas_call x5 -> x7, Pallas kernels: 30 us -> 9.74 us  [call(): pl.pallas_call(kernel, out_shape=outs, in_specs=[SM] * scalars + [VM] * (...]
    another operation x5 -> x0, other arithmetic: 3.16 us -> none  [the longest x4 2.49 us: flags(): return jnp.stack([left_flag, second.astype(jnp.int32)])]
    ppermute x2, starting transfers between devices: 1.66 us -> 3.14 us  [energy_exchange(): return lax.ppermute(value, 'energy', pairs)]
    mul x1 -> x0, other arithmetic: 1.31 us -> none  [body(): total = total[0:1] * (1.0 / (probe_count * energies))]
    ppermute x7, waiting for transfers between devices: 3.87 us -> 5.13 us  [slab_exchange(): return lax.ppermute(value, ('slab', 'energy'), whole)]
    concatenate x3 -> x0, other arithmetic: 1.19 us -> none  [the longest x1 0.59 us: body(): jnp.concatenate([cells_here, near[1:2].astype(jnp.int32), jnp.where(alone...]
    unnamed x14 -> x18, local copies, waits for them, and re-layouts: 3.37 us -> 3.11 us
  transfers between devices with their start and end apart: 12 -> 13, of which waited for: 6 -> 6; matrix products, arithmetic and copies ran while one was open for 3% -> 1% of each run, Pallas kernels for 16% -> 0%
where the time goes in v2:
time: 55.5 us; the launch traced here: 55.2 us
  starting transfers between devices  32.7 us (59%)
  Pallas kernels  9.74 us (18%)
  waiting for transfers between devices  7.52 us (14%)
  local copies, waits for them, and re-layouts  3.72 us (7%)
  between operations  1.43 us (3%)
    ppermute x7, starting transfers between devices, slab_exchange(): return lax.ppermute(value, ('slab', 'energy'), whole)  26.9 us
    pallas_call x7, Pallas kernels, call(): pl.pallas_call(kernel, out_shape=outs, in_specs=[SM] * scalars + [VM] * (...  9.74 us
    ppermute x7, waiting for transfers between devices, slab_exchange(): return lax.ppermute(value, ('slab', 'energy'), whole)  5.13 us
    ppermute x2, starting transfers between devices, energy_exchange(): return lax.ppermute(value, 'energy', pairs)  3.14 us
    unnamed x18, local copies, waits for them, and re-layouts  3.11 us
    ppermute x3, waiting for transfers between devices, body(): lax.ppermute(dens, 'energy', [(e, e ^ k) for e in range(energies)])  1.89 us
    ppermute x3, starting transfers between devices, body(): lax.ppermute(dens, 'energy', [(e, e ^ k) for e in range(energies)])  1.86 us
  transfers between devices with their start and end apart: 13, of which 6 were waited for; matrix products, arithmetic and copies ran while one was open for 1% of the time, Pallas kernels for 0%

profile of v2, /device:TPU:0, one launch (start us, length us, event | category | flops | bytes accessed | tf_op | source)
XLA Modules:
  0.0 55.2 jit_solution(2327472089782627123)
XLA Ops:
  1.3 1.0 %copy-done = f32[2,192,192]{2,1,0:T(8,128)S(1)} copy-done((f32[2,192,192]{2,1,0:T(8,128)S(1)}, f32[2,192,192]{2,1,0:T(8,128)}, u32[]{:S(2)}) %copy-start) | copy-done | bytes 294936
  2.3 0.9 %copy-done.2 = f32[384,128]{1,0:T(8,128)S(1)} copy-done((f32[384,128]{1,0:T(8,128)S(1)}, f32[384,128]{1,0:T(8,128)}, u32[]{:S(2)}) %copy-start.2) | copy-done | bytes 196632
  3.2 1.0 %copy-done.4 = f32[2,192,192]{2,1,0:T(8,128)S(1)} copy-done((f32[2,192,192]{2,1,0:T(8,128)S(1)}, f32[2,192,192]{2,1,0:T(8,128)}, u32[]{:S(2)}) %copy-start.4) | copy-done | bytes 294936
  4.2 6.6 %stage0.1 = (f32[192,192]{1,0:T(8,128)S(1)}, f32[192,128]{1,0:T(8,128)S(1)}, f32[192,192]{1,0:T(8,128)S(1)}, f32[192,192]{1,0:T(8,128)S(1)}, f32[192,128]{1,0:T(...) custom-call(s32[1]{0:T(128)S(6)} %copy.9.energy, ...), custom_call_target="tpu_custom_call" | custom-call | flops 100000000 | bytes 1000000 | tf_op jit(solution)/shard_map/stage0/pallas_call | solution.py:394
  10.8 0.0 copy-start.5
  10.9 0.1 collective-permute-start
  11.0 0.6 collective-permute-start.9
  11.5 2.6 %collective-permute-start.10 = (f32[8,2,128]{2,1,0:T(2,128)S(1)}, f32[8,2,128]{2,1,0:T(2,128)S(1)}, u32[]{:S(2)}, u32[]{:S(2)}) collective-permute-start(f32[8,2,128]{2,1,0:T(2,128)S(1)} %get-tuple-element.52), channel_id=1, source_target_pairs={{1,2},{2,1},{3,0},{0,3},{5,6},{6,5},{7,4},{4,7},{9,10},{10,9},{11,... | collective-permute-start | bytes 24584 | tf_op jit(solution)/shard_map/ppermute | solution.py:429
  14.1 0.0 copy-start.3
  14.2 0.8 %collective-permute-start.1 = (f32[192,192]{1,0:T(8,128)S(1)}, f32[192,192]{1,0:T(8,128)S(1)}, u32[]{:S(2)}, u32[]{:S(2)}) collective-permute-start(f32[192,192]{1,0:T(8,128)S(1)} %slice_bitcast_fusion), channel_id=1, source_target_pairs={{8,4},{9,5},{10,6},{11,7},{24,20},{25,21},{26,22},{27,23}} | collective-permute-start | bytes 442376 | tf_op jit(solution)/shard_map/ppermute | solution.py:442
  15.0 0.5 collective-permute-done.10
  15.5 2.2 %collective-permute-start.11 = (f32[2,20,128]{2,1,0:T(8,128)S(1)}, f32[2,20,128]{2,1,0:T(8,128)S(1)}, u32[]{:S(2)}, u32[]{:S(2)}) collective-permute-start(f32[2,20,128]{2,1,0:T(8,128)S(1)} %get-tuple-element.48), channel_id=1, source_target_pairs={{0,4},{1,5},{2,6},{3,7},{4,0},{5,1},{6,2},{7,3},{8,12},{9,13},{10,... | collective-permute-start | bytes 61448 | tf_op jit(solution)/shard_map/ppermute | solution.py:421
  17.7 0.0 collective-permute-done.1.following
  17.8 0.5 collective-permute-done.message
  18.2 0.5 collective-permute-start.12
  18.7 0.2 copy-done.8
  18.9 0.8 %collective-permute-done.2.message = f32[384,128]{1,0:T(8,128)S(1)} collective-permute-done((f32[384,128]{1,0:T(8,128)S(1)}, f32[384,128]{1,0:T(8,128)S(1)}, u32[]{:S(2)}, u32[]{:S(2)}) %collective-permute-start.2) | collective-permute-done | bytes 196640 | tf_op jit(solution)/shard_map/ppermute | solution.py:421
  19.7 22.3 %collective-permute-start.3 = (f32[192,128]{1,0:T(8,128)S(1)}, f32[192,128]{1,0:T(8,128)S(1)}, u32[]{:S(2)}, u32[]{:S(2)}) collective-permute-start(f32[192,128]{1,0:T(8,128)S(1)} %get-tuple-element.41), channel_id=1, source_target_pairs={{0,4},{1,5},{2,6},{3,7},{4,0},{5,1},{6,2},{7,3},{8,12},{9,13},{10,... | collective-permute-start | bytes 294920 | tf_op jit(solution)/shard_map/ppermute | solution.py:421
  42.0 0.0 collective-permute-done.11
  42.0 0.0 collective-permute-done.12
  42.0 2.6 %collective-permute-done.3.message = f32[192,128]{1,0:T(8,128)S(1)} collective-permute-done((f32[192,128]{1,0:T(8,128)S(1)}, f32[192,128]{1,0:T(8,128)S(1)}, u32[]{:S(2)}, u32[]{:S(2)}) %collective-permute-start.3) | collective-permute-done | bytes 98336 | tf_op jit(solution)/shard_map/ppermute | solution.py:421
  44.6 1.3 %back0.1 = (f32[192,128]{1,0:T(8,128)}, f32[192,128]{1,0:T(8,128)}, f32[192,128]{1,0:T(8,128)}, f32[8,384]{1,0:T(8,128)S(1)}) custom-call(s32[1,384]{1,0:T(1,128)S(1)} %reshape.10.cells, f32[2,192,192]{2,1,0:T(8,128)S(1)} %copy-done.1, f32[384,128]{1,0:T(8,128)S(1)} %copy-done.3, f32[192,128]{1,0:T(8,128)S(1)} %collective-permute-done.3.message, ...), custom_call_target="tpu_custom_call" | custom-call | flops 100000000 | bytes 1000000 | tf_op jit(solution)/shard_map/back0/pallas_call | solution.py:394
  45.9 0.0 collective-permute-start.4
  45.9 0.5 collective-permute-start.5
  46.4 1.3 %collective-permute-start.6 = (f32[8,384]{1,0:T(8,128)S(1)}, f32[8,384]{1,0:T(8,128)S(1)}, u32[]{:S(2)}, u32[]{:S(2)}) collective-permute-start(f32[8,384]{1,0:T(8,128)S(1)} %get-tuple-element.47.rest_0_), channel_id=1, source_target_pairs={{0,3},{1,2},{2,1},{3,0},{4,7},{5,6},{6,5},{7,4},{8,11},{9,10},{10,... | collective-permute-start | bytes 36872 | tf_op jit(solution)/shard_map/ppermute | solution.py:490
  47.8 0.0 collective-permute-done.4.rest_1_
  47.8 1.9 %collective-permute-done.5.rest_2_ = f32[8,384]{1,0:T(8,128)S(1)} collective-permute-done((f32[8,384]{1,0:T(8,128)S(1)}, f32[8,384]{1,0:T(8,128)S(1)}, u32[]{:S(2)}, u32[]{:S(2)}) %collective-permute-start.5) | collective-permute-done | bytes 12320 | tf_op jit(solution)/shard_map/ppermute | solution.py:490
  49.7 0.0 copy-start.6
  49.7 1.8 %collective-permute-start.7 = (f32[8,384]{1,0:T(8,128)S(1)}, f32[8,384]{1,0:T(8,128)S(1)}, u32[]{:S(2)}, u32[]{:S(2)}) collective-permute-start(f32[8,384]{1,0:T(8,128)S(1)} %total.1.packet), channel_id=1, source_target_pairs={{0,4},{1,5},{2,6},{3,7},{4,0},{5,1},{6,2},{7,3},{8,12},{9,13},{10,... | collective-permute-start | bytes 36872 | tf_op jit(solution)/shard_map/ppermute | solution.py:421
  51.5 0.6 %slice_reduce_fusion = f32[384]{0:T(512)} fusion(f32[8,384]{1,0:T(8,128)S(1)} %total.1.packet), kind=kLoop, calls=%fused_computation.20 | loop fusion | bytes 3072 | tf_op jit(solution)/shard_map/slice | solution.py:497
  52.1 1.3 %collective-permute-done.7.near = f32[8,384]{1,0:T(8,128)S(1)} collective-permute-done((f32[8,384]{1,0:T(8,128)S(1)}, f32[8,384]{1,0:T(8,128)S(1)}, u32[]{:S(2)}, u32[]{:S(2)}) %collective-permute-start.7) | collective-permute-done | bytes 12320 | tf_op jit(solution)/shard_map/ppermute | solution.py:421
  53.5 1.8 %poisson.1 = f32[8,16,128]{2,1,0:T(8,128)} custom-call(f32[8,384]{1,0:T(8,128)S(1)} %total.1.packet, f32[8,384]{1,0:T(8,128)S(1)} %collective-permute-done.7.near, f32[8,384]{1,0:T(8,128)S(1)} %collective-permute-done.8.far, s32[1,1024]{1,0:T(1,128)S(1)} %bitcast.7, f32[12,24,128]{2,1,0:T(8,128)S(1)} %select_maximum_fusion.around), custom_call_target="tpu_custom_call" | custom-call | flops 100000000 | bytes 1000000 | tf_op jit(solution)/shard_map/poisson/pallas_call | solution.py:394
  (28 shorter events, 0.2 us)
Async XLA Ops:
  1.3 1.0 %copy-start = (f32[2,192,192]{2,1,0:T(8,128)S(1)}, f32[2,192,192]{2,1,0:T(8,128)}, u32[]{:S(2)}) copy-start(f32[2,192,192]{2,1,0:T(8,128)} %couple.9) | copy-start | bytes 884740
  2.3 0.9 %copy-start.2 = (f32[384,128]{1,0:T(8,128)S(1)}, f32[384,128]{1,0:T(8,128)}, u32[]{:S(2)}) copy-start(f32[384,128]{1,0:T(8,128)} %probes.5) | copy-start | bytes 589828
  3.2 1.0 %copy-start.4 = (f32[2,192,192]{2,1,0:T(8,128)S(1)}, f32[2,192,192]{2,1,0:T(8,128)}, u32[]{:S(2)}) copy-start(f32[2,192,192]{2,1,0:T(8,128)} %diag.3) | copy-start | bytes 884740
  4.2 6.8 %copy-start.7 = (f32[8,16,128]{2,1,0:T(8,128)S(1)}, f32[8,16,128]{2,1,0:T(8,128)}, u32[]{:S(2)}) copy-start(f32[8,16,128]{2,1,0:T(8,128)} %param.13) | copy-start | bytes 196612
  4.2 9.9 %copy-start.1 = (f32[2,192,192]{2,1,0:T(8,128)S(1)}, f32[2,192,192]{2,1,0:T(8,128)}, u32[]{:S(2)}) copy-start(f32[2,192,192]{2,1,0:T(8,128)} %couple.9) | copy-start | bytes 884740
  10.8 6.9 %copy-start.5 = (f32[2,192,192]{2,1,0:T(8,128)S(1)}, f32[2,192,192]{2,1,0:T(8,128)}, u32[]{:S(2)}) copy-start(f32[2,192,192]{2,1,0:T(8,128)} %diag.3) | copy-start | bytes 884740
  10.9 7.4 %collective-permute-start = (f32[384,128]{1,0:T(8,128)S(1)}, f32[384,128]{1,0:T(8,128)S(1)}, u32[]{:S(2)}, u32[]{:S(2)}) collective-permute-start(f32[384,128]{1,0:T(8,128)S(1)} %get-tuple-element.25), channel_id=1, source_target_pairs={{0,4},{1,5},{2,6},{3,7},{4,0},{5,1},{6,2},{7,3},{8,12},{9,13},{10,... | collective-permute-start | bytes 589832 | tf_op jit(solution)/shard_map/ppermute | solution.py:421
  11.0 4.0 %collective-permute-start.9 = (f32[8,2,128]{2,1,0:T(2,128)S(1)}, f32[8,2,128]{2,1,0:T(2,128)S(1)}, u32[]{:S(2)}, u32[]{:S(2)}) collective-permute-start(f32[8,2,128]{2,1,0:T(2,128)S(1)} %get-tuple-element.51), channel_id=1, source_target_pairs={{0,1},{1,0},{2,3},{3,2},{4,5},{5,4},{6,7},{7,6},{8,9},{9,8},{10,11... | collective-permute-start | bytes 24584 | tf_op jit(solution)/shard_map/ppermute | solution.py:429
  11.5 4.0 %collective-permute-start.10 = (f32[8,2,128]{2,1,0:T(2,128)S(1)}, f32[8,2,128]{2,1,0:T(2,128)S(1)}, u32[]{:S(2)}, u32[]{:S(2)}) collective-permute-start(f32[8,2,128]{2,1,0:T(2,128)S(1)} %get-tuple-element.52), channel_id=1, source_target_pairs={{1,2},{2,1},{3,0},{0,3},{5,6},{6,5},{7,4},{4,7},{9,10},{10,9},{11,... | collective-permute-start | bytes 24584 | tf_op jit(solution)/shard_map/ppermute | solution.py:429
  14.1 3.6 %copy-start.3 = (f32[384,128]{1,0:T(8,128)S(1)}, f32[384,128]{1,0:T(8,128)}, u32[]{:S(2)}) copy-start(f32[384,128]{1,0:T(8,128)} %probes.5) | copy-start | bytes 589828
  14.2 3.6 %collective-permute-start.1 = (f32[192,192]{1,0:T(8,128)S(1)}, f32[192,192]{1,0:T(8,128)S(1)}, u32[]{:S(2)}, u32[]{:S(2)}) collective-permute-start(f32[192,192]{1,0:T(8,128)S(1)} %slice_bitcast_fusion), channel_id=1, source_target_pairs={{8,4},{9,5},{10,6},{11,7},{24,20},{25,21},{26,22},{27,23}} | collective-permute-start | bytes 442376 | tf_op jit(solution)/shard_map/ppermute | solution.py:442
  15.5 26.5 %collective-permute-start.11 = (f32[2,20,128]{2,1,0:T(8,128)S(1)}, f32[2,20,128]{2,1,0:T(8,128)S(1)}, u32[]{:S(2)}, u32[]{:S(2)}) collective-permute-start(f32[2,20,128]{2,1,0:T(8,128)S(1)} %get-tuple-element.48), channel_id=1, source_target_pairs={{0,4},{1,5},{2,6},{3,7},{4,0},{5,1},{6,2},{7,3},{8,12},{9,13},{10,... | collective-permute-start | bytes 61448 | tf_op jit(solution)/shard_map/ppermute | solution.py:421
  18.2 1.4 %collective-permute-start.2 = (f32[384,128]{1,0:T(8,128)S(1)}, f32[384,128]{1,0:T(8,128)S(1)}, u32[]{:S(2)}, u32[]{:S(2)}) collective-permute-start(f32[384,128]{1,0:T(8,128)S(1)} %get-tuple-element.36), channel_id=1, source_target_pairs={{4,8},{5,9},{6,10},{7,11},{8,4},{9,5},{10,6},{11,7},{0,1},{1,0},{2... | collective-permute-start | bytes 589832 | tf_op jit(solution)/shard_map/ppermute | solution.py:421
  18.2 0.7 %copy-start.8 = (s32[384]{0:T(512)S(1)}, s32[384]{0:T(512)}, u32[]{:S(2)}) copy-start(s32[384]{0:T(512)} %param.11) | copy-start | bytes 4612
  18.2 23.7 %collective-permute-start.12 = (f32[2,20,128]{2,1,0:T(8,128)S(1)}, f32[2,20,128]{2,1,0:T(8,128)S(1)}, u32[]{:S(2)}, u32[]{:S(2)}) collective-permute-start(f32[2,20,128]{2,1,0:T(8,128)S(1)} %broadcast_select_fusion.2), channel_id=1, source_target_pairs={{4,8},{5,9},{6,10},{7,11},{8,4},{9,5},{10,6},{11,7},{0,1},{1,0},{2... | collective-permute-start | bytes 61448 | tf_op jit(solution)/shard_map/ppermute | solution.py:421
  19.7 24.9 %collective-permute-start.3 = (f32[192,128]{1,0:T(8,128)S(1)}, f32[192,128]{1,0:T(8,128)S(1)}, u32[]{:S(2)}, u32[]{:S(2)}) collective-permute-start(f32[192,128]{1,0:T(8,128)S(1)} %get-tuple-element.41), channel_id=1, source_target_pairs={{0,4},{1,5},{2,6},{3,7},{4,0},{5,1},{6,2},{7,3},{8,12},{9,13},{10,... | collective-permute-start | bytes 294920 | tf_op jit(solution)/shard_map/ppermute | solution.py:421
  45.9 1.9 %collective-permute-start.4 = (f32[8,384]{1,0:T(8,128)S(1)}, f32[8,384]{1,0:T(8,128)S(1)}, u32[]{:S(2)}, u32[]{:S(2)}) collective-permute-start(f32[8,384]{1,0:T(8,128)S(1)} %get-tuple-element.47.rest_0_), channel_id=1, source_target_pairs={{0,1},{1,0},{2,3},{3,2},{4,5},{5,4},{6,7},{7,6},{8,9},{9,8},{10,11... | collective-permute-start | bytes 36872 | tf_op jit(solution)/shard_map/ppermute | solution.py:490
  45.9 3.8 %collective-permute-start.5 = (f32[8,384]{1,0:T(8,128)S(1)}, f32[8,384]{1,0:T(8,128)S(1)}, u32[]{:S(2)}, u32[]{:S(2)}) collective-permute-start(f32[8,384]{1,0:T(8,128)S(1)} %get-tuple-element.47.rest_0_), channel_id=1, source_target_pairs={{0,2},{1,3},{2,0},{3,1},{4,6},{5,7},{6,4},{7,5},{8,10},{9,11},{10,... | collective-permute-start | bytes 36872 | tf_op jit(solution)/shard_map/ppermute | solution.py:490
  46.4 3.3 %collective-permute-start.6 = (f32[8,384]{1,0:T(8,128)S(1)}, f32[8,384]{1,0:T(8,128)S(1)}, u32[]{:S(2)}, u32[]{:S(2)}) collective-permute-start(f32[8,384]{1,0:T(8,128)S(1)} %get-tuple-element.47.rest_0_), channel_id=1, source_target_pairs={{0,3},{1,2},{2,1},{3,0},{4,7},{5,6},{6,5},{7,4},{8,11},{9,10},{10,... | collective-permute-start | bytes 36872 | tf_op jit(solution)/shard_map/ppermute | solution.py:490
  49.7 3.8 %copy-start.6 = (s32[1024]{0:T(1024)S(1)}, s32[1024]{0:T(1024)}, u32[]{:S(2)}) copy-start(s32[1024]{0:T(1024)} %param.12) | copy-start | bytes 12292
  49.7 3.8 %collective-permute-start.7 = (f32[8,384]{1,0:T(8,128)S(1)}, f32[8,384]{1,0:T(8,128)S(1)}, u32[]{:S(2)}, u32[]{:S(2)}) collective-permute-start(f32[8,384]{1,0:T(8,128)S(1)} %total.1.packet), channel_id=1, source_target_pairs={{0,4},{1,5},{2,6},{3,7},{4,0},{5,1},{6,2},{7,3},{8,12},{9,13},{10,... | collective-permute-start | bytes 36872 | tf_op jit(solution)/shard_map/ppermute | solution.py:421
  51.5 1.9 %collective-permute-start.8 = (f32[8,384]{1,0:T(8,128)S(1)}, f32[8,384]{1,0:T(8,128)S(1)}, u32[]{:S(2)}, u32[]{:S(2)}) collective-permute-start(f32[8,384]{1,0:T(8,128)S(1)} %total.1.packet), channel_id=1, source_target_pairs={{4,8},{5,9},{6,10},{7,11},{8,4},{9,5},{10,6},{11,7},{0,1},{1,0},{2... | collective-permute-start | bytes 36872 | tf_op jit(solution)/shard_map/ppermute | solution.py:421

commit v3 on v2

--- a/solution.py
+++ b/solution.py
@@ -122,23 +122,18 @@
     return slab, left, jnp.where(left, slab, slabs - 1 - slab)
 
 
-def take_message(message, couple, left, transform_left, block, column):
+def take_message(message, couple, following, left, block, column):
     width = block.shape[0]
-    block[...] = unpack_symmetric(message[0:width, :])
-    column[...] = message[width : 2 * width, :]
-
-    @pl.when(left if transform_left else jnp.logical_not(left))
-    def _():
-        own = couple[0]
-        term = dot3(own, dot3(block[...], own.T))
-        column[...] = dot3(own, column[...])
-        block[...] = term
+    link = jnp.where(left, couple[0], following[...].T)
+    link_t = jnp.where(left, couple[0].T, following[...])
+    block[...] = dot3(link, dot3(unpack_symmetric(message[0:width, :]), link_t))
+    column[...] = dot3(link, message[width : 2 * width, :])
 
 
 def stage_kernel(step, energy, diag, couple, probes, *rest):
     if step > 0:
-        message, rest = rest[0], rest[1:]
-    factor_p, value_p, inverse_p, matrix_q, source_q, inverse_q, value_q, out, hold, column = rest
+        message, following, rest = rest[0], rest[1], rest[2:]
+    factor_p, value_p, inverse_p, matrix_q, source_q, inverse_q, value_q, out, hold = rest
     _, left, distance = place()
     centre = lax.axis_size("slab") // 2 - 1
     forward = jnp.logical_and(left, distance < centre)
@@ -151,7 +146,7 @@
     rq = probes[pl.ds(pl.multiple_of((1 - first) * width, width), width), :]
     if step > 0:
         taken = jnp.logical_and(distance >= 1, distance <= step)
-        take_message(message, couple, left, True, matrix_q, source_q)
+        take_message(message, couple, following, left, matrix_q, source_q)
         sp = sp - jnp.where(taken, matrix_q[...], 0.0)
         rp = rp - jnp.where(taken, source_q[...], 0.0)
     inner = couple[1]
@@ -176,24 +171,51 @@
         inverse_q[...] = xq
         value_q[...] = yq
 
-        @pl.when(left)
-        def _():
-            pack_symmetric(xq, out)
-            out[width : 2 * width, :] = yq
-
-        @pl.when(jnp.logical_not(left))
-        def _():
-            own = couple[0]
-            own_t = own.T
-            pack_symmetric(dot3(own_t, dot3(xq, own)), out)
-            out[width : 2 * width, :] = dot3(own_t, yq)
-
-
-def ready_kernel(energy, diag, couple, probes, following, factor_p, value_p, inverse_p, matrix_q,
-                 source_q, matrix, source, link, base, base_source, reach):
+        pack_symmetric(xq, out)
+        out[width : 2 * width, :] = yq
+
+
+def pack_full(matrix, out):
+    n = matrix.shape[0]
+    lanes = out.shape[1]
+    out[0:n, :] = matrix[:, 0:lanes]
+    out[n : n + n // 2, :] = jnp.concatenate(
+        [matrix[0 : n // 2, lanes:], matrix[n // 2 :, lanes:]], axis=1
+    )
+
+
+def unpack_full(packed, n):
+    rest = packed[n : n + n // 2]
+    lanes = packed.shape[1]
+    tail = jnp.concatenate([rest[:, : n - lanes], rest[:, n - lanes :]], axis=0)
+    return jnp.concatenate([packed[0:n], tail], axis=1)
+
+
+def spots(index, rows_all, depth, pitch, across, first_z, first_x):
+    plane = rows_all * across
+    z = index // plane - first_z
+    x = index // across % rows_all - first_x
+    y = index % across
+    inside = (z >= 0) & (z < depth) & (x >= 0) & (x < pitch)
+    row = jnp.where(inside, z * pitch + x, -1)
+    n = index.shape[1]
+    pick_row = lax.broadcasted_iota(jnp.int32, (depth * pitch, n), 0) == row
+    pick_y = lax.broadcasted_iota(jnp.int32, (across, n), 0) == y
+    return pick_row.astype(F32).astype(BF16), pick_y.astype(F32)
+
+
+def region_start(depth_here, rows_here):
+    first_z = lax.axis_index("slab") * depth_here - SWEEPS
+    return first_z, lax.axis_index("energy") * rows_here - SWEEPS
+
+
+def ready_kernel(rows_all, energy, diag, couple, probes, following, dopants, potential, got_even,
+                 got_odd, factor_p, value_p, inverse_p, matrix_q, source_q, matrix, source, link,
+                 base, base_source, reach, out, wide, dopant):
     slab, left, distance = place()
     half = lax.axis_size("slab") // 2
     width = diag.shape[1]
+    packed = width + width // 2
 
     @pl.when(slab == half - 1)
     def _():
@@ -216,16 +238,45 @@
         base[...] = diag[0] + shifted
         base_source[...] = probes[0:width, :]
 
-
-def centre_kernel(couple, message, matrix, source, link, base, base_source, factor, value,
-                  total, total_source, out, hold, block, column):
+    @pl.when(distance < half - 1)
+    def _():
+        pack_full(factor_p[...], out)
+        out[packed : packed + width, :] = value_p[...]
+
+    depth, rows_here, across = potential.shape
+    even_e = lax.axis_index("energy") % 2 == 0
+    below = jnp.where(even_e, got_odd[...], got_even[...])
+    above = jnp.where(even_e, got_even[...], got_odd[...])
+    spare = wide.shape[1] - rows_here - 2 * SWEEPS
+    parts = [below, potential[...], above]
+    if spare > 0:
+        parts.append(jnp.zeros((depth, spare, across), F32))
+    wide[...] = jnp.concatenate(parts, axis=1)
+    put_planes(out, packed + width, wide, slab % 2 == 0)
+    first_z, first_x = region_start(depth, rows_here)
+    rows, ys = spots(dopants[...], rows_all, depth + 2 * SWEEPS, wide.shape[1], across, first_z,
+                     first_x)
+    dopant[...] = dopant_charge * one_pass(rows, ys.astype(BF16), NT)
+
+
+def put_planes(out, start, wide, high):
+    pitch = wide.shape[1]
+    last = wide.shape[0] - SWEEPS
+    for k in range(SWEEPS):
+        plane = jnp.where(high, wide[last + k], wide[k])
+        out[start + k * pitch : start + (k + 1) * pitch, :] = plane
+
+
+def centre_kernel(couple, following, message, matrix, source, link, base, base_source, wide,
+                  factor, value, total, total_source, out, hold, block, column):
     slab, left, distance = place()
     half = lax.axis_size("slab") // 2
     width = matrix.shape[0]
+    put_planes(out, 2 * width, wide, slab % 2 == 1)
 
     @pl.when(jnp.logical_or(slab == half - 1, slab == half))
     def _():
-        take_message(message, couple, left, True, block, column)
+        take_message(message, couple, following, left, block, column)
         solved = invert(matrix[...] - block[...], hold, 1 / 16, 4)
         right_side = source[...] - column[...]
         near = link[...]
@@ -243,30 +294,79 @@
         out[width : 2 * width, :] = both_source
 
 
-def join_kernel(couple, message, total, total_source, factor, value, out_first, out_middle, out,
-                hold):
+def expand_kernel(couple, following, probes, probes_near, letter, second, factor, value, factor_p,
+                  value_p, reach, slope, offset, weights):
     slab, left, distance = place()
     half = lax.axis_size("slab") // 2
-    width = total.shape[0]
+    width = value.shape[0]
+    packed = width + width // 2
+
+    def put(block, m, v):
+        at = pl.ds(pl.multiple_of(block * width, width), width)
+        slope[at, :] = m
+        offset[at, :] = v
 
     @pl.when(jnp.logical_or(slab == half - 1, slab == half))
     def _():
+        own = jnp.where(left, 0, 1)
         sign = jnp.where(left, 1.0, -1.0)
-        matrix = sign * (unpack_symmetric(message[0:width, :]) - total[...])
-        right_side = sign * (message[width : 2 * width, :] - total_source[...])
-        middle = dot3(invert(matrix, hold, 1 / 64, 5), right_side)
-        first = value[...] + sign * dot3(factor[...], middle)
-        out_first[...] = first
-        out_middle[...] = middle
-        out[...] = first
+        m1 = sign * factor[...]
+        v1 = value[...]
+        put(own, m1, v1)
 
         @pl.when(left)
         def _():
-            out[...] = dot3(couple[0].T, first)
-
-
-def back_kernel(step, cells, couple, probes, message, first, middle, known_p, known_q, factor_p,
-                value_p, inverse_q, value_q, reach, out_p, out_q, out, dens):
+            put(1, -(dot3(factor_p[...], m1) + reach[...]), value_p[...] - dot3(factor_p[...], v1))
+
+        @pl.when(jnp.logical_not(left))
+        def _():
+            put(0, eye(width), jnp.zeros_like(v1))
+
+        link = jnp.where(left, couple[0].T, following[...])
+        carry = dot3(unpack_symmetric(letter[0:width, :]), link)
+        mq = -dot3(carry, m1)
+        vq = letter[width : 2 * width, :] - dot3(carry, v1)
+        put(jnp.where(left, 3, 2), mq, vq)
+        outer = unpack_full(second[0:packed, :], width)
+        put(jnp.where(left, 2, 3), -dot3(outer, mq),
+            second[packed : packed + width, :] - dot3(outer, vq))
+        weights[0 : 2 * width, :] = probes[...]
+        weights[2 * width :, :] = probes_near[...]
+
+
+def join_middle(message, total, total_source, hold, left):
+    width = total.shape[0]
+    sign = jnp.where(left, 1.0, -1.0)
+    matrix = sign * (unpack_symmetric(message[0:width, :]) - total[...])
+    right_side = sign * (message[width : 2 * width, :] - total_source[...])
+    return dot3(invert(matrix, hold, 1 / 64, 5), right_side)
+
+
+def join_pair_kernel(message, total, total_source, slope, offset, weights, dens, hold):
+    slab, left, distance = place()
+    half = lax.axis_size("slab") // 2
+
+    @pl.when(jnp.logical_or(slab == half - 1, slab == half))
+    def _():
+        middle = join_middle(message, total, total_source, hold, left)
+        terms = weights[...] * (offset[...] + dot3(slope[...], middle))
+        dens[...] = dot6(jnp.ones((8, terms.shape[1]), F32), terms, NT)
+
+
+def join_kernel(message, total, total_source, factor, value, out_first, out_middle, hold):
+    slab, left, distance = place()
+    half = lax.axis_size("slab") // 2
+
+    @pl.when(jnp.logical_or(slab == half - 1, slab == half))
+    def _():
+        middle = join_middle(message, total, total_source, hold, left)
+        sign = jnp.where(left, 1.0, -1.0)
+        out_first[...] = value[...] + sign * dot3(factor[...], middle)
+        out_middle[...] = middle
+
+
+def back_kernel(step, couple, following, probes, message, first, middle, known_p, known_q,
+                factor_p, value_p, inverse_q, value_q, reach, out_p, out_q, dens):
     slab, left, distance = place()
     centre = lax.axis_size("slab") // 2 - 1
     width = couple.shape[1]
@@ -278,13 +378,8 @@
 
     @pl.when(distance == step)
     def _():
-        out_q[...] = message[...]
-
-        @pl.when(jnp.logical_not(left))
-        def _():
-            out_q[...] = dot3(couple[0], message[...])
-
-        xq = value_q[...] - dot3(inverse_q[...], out_q[...])
+        link = jnp.where(left, following[...].T, couple[0])
+        xq = value_q[...] - dot3(inverse_q[...], dot3(link, message[...]))
         out_q[...] = xq
         out_p[...] = value_p[...] - dot3(factor_p[...], xq)
 
@@ -301,14 +396,6 @@
 
     xp = out_p[...]
     xq = out_q[...]
-    out[...] = xp
-
-    if step > 0:
-
-        @pl.when(left)
-        def _():
-            out[...] = dot3(couple[0].T, xp)
-
     xa = jnp.where(left, xp, xq)
     xb = jnp.where(left, xq, xp)
     terms = jnp.concatenate([probes[0:width, :] * xa, probes[width:, :] * xb], axis=0)
@@ -321,35 +408,27 @@
     for part in parts[1:]:
         total = total + part[0:1, :]
     out[0:1, :] = total * scale
-    out[1:2, :] = cells[...].astype(F32)
-
-
-def poisson_kernel(rows_all, planes, packet, near, far, dopants, around, out):
+    out[1:2, 0 : cells.shape[1]] = cells[...].astype(F32)
+
+
+def poisson_kernel(rows_all, planes, paired, packet, near, far, dopant_grid, wide, near_letter,
+                   near_at, far_letter, far_at, out, density):
     slab, slabs = lax.axis_index("slab"), lax.axis_size("slab")
-    depth, pitch, across = around.shape
-    total = depth * pitch
-    first_z = slab * out.shape[0] - SWEEPS
-    first_x = lax.axis_index("energy") * out.shape[1] - SWEEPS
-    plane = rows_all * across
-
-    def spots(index):
-        z = index // plane - first_z
-        x = index // across % rows_all - first_x
-        y = index % across
-        inside = (z >= 0) & (z < depth) & (x >= 0) & (x < pitch)
-        row = jnp.where(inside, z * pitch + x, -1)
-        n = index.shape[1]
-        pick_row = lax.broadcasted_iota(jnp.int32, (total, n), 0) == row
-        pick_y = lax.broadcasted_iota(jnp.int32, (across, n), 0) == y
-        return pick_row.astype(F32).astype(BF16), pick_y.astype(F32)
-
-    rows, ys = spots(dopants[...])
-    dopant = dopant_charge * one_pass(rows, ys.astype(BF16), NT)
+    depth, pitch, across = wide.shape
+    depth = depth + 2 * SWEEPS
+    first_z, first_x = region_start(out.shape[0], out.shape[1])
+    n = density.shape[1]
+    even = slab % 2 == 0
     alone = jnp.logical_or(slab == 0, slab == slabs - 1)
-    lonely = jnp.where(alone, 0.0, far[0:1, :])
-    weights = jnp.concatenate([packet[0:1, :], near[0:1, :], lonely], axis=1)
-    orbitals = jnp.concatenate([packet[1:2, :], near[1:2, :], far[1:2, :]], axis=1)
-    rows, ys = spots(orbitals.astype(jnp.int32))
+    own, beside, beyond = packet[0:1, 0:n], near[0:1, 0:n], far[0:1, 0:n]
+    if paired:
+        own = jnp.where(alone, near[0:1, n : 2 * n], own)
+        beside = jnp.where(alone, beside, packet[0:1, n : 2 * n])
+    density[...] = own
+    weights = jnp.concatenate([own, beside, jnp.where(alone, 0.0, beyond)], axis=1)
+    orbitals = jnp.concatenate([packet[1:2, 0:n], near[1:2, 0:n], far[1:2, 0:n]], axis=1)
+    orbitals = jnp.where(jnp.abs(orbitals) < 2.0**30, orbitals, -1.0).astype(jnp.int32)
+    rows, ys = spots(orbitals, rows_all, depth, pitch, across, first_z, first_x)
     spread = ys * weights
     h = spread.astype(BF16)
     rest = spread - h.astype(F32)
@@ -357,8 +436,15 @@
     low = (rest - m.astype(F32)).astype(BF16)
     electron = one_pass(rows, h, NT) + (one_pass(rows, m, NT) + one_pass(rows, low, NT))
     electron = electron.reshape(depth, pitch, across)
-    dopant = dopant.reshape(depth, pitch, across)
-    start = around[...]
+    dopant = dopant_grid[...].reshape(depth, pitch, across)
+    size = SWEEPS * pitch
+    near_planes = near_letter[near_at : near_at + size, :].reshape(SWEEPS, pitch, across)
+    far_planes = far_letter[far_at : far_at + size, :].reshape(SWEEPS, pitch, across)
+    start = jnp.concatenate(
+        [jnp.where(even, far_planes, near_planes), wide[...],
+         jnp.where(even, near_planes, far_planes)],
+        axis=0,
+    )
     zs = lax.broadcasted_iota(jnp.int32, start.shape, 0) + first_z
     xs = lax.broadcasted_iota(jnp.int32, start.shape, 1) + first_x
     ys = lax.broadcasted_iota(jnp.int32, start.shape, 2)
@@ -439,7 +525,9 @@
     letter = like(2 * width, probe_count)
     sq, col = (width, width), (width, probe_count)
 
-    following = lax.ppermute(couple[0], "slab", [(s + 1, s) for s in range(half - 1, half)])
+    following = lax.ppermute(couple[0], "slab", [((s + 1) % slabs, s) for s in range(slabs)])
+    paired = half == 2
+    probes_near = slab_exchange(probes, False) if paired else None
 
     message = None
     for t in range(half - 1):
@@ -449,79 +537,94 @@
                 _, _, distance = place()
                 message = jnp.where(distance == t, message, kept)
             kept = message
-            args.append(message)
+            args += [message, following]
         state = call(
             functools.partial(stage_kernel, t), f"stage{t}",
             (square, column, square, square, column, square, column, letter),
-            args, (sq, col), 1,
+            args, (sq,), 1,
         )
         if t == 0:
             prepared = state
         message = slab_exchange(state[-1], t % 2 == 1)
     factor_p, value_p, _, _, _, inverse_q, value_q, _ = state
-    matrix, source, link, base, base_source, reach = call(
-        ready_kernel, "ready", (square, column, square, square, column, square),
-        [energy_index, diag_blocks, couple, probes, following, *prepared[:5]], (), 1,
-    )
+
+    depth, rows_here, across = initial_potential.shape
+    halo = SWEEPS
+    rows_all = rows_here * energies
+    pitch = -(-(rows_here + 2 * halo) // 8) * 8
+    strip = halo * pitch
+    odd_e = lax.axis_index("energy") % 2 == 1
+    low, high = initial_potential[:, :halo], initial_potential[:, rows_here - halo :]
+    got_even = energy_exchange(jnp.where(odd_e, low, high), False)
+    got_odd = energy_exchange(jnp.where(odd_e, high, low), True)
+    packed = width + width // 2
+    near_at, far_at = packed + width, 2 * width
+    cells = (depth + 2 * halo) * pitch
+
+    matrix, source, link, base, base_source, reach, second, wide, dopant_grid = call(
+        functools.partial(ready_kernel, rows_all), "ready",
+        (square, column, square, square, column, square, like(near_at + strip, probe_count),
+         like(depth, pitch, across), like(cells, across)),
+        [energy_index, diag_blocks, couple, probes, following, dopant_cells.reshape(1, -1),
+         initial_potential, got_even, got_odd, *prepared[:5]], (), 1,
+    )
+    message, second = lax.optimization_barrier((message, second))
+    second = slab_exchange(second, False)
     factor, value, total, total_source, sent = call(
-        centre_kernel, "centre", (square, column, square, column, letter),
-        [couple, message, matrix, source, link, base, base_source], (sq, sq, col),
-    )
-    message = slab_exchange(sent, half % 2 == 0)
-    first, middle, sent = call(
-        join_kernel, "join", (column, column, column),
-        [couple, message, total, total_source, factor, value], (sq,),
-    )
-    cells_here = orbital_cell.reshape(1, -1)
-    centred = lax.axis_index("slab") == half - 1
-    if half > 2:
+        centre_kernel, "centre",
+        (square, column, square, column, like(far_at + strip, probe_count)),
+        [couple, following, message, matrix, source, link, base, base_source, wide],
+        (sq, sq, col),
+    )
+    across_middle = slab_exchange(sent, half % 2 == 0)
+    far_letter = across_middle if paired else slab_exchange(sent, True)
+    if paired:
+        slope, offset, weights = call(
+            expand_kernel, "expand",
+            (like(4 * width, width), like(4 * width, probe_count), like(4 * width, probe_count)),
+            [couple, following, probes, probes_near, message, second, factor, value,
+             prepared[0], prepared[1], reach],
+        )
+        dens = call(
+            join_pair_kernel, "join", like(8, 4 * width),
+            [across_middle, total, total_source, slope, offset, weights], (sq,),
+        )
+    else:
+        first, middle = call(
+            join_kernel, "join", (column, column),
+            [across_middle, total, total_source, factor, value], (sq,),
+        )
+        centred = lax.axis_index("slab") == half - 1
         factor_p = jnp.where(centred, prepared[0], factor_p)
         value_p = jnp.where(centred, prepared[1], value_p)
-    known_p, known_q = first, middle
-    for t in range(half - 2, -1, -1):
-        message = slab_exchange(sent, t % 2 == 1)
-        known_p, known_q, sent, dens = call(
-            functools.partial(back_kernel, t), f"back{t}",
-            (column, column, column, like(8, 2 * width)),
-            [cells_here, couple, probes, message, first, middle, known_p, known_q, factor_p,
-             value_p, inverse_q, value_q, reach],
-        )
+        known_p, known_q = first, middle
+        for t in range(half - 2, -1, -1):
+            known_p, known_q, dens = call(
+                functools.partial(back_kernel, t), f"back{t}",
+                (column, column, like(8, 2 * width)),
+                [couple, following, probes, slab_exchange(known_p, t % 2 == 1), first, middle,
+                 known_p, known_q, factor_p, value_p, inverse_q, value_q, reach],
+            )
     parts = [dens] + [
         lax.ppermute(dens, "energy", [(e, e ^ k) for e in range(energies)])
         for k in range(1, energies)
     ]
     packet = call(
         functools.partial(total_kernel, 1.0 / (probe_count * energies)), "total",
-        like(8, 2 * width), [cells_here, *parts],
-    )
-    density = packet[0]
+        like(*dens.shape), [orbital_cell.reshape(1, -1), *parts],
+    )
     near = slab_exchange(packet, False)
     far = slab_exchange(packet, True)
 
-    depth, rows_here, across = initial_potential.shape
-    halo = SWEEPS
-    odd_e = energy % 2 == 1
-    low, high = initial_potential[:, :halo], initial_potential[:, rows_here - halo :]
-    got_even = energy_exchange(jnp.where(odd_e, low, high), False)
-    got_odd = energy_exchange(jnp.where(odd_e, high, low), True)
-    below = jnp.where(odd_e, got_even, got_odd)
-    above = jnp.where(odd_e, got_odd, got_even)
-    wide = jnp.concatenate([below, initial_potential, above], axis=1)
-    odd_s = slab % 2 == 1
-    low, high = wide[:halo], wide[depth - halo :]
-    got_even = slab_exchange(jnp.where(odd_s, low, high), False)
-    got_odd = slab_exchange(jnp.where(odd_s, high, low), True)
-    below = jnp.where(odd_s, got_even, got_odd)
-    above = jnp.where(odd_s, got_odd, got_even)
-    region = jnp.concatenate([below, wide, above], axis=0)
-    pitch = -(-region.shape[1] // 8) * 8
-    region = jnp.pad(region, ((0, 0), (0, pitch - region.shape[1]), (0, 0)))
-    rows_all = rows_here * energies
-    potential = call(
-        functools.partial(poisson_kernel, rows_all, depth * slabs), "poisson",
-        like(depth, rows_here, across),
-        [packet, near, far, dopant_cells.reshape(1, -1), region],
-    )
+    def poisson(packet, near, far, dopant_grid, wide, near_letter, far_letter, out, density):
+        poisson_kernel(rows_all, depth * slabs, paired, packet, near, far, dopant_grid, wide,
+                       near_letter, near_at, far_letter, far_at, out, density)
+
+    potential, density = call(
+        poisson, "poisson", (like(depth, rows_here, across), like(1, 2 * width)),
+        [packet, near, far, dopant_grid, wide, second, far_letter],
+    )
+    density = density.reshape(-1)
     return (potential, density)
 
 

time: 55.5 us -> 52.4 us (0.944)
  starting transfers between devices: 32.7 us -> 22.9 us
  waiting for transfers between devices: 7.52 us -> 14.2 us
    ppermute x7 -> x6, starting transfers between devices: 26.9 us -> 14.1 us  [slab_exchange(): return lax.ppermute(value, ('slab', 'energy'), whole)]
    ppermute x7 -> x6, waiting for transfers between devices: 5.13 us -> 9.73 us  [slab_exchange(): return lax.ppermute(value, ('slab', 'energy'), whole)]
    ppermute x1, starting transfers between devices: 0.8 us -> 5.13 us  [body(): lax.ppermute(couple[0], 'slab', [((s + 1) % slabs, s) for s in range(slab...]
    ppermute x2, starting transfers between devices: 3.14 us -> 1.67 us  [energy_exchange(): return lax.ppermute(value, 'energy', pairs)]
    ppermute x3, waiting for transfers between devices: 1.89 us -> 2.96 us  [body(): lax.ppermute(dens, 'energy', [(e, e ^ k) for e in range(energies)])]
    ppermute x2, waiting for transfers between devices: 0.5 us -> 1.54 us  [energy_exchange(): return lax.ppermute(value, 'energy', pairs)]
    squeeze x1, local copies, waits for them, and re-layouts: 0.01 us -> 1 us  [body(): couple[0]]
    slice x1 -> x0, local copies, waits for them, and re-layouts: 0.6 us -> none  [body(): density = packet[0]]
  transfers between devices with their start and end apart: 13 -> 12, of which waited for: 6 -> 6; matrix products, arithmetic and copies ran while one was open for 1% -> 0% of each run, Pallas kernels for 0% -> 15%
where the time goes in v3:
time: 52.4 us; the launch traced here: 52.1 us
  starting transfers between devices  22.9 us (44%)
  waiting for transfers between devices  14.2 us (27%)
  Pallas kernels  9.42 us (18%)
  local copies, waits for them, and re-layouts  3.62 us (7%)
  between operations  1.38 us (3%)
  other arithmetic  0.6 us (1%)
    ppermute x6, starting transfers between devices, slab_exchange(): return lax.ppermute(value, ('slab', 'energy'), whole)  14.1 us
    ppermute x6, waiting for transfers between devices, slab_exchange(): return lax.ppermute(value, ('slab', 'energy'), whole)  9.73 us
    pallas_call x7, Pallas kernels, call(): pl.pallas_call(kernel, out_shape=outs, in_specs=[SM] * scalars + [VM] * (...  9.42 us
    ppermute x1, starting transfers between devices, body(): lax.ppermute(couple[0], 'slab', [((s + 1) % slabs, s) for s in range(slab...  5.13 us
    ppermute x3, waiting for transfers between devices, body(): lax.ppermute(dens, 'energy', [(e, e ^ k) for e in range(energies)])  2.96 us
    unnamed x16, local copies, waits for them, and re-layouts  2.61 us
    ppermute x3, starting transfers between devices, body(): lax.ppermute(dens, 'energy', [(e, e ^ k) for e in range(energies)])  1.92 us
    ppermute x2, starting transfers between devices, energy_exchange(): return lax.ppermute(value, 'energy', pairs)  1.67 us
  transfers between devices with their start and end apart: 12, of which 6 were waited for; matrix products, arithmetic and copies ran while one was open for 0% of the time, Pallas kernels for 15%

profile of v3, /device:TPU:0, one launch (start us, length us, event | category | flops | bytes accessed | tf_op | source)
XLA Modules:
  0.0 52.1 jit_solution(6515992198174417708)
XLA Ops:
  0.6 1.0 %slice_bitcast_fusion = f32[192,192]{1,0:T(8,128)S(1)} fusion(f32[2,192,192]{2,1,0:T(8,128)} %couple.7), kind=kLoop, calls=%fused_computation | loop fusion | bytes 294912 | tf_op jit(solution)/shard_map/squeeze | solution.py:528
  1.6 5.1 %collective-permute-start = (f32[192,192]{1,0:T(8,128)S(1)}, f32[192,192]{1,0:T(8,128)S(1)}, u32[]{:S(2)}, u32[]{:S(2)}) collective-permute-start(f32[192,192]{1,0:T(8,128)S(1)} %slice_bitcast_fusion), channel_id=1, source_target_pairs={{4,0},{8,4},{12,8},{0,12},{5,1},{9,5},{13,9},{1,13},{6,2},{10,6},{... | collective-permute-start | bytes 442376 | tf_op jit(solution)/shard_map/ppermute | solution.py:528
  7.4 0.0 copy-start.1
  7.5 0.9 %copy-done.1 = f32[384,128]{1,0:T(8,128)S(1)} copy-done((f32[384,128]{1,0:T(8,128)S(1)}, f32[384,128]{1,0:T(8,128)}, u32[]{:S(2)}) %copy-start.1) | copy-done | bytes 196632
  8.4 1.0 %copy-done.3 = f32[2,192,192]{2,1,0:T(8,128)S(1)} copy-done((f32[2,192,192]{2,1,0:T(8,128)S(1)}, f32[2,192,192]{2,1,0:T(8,128)}, u32[]{:S(2)}) %copy-start.3) | copy-done | bytes 294936
  9.4 7.3 %stage0.1 = (f32[192,192]{1,0:T(8,128)S(1)}, f32[192,128]{1,0:T(8,128)S(1)}, f32[192,192]{1,0:T(8,128)S(1)}, f32[192,192]{1,0:T(8,128)S(1)}, f32[192,128]{1,0:T(...) custom-call(s32[1]{0:T(128)S(6)} %copy.9.energy, f32[2,192,192]{2,1,0:T(8,128)S(1)} %copy-done.3, ...), custom_call_target="tpu_custom_call" | custom-call | flops 100000000 | bytes 1000000 | tf_op jit(solution)/shard_map/stage0/pallas_call | solution.py:480
  16.7 0.0 collective-permute-start.1
  16.7 0.1 collective-permute-start.2
  16.8 1.6 %collective-permute-start.3 = (f32[8,2,128]{2,1,0:T(2,128)S(1)}, f32[8,2,128]{2,1,0:T(2,128)S(1)}, u32[]{:S(2)}, u32[]{:S(2)}) collective-permute-start(f32[8,2,128]{2,1,0:T(2,128)S(1)} %get-tuple-element.56), channel_id=1, source_target_pairs={{1,2},{2,1},{3,0},{0,3},{5,6},{6,5},{7,4},{4,7},{9,10},{10,9},{11,... | collective-permute-start | bytes 24584 | tf_op jit(solution)/shard_map/ppermute | solution.py:515
  18.4 0.0 collective-permute-done.2.got_even
  18.4 1.5 %collective-permute-done.3.got_odd = f32[8,2,128]{2,1,0:T(2,128)S(1)} collective-permute-done((f32[8,2,128]{2,1,0:T(2,128)S(1)}, f32[8,2,128]{2,1,0:T(2,128)S(1)}, u32[]{:S(2)}, u32[]{:S(2)}) %collective-permute-start.3) | collective-permute-done | bytes 8224 | tf_op jit(solution)/shard_map/ppermute | solution.py:515
  19.9 0.0 collective-permute-done.following
  19.9 0.7 %copy-done.6 = s32[1024]{0:T(1024)S(1)} copy-done((s32[1024]{0:T(1024)S(1)}, s32[1024]{0:T(1024)}, u32[]{:S(2)}) %copy-start.6) | copy-done | bytes 4120
  20.6 0.4 ready.1
  21.0 2.0 %collective-permute-done.1.message.letter = f32[384,128]{1,0:T(8,128)S(1)} collective-permute-done((f32[384,128]{1,0:T(8,128)S(1)}, f32[384,128]{1,0:T(8,128)S(1)}, u32[]{:S(2)}, u32[]{:S(2)}) %collective-permute-start.1) | collective-permute-done | bytes 196640 | tf_op jit(solution)/shard_map/ppermute | solution.py:507
  23.0 0.9 %collective-permute-start.6 = (f32[528,128]{1,0:T(8,128)S(1)}, f32[528,128]{1,0:T(8,128)S(1)}, u32[]{:S(2)}, u32[]{:S(2)}) collective-permute-start(f32[528,128]{1,0:T(8,128)S(1)} %get-tuple-element.46), channel_id=1, source_target_pairs={{0,4},{1,5},{2,6},{3,7},{4,0},{5,1},{6,2},{7,3},{8,12},{9,13},{10,... | collective-permute-start | bytes 811016 | tf_op jit(solution)/shard_map/ppermute | solution.py:507
  23.9 0.4 collective-permute-start.4
  24.3 5.2 %collective-permute-start.5 = (f32[384,128]{1,0:T(8,128)S(1)}, f32[384,128]{1,0:T(8,128)S(1)}, u32[]{:S(2)}, u32[]{:S(2)}) collective-permute-start(f32[384,128]{1,0:T(8,128)S(1)} %copy-done.2), channel_id=1, source_target_pairs={{0,4},{1,5},{2,6},{3,7},{4,0},{5,1},{6,2},{7,3},{8,12},{9,13},{10,... | collective-permute-start | bytes 589832 | tf_op jit(solution)/shard_map/ppermute | solution.py:507
  29.6 5.9 %collective-permute-done.5.probes_near = f32[384,128]{1,0:T(8,128)S(1)} collective-permute-done((f32[384,128]{1,0:T(8,128)S(1)}, f32[384,128]{1,0:T(8,128)S(1)}, u32[]{:S(2)}, u32[]{:S(2)}) %collective-permute-start.5) | collective-permute-done | bytes 196640 | tf_op jit(solution)/shard_map/ppermute | solution.py:507
  35.5 0.0 collective-permute-done.6.second.near_letter
  35.5 0.1 collective-permute-start.7
  35.6 1.6 %collective-permute-start.8 = (f32[8,768]{1,0:T(8,128)S(1)}, f32[8,768]{1,0:T(8,128)S(1)}, u32[]{:S(2)}, u32[]{:S(2)}) collective-permute-start(f32[8,768]{1,0:T(8,128)S(1)} %join.1.rest_0_), channel_id=1, source_target_pairs={{0,2},{1,3},{2,0},{3,1},{4,6},{5,7},{6,4},{7,5},{8,10},{9,11},{10,... | collective-permute-start | bytes 73736 | tf_op jit(solution)/shard_map/ppermute | solution.py:609
  37.2 0.3 collective-permute-start.9
  37.4 0.0 collective-permute-done.7.rest_1_
  37.5 2.0 %collective-permute-done.8.rest_2_ = f32[8,768]{1,0:T(8,128)S(1)} collective-permute-done((f32[8,768]{1,0:T(8,128)S(1)}, f32[8,768]{1,0:T(8,128)S(1)}, u32[]{:S(2)}, u32[]{:S(2)}) %collective-permute-start.8) | collective-permute-done | bytes 24608 | tf_op jit(solution)/shard_map/ppermute | solution.py:609
  39.5 0.9 %collective-permute-done.9.rest_3_ = f32[8,768]{1,0:T(8,128)S(1)} collective-permute-done((f32[8,768]{1,0:T(8,128)S(1)}, f32[8,768]{1,0:T(8,128)S(1)}, u32[]{:S(2)}, u32[]{:S(2)}) %collective-permute-start.9) | collective-permute-done | bytes 24608 | tf_op jit(solution)/shard_map/ppermute | solution.py:609
  40.4 7.6 %collective-permute-start.10 = (f32[8,768]{1,0:T(8,128)S(1)}, f32[8,768]{1,0:T(8,128)S(1)}, u32[]{:S(2)}, u32[]{:S(2)}) collective-permute-start(f32[8,768]{1,0:T(8,128)S(1)} %total.1.packet), channel_id=1, source_target_pairs={{0,4},{1,5},{2,6},{3,7},{4,0},{5,1},{6,2},{7,3},{8,12},{9,13},{10,... | collective-permute-start | bytes 73736 | tf_op jit(solution)/shard_map/ppermute | solution.py:507
  48.1 0.0 collective-permute-start.11
  48.1 1.8 %collective-permute-done.10.near = f32[8,768]{1,0:T(8,128)S(1)} collective-permute-done((f32[8,768]{1,0:T(8,128)S(1)}, f32[8,768]{1,0:T(8,128)S(1)}, u32[]{:S(2)}, u32[]{:S(2)}) %collective-permute-start.10) | collective-permute-done | bytes 24608 | tf_op jit(solution)/shard_map/ppermute | solution.py:507
  49.9 0.0 collective-permute-done.11.far
  49.9 1.7 %poisson.1 = (f32[8,16,128]{2,1,0:T(8,128)}, f32[1,384]{1,0:T(1,128)S(1)}) custom-call(f32[8,768]{1,0:T(8,128)S(1)} %total.1.packet, f32[8,768]{1,0:T(8,128)S(1)} %collective-permute-done.10.near, f32[8,768]{1,0:T(8,128)S(1)} %collective-permute-done.11.far, f32[288,128]{1,0:T(8,128)S(1)} %get-tuple-element.53.dopant_grid, ...), custom_call_target="tpu_custom_call" | custom-call | flops 100000000 | bytes 1000000 | tf_op jit(solution)/shard_map/poisson/pallas_call | solution.py:480
  51.5 0.6 %reduce = f32[384]{0:T(512)} reduce(f32[1,384]{1,0:T(1,128)S(1)} %get-tuple-element.55, f32[]{:T(128)} %constant.21), dimensions={0}, to_apply=%get-tuple-element.55.reduce_sub_computation | reduce | bytes 3076 | tf_op jit(solution)/shard_map/poisson/pallas_call | solution.py:480
  (19 shorter events, 0.1 us)
Async XLA Ops:
  0.6 6.8 %copy-start = (f32[2,192,192]{2,1,0:T(8,128)S(1)}, f32[2,192,192]{2,1,0:T(8,128)}, u32[]{:S(2)}) copy-start(f32[2,192,192]{2,1,0:T(8,128)} %couple.7) | copy-start | bytes 884740
  1.6 18.3 %collective-permute-start = (f32[192,192]{1,0:T(8,128)S(1)}, f32[192,192]{1,0:T(8,128)S(1)}, u32[]{:S(2)}, u32[]{:S(2)}) collective-permute-start(f32[192,192]{1,0:T(8,128)S(1)} %slice_bitcast_fusion), channel_id=1, source_target_pairs={{4,0},{8,4},{12,8},{0,12},{5,1},{9,5},{13,9},{1,13},{6,2},{10,6},{... | collective-permute-start | bytes 442376 | tf_op jit(solution)/shard_map/ppermute | solution.py:528
  7.4 0.9 %copy-start.1 = (f32[384,128]{1,0:T(8,128)S(1)}, f32[384,128]{1,0:T(8,128)}, u32[]{:S(2)}) copy-start(f32[384,128]{1,0:T(8,128)} %probes.5) | copy-start | bytes 589828
  8.4 1.0 %copy-start.3 = (f32[2,192,192]{2,1,0:T(8,128)S(1)}, f32[2,192,192]{2,1,0:T(8,128)}, u32[]{:S(2)}) copy-start(f32[2,192,192]{2,1,0:T(8,128)} %diag.3) | copy-start | bytes 884740
  9.4 7.3 %copy-start.5 = (f32[8,16,128]{2,1,0:T(8,128)S(1)}, f32[8,16,128]{2,1,0:T(8,128)}, u32[]{:S(2)}) copy-start(f32[8,16,128]{2,1,0:T(8,128)} %potential.1) | copy-start | bytes 196612
  9.4 10.5 %copy-start.2 = (f32[384,128]{1,0:T(8,128)S(1)}, f32[384,128]{1,0:T(8,128)}, u32[]{:S(2)}) copy-start(f32[384,128]{1,0:T(8,128)} %probes.5) | copy-start | bytes 589828
  9.4 10.5 %copy-start.4 = (f32[2,192,192]{2,1,0:T(8,128)S(1)}, f32[2,192,192]{2,1,0:T(8,128)}, u32[]{:S(2)}) copy-start(f32[2,192,192]{2,1,0:T(8,128)} %diag.3) | copy-start | bytes 884740
  16.7 6.4 %collective-permute-start.1 = (f32[384,128]{1,0:T(8,128)S(1)}, f32[384,128]{1,0:T(8,128)S(1)}, u32[]{:S(2)}, u32[]{:S(2)}) collective-permute-start(f32[384,128]{1,0:T(8,128)S(1)} %get-tuple-element.29), channel_id=1, source_target_pairs={{0,4},{1,5},{2,6},{3,7},{4,0},{5,1},{6,2},{7,3},{8,12},{9,13},{10,... | collective-permute-start | bytes 589832 | tf_op jit(solution)/shard_map/ppermute | solution.py:507
  16.7 1.7 %collective-permute-start.2 = (f32[8,2,128]{2,1,0:T(2,128)S(1)}, f32[8,2,128]{2,1,0:T(2,128)S(1)}, u32[]{:S(2)}, u32[]{:S(2)}) collective-permute-start(f32[8,2,128]{2,1,0:T(2,128)S(1)} %get-tuple-element.57), channel_id=1, source_target_pairs={{0,1},{1,0},{2,3},{3,2},{4,5},{5,4},{6,7},{7,6},{8,9},{9,8},{10,11... | collective-permute-start | bytes 24584 | tf_op jit(solution)/shard_map/ppermute | solution.py:515
  16.8 3.1 %collective-permute-start.3 = (f32[8,2,128]{2,1,0:T(2,128)S(1)}, f32[8,2,128]{2,1,0:T(2,128)S(1)}, u32[]{:S(2)}, u32[]{:S(2)}) collective-permute-start(f32[8,2,128]{2,1,0:T(2,128)S(1)} %get-tuple-element.56), channel_id=1, source_target_pairs={{1,2},{2,1},{3,0},{0,3},{5,6},{6,5},{7,4},{4,7},{9,10},{10,9},{11,... | collective-permute-start | bytes 24584 | tf_op jit(solution)/shard_map/ppermute | solution.py:515
  19.9 0.7 %copy-start.6 = (s32[1024]{0:T(1024)S(1)}, s32[1024]{0:T(1024)}, u32[]{:S(2)}) copy-start(s32[1024]{0:T(1024)} %param.12) | copy-start | bytes 12292
  23.0 12.4 %collective-permute-start.6 = (f32[528,128]{1,0:T(8,128)S(1)}, f32[528,128]{1,0:T(8,128)S(1)}, u32[]{:S(2)}, u32[]{:S(2)}) collective-permute-start(f32[528,128]{1,0:T(8,128)S(1)} %get-tuple-element.46), channel_id=1, source_target_pairs={{0,4},{1,5},{2,6},{3,7},{4,0},{5,1},{6,2},{7,3},{8,12},{9,13},{10,... | collective-permute-start | bytes 811016 | tf_op jit(solution)/shard_map/ppermute | solution.py:507
  23.9 11.6 %collective-permute-start.4 = (f32[432,128]{1,0:T(8,128)S(1)}, f32[432,128]{1,0:T(8,128)S(1)}, u32[]{:S(2)}, u32[]{:S(2)}) collective-permute-start(f32[432,128]{1,0:T(8,128)S(1)} %get-tuple-element.43), channel_id=1, source_target_pairs={{4,8},{5,9},{6,10},{7,11},{8,4},{9,5},{10,6},{11,7},{0,1},{1,0},{2... | collective-permute-start | bytes 663560 | tf_op jit(solution)/shard_map/ppermute | solution.py:507
  24.3 11.1 %collective-permute-start.5 = (f32[384,128]{1,0:T(8,128)S(1)}, f32[384,128]{1,0:T(8,128)S(1)}, u32[]{:S(2)}, u32[]{:S(2)}) collective-permute-start(f32[384,128]{1,0:T(8,128)S(1)} %copy-done.2), channel_id=1, source_target_pairs={{0,4},{1,5},{2,6},{3,7},{4,0},{5,1},{6,2},{7,3},{8,12},{9,13},{10,... | collective-permute-start | bytes 589832 | tf_op jit(solution)/shard_map/ppermute | solution.py:507
  35.5 2.0 %copy-start.7 = (s32[384]{0:T(512)S(1)}, s32[384]{0:T(512)}, u32[]{:S(2)}) copy-start(s32[384]{0:T(512)} %param.11) | copy-start | bytes 4612
  35.5 1.9 %collective-permute-start.7 = (f32[8,768]{1,0:T(8,128)S(1)}, f32[8,768]{1,0:T(8,128)S(1)}, u32[]{:S(2)}, u32[]{:S(2)}) collective-permute-start(f32[8,768]{1,0:T(8,128)S(1)} %join.1.rest_0_), channel_id=1, source_target_pairs={{0,1},{1,0},{2,3},{3,2},{4,5},{5,4},{6,7},{7,6},{8,9},{9,8},{10,11... | collective-permute-start | bytes 73736 | tf_op jit(solution)/shard_map/ppermute | solution.py:609
  35.6 3.9 %collective-permute-start.8 = (f32[8,768]{1,0:T(8,128)S(1)}, f32[8,768]{1,0:T(8,128)S(1)}, u32[]{:S(2)}, u32[]{:S(2)}) collective-permute-start(f32[8,768]{1,0:T(8,128)S(1)} %join.1.rest_0_), channel_id=1, source_target_pairs={{0,2},{1,3},{2,0},{3,1},{4,6},{5,7},{6,4},{7,5},{8,10},{9,11},{10,... | collective-permute-start | bytes 73736 | tf_op jit(solution)/shard_map/ppermute | solution.py:609
  37.2 3.3 %collective-permute-start.9 = (f32[8,768]{1,0:T(8,128)S(1)}, f32[8,768]{1,0:T(8,128)S(1)}, u32[]{:S(2)}, u32[]{:S(2)}) collective-permute-start(f32[8,768]{1,0:T(8,128)S(1)} %join.1.rest_0_), channel_id=1, source_target_pairs={{0,3},{1,2},{2,1},{3,0},{4,7},{5,6},{6,5},{7,4},{8,11},{9,10},{10,... | collective-permute-start | bytes 73736 | tf_op jit(solution)/shard_map/ppermute | solution.py:609
  40.4 9.4 %collective-permute-start.10 = (f32[8,768]{1,0:T(8,128)S(1)}, f32[8,768]{1,0:T(8,128)S(1)}, u32[]{:S(2)}, u32[]{:S(2)}) collective-permute-start(f32[8,768]{1,0:T(8,128)S(1)} %total.1.packet), channel_id=1, source_target_pairs={{0,4},{1,5},{2,6},{3,7},{4,0},{5,1},{6,2},{7,3},{8,12},{9,13},{10,... | collective-permute-start | bytes 73736 | tf_op jit(solution)/shard_map/ppermute | solution.py:507
  48.1 1.8 %collective-permute-start.11 = (f32[8,768]{1,0:T(8,128)S(1)}, f32[8,768]{1,0:T(8,128)S(1)}, u32[]{:S(2)}, u32[]{:S(2)}) collective-permute-start(f32[8,768]{1,0:T(8,128)S(1)} %total.1.packet), channel_id=1, source_target_pairs={{4,8},{5,9},{6,10},{7,11},{8,4},{9,5},{10,6},{11,7},{0,1},{1,0},{2... | collective-permute-start | bytes 73736 | tf_op jit(solution)/shard_map/ppermute | solution.py:507

commit v4 on v3

--- a/solution.py
+++ b/solution.py
@@ -122,44 +122,64 @@
     return slab, left, jnp.where(left, slab, slabs - 1 - slab)
 
 
-def take_message(message, couple, following, left, block, column):
+def following(ahead):
+    even, odd = ahead
+    return jnp.where(lax.axis_index("slab") % 2 == 0, even[0], odd[0])
+
+
+def take_message(message, couple, ahead, left, block, column):
     width = block.shape[0]
-    link = jnp.where(left, couple[0], following[...].T)
-    link_t = jnp.where(left, couple[0].T, following[...])
+    link_t = jnp.where(left, couple[0].T, following(ahead))
+    link = jnp.where(left, couple[0], following(ahead).T)
     block[...] = dot3(link, dot3(unpack_symmetric(message[0:width, :]), link_t))
     column[...] = dot3(link, message[width : 2 * width, :])
 
 
-def stage_kernel(step, energy, diag, couple, probes, *rest):
+def stage_kernel(step, energy, diag_far, couple_far, probes_far, *rest):
     if step > 0:
-        message, following, rest = rest[0], rest[1], rest[2:]
-    factor_p, value_p, inverse_p, matrix_q, source_q, inverse_q, value_q, out, hold = rest
+        message, even, odd, rest = rest[0], rest[1], rest[2], rest[3:]
+    factor_p, value_p, inverse_p, matrix_q, source_q, inverse_q, value_q, out = rest[:8]
+    hold, diag, couple, probes, sems = rest[8:]
     _, left, distance = place()
     centre = lax.axis_size("slab") // 2 - 1
     forward = jnp.logical_and(left, distance < centre)
     first = jnp.where(forward, 0, 1)
     width = diag.shape[1]
+    loads = [
+        pltpu.make_async_copy(diag_far.at[first], diag.at[0], sems.at[0]),
+        pltpu.make_async_copy(couple_far, couple, sems.at[1]),
+        pltpu.make_async_copy(probes_far, probes, sems.at[2]),
+        pltpu.make_async_copy(diag_far.at[1 - first], diag.at[1], sems.at[3]),
+    ]
+    for load in loads:
+        load.start()
+    loads[0].wait()
     shift = sigma_base + sigma_step * jnp.full((1, 1), energy[0], jnp.int32).astype(F32)
     shifted = shift * eye(width)
-    sp = diag[first] + shifted
+    sp = diag[0] + shifted
+    if step > 0:
+        loads[1].wait()
+        taken = jnp.logical_and(distance >= 1, distance <= step)
+        take_message(message, couple, (even, odd), left, matrix_q, source_q)
+        sp = sp - jnp.where(taken, matrix_q[...], 0.0)
+        extra = jnp.where(taken, source_q[...], 0.0)
+    xp = invert(sp, hold, 1 / 16, 4)
+    inverse_p[...] = xp
+    for k in range(2 if step > 0 else 1, 4):
+        loads[k].wait()
     rp = probes[pl.ds(pl.multiple_of(first * width, width), width), :]
     rq = probes[pl.ds(pl.multiple_of((1 - first) * width, width), width), :]
     if step > 0:
-        taken = jnp.logical_and(distance >= 1, distance <= step)
-        take_message(message, couple, following, left, matrix_q, source_q)
-        sp = sp - jnp.where(taken, matrix_q[...], 0.0)
-        rp = rp - jnp.where(taken, source_q[...], 0.0)
+        rp = rp - extra
     inner = couple[1]
     inner_t = inner.T
     apq = jnp.where(forward, inner_t, inner)
     aqp = jnp.where(forward, inner, inner_t)
-    xp = invert(sp, hold, 1 / 16, 4)
-    inverse_p[...] = xp
     fp = dot3(xp, apq)
     yp = dot3(xp, rp)
     factor_p[...] = fp
     value_p[...] = yp
-    sq = diag[1 - first] + shifted - dot3(aqp, fp)
+    sq = diag[1] + shifted - dot3(aqp, fp)
     rq = rq - dot3(aqp, yp)
     matrix_q[...] = sq
     source_q[...] = rq
@@ -209,7 +229,7 @@
     return first_z, lax.axis_index("energy") * rows_here - SWEEPS
 
 
-def ready_kernel(rows_all, energy, diag, couple, probes, following, dopants, potential, got_even,
+def ready_kernel(rows_all, energy, diag, couple, probes, even, odd, dopants, potential, got_even,
                  got_odd, factor_p, value_p, inverse_p, matrix_q, source_q, matrix, source, link,
                  base, base_source, reach, out, wide, dopant):
     slab, left, distance = place()
@@ -219,7 +239,7 @@
 
     @pl.when(slab == half - 1)
     def _():
-        ahead = following[...]
+        ahead = following((even, odd))
         across = dot3(inverse_p[...], ahead.T)
         reach[...] = across
         matrix[...] = matrix_q[...]
@@ -242,6 +262,8 @@
     def _():
         pack_full(factor_p[...], out)
         out[packed : packed + width, :] = value_p[...]
+        if out.shape[0] > packed + 3 * width:
+            out[packed + width : packed + 3 * width, :] = probes[...]
 
     depth, rows_here, across = potential.shape
     even_e = lax.axis_index("energy") % 2 == 0
@@ -252,7 +274,7 @@
     if spare > 0:
         parts.append(jnp.zeros((depth, spare, across), F32))
     wide[...] = jnp.concatenate(parts, axis=1)
-    put_planes(out, packed + width, wide, slab % 2 == 0)
+    put_planes(out, out.shape[0] - SWEEPS * wide.shape[1], wide, slab % 2 == 0)
     first_z, first_x = region_start(depth, rows_here)
     rows, ys = spots(dopants[...], rows_all, depth + 2 * SWEEPS, wide.shape[1], across, first_z,
                      first_x)
@@ -267,7 +289,7 @@
         out[start + k * pitch : start + (k + 1) * pitch, :] = plane
 
 
-def centre_kernel(couple, following, message, matrix, source, link, base, base_source, wide,
+def centre_kernel(couple, even, odd, message, matrix, source, link, base, base_source, wide,
                   factor, value, total, total_source, out, hold, block, column):
     slab, left, distance = place()
     half = lax.axis_size("slab") // 2
@@ -276,7 +298,7 @@
 
     @pl.when(jnp.logical_or(slab == half - 1, slab == half))
     def _():
-        take_message(message, couple, following, left, block, column)
+        take_message(message, couple, (even, odd), left, block, column)
         solved = invert(matrix[...] - block[...], hold, 1 / 16, 4)
         right_side = source[...] - column[...]
         near = link[...]
@@ -294,7 +316,7 @@
         out[width : 2 * width, :] = both_source
 
 
-def expand_kernel(couple, following, probes, probes_near, letter, second, factor, value, factor_p,
+def expand_kernel(couple, even, odd, probes, letter, second, factor, value, factor_p,
                   value_p, reach, slope, offset, weights):
     slab, left, distance = place()
     half = lax.axis_size("slab") // 2
@@ -322,7 +344,7 @@
         def _():
             put(0, eye(width), jnp.zeros_like(v1))
 
-        link = jnp.where(left, couple[0].T, following[...])
+        link = jnp.where(left, couple[0].T, following((even, odd)))
         carry = dot3(unpack_symmetric(letter[0:width, :]), link)
         mq = -dot3(carry, m1)
         vq = letter[width : 2 * width, :] - dot3(carry, v1)
@@ -331,7 +353,7 @@
         put(jnp.where(left, 2, 3), -dot3(outer, mq),
             second[packed : packed + width, :] - dot3(outer, vq))
         weights[0 : 2 * width, :] = probes[...]
-        weights[2 * width :, :] = probes_near[...]
+        weights[2 * width :, :] = second[packed + width : packed + 3 * width, :]
 
 
 def join_middle(message, total, total_source, hold, left):
@@ -350,7 +372,7 @@
     def _():
         middle = join_middle(message, total, total_source, hold, left)
         terms = weights[...] * (offset[...] + dot3(slope[...], middle))
-        dens[...] = dot6(jnp.ones((8, terms.shape[1]), F32), terms, NT)
+        dens[...] = dot6(jnp.ones((8, terms.shape[1]), F32), terms, NT)[0:1]
 
 
 def join_kernel(message, total, total_source, factor, value, out_first, out_middle, hold):
@@ -365,7 +387,7 @@
         out_middle[...] = middle
 
 
-def back_kernel(step, couple, following, probes, message, first, middle, known_p, known_q,
+def back_kernel(step, couple, even, odd, probes, message, first, middle, known_p, known_q,
                 factor_p, value_p, inverse_q, value_q, reach, out_p, out_q, dens):
     slab, left, distance = place()
     centre = lax.axis_size("slab") // 2 - 1
@@ -378,7 +400,7 @@
 
     @pl.when(distance == step)
     def _():
-        link = jnp.where(left, following[...].T, couple[0])
+        link = jnp.where(left, following((even, odd)).T, couple[0])
         xq = value_q[...] - dot3(inverse_q[...], dot3(link, message[...]))
         out_q[...] = xq
         out_p[...] = value_p[...] - dot3(factor_p[...], xq)
@@ -399,7 +421,7 @@
     xa = jnp.where(left, xp, xq)
     xb = jnp.where(left, xq, xp)
     terms = jnp.concatenate([probes[0:width, :] * xa, probes[width:, :] * xb], axis=0)
-    dens[...] = dot6(jnp.ones((8, terms.shape[1]), F32), terms, NT)
+    dens[...] = dot6(jnp.ones((8, terms.shape[1]), F32), terms, NT)[0:1]
 
 
 def total_kernel(scale, cells, *rest):
@@ -469,6 +491,7 @@
 
 VM = pl.BlockSpec(memory_space=pltpu.VMEM)
 SM = pl.BlockSpec(memory_space=pltpu.SMEM)
+FAR = pl.BlockSpec(memory_space=pltpu.HBM)
 GRANT = 16 << 20
 
 
@@ -476,13 +499,18 @@
     return jax.ShapeDtypeStruct(shape, dtype)
 
 
-def call(kernel, name, outs, args, scratch=(), scalars=0, flops=10**8):
+def call(kernel, name, outs, args, scratch=(), scalars=0, distant=0, flops=10**8):
+    near = len(args) - scalars - distant
+    args = list(args)
+    for k in range(scalars, scalars + distant):
+        args[k] = pltpu.with_memory_space_constraint(args[k], pltpu.HBM)
+    sems = [pltpu.SemaphoreType.DMA((4,))] if distant else []
     return pl.pallas_call(
         kernel,
         out_shape=outs,
-        in_specs=[SM] * scalars + [VM] * (len(args) - scalars),
+        in_specs=[SM] * scalars + [FAR] * distant + [VM] * near,
         out_specs=jax.tree.map(lambda _: VM, outs),
-        scratch_shapes=[pltpu.VMEM(shape, F32) for shape in scratch],
+        scratch_shapes=[pltpu.VMEM(shape, F32) for shape in scratch] + sems,
         compiler_params=pltpu.CompilerParams(vmem_limit_bytes=GRANT),
         cost_estimate=pl.CostEstimate(flops=flops, bytes_accessed=10**6, transcendentals=0),
         name=name,
@@ -525,9 +553,9 @@
     letter = like(2 * width, probe_count)
     sq, col = (width, width), (width, probe_count)
 
-    following = lax.ppermute(couple[0], "slab", [((s + 1) % slabs, s) for s in range(slabs)])
+    even = slab_exchange(couple, False)
+    odd = lax.ppermute(couple, "slab", [(s + 1, s) for s in range(1, slabs - 1, 2)])
     paired = half == 2
-    probes_near = slab_exchange(probes, False) if paired else None
 
     message = None
     for t in range(half - 1):
@@ -537,11 +565,11 @@
                 _, _, distance = place()
                 message = jnp.where(distance == t, message, kept)
             kept = message
-            args += [message, following]
+            args += [message, even, odd]
         state = call(
             functools.partial(stage_kernel, t), f"stage{t}",
             (square, column, square, square, column, square, column, letter),
-            args, (sq,), 1,
+            args, (sq, diag_blocks.shape, couple.shape, probes.shape), 1, 3,
         )
         if t == 0:
             prepared = state
@@ -558,14 +586,14 @@
     got_even = energy_exchange(jnp.where(odd_e, low, high), False)
     got_odd = energy_exchange(jnp.where(odd_e, high, low), True)
     packed = width + width // 2
-    near_at, far_at = packed + width, 2 * width
+    near_at, far_at = packed + (3 if paired else 1) * width, 2 * width
     cells = (depth + 2 * halo) * pitch
 
     matrix, source, link, base, base_source, reach, second, wide, dopant_grid = call(
         functools.partial(ready_kernel, rows_all), "ready",
         (square, column, square, square, column, square, like(near_at + strip, probe_count),
          like(depth, pitch, across), like(cells, across)),
-        [energy_index, diag_blocks, couple, probes, following, dopant_cells.reshape(1, -1),
+        [energy_index, diag_blocks, couple, probes, even, odd, dopant_cells.reshape(1, -1),
          initial_potential, got_even, got_odd, *prepared[:5]], (), 1,
     )
     message, second = lax.optimization_barrier((message, second))
@@ -573,7 +601,7 @@
     factor, value, total, total_source, sent = call(
         centre_kernel, "centre",
         (square, column, square, column, like(far_at + strip, probe_count)),
-        [couple, following, message, matrix, source, link, base, base_source, wide],
+        [couple, even, odd, message, matrix, source, link, base, base_source, wide],
         (sq, sq, col),
     )
     across_middle = slab_exchange(sent, half % 2 == 0)
@@ -582,11 +610,11 @@
         slope, offset, weights = call(
             expand_kernel, "expand",
             (like(4 * width, width), like(4 * width, probe_count), like(4 * width, probe_count)),
-            [couple, following, probes, probes_near, message, second, factor, value,
+            [couple, even, odd, probes, message, second, factor, value,
              prepared[0], prepared[1], reach],
         )
         dens = call(
-            join_pair_kernel, "join", like(8, 4 * width),
+            join_pair_kernel, "join", like(1, 4 * width),
             [across_middle, total, total_source, slope, offset, weights], (sq,),
         )
     else:
@@ -601,8 +629,8 @@
         for t in range(half - 2, -1, -1):
             known_p, known_q, dens = call(
                 functools.partial(back_kernel, t), f"back{t}",
-                (column, column, like(8, 2 * width)),
-                [couple, following, probes, slab_exchange(known_p, t % 2 == 1), first, middle,
+                (column, column, like(1, 2 * width)),
+                [couple, even, odd, probes, slab_exchange(known_p, t % 2 == 1), first, middle,
                  known_p, known_q, factor_p, value_p, inverse_q, value_q, reach],
             )
     parts = [dens] + [
@@ -611,7 +639,7 @@
     ]
     packet = call(
         functools.partial(total_kernel, 1.0 / (probe_count * energies)), "total",
-        like(*dens.shape), [orbital_cell.reshape(1, -1), *parts],
+        like(2, dens.shape[1]), [orbital_cell.reshape(1, -1), *parts],
     )
     near = slab_exchange(packet, False)
     far = slab_exchange(packet, True)

time: 52.4 us -> 49.5 us (0.945)
  starting transfers between devices: 22.9 us -> 17.1 us
  waiting for transfers between devices: 14.2 us -> 18.2 us
  local copies, waits for them, and re-layouts: 3.62 us -> 0.67 us
  Pallas kernels: 9.42 us -> 10.5 us
  other arithmetic: 0.6 us -> 1.38 us
    ppermute x1, starting transfers between devices: 5.13 us -> 0.67 us  [body(): lax.ppermute(couple, 'slab', [(s + 1, s) for s in range(1, slabs - 1, 2)])]
    ppermute x6, waiting for transfers between devices: 9.73 us -> 14 us  [slab_exchange(): return lax.ppermute(value, ('slab', 'energy'), whole)]
    unnamed x16 -> x12, local copies, waits for them, and re-layouts: 2.61 us -> 0.67 us
    ppermute x6, starting transfers between devices: 14.1 us -> 12.9 us  [slab_exchange(): return lax.ppermute(value, ('slab', 'energy'), whole)]
    pallas_call x7, Pallas kernels: 9.42 us -> 10.5 us  [call(): pl.pallas_call(kernel, out_shape=outs, in_specs=[SM] * scalars + [FAR] *...]
    squeeze x1 -> x0, local copies, waits for them, and re-layouts: 1 us -> none  [body(): couple[0]]
    select_n x1, other arithmetic: 0.01 us -> 0.79 us  [body(): got_odd = energy_exchange(jnp.where(odd_e, high, low), True)]
  transfers between devices with their start and end apart: 12 -> 12, of which waited for: 6 -> 6; matrix products, arithmetic and copies ran while one was open for 0% -> 2% of each run, Pallas kernels for 15% -> 18%
where the time goes in v4:
time: 49.5 us; the launch traced here: 49.3 us
  waiting for transfers between devices  18.2 us (37%)
  starting transfers between devices  17.1 us (35%)
  Pallas kernels  10.5 us (21%)
  between operations  1.42 us (3%)
  other arithmetic  1.38 us (3%)
  local copies, waits for them, and re-layouts  0.67 us (1%)
    ppermute x6, waiting for transfers between devices, slab_exchange(): return lax.ppermute(value, ('slab', 'energy'), whole)  14 us
    ppermute x6, starting transfers between devices, slab_exchange(): return lax.ppermute(value, ('slab', 'energy'), whole)  12.9 us
    pallas_call x7, Pallas kernels, call(): pl.pallas_call(kernel, out_shape=outs, in_specs=[SM] * scalars + [FAR] *...  10.5 us
    ppermute x3, waiting for transfers between devices, body(): lax.ppermute(dens, 'energy', [(e, e ^ k) for e in range(energies)])  2.73 us
    ppermute x3, starting transfers between devices, body(): lax.ppermute(dens, 'energy', [(e, e ^ k) for e in range(energies)])  1.91 us
    ppermute x2, starting transfers between devices, energy_exchange(): return lax.ppermute(value, 'energy', pairs)  1.66 us
    ppermute x2, waiting for transfers between devices, energy_exchange(): return lax.ppermute(value, 'energy', pairs)  1.54 us
  transfers between devices with their start and end apart: 12, of which 6 were waited for; matrix products, arithmetic and copies ran while one was open for 2% of the time, Pallas kernels for 18%

profile of v4, /device:TPU:0, one launch (start us, length us, event | category | flops | bytes accessed | tf_op | source)
XLA Modules:
  0.0 49.3 jit_solution(7591460728134980310)
XLA Ops:
  0.6 3.1 %collective-permute-start = (f32[2,192,192]{2,1,0:T(8,128)}, f32[2,192,192]{2,1,0:T(8,128)S(1)}, u32[]{:S(2)}, u32[]{:S(2)}) collective-permute-start(f32[2,192,192]{2,1,0:T(8,128)} %couple.5), channel_id=1, source_target_pairs={{0,4},{1,5},{2,6},{3,7},{4,0},{5,1},{6,2},{7,3},{8,12},{9,13},{10,... | collective-permute-start | bytes 884744 | tf_op jit(solution)/shard_map/ppermute | solution.py:535
  3.7 0.7 %collective-permute-start.1 = (f32[2,192,192]{2,1,0:T(8,128)}, f32[2,192,192]{2,1,0:T(8,128)S(1)}, u32[]{:S(2)}, u32[]{:S(2)}) collective-permute-start(f32[2,192,192]{2,1,0:T(8,128)} %couple.5), channel_id=1, source_target_pairs={{8,4},{9,5},{10,6},{11,7},{24,20},{25,21},{26,22},{27,23}} | collective-permute-start | bytes 884744 | tf_op jit(solution)/shard_map/ppermute | solution.py:557
  5.1 0.0 copy-start
  5.1 8.4 %stage0.1 = (f32[192,192]{1,0:T(8,128)S(1)}, f32[192,128]{1,0:T(8,128)S(1)}, f32[192,192]{1,0:T(8,128)S(1)}, f32[192,192]{1,0:T(8,128)S(1)}, f32[192,128]{1,0:T(...) custom-call(s32[1]{0:T(128)S(6)} %copy.9.energy, f32[2,192,192]{2,1,0:T(8,128)} %diag.1, ...), custom_call_target="tpu_custom_call" | custom-call | flops 100000000 | bytes 1000000 | tf_op jit(solution)/shard_map/stage0/pallas_call | solution.py:508
  13.5 0.0 copy-start.3
  13.5 0.1 collective-permute-start.2
  13.6 0.8 %broadcast_select_fusion = (f32[8,2,128]{2,1,0:T(2,128)S(1)}, f32[8,2,128]{2,1,0:T(2,128)S(1)}) fusion(pred[]{:T(512)S(6)} %eq.5, f32[8,16,128]{2,1,0:T(8,128)} %potential.1), kind=kLoop, calls=%fused_computation | loop fusion | flops 4096 | bytes 32769 | tf_op jit(solution)/shard_map/jit(_where)/select_n | solution.py:587
  14.4 0.1 collective-permute-start.3
  14.5 1.6 %collective-permute-start.4 = (f32[8,2,128]{2,1,0:T(2,128)S(1)}, f32[8,2,128]{2,1,0:T(2,128)S(1)}, u32[]{:S(2)}, u32[]{:S(2)}) collective-permute-start(f32[8,2,128]{2,1,0:T(2,128)S(1)} %get-tuple-element.56), channel_id=1, source_target_pairs={{1,2},{2,1},{3,0},{0,3},{5,6},{6,5},{7,4},{4,7},{9,10},{10,9},{11,... | collective-permute-start | bytes 24584 | tf_op jit(solution)/shard_map/ppermute | solution.py:543
  16.1 0.0 collective-permute-done.3.got_even
  16.1 1.5 %collective-permute-done.4.got_odd = f32[8,2,128]{2,1,0:T(2,128)S(1)} collective-permute-done((f32[8,2,128]{2,1,0:T(2,128)S(1)}, f32[8,2,128]{2,1,0:T(2,128)S(1)}, u32[]{:S(2)}, u32[]{:S(2)}) %collective-permute-start.4) | collective-permute-done | bytes 8224 | tf_op jit(solution)/shard_map/ppermute | solution.py:543
  17.6 0.0 collective-permute-done.even
  17.6 0.0 collective-permute-done.1.odd
  17.7 0.6 %copy-done.4 = s32[1024]{0:T(1024)S(1)} copy-done((s32[1024]{0:T(1024)S(1)}, s32[1024]{0:T(1024)}, u32[]{:S(2)}) %copy-start.4) | copy-done | bytes 4120
  18.3 0.4 ready.1
  18.7 1.2 %collective-permute-done.2.message.letter = f32[384,128]{1,0:T(8,128)S(1)} collective-permute-done((f32[384,128]{1,0:T(8,128)S(1)}, f32[384,128]{1,0:T(8,128)S(1)}, u32[]{:S(2)}, u32[]{:S(2)}) %collective-permute-start.2) | collective-permute-done | bytes 196640 | tf_op jit(solution)/shard_map/ppermute | solution.py:535
  19.9 1.6 %collective-permute-start.6 = (f32[912,128]{1,0:T(8,128)S(1)}, f32[912,128]{1,0:T(8,128)S(1)}, u32[]{:S(2)}, u32[]{:S(2)}) collective-permute-start(f32[912,128]{1,0:T(8,128)S(1)} %get-tuple-element.46), channel_id=1, source_target_pairs={{0,4},{1,5},{2,6},{3,7},{4,0},{5,1},{6,2},{7,3},{8,12},{9,13},{10,... | collective-permute-start | bytes 1400840 | tf_op jit(solution)/shard_map/ppermute | solution.py:535
  21.6 0.4 collective-permute-start.5
  22.0 11.1 %collective-permute-done.6.second.near_letter = f32[912,128]{1,0:T(8,128)S(1)} collective-permute-done((f32[912,128]{1,0:T(8,128)S(1)}, f32[912,128]{1,0:T(8,128)S(1)}, u32[]{:S(2)}, u32[]{:S(2)}) %collective-permute-start.6) | collective-permute-done | bytes 466976 | tf_op jit(solution)/shard_map/ppermute | solution.py:535
  33.2 0.0 collective-permute-done.5.message.far_letter
  33.2 0.1 collective-permute-start.7
  33.2 1.6 %collective-permute-start.8 = (f32[1,768]{1,0:T(1,128)S(1)}, f32[1,768]{1,0:T(1,128)S(1)}, u32[]{:S(2)}, u32[]{:S(2)}) collective-permute-start(f32[1,768]{1,0:T(1,128)S(1)} %join.1.rest_0_), channel_id=1, source_target_pairs={{0,2},{1,3},{2,0},{3,1},{4,6},{5,7},{6,4},{7,5},{8,10},{9,11},{10,... | collective-permute-start | bytes 9224 | tf_op jit(solution)/shard_map/ppermute | solution.py:637
  34.8 0.3 collective-permute-start.9
  35.1 0.0 collective-permute-done.7.rest_1_
  35.1 1.8 %collective-permute-done.8.rest_2_ = f32[1,768]{1,0:T(1,128)S(1)} collective-permute-done((f32[1,768]{1,0:T(1,128)S(1)}, f32[1,768]{1,0:T(1,128)S(1)}, u32[]{:S(2)}, u32[]{:S(2)}) %collective-permute-start.8) | collective-permute-done | bytes 3104 | tf_op jit(solution)/shard_map/ppermute | solution.py:637
  36.9 0.9 %collective-permute-done.9.rest_3_ = f32[1,768]{1,0:T(1,128)S(1)} collective-permute-done((f32[1,768]{1,0:T(1,128)S(1)}, f32[1,768]{1,0:T(1,128)S(1)}, u32[]{:S(2)}, u32[]{:S(2)}) %collective-permute-start.9) | collective-permute-done | bytes 3104 | tf_op jit(solution)/shard_map/ppermute | solution.py:637
  37.8 7.6 %collective-permute-start.10 = (f32[2,768]{1,0:T(2,128)S(1)}, f32[2,768]{1,0:T(2,128)S(1)}, u32[]{:S(2)}, u32[]{:S(2)}) collective-permute-start(f32[2,768]{1,0:T(2,128)S(1)} %total.1.packet), channel_id=1, source_target_pairs={{0,4},{1,5},{2,6},{3,7},{4,0},{5,1},{6,2},{7,3},{8,12},{9,13},{10,... | collective-permute-start | bytes 18440 | tf_op jit(solution)/shard_map/ppermute | solution.py:535
  45.4 0.0 collective-permute-start.11
  45.4 1.6 %collective-permute-done.10.near = f32[2,768]{1,0:T(2,128)S(1)} collective-permute-done((f32[2,768]{1,0:T(2,128)S(1)}, f32[2,768]{1,0:T(2,128)S(1)}, u32[]{:S(2)}, u32[]{:S(2)}) %collective-permute-start.10) | collective-permute-done | bytes 6176 | tf_op jit(solution)/shard_map/ppermute | solution.py:535
  47.0 0.0 collective-permute-done.11.far
  47.0 1.7 %poisson.1 = (f32[8,16,128]{2,1,0:T(8,128)}, f32[1,384]{1,0:T(1,128)S(1)}) custom-call(f32[2,768]{1,0:T(2,128)S(1)} %total.1.packet, f32[2,768]{1,0:T(2,128)S(1)} %collective-permute-done.10.near, f32[2,768]{1,0:T(2,128)S(1)} %collective-permute-done.11.far, f32[288,128]{1,0:T(8,128)S(1)} %get-tuple-element.53.dopant_grid, ...), custom_call_target="tpu_custom_call" | custom-call | flops 100000000 | bytes 1000000 | tf_op jit(solution)/shard_map/poisson/pallas_call | solution.py:508
  48.7 0.6 %reduce = f32[384]{0:T(512)} reduce(f32[1,384]{1,0:T(1,128)S(1)} %get-tuple-element.55, f32[]{:T(128)} %constant.21), dimensions={0}, to_apply=%get-tuple-element.55.reduce_sub_computation | reduce | bytes 3076 | tf_op jit(solution)/shard_map/poisson/pallas_call | solution.py:508
  (14 shorter events, 0.0 us)
Async XLA Ops:
  0.6 17.0 %collective-permute-start = (f32[2,192,192]{2,1,0:T(8,128)}, f32[2,192,192]{2,1,0:T(8,128)S(1)}, u32[]{:S(2)}, u32[]{:S(2)}) collective-permute-start(f32[2,192,192]{2,1,0:T(8,128)} %couple.5), channel_id=1, source_target_pairs={{0,4},{1,5},{2,6},{3,7},{4,0},{5,1},{6,2},{7,3},{8,12},{9,13},{10,... | collective-permute-start | bytes 884744 | tf_op jit(solution)/shard_map/ppermute | solution.py:535
  3.7 13.9 %collective-permute-start.1 = (f32[2,192,192]{2,1,0:T(8,128)}, f32[2,192,192]{2,1,0:T(8,128)S(1)}, u32[]{:S(2)}, u32[]{:S(2)}) collective-permute-start(f32[2,192,192]{2,1,0:T(8,128)} %couple.5), channel_id=1, source_target_pairs={{8,4},{9,5},{10,6},{11,7},{24,20},{25,21},{26,22},{27,23}} | collective-permute-start | bytes 884744 | tf_op jit(solution)/shard_map/ppermute | solution.py:557
  5.1 12.5 %copy-start = (f32[2,192,192]{2,1,0:T(8,128)S(1)}, f32[2,192,192]{2,1,0:T(8,128)}, u32[]{:S(2)}) copy-start(f32[2,192,192]{2,1,0:T(8,128)} %couple.5) | copy-start | bytes 884740
  5.1 12.5 %copy-start.1 = (f32[384,128]{1,0:T(8,128)S(1)}, f32[384,128]{1,0:T(8,128)}, u32[]{:S(2)}) copy-start(f32[384,128]{1,0:T(8,128)} %probes.3) | copy-start | bytes 589828
  5.1 12.5 %copy-start.2 = (f32[2,192,192]{2,1,0:T(8,128)S(1)}, f32[2,192,192]{2,1,0:T(8,128)}, u32[]{:S(2)}) copy-start(f32[2,192,192]{2,1,0:T(8,128)} %diag.1) | copy-start | bytes 884740
  13.5 4.1 %copy-start.3 = (f32[8,16,128]{2,1,0:T(8,128)S(1)}, f32[8,16,128]{2,1,0:T(8,128)}, u32[]{:S(2)}) copy-start(f32[8,16,128]{2,1,0:T(8,128)} %potential.1) | copy-start | bytes 196612
  13.5 6.4 %collective-permute-start.2 = (f32[384,128]{1,0:T(8,128)S(1)}, f32[384,128]{1,0:T(8,128)S(1)}, u32[]{:S(2)}, u32[]{:S(2)}) collective-permute-start(f32[384,128]{1,0:T(8,128)S(1)} %get-tuple-element.29), channel_id=1, source_target_pairs={{0,4},{1,5},{2,6},{3,7},{4,0},{5,1},{6,2},{7,3},{8,12},{9,13},{10,... | collective-permute-start | bytes 589832 | tf_op jit(solution)/shard_map/ppermute | solution.py:535
  14.4 1.7 %collective-permute-start.3 = (f32[8,2,128]{2,1,0:T(2,128)S(1)}, f32[8,2,128]{2,1,0:T(2,128)S(1)}, u32[]{:S(2)}, u32[]{:S(2)}) collective-permute-start(f32[8,2,128]{2,1,0:T(2,128)S(1)} %get-tuple-element.57), channel_id=1, source_target_pairs={{0,1},{1,0},{2,3},{3,2},{4,5},{5,4},{6,7},{7,6},{8,9},{9,8},{10,11... | collective-permute-start | bytes 24584 | tf_op jit(solution)/shard_map/ppermute | solution.py:543
  14.5 3.1 %collective-permute-start.4 = (f32[8,2,128]{2,1,0:T(2,128)S(1)}, f32[8,2,128]{2,1,0:T(2,128)S(1)}, u32[]{:S(2)}, u32[]{:S(2)}) collective-permute-start(f32[8,2,128]{2,1,0:T(2,128)S(1)} %get-tuple-element.56), channel_id=1, source_target_pairs={{1,2},{2,1},{3,0},{0,3},{5,6},{6,5},{7,4},{4,7},{9,10},{10,9},{11,... | collective-permute-start | bytes 24584 | tf_op jit(solution)/shard_map/ppermute | solution.py:543
  17.6 0.7 %copy-start.4 = (s32[1024]{0:T(1024)S(1)}, s32[1024]{0:T(1024)}, u32[]{:S(2)}) copy-start(s32[1024]{0:T(1024)} %param.12) | copy-start | bytes 12292
  19.9 13.2 %collective-permute-start.6 = (f32[912,128]{1,0:T(8,128)S(1)}, f32[912,128]{1,0:T(8,128)S(1)}, u32[]{:S(2)}, u32[]{:S(2)}) collective-permute-start(f32[912,128]{1,0:T(8,128)S(1)} %get-tuple-element.46), channel_id=1, source_target_pairs={{0,4},{1,5},{2,6},{3,7},{4,0},{5,1},{6,2},{7,3},{8,12},{9,13},{10,... | collective-permute-start | bytes 1400840 | tf_op jit(solution)/shard_map/ppermute | solution.py:535
  21.6 11.6 %collective-permute-start.5 = (f32[432,128]{1,0:T(8,128)S(1)}, f32[432,128]{1,0:T(8,128)S(1)}, u32[]{:S(2)}, u32[]{:S(2)}) collective-permute-start(f32[432,128]{1,0:T(8,128)S(1)} %get-tuple-element.43), channel_id=1, source_target_pairs={{4,8},{5,9},{6,10},{7,11},{8,4},{9,5},{10,6},{11,7},{0,1},{1,0},{2... | collective-permute-start | bytes 663560 | tf_op jit(solution)/shard_map/ppermute | solution.py:535
  33.2 1.9 %copy-start.5 = (s32[384]{0:T(512)S(1)}, s32[384]{0:T(512)}, u32[]{:S(2)}) copy-start(s32[384]{0:T(512)} %param.11) | copy-start | bytes 4612
  33.2 1.9 %collective-permute-start.7 = (f32[1,768]{1,0:T(1,128)S(1)}, f32[1,768]{1,0:T(1,128)S(1)}, u32[]{:S(2)}, u32[]{:S(2)}) collective-permute-start(f32[1,768]{1,0:T(1,128)S(1)} %join.1.rest_0_), channel_id=1, source_target_pairs={{0,1},{1,0},{2,3},{3,2},{4,5},{5,4},{6,7},{7,6},{8,9},{9,8},{10,11... | collective-permute-start | bytes 9224 | tf_op jit(solution)/shard_map/ppermute | solution.py:637
  33.2 3.7 %collective-permute-start.8 = (f32[1,768]{1,0:T(1,128)S(1)}, f32[1,768]{1,0:T(1,128)S(1)}, u32[]{:S(2)}, u32[]{:S(2)}) collective-permute-start(f32[1,768]{1,0:T(1,128)S(1)} %join.1.rest_0_), channel_id=1, source_target_pairs={{0,2},{1,3},{2,0},{3,1},{4,6},{5,7},{6,4},{7,5},{8,10},{9,11},{10,... | collective-permute-start | bytes 9224 | tf_op jit(solution)/shard_map/ppermute | solution.py:637
  34.8 3.0 %collective-permute-start.9 = (f32[1,768]{1,0:T(1,128)S(1)}, f32[1,768]{1,0:T(1,128)S(1)}, u32[]{:S(2)}, u32[]{:S(2)}) collective-permute-start(f32[1,768]{1,0:T(1,128)S(1)} %join.1.rest_0_), channel_id=1, source_target_pairs={{0,3},{1,2},{2,1},{3,0},{4,7},{5,6},{6,5},{7,4},{8,11},{9,10},{10,... | collective-permute-start | bytes 9224 | tf_op jit(solution)/shard_map/ppermute | solution.py:637
  37.8 9.2 %collective-permute-start.10 = (f32[2,768]{1,0:T(2,128)S(1)}, f32[2,768]{1,0:T(2,128)S(1)}, u32[]{:S(2)}, u32[]{:S(2)}) collective-permute-start(f32[2,768]{1,0:T(2,128)S(1)} %total.1.packet), channel_id=1, source_target_pairs={{0,4},{1,5},{2,6},{3,7},{4,0},{5,1},{6,2},{7,3},{8,12},{9,13},{10,... | collective-permute-start | bytes 18440 | tf_op jit(solution)/shard_map/ppermute | solution.py:535
  45.4 1.6 %collective-permute-start.11 = (f32[2,768]{1,0:T(2,128)S(1)}, f32[2,768]{1,0:T(2,128)S(1)}, u32[]{:S(2)}, u32[]{:S(2)}) collective-permute-start(f32[2,768]{1,0:T(2,128)S(1)} %total.1.packet), channel_id=1, source_target_pairs={{4,8},{5,9},{6,10},{7,11},{8,4},{9,5},{10,6},{11,7},{0,1},{1,0},{2... | collective-permute-start | bytes 18440 | tf_op jit(solution)/shard_map/ppermute | solution.py:535

commit v5 on v4

--- a/solution.py
+++ b/solution.py
@@ -47,28 +47,39 @@
     ).astype(F32)
 
 
-def invert(matrix, hold, ratio, doublings):
+def estimate(matrix, ratio, doublings):
     unit = eye(matrix.shape[0])
-    sums = jnp.sum(jnp.abs(matrix), axis=0, keepdims=True)
-    bound = jnp.max(sums, axis=1, keepdims=True)
+    square = dot3(matrix, matrix)
+    sums = jnp.sum(jnp.abs(square), axis=0, keepdims=True)
+    bound = jnp.sqrt(jnp.max(sums, axis=1, keepdims=True))
     first = 2.0 / (bound * (1.0 + ratio))
-    error = unit - first * matrix
-    guess = first * unit
     tau = (1.0 + ratio) / (1.0 - ratio)
     for k in range(doublings):
         after = 2.0 * tau * tau - 1.0
         scale = (after + 1.0) / after
         if k == 0:
-            grown = guess + first * error
+            grown = (2.0 * first) * unit - (first * first) * matrix
+            squared = unit - (2.0 * first) * matrix + (first * first) * square
         else:
             grown = guess + dot3(guess, error)
+            squared = dot3(error, error) if k + 1 < doublings else None
+        guess = scale * grown
         if k + 1 < doublings:
-            error = scale * dot3(error, error) - (scale - 1.0) * unit
-        guess = scale * grown
+            error = scale * squared - (scale - 1.0) * unit
         tau = after
     residual = unit - dot6(matrix, guess)
-    size = jnp.sum(residual * residual)
-    hold[...] = guess + dot3(guess, residual)
+    return guess + dot3(guess, residual), jnp.sum(residual * residual), first
+
+
+def fast(matrix, hold, ratio, doublings):
+    found, size, _ = estimate(matrix, ratio, doublings)
+    return found, size
+
+
+def careful(matrix, hold, ratio, doublings):
+    unit = eye(matrix.shape[0])
+    found, size, first = estimate(matrix, ratio, doublings)
+    hold[...] = found
 
     @pl.when(jnp.logical_not(size < 0.9))
     def _():
@@ -76,7 +87,7 @@
 
     def go_on(state):
         count, last = state
-        return jnp.logical_and(count < 64, jnp.logical_not(last < 1e-5))
+        return jnp.logical_and(count < 64, jnp.logical_not(last < 1e-6))
 
     def newton(state):
         count, _ = state
@@ -86,7 +97,15 @@
         return count + 1, jnp.sum(left * left)
 
     lax.while_loop(go_on, newton, (jnp.int32(0), size))
-    return hold[...]
+    return hold[...], size
+
+
+def guarded(run):
+    worst = run(fast)
+
+    @pl.when(jnp.logical_not(worst < 4e-5))
+    def _():
+        run(careful)
 
 
 def pack_symmetric(matrix, out):
@@ -135,7 +154,7 @@
     column[...] = dot3(link, message[width : 2 * width, :])
 
 
-def stage_kernel(step, energy, diag_far, couple_far, probes_far, *rest):
+def stage_kernel(step, diag_far, couple_far, probes_far, energy, *rest):
     if step > 0:
         message, even, odd, rest = rest[0], rest[1], rest[2], rest[3:]
     factor_p, value_p, inverse_p, matrix_q, source_q, inverse_q, value_q, out = rest[:8]
@@ -153,46 +172,43 @@
     ]
     for load in loads:
         load.start()
-    loads[0].wait()
-    shift = sigma_base + sigma_step * jnp.full((1, 1), energy[0], jnp.int32).astype(F32)
+    for load in loads:
+        load.wait()
+    shift = sigma_base + sigma_step * energy[...].astype(F32)
     shifted = shift * eye(width)
     sp = diag[0] + shifted
+    rp = probes[pl.ds(pl.multiple_of(first * width, width), width), :]
+    rq = probes[pl.ds(pl.multiple_of((1 - first) * width, width), width), :]
     if step > 0:
-        loads[1].wait()
         taken = jnp.logical_and(distance >= 1, distance <= step)
         take_message(message, couple, (even, odd), left, matrix_q, source_q)
         sp = sp - jnp.where(taken, matrix_q[...], 0.0)
-        extra = jnp.where(taken, source_q[...], 0.0)
-    xp = invert(sp, hold, 1 / 16, 4)
-    inverse_p[...] = xp
-    for k in range(2 if step > 0 else 1, 4):
-        loads[k].wait()
-    rp = probes[pl.ds(pl.multiple_of(first * width, width), width), :]
-    rq = probes[pl.ds(pl.multiple_of((1 - first) * width, width), width), :]
-    if step > 0:
-        rp = rp - extra
+        rp = rp - jnp.where(taken, source_q[...], 0.0)
     inner = couple[1]
     inner_t = inner.T
     apq = jnp.where(forward, inner_t, inner)
     aqp = jnp.where(forward, inner, inner_t)
-    fp = dot3(xp, apq)
-    yp = dot3(xp, rp)
-    factor_p[...] = fp
-    value_p[...] = yp
-    sq = diag[1] + shifted - dot3(aqp, fp)
-    rq = rq - dot3(aqp, yp)
-    matrix_q[...] = sq
-    source_q[...] = rq
-
-    @pl.when(distance < centre)
-    def _():
-        xq = invert(sq, hold, 1 / 16, 4)
-        yq = dot3(xq, rq)
+
+    def run(invert):
+        xp, size_p = invert(sp, hold, 1 / 12, 4)
+        inverse_p[...] = xp
+        fp = dot3(xp, apq)
+        yp = dot3(xp, rp)
+        factor_p[...] = fp
+        value_p[...] = yp
+        sq = diag[1] + shifted - dot3(aqp, fp)
+        source = rq - dot3(aqp, yp)
+        matrix_q[...] = sq
+        source_q[...] = source
+        xq, size_q = invert(sq, hold, 1 / 12, 4)
+        yq = dot3(xq, source)
         inverse_q[...] = xq
         value_q[...] = yq
-
         pack_symmetric(xq, out)
         out[width : 2 * width, :] = yq
+        return jnp.maximum(size_p, size_q)
+
+    guarded(run)
 
 
 def pack_full(matrix, out):
@@ -229,7 +245,7 @@
     return first_z, lax.axis_index("energy") * rows_here - SWEEPS
 
 
-def ready_kernel(rows_all, energy, diag, couple, probes, even, odd, dopants, potential, got_even,
+def ready_kernel(rows_all, energy, diag, couple, probes, probes_near, even, odd, dopants, potential, got_even,
                  got_odd, factor_p, value_p, inverse_p, matrix_q, source_q, matrix, source, link,
                  base, base_source, reach, out, wide, dopant):
     slab, left, distance = place()
@@ -250,7 +266,7 @@
 
     @pl.when(slab == half)
     def _():
-        shift = sigma_base + sigma_step * jnp.full((1, 1), energy[0], jnp.int32).astype(F32)
+        shift = sigma_base + sigma_step * energy[...].astype(F32)
         shifted = shift * eye(width)
         matrix[...] = diag[1] + shifted
         source[...] = probes[width : 2 * width, :]
@@ -262,8 +278,6 @@
     def _():
         pack_full(factor_p[...], out)
         out[packed : packed + width, :] = value_p[...]
-        if out.shape[0] > packed + 3 * width:
-            out[packed + width : packed + 3 * width, :] = probes[...]
 
     depth, rows_here, across = potential.shape
     even_e = lax.axis_index("energy") % 2 == 0
@@ -299,24 +313,29 @@
     @pl.when(jnp.logical_or(slab == half - 1, slab == half))
     def _():
         take_message(message, couple, (even, odd), left, block, column)
-        solved = invert(matrix[...] - block[...], hold, 1 / 16, 4)
         right_side = source[...] - column[...]
         near = link[...]
         near_t = near.T
-        reach = dot3(solved, near)
-        found = dot3(solved, right_side)
-        factor[...] = reach
-        value[...] = found
         sign = jnp.where(left, 1.0, -1.0)
-        both = base[...] + sign * dot3(near_t, reach)
-        both_source = base_source[...] - dot3(near_t, found)
-        total[...] = both
-        total_source[...] = both_source
-        pack_symmetric(both, out)
-        out[width : 2 * width, :] = both_source
-
-
-def expand_kernel(couple, even, odd, probes, letter, second, factor, value, factor_p,
+
+        def run(invert):
+            solved, size = invert(matrix[...] - block[...], hold, 1 / 12, 4)
+            reach = dot3(solved, near)
+            found = dot3(solved, right_side)
+            factor[...] = reach
+            value[...] = found
+            both = base[...] + sign * dot3(near_t, reach)
+            both_source = base_source[...] - dot3(near_t, found)
+            total[...] = both
+            total_source[...] = both_source
+            pack_symmetric(both, out)
+            out[width : 2 * width, :] = both_source
+            return size
+
+        guarded(run)
+
+
+def expand_kernel(couple, even, odd, probes, probes_near, letter, second, factor, value, factor_p,
                   value_p, reach, slope, offset, weights):
     slab, left, distance = place()
     half = lax.axis_size("slab") // 2
@@ -353,15 +372,16 @@
         put(jnp.where(left, 2, 3), -dot3(outer, mq),
             second[packed : packed + width, :] - dot3(outer, vq))
         weights[0 : 2 * width, :] = probes[...]
-        weights[2 * width :, :] = second[packed + width : packed + 3 * width, :]
-
-
-def join_middle(message, total, total_source, hold, left):
+        weights[2 * width :, :] = probes_near[...]
+
+
+def join_middle(invert, message, total, total_source, hold, left):
     width = total.shape[0]
     sign = jnp.where(left, 1.0, -1.0)
     matrix = sign * (unpack_symmetric(message[0:width, :]) - total[...])
     right_side = sign * (message[width : 2 * width, :] - total_source[...])
-    return dot3(invert(matrix, hold, 1 / 64, 5), right_side)
+    inverse, size = invert(matrix, hold, 1 / 48, 5)
+    return dot3(inverse, right_side), size
 
 
 def join_pair_kernel(message, total, total_source, slope, offset, weights, dens, hold):
@@ -370,9 +390,13 @@
 
     @pl.when(jnp.logical_or(slab == half - 1, slab == half))
     def _():
-        middle = join_middle(message, total, total_source, hold, left)
-        terms = weights[...] * (offset[...] + dot3(slope[...], middle))
-        dens[...] = dot6(jnp.ones((8, terms.shape[1]), F32), terms, NT)[0:1]
+        def run(invert):
+            middle, size = join_middle(invert, message, total, total_source, hold, left)
+            terms = weights[...] * (offset[...] + dot3(slope[...], middle))
+            dens[...] = dot6(jnp.ones((8, terms.shape[1]), F32), terms, NT)[0:1]
+            return size
+
+        guarded(run)
 
 
 def join_kernel(message, total, total_source, factor, value, out_first, out_middle, hold):
@@ -381,10 +405,14 @@
 
     @pl.when(jnp.logical_or(slab == half - 1, slab == half))
     def _():
-        middle = join_middle(message, total, total_source, hold, left)
-        sign = jnp.where(left, 1.0, -1.0)
-        out_first[...] = value[...] + sign * dot3(factor[...], middle)
-        out_middle[...] = middle
+        def run(invert):
+            middle, size = join_middle(invert, message, total, total_source, hold, left)
+            sign = jnp.where(left, 1.0, -1.0)
+            out_first[...] = value[...] + sign * dot3(factor[...], middle)
+            out_middle[...] = middle
+            return size
+
+        guarded(run)
 
 
 def back_kernel(step, couple, even, odd, probes, message, first, middle, known_p, known_q,
@@ -439,14 +467,14 @@
     depth, pitch, across = wide.shape
     depth = depth + 2 * SWEEPS
     first_z, first_x = region_start(out.shape[0], out.shape[1])
-    n = density.shape[1]
+    n = density.shape[0]
     even = slab % 2 == 0
     alone = jnp.logical_or(slab == 0, slab == slabs - 1)
     own, beside, beyond = packet[0:1, 0:n], near[0:1, 0:n], far[0:1, 0:n]
     if paired:
         own = jnp.where(alone, near[0:1, n : 2 * n], own)
         beside = jnp.where(alone, beside, packet[0:1, n : 2 * n])
-    density[...] = own
+    density[...] = own.reshape(n)
     weights = jnp.concatenate([own, beside, jnp.where(alone, 0.0, beyond)], axis=1)
     orbitals = jnp.concatenate([packet[1:2, 0:n], near[1:2, 0:n], far[1:2, 0:n]], axis=1)
     orbitals = jnp.where(jnp.abs(orbitals) < 2.0**30, orbitals, -1.0).astype(jnp.int32)
@@ -490,7 +518,6 @@
 
 
 VM = pl.BlockSpec(memory_space=pltpu.VMEM)
-SM = pl.BlockSpec(memory_space=pltpu.SMEM)
 FAR = pl.BlockSpec(memory_space=pltpu.HBM)
 GRANT = 16 << 20
 
@@ -499,18 +526,19 @@
     return jax.ShapeDtypeStruct(shape, dtype)
 
 
-def call(kernel, name, outs, args, scratch=(), scalars=0, distant=0, flops=10**8):
-    near = len(args) - scalars - distant
+def call(kernel, name, outs, args, scratch=(), distant=0, flops=10**8):
     args = list(args)
-    for k in range(scalars, scalars + distant):
+    for k in range(distant):
         args[k] = pltpu.with_memory_space_constraint(args[k], pltpu.HBM)
-    sems = [pltpu.SemaphoreType.DMA((4,))] if distant else []
+    own = [pltpu.VMEM(shape, F32) for shape in scratch]
+    if distant:
+        own += [pltpu.SemaphoreType.DMA((distant + 1,))]
     return pl.pallas_call(
         kernel,
         out_shape=outs,
-        in_specs=[SM] * scalars + [FAR] * distant + [VM] * near,
+        in_specs=[FAR] * distant + [VM] * (len(args) - distant),
         out_specs=jax.tree.map(lambda _: VM, outs),
-        scratch_shapes=[pltpu.VMEM(shape, F32) for shape in scratch] + sems,
+        scratch_shapes=own,
         compiler_params=pltpu.CompilerParams(vmem_limit_bytes=GRANT),
         cost_estimate=pl.CostEstimate(flops=flops, bytes_accessed=10**6, transcendentals=0),
         name=name,
@@ -556,10 +584,11 @@
     even = slab_exchange(couple, False)
     odd = lax.ppermute(couple, "slab", [(s + 1, s) for s in range(1, slabs - 1, 2)])
     paired = half == 2
+    probes_near = slab_exchange(probes, False) if paired else probes
 
     message = None
     for t in range(half - 1):
-        args = [energy_index, diag_blocks, couple, probes]
+        args = [diag_blocks, couple, probes, energy_index.reshape(1, 1)]
         if t > 0:
             if t > 1:
                 _, _, distance = place()
@@ -569,7 +598,7 @@
         state = call(
             functools.partial(stage_kernel, t), f"stage{t}",
             (square, column, square, square, column, square, column, letter),
-            args, (sq, diag_blocks.shape, couple.shape, probes.shape), 1, 3,
+            args, (sq, diag_blocks.shape, couple.shape, probes.shape), 3,
         )
         if t == 0:
             prepared = state
@@ -586,17 +615,16 @@
     got_even = energy_exchange(jnp.where(odd_e, low, high), False)
     got_odd = energy_exchange(jnp.where(odd_e, high, low), True)
     packed = width + width // 2
-    near_at, far_at = packed + (3 if paired else 1) * width, 2 * width
+    near_at, far_at = packed + width, 2 * width
     cells = (depth + 2 * halo) * pitch
 
     matrix, source, link, base, base_source, reach, second, wide, dopant_grid = call(
         functools.partial(ready_kernel, rows_all), "ready",
         (square, column, square, square, column, square, like(near_at + strip, probe_count),
          like(depth, pitch, across), like(cells, across)),
-        [energy_index, diag_blocks, couple, probes, even, odd, dopant_cells.reshape(1, -1),
-         initial_potential, got_even, got_odd, *prepared[:5]], (), 1,
-    )
-    message, second = lax.optimization_barrier((message, second))
+        [energy_index.reshape(1, 1), diag_blocks, couple, probes, probes_near, even, odd,
+         dopant_cells.reshape(1, -1), initial_potential, got_even, got_odd, *prepared[:5]],
+    )
     second = slab_exchange(second, False)
     factor, value, total, total_source, sent = call(
         centre_kernel, "centre",
@@ -610,7 +638,7 @@
         slope, offset, weights = call(
             expand_kernel, "expand",
             (like(4 * width, width), like(4 * width, probe_count), like(4 * width, probe_count)),
-            [couple, even, odd, probes, message, second, factor, value,
+            [couple, even, odd, probes, probes_near, message, second, factor, value,
              prepared[0], prepared[1], reach],
         )
         dens = call(
@@ -649,10 +677,9 @@
                        near_letter, near_at, far_letter, far_at, out, density)
 
     potential, density = call(
-        poisson, "poisson", (like(depth, rows_here, across), like(1, 2 * width)),
+        poisson, "poisson", (like(depth, rows_here, across), like(2 * width)),
         [packet, near, far, dopant_grid, wide, second, far_letter],
     )
-    density = density.reshape(-1)
     return (potential, density)
 
 

time: 49.5 us -> 46.4 us (0.937)
  waiting for transfers between devices: 18.2 us -> 14.8 us
  starting transfers between devices: 17.1 us -> 19.4 us
  Pallas kernels: 10.5 us -> 9.06 us
  other arithmetic: 1.38 us -> 0.78 us
    ppermute x6 -> x7, waiting for transfers between devices: 14 us -> 8.69 us  [slab_exchange(): return lax.ppermute(value, ('slab', 'energy'), whole)]
    ppermute x6 -> x7, starting transfers between devices: 12.9 us -> 15.2 us  [slab_exchange(): return lax.ppermute(value, ('slab', 'energy'), whole)]
    pallas_call x7, Pallas kernels: 10.5 us -> 9.06 us  [call(): pl.pallas_call(kernel, out_shape=outs, in_specs=[FAR] * distant + [VM] *...]
    ppermute x2, waiting for transfers between devices: 1.54 us -> 2.97 us  [energy_exchange(): return lax.ppermute(value, 'energy', pairs)]
    pallas_call x1 -> x0, other arithmetic: 0.6 us -> none  [call(): pl.pallas_call(kernel, out_shape=outs, in_specs=[SM] * scalars + [FAR] *...]
  transfers between devices with their start and end apart: 12 -> 13, of which waited for: 6 -> 6; matrix products, arithmetic and copies ran while one was open for 2% -> 2% of each run, Pallas kernels for 18% -> 16%
where the time goes in v5:
time: 46.4 us; the launch traced here: 46.1 us
  starting transfers between devices  19.4 us (42%)
  waiting for transfers between devices  14.8 us (32%)
  Pallas kernels  9.06 us (20%)
  between operations  1.41 us (3%)
  other arithmetic  0.78 us (2%)
  local copies, waits for them, and re-layouts  0.67 us (1%)
    ppermute x7, starting transfers between devices, slab_exchange(): return lax.ppermute(value, ('slab', 'energy'), whole)  15.2 us
    pallas_call x7, Pallas kernels, call(): pl.pallas_call(kernel, out_shape=outs, in_specs=[FAR] * distant + [VM] *...  9.06 us
    ppermute x7, waiting for transfers between devices, slab_exchange(): return lax.ppermute(value, ('slab', 'energy'), whole)  8.69 us
    ppermute x3, waiting for transfers between devices, body(): lax.ppermute(dens, 'energy', [(e, e ^ k) for e in range(energies)])  3.13 us
    ppermute x2, waiting for transfers between devices, energy_exchange(): return lax.ppermute(value, 'energy', pairs)  2.97 us
    ppermute x3, starting transfers between devices, body(): lax.ppermute(dens, 'energy', [(e, e ^ k) for e in range(energies)])  2.21 us
    ppermute x2, starting transfers between devices, energy_exchange(): return lax.ppermute(value, 'energy', pairs)  1.32 us
  transfers between devices with their start and end apart: 13, of which 6 were waited for; matrix products, arithmetic and copies ran while one was open for 2% of the time, Pallas kernels for 16%

profile of v5, /device:TPU:0, one launch (start us, length us, event | category | flops | bytes accessed | tf_op | source)
XLA Modules:
  0.0 46.1 jit_solution(8230880052404480426)
XLA Ops:
  0.6 3.1 %collective-permute-start = (f32[2,192,192]{2,1,0:T(8,128)}, f32[2,192,192]{2,1,0:T(8,128)S(1)}, u32[]{:S(2)}, u32[]{:S(2)}) collective-permute-start(f32[2,192,192]{2,1,0:T(8,128)} %couple.5), channel_id=1, source_target_pairs={{0,4},{1,5},{2,6},{3,7},{4,0},{5,1},{6,2},{7,3},{8,12},{9,13},{10,... | collective-permute-start | bytes 884744 | tf_op jit(solution)/shard_map/ppermute | solution.py:563
  3.7 0.7 %collective-permute-start.1 = (f32[2,192,192]{2,1,0:T(8,128)}, f32[2,192,192]{2,1,0:T(8,128)S(1)}, u32[]{:S(2)}, u32[]{:S(2)}) collective-permute-start(f32[2,192,192]{2,1,0:T(8,128)} %couple.5), channel_id=1, source_target_pairs={{8,4},{9,5},{10,6},{11,7},{24,20},{25,21},{26,22},{27,23}} | collective-permute-start | bytes 884744 | tf_op jit(solution)/shard_map/ppermute | solution.py:585
  4.4 0.7 %collective-permute-start.3 = (f32[384,128]{1,0:T(8,128)}, f32[384,128]{1,0:T(8,128)S(1)}, u32[]{:S(2)}, u32[]{:S(2)}) collective-permute-start(f32[384,128]{1,0:T(8,128)} %probes.3), channel_id=1, source_target_pairs={{0,4},{1,5},{2,6},{3,7},{4,0},{5,1},{6,2},{7,3},{8,12},{9,13},{10,... | collective-permute-start | bytes 589832 | tf_op jit(solution)/shard_map/ppermute | solution.py:563
  5.8 6.9 %stage0.1 = (f32[192,192]{1,0:T(8,128)S(1)}, f32[192,128]{1,0:T(8,128)S(1)}, f32[192,192]{1,0:T(8,128)S(1)}, f32[192,192]{1,0:T(8,128)S(1)}, f32[192,128]{1,0:T(...) custom-call(f32[2,192,192]{2,1,0:T(8,128)} %diag.1, f32[2,192,192]{2,1,0:T(8,128)} %couple.5, ...), custom_call_target="tpu_custom_call" | custom-call | flops 100000000 | bytes 1000000 | tf_op jit(solution)/shard_map/stage0/pallas_call | solution.py:536
  12.8 0.0 copy-start.3
  12.8 1.5 %collective-permute-start.2 = (f32[384,128]{1,0:T(8,128)S(1)}, f32[384,128]{1,0:T(8,128)S(1)}, u32[]{:S(2)}, u32[]{:S(2)}) collective-permute-start(f32[384,128]{1,0:T(8,128)S(1)} %get-tuple-element.25), channel_id=1, source_target_pairs={{0,4},{1,5},{2,6},{3,7},{4,0},{5,1},{6,2},{7,3},{8,12},{9,13},{10,... | collective-permute-start | bytes 589832 | tf_op jit(solution)/shard_map/ppermute | solution.py:563
  14.2 0.8 %broadcast_select_fusion = (f32[8,2,128]{2,1,0:T(2,128)S(1)}, f32[8,2,128]{2,1,0:T(2,128)S(1)}) fusion(pred[]{:T(512)S(6)} %eq.5, f32[8,16,128]{2,1,0:T(8,128)} %potential.1), kind=kLoop, calls=%fused_computation | loop fusion | flops 4096 | bytes 32769 | tf_op jit(solution)/shard_map/jit(_where)/select_n | solution.py:616
  15.0 0.1 collective-permute-start.4
  15.1 1.2 %collective-permute-done.4.got_even = f32[8,2,128]{2,1,0:T(2,128)S(1)} collective-permute-done((f32[8,2,128]{2,1,0:T(2,128)S(1)}, f32[8,2,128]{2,1,0:T(2,128)S(1)}, u32[]{:S(2)}, u32[]{:S(2)}) %collective-permute-start.4) | collective-permute-done | bytes 8224 | tf_op jit(solution)/shard_map/ppermute | solution.py:571
  16.2 1.3 %collective-permute-start.5 = (f32[8,2,128]{2,1,0:T(2,128)S(1)}, f32[8,2,128]{2,1,0:T(2,128)S(1)}, u32[]{:S(2)}, u32[]{:S(2)}) collective-permute-start(f32[8,2,128]{2,1,0:T(2,128)S(1)} %get-tuple-element.48), channel_id=1, source_target_pairs={{1,2},{2,1},{3,0},{0,3},{5,6},{6,5},{7,4},{4,7},{9,10},{10,9},{11,... | collective-permute-start | bytes 24584 | tf_op jit(solution)/shard_map/ppermute | solution.py:571
  17.5 1.8 %collective-permute-done.5.got_odd = f32[8,2,128]{2,1,0:T(2,128)S(1)} collective-permute-done((f32[8,2,128]{2,1,0:T(2,128)S(1)}, f32[8,2,128]{2,1,0:T(2,128)S(1)}, u32[]{:S(2)}, u32[]{:S(2)}) %collective-permute-start.5) | collective-permute-done | bytes 8224 | tf_op jit(solution)/shard_map/ppermute | solution.py:571
  19.3 0.0 collective-permute-done.3.probes_near
  19.3 0.0 collective-permute-done.even
  19.3 0.0 collective-permute-done.1.odd
  19.3 0.0 copy-start.4
  19.4 0.6 %copy-done.4 = s32[1024]{0:T(1024)S(1)} copy-done((s32[1024]{0:T(1024)S(1)}, s32[1024]{0:T(1024)}, u32[]{:S(2)}) %copy-start.4) | copy-done | bytes 4120
  20.0 0.4 ready.1
  20.5 1.7 %collective-permute-start.7 = (f32[528,128]{1,0:T(8,128)S(1)}, f32[528,128]{1,0:T(8,128)S(1)}, u32[]{:S(2)}, u32[]{:S(2)}) collective-permute-start(f32[528,128]{1,0:T(8,128)S(1)} %get-tuple-element.40), channel_id=1, source_target_pairs={{0,4},{1,5},{2,6},{3,7},{4,0},{5,1},{6,2},{7,3},{8,12},{9,13},{10,... | collective-permute-start | bytes 811016 | tf_op jit(solution)/shard_map/ppermute | solution.py:563
  22.1 0.0 collective-permute-done.2.message.letter
  22.1 0.2 collective-permute-start.6
  22.3 7.1 %collective-permute-done.7.second.near_letter = f32[528,128]{1,0:T(8,128)S(1)} collective-permute-done((f32[528,128]{1,0:T(8,128)S(1)}, f32[528,128]{1,0:T(8,128)S(1)}, u32[]{:S(2)}, u32[]{:S(2)}) %collective-permute-start.7) | collective-permute-done | bytes 270368 | tf_op jit(solution)/shard_map/ppermute | solution.py:563
  29.4 0.9 %collective-permute-start.10 = (f32[1,768]{1,0:T(1,128)S(1)}, f32[1,768]{1,0:T(1,128)S(1)}, u32[]{:S(2)}, u32[]{:S(2)}) collective-permute-start(f32[1,768]{1,0:T(1,128)S(1)} %join.1.rest_0_), channel_id=1, source_target_pairs={{0,3},{1,2},{2,1},{3,0},{4,7},{5,6},{6,5},{7,4},{8,11},{9,10},{10,... | collective-permute-start | bytes 9224 | tf_op jit(solution)/shard_map/ppermute | solution.py:665
  30.3 0.8 %collective-permute-start.8 = (f32[1,768]{1,0:T(1,128)S(1)}, f32[1,768]{1,0:T(1,128)S(1)}, u32[]{:S(2)}, u32[]{:S(2)}) collective-permute-start(f32[1,768]{1,0:T(1,128)S(1)} %join.1.rest_0_), channel_id=1, source_target_pairs={{0,1},{1,0},{2,3},{3,2},{4,5},{5,4},{6,7},{7,6},{8,9},{9,8},{10,11... | collective-permute-start | bytes 9224 | tf_op jit(solution)/shard_map/ppermute | solution.py:665
  31.1 0.5 collective-permute-start.9
  31.6 0.9 %collective-permute-done.10.rest_3_ = f32[1,768]{1,0:T(1,128)S(1)} collective-permute-done((f32[1,768]{1,0:T(1,128)S(1)}, f32[1,768]{1,0:T(1,128)S(1)}, u32[]{:S(2)}, u32[]{:S(2)}) %collective-permute-start.10) | collective-permute-done | bytes 3104 | tf_op jit(solution)/shard_map/ppermute | solution.py:665
  32.5 0.0 collective-permute-done.8.rest_1_
  32.5 2.3 %collective-permute-done.9.rest_2_ = f32[1,768]{1,0:T(1,128)S(1)} collective-permute-done((f32[1,768]{1,0:T(1,128)S(1)}, f32[1,768]{1,0:T(1,128)S(1)}, u32[]{:S(2)}, u32[]{:S(2)}) %collective-permute-start.9) | collective-permute-done | bytes 3104 | tf_op jit(solution)/shard_map/ppermute | solution.py:665
  34.7 8.1 %collective-permute-start.11 = (f32[2,768]{1,0:T(2,128)S(1)}, f32[2,768]{1,0:T(2,128)S(1)}, u32[]{:S(2)}, u32[]{:S(2)}) collective-permute-start(f32[2,768]{1,0:T(2,128)S(1)} %total.1.packet), channel_id=1, source_target_pairs={{0,4},{1,5},{2,6},{3,7},{4,0},{5,1},{6,2},{7,3},{8,12},{9,13},{10,... | collective-permute-start | bytes 18440 | tf_op jit(solution)/shard_map/ppermute | solution.py:563
  42.8 0.0 collective-permute-start.12
  42.8 1.6 %collective-permute-done.11.near = f32[2,768]{1,0:T(2,128)S(1)} collective-permute-done((f32[2,768]{1,0:T(2,128)S(1)}, f32[2,768]{1,0:T(2,128)S(1)}, u32[]{:S(2)}, u32[]{:S(2)}) %collective-permute-start.11) | collective-permute-done | bytes 6176 | tf_op jit(solution)/shard_map/ppermute | solution.py:563
  44.4 0.0 collective-permute-done.12.far
  44.4 1.7 %poisson.1 = (f32[8,16,128]{2,1,0:T(8,128)}, f32[384]{0:T(512)}) custom-call(f32[2,768]{1,0:T(2,128)S(1)} %total.1.packet, f32[2,768]{1,0:T(2,128)S(1)} %collective-permute-done.11.near, f32[2,768]{1,0:T(2,128)S(1)} %collective-permute-done.12.far, f32[288,128]{1,0:T(8,128)S(1)} %get-tuple-element.47.dopant_grid, f32[8,24,128]{2,1,0:T(8,128)S(1)} %get-tuple-element.36.wide, ...), custom_call_target="tpu_custom_call" | custom-call | flops 100000000 | bytes 1000000 | tf_op jit(solution)/shard_map/poisson/pallas_call | solution.py:536
  (15 shorter events, 0.0 us)
Async XLA Ops:
  0.6 18.7 %collective-permute-start = (f32[2,192,192]{2,1,0:T(8,128)}, f32[2,192,192]{2,1,0:T(8,128)S(1)}, u32[]{:S(2)}, u32[]{:S(2)}) collective-permute-start(f32[2,192,192]{2,1,0:T(8,128)} %couple.5), channel_id=1, source_target_pairs={{0,4},{1,5},{2,6},{3,7},{4,0},{5,1},{6,2},{7,3},{8,12},{9,13},{10,... | collective-permute-start | bytes 884744 | tf_op jit(solution)/shard_map/ppermute | solution.py:563
  3.7 15.6 %collective-permute-start.1 = (f32[2,192,192]{2,1,0:T(8,128)}, f32[2,192,192]{2,1,0:T(8,128)S(1)}, u32[]{:S(2)}, u32[]{:S(2)}) collective-permute-start(f32[2,192,192]{2,1,0:T(8,128)} %couple.5), channel_id=1, source_target_pairs={{8,4},{9,5},{10,6},{11,7},{24,20},{25,21},{26,22},{27,23}} | collective-permute-start | bytes 884744 | tf_op jit(solution)/shard_map/ppermute | solution.py:585
  4.4 14.9 %collective-permute-start.3 = (f32[384,128]{1,0:T(8,128)}, f32[384,128]{1,0:T(8,128)S(1)}, u32[]{:S(2)}, u32[]{:S(2)}) collective-permute-start(f32[384,128]{1,0:T(8,128)} %probes.3), channel_id=1, source_target_pairs={{0,4},{1,5},{2,6},{3,7},{4,0},{5,1},{6,2},{7,3},{8,12},{9,13},{10,... | collective-permute-start | bytes 589832 | tf_op jit(solution)/shard_map/ppermute | solution.py:563
  5.8 13.6 %copy-start = (f32[2,192,192]{2,1,0:T(8,128)S(1)}, f32[2,192,192]{2,1,0:T(8,128)}, u32[]{:S(2)}) copy-start(f32[2,192,192]{2,1,0:T(8,128)} %couple.5) | copy-start | bytes 884740
  5.8 13.6 %copy-start.1 = (f32[384,128]{1,0:T(8,128)S(1)}, f32[384,128]{1,0:T(8,128)}, u32[]{:S(2)}) copy-start(f32[384,128]{1,0:T(8,128)} %probes.3) | copy-start | bytes 589828
  5.8 13.6 %copy-start.2 = (f32[2,192,192]{2,1,0:T(8,128)S(1)}, f32[2,192,192]{2,1,0:T(8,128)}, u32[]{:S(2)}) copy-start(f32[2,192,192]{2,1,0:T(8,128)} %diag.1) | copy-start | bytes 884740
  12.8 6.6 %copy-start.3 = (f32[8,16,128]{2,1,0:T(8,128)S(1)}, f32[8,16,128]{2,1,0:T(8,128)}, u32[]{:S(2)}) copy-start(f32[8,16,128]{2,1,0:T(8,128)} %potential.1) | copy-start | bytes 196612
  12.8 9.3 %collective-permute-start.2 = (f32[384,128]{1,0:T(8,128)S(1)}, f32[384,128]{1,0:T(8,128)S(1)}, u32[]{:S(2)}, u32[]{:S(2)}) collective-permute-start(f32[384,128]{1,0:T(8,128)S(1)} %get-tuple-element.25), channel_id=1, source_target_pairs={{0,4},{1,5},{2,6},{3,7},{4,0},{5,1},{6,2},{7,3},{8,12},{9,13},{10,... | collective-permute-start | bytes 589832 | tf_op jit(solution)/shard_map/ppermute | solution.py:563
  15.0 1.2 %collective-permute-start.4 = (f32[8,2,128]{2,1,0:T(2,128)S(1)}, f32[8,2,128]{2,1,0:T(2,128)S(1)}, u32[]{:S(2)}, u32[]{:S(2)}) collective-permute-start(f32[8,2,128]{2,1,0:T(2,128)S(1)} %get-tuple-element.49), channel_id=1, source_target_pairs={{0,1},{1,0},{2,3},{3,2},{4,5},{5,4},{6,7},{7,6},{8,9},{9,8},{10,11... | collective-permute-start | bytes 24584 | tf_op jit(solution)/shard_map/ppermute | solution.py:571
  16.2 3.1 %collective-permute-start.5 = (f32[8,2,128]{2,1,0:T(2,128)S(1)}, f32[8,2,128]{2,1,0:T(2,128)S(1)}, u32[]{:S(2)}, u32[]{:S(2)}) collective-permute-start(f32[8,2,128]{2,1,0:T(2,128)S(1)} %get-tuple-element.48), channel_id=1, source_target_pairs={{1,2},{2,1},{3,0},{0,3},{5,6},{6,5},{7,4},{4,7},{9,10},{10,9},{11,... | collective-permute-start | bytes 24584 | tf_op jit(solution)/shard_map/ppermute | solution.py:571
  19.3 0.7 %copy-start.4 = (s32[1024]{0:T(1024)S(1)}, s32[1024]{0:T(1024)}, u32[]{:S(2)}) copy-start(s32[1024]{0:T(1024)} %param.12) | copy-start | bytes 12292
  20.5 8.9 %collective-permute-start.7 = (f32[528,128]{1,0:T(8,128)S(1)}, f32[528,128]{1,0:T(8,128)S(1)}, u32[]{:S(2)}, u32[]{:S(2)}) collective-permute-start(f32[528,128]{1,0:T(8,128)S(1)} %get-tuple-element.40), channel_id=1, source_target_pairs={{0,4},{1,5},{2,6},{3,7},{4,0},{5,1},{6,2},{7,3},{8,12},{9,13},{10,... | collective-permute-start | bytes 811016 | tf_op jit(solution)/shard_map/ppermute | solution.py:563
  22.1 7.2 %collective-permute-start.6 = (f32[432,128]{1,0:T(8,128)S(1)}, f32[432,128]{1,0:T(8,128)S(1)}, u32[]{:S(2)}, u32[]{:S(2)}) collective-permute-start(f32[432,128]{1,0:T(8,128)S(1)} %get-tuple-element.37), channel_id=1, source_target_pairs={{4,8},{5,9},{6,10},{7,11},{8,4},{9,5},{10,6},{11,7},{0,1},{1,0},{2... | collective-permute-start | bytes 663560 | tf_op jit(solution)/shard_map/ppermute | solution.py:563
  29.4 2.2 %copy-start.5 = (s32[384]{0:T(512)S(1)}, s32[384]{0:T(512)}, u32[]{:S(2)}) copy-start(s32[384]{0:T(512)} %param.11) | copy-start | bytes 4612
  29.4 3.1 %collective-permute-start.10 = (f32[1,768]{1,0:T(1,128)S(1)}, f32[1,768]{1,0:T(1,128)S(1)}, u32[]{:S(2)}, u32[]{:S(2)}) collective-permute-start(f32[1,768]{1,0:T(1,128)S(1)} %join.1.rest_0_), channel_id=1, source_target_pairs={{0,3},{1,2},{2,1},{3,0},{4,7},{5,6},{6,5},{7,4},{8,11},{9,10},{10,... | collective-permute-start | bytes 9224 | tf_op jit(solution)/shard_map/ppermute | solution.py:665
  30.3 2.2 %collective-permute-start.8 = (f32[1,768]{1,0:T(1,128)S(1)}, f32[1,768]{1,0:T(1,128)S(1)}, u32[]{:S(2)}, u32[]{:S(2)}) collective-permute-start(f32[1,768]{1,0:T(1,128)S(1)} %join.1.rest_0_), channel_id=1, source_target_pairs={{0,1},{1,0},{2,3},{3,2},{4,5},{5,4},{6,7},{7,6},{8,9},{9,8},{10,11... | collective-permute-start | bytes 9224 | tf_op jit(solution)/shard_map/ppermute | solution.py:665
  31.1 3.6 %collective-permute-start.9 = (f32[1,768]{1,0:T(1,128)S(1)}, f32[1,768]{1,0:T(1,128)S(1)}, u32[]{:S(2)}, u32[]{:S(2)}) collective-permute-start(f32[1,768]{1,0:T(1,128)S(1)} %join.1.rest_0_), channel_id=1, source_target_pairs={{0,2},{1,3},{2,0},{3,1},{4,6},{5,7},{6,4},{7,5},{8,10},{9,11},{10,... | collective-permute-start | bytes 9224 | tf_op jit(solution)/shard_map/ppermute | solution.py:665
  34.7 9.7 %collective-permute-start.11 = (f32[2,768]{1,0:T(2,128)S(1)}, f32[2,768]{1,0:T(2,128)S(1)}, u32[]{:S(2)}, u32[]{:S(2)}) collective-permute-start(f32[2,768]{1,0:T(2,128)S(1)} %total.1.packet), channel_id=1, source_target_pairs={{0,4},{1,5},{2,6},{3,7},{4,0},{5,1},{6,2},{7,3},{8,12},{9,13},{10,... | collective-permute-start | bytes 18440 | tf_op jit(solution)/shard_map/ppermute | solution.py:563
  42.8 1.6 %collective-permute-start.12 = (f32[2,768]{1,0:T(2,128)S(1)}, f32[2,768]{1,0:T(2,128)S(1)}, u32[]{:S(2)}, u32[]{:S(2)}) collective-permute-start(f32[2,768]{1,0:T(2,128)S(1)} %total.1.packet), channel_id=1, source_target_pairs={{4,8},{5,9},{6,10},{7,11},{8,4},{9,5},{10,6},{11,7},{0,1},{1,0},{2... | collective-permute-start | bytes 18440 | tf_op jit(solution)/shard_map/ppermute | solution.py:563

commit v6 on v5

--- a/solution.py
+++ b/solution.py
@@ -6,6 +6,7 @@
 from jax.experimental import pallas as pl
 from jax.experimental.pallas import tpu as pltpu
 from jax.sharding import PartitionSpec as P
+
 
 SWEEPS = 2
 
@@ -160,8 +161,7 @@
     factor_p, value_p, inverse_p, matrix_q, source_q, inverse_q, value_q, out = rest[:8]
     hold, diag, couple, probes, sems = rest[8:]
     _, left, distance = place()
-    centre = lax.axis_size("slab") // 2 - 1
-    forward = jnp.logical_and(left, distance < centre)
+    forward = lax.axis_index("slab") <= lax.axis_size("slab") // 2
     first = jnp.where(forward, 0, 1)
     width = diag.shape[1]
     loads = [
@@ -172,26 +172,32 @@
     ]
     for load in loads:
         load.start()
-    for load in loads:
-        load.wait()
+    loads[0].wait()
+    if step > 0:
+        loads[1].wait()
     shift = sigma_base + sigma_step * energy[...].astype(F32)
     shifted = shift * eye(width)
     sp = diag[0] + shifted
-    rp = probes[pl.ds(pl.multiple_of(first * width, width), width), :]
-    rq = probes[pl.ds(pl.multiple_of((1 - first) * width, width), width), :]
     if step > 0:
         taken = jnp.logical_and(distance >= 1, distance <= step)
         take_message(message, couple, (even, odd), left, matrix_q, source_q)
         sp = sp - jnp.where(taken, matrix_q[...], 0.0)
-        rp = rp - jnp.where(taken, source_q[...], 0.0)
-    inner = couple[1]
-    inner_t = inner.T
-    apq = jnp.where(forward, inner_t, inner)
-    aqp = jnp.where(forward, inner, inner_t)
+        extra = jnp.where(taken, source_q[...], 0.0)
 
     def run(invert):
         xp, size_p = invert(sp, hold, 1 / 12, 4)
         inverse_p[...] = xp
+        if invert is fast:
+            for load in loads[2 if step > 0 else 1 :]:
+                load.wait()
+        rp = probes[pl.ds(pl.multiple_of(first * width, width), width), :]
+        rq = probes[pl.ds(pl.multiple_of((1 - first) * width, width), width), :]
+        if step > 0:
+            rp = rp - extra
+        inner = couple[1]
+        inner_t = inner.T
+        apq = jnp.where(forward, inner_t, inner)
+        aqp = jnp.where(forward, inner, inner_t)
         fp = dot3(xp, apq)
         yp = dot3(xp, rp)
         factor_p[...] = fp
@@ -245,40 +251,42 @@
     return first_z, lax.axis_index("energy") * rows_here - SWEEPS
 
 
-def ready_kernel(rows_all, energy, diag, couple, probes, probes_near, even, odd, dopants, potential, got_even,
-                 got_odd, factor_p, value_p, inverse_p, matrix_q, source_q, matrix, source, link,
-                 base, base_source, reach, out, wide, dopant):
-    slab, left, distance = place()
+def ready_kernel(energy, diag, couple, probes, factor_p, value_p, inverse_p, matrix_q, source_q,
+                 matrix, source, link, base, base_source, reach, out):
+    slab, _, distance = place()
     half = lax.axis_size("slab") // 2
     width = diag.shape[1]
     packed = width + width // 2
 
-    @pl.when(slab == half - 1)
-    def _():
-        ahead = following((even, odd))
-        across = dot3(inverse_p[...], ahead.T)
+    @pl.when(slab == half)
+    def _():
+        behind = couple[0]
+        behind_t = behind.T
+        across = dot3(inverse_p[...], behind)
         reach[...] = across
         matrix[...] = matrix_q[...]
         source[...] = source_q[...]
-        link[...] = dot3(couple[1].T, across)
-        base[...] = dot3(ahead, across)
-        base_source[...] = dot3(ahead, value_p[...])
-
-    @pl.when(slab == half)
+        link[...] = dot3(couple[1], across)
+        base[...] = dot3(behind_t, across)
+        base_source[...] = dot3(behind_t, value_p[...])
+
+    @pl.when(slab == half - 1)
     def _():
         shift = sigma_base + sigma_step * energy[...].astype(F32)
         shifted = shift * eye(width)
-        matrix[...] = diag[1] + shifted
-        source[...] = probes[width : 2 * width, :]
-        link[...] = couple[1]
-        base[...] = diag[0] + shifted
-        base_source[...] = probes[0:width, :]
+        matrix[...] = diag[0] + shifted
+        source[...] = probes[0:width, :]
+        link[...] = couple[1].T
+        base[...] = diag[1] + shifted
+        base_source[...] = probes[width : 2 * width, :]
 
     @pl.when(distance < half - 1)
     def _():
         pack_full(factor_p[...], out)
         out[packed : packed + width, :] = value_p[...]
 
+
+def halo_kernel(rows_all, dopants, potential, got_even, got_odd, wide, dopant, planes):
     depth, rows_here, across = potential.shape
     even_e = lax.axis_index("energy") % 2 == 0
     below = jnp.where(even_e, got_odd[...], got_even[...])
@@ -288,7 +296,7 @@
     if spare > 0:
         parts.append(jnp.zeros((depth, spare, across), F32))
     wide[...] = jnp.concatenate(parts, axis=1)
-    put_planes(out, out.shape[0] - SWEEPS * wide.shape[1], wide, slab % 2 == 0)
+    put_planes(planes, 0, wide, lax.axis_index("slab") % 2 == 0)
     first_z, first_x = region_start(depth, rows_here)
     rows, ys = spots(dopants[...], rows_all, depth + 2 * SWEEPS, wide.shape[1], across, first_z,
                      first_x)
@@ -305,7 +313,7 @@
 
 def centre_kernel(couple, even, odd, message, matrix, source, link, base, base_source, wide,
                   factor, value, total, total_source, out, hold, block, column):
-    slab, left, distance = place()
+    slab, left, _ = place()
     half = lax.axis_size("slab") // 2
     width = matrix.shape[0]
     put_planes(out, 2 * width, wide, slab % 2 == 1)
@@ -316,7 +324,7 @@
         right_side = source[...] - column[...]
         near = link[...]
         near_t = near.T
-        sign = jnp.where(left, 1.0, -1.0)
+        sign = jnp.where(left, -1.0, 1.0)
 
         def run(invert):
             solved, size = invert(matrix[...] - block[...], hold, 1 / 12, 4)
@@ -337,7 +345,7 @@
 
 def expand_kernel(couple, even, odd, probes, probes_near, letter, second, factor, value, factor_p,
                   value_p, reach, slope, offset, weights):
-    slab, left, distance = place()
+    slab, left, _ = place()
     half = lax.axis_size("slab") // 2
     width = value.shape[0]
     packed = width + width // 2
@@ -350,18 +358,17 @@
     @pl.when(jnp.logical_or(slab == half - 1, slab == half))
     def _():
         own = jnp.where(left, 0, 1)
-        sign = jnp.where(left, 1.0, -1.0)
-        m1 = sign * factor[...]
+        m1 = jnp.where(left, -1.0, 1.0) * factor[...]
         v1 = value[...]
         put(own, m1, v1)
 
         @pl.when(left)
         def _():
-            put(1, -(dot3(factor_p[...], m1) + reach[...]), value_p[...] - dot3(factor_p[...], v1))
+            put(1, eye(width), jnp.zeros_like(v1))
 
         @pl.when(jnp.logical_not(left))
         def _():
-            put(0, eye(width), jnp.zeros_like(v1))
+            put(0, -(dot3(factor_p[...], m1) + reach[...]), value_p[...] - dot3(factor_p[...], v1))
 
         link = jnp.where(left, couple[0].T, following((even, odd)))
         carry = dot3(unpack_symmetric(letter[0:width, :]), link)
@@ -377,7 +384,7 @@
 
 def join_middle(invert, message, total, total_source, hold, left):
     width = total.shape[0]
-    sign = jnp.where(left, 1.0, -1.0)
+    sign = jnp.where(left, -1.0, 1.0)
     matrix = sign * (unpack_symmetric(message[0:width, :]) - total[...])
     right_side = sign * (message[width : 2 * width, :] - total_source[...])
     inverse, size = invert(matrix, hold, 1 / 48, 5)
@@ -385,7 +392,7 @@
 
 
 def join_pair_kernel(message, total, total_source, slope, offset, weights, dens, hold):
-    slab, left, distance = place()
+    slab, left, _ = place()
     half = lax.axis_size("slab") // 2
 
     @pl.when(jnp.logical_or(slab == half - 1, slab == half))
@@ -400,14 +407,14 @@
 
 
 def join_kernel(message, total, total_source, factor, value, out_first, out_middle, hold):
-    slab, left, distance = place()
+    slab, left, _ = place()
     half = lax.axis_size("slab") // 2
 
     @pl.when(jnp.logical_or(slab == half - 1, slab == half))
     def _():
         def run(invert):
             middle, size = join_middle(invert, message, total, total_source, hold, left)
-            sign = jnp.where(left, 1.0, -1.0)
+            sign = jnp.where(left, -1.0, 1.0)
             out_first[...] = value[...] + sign * dot3(factor[...], middle)
             out_middle[...] = middle
             return size
@@ -417,7 +424,7 @@
 
 def back_kernel(step, couple, even, odd, probes, message, first, middle, known_p, known_q,
                 factor_p, value_p, inverse_q, value_q, reach, out_p, out_q, dens):
-    slab, left, distance = place()
+    _, left, distance = place()
     centre = lax.axis_size("slab") // 2 - 1
     width = couple.shape[1]
 
@@ -435,14 +442,14 @@
 
     @pl.when(jnp.logical_and(distance == centre, left))
     def _():
-        xa = first[...]
-        out_p[...] = xa
-        out_q[...] = value_p[...] - dot3(factor_p[...], xa) - dot3(reach[...], middle[...])
-
-    @pl.when(jnp.logical_and(distance == centre, jnp.logical_not(left)))
-    def _():
         out_p[...] = first[...]
         out_q[...] = middle[...]
+
+    @pl.when(jnp.logical_and(distance == centre, jnp.logical_not(left)))
+    def _():
+        xb = first[...]
+        out_p[...] = xb
+        out_q[...] = value_p[...] - dot3(factor_p[...], xb) - dot3(reach[...], middle[...])
 
     xp = out_p[...]
     xq = out_q[...]
@@ -462,7 +469,7 @@
 
 
 def poisson_kernel(rows_all, planes, paired, packet, near, far, dopant_grid, wide, near_letter,
-                   near_at, far_letter, far_at, out, density):
+                   far_letter, far_at, out, density):
     slab, slabs = lax.axis_index("slab"), lax.axis_size("slab")
     depth, pitch, across = wide.shape
     depth = depth + 2 * SWEEPS
@@ -488,7 +495,7 @@
     electron = electron.reshape(depth, pitch, across)
     dopant = dopant_grid[...].reshape(depth, pitch, across)
     size = SWEEPS * pitch
-    near_planes = near_letter[near_at : near_at + size, :].reshape(SWEEPS, pitch, across)
+    near_planes = near_letter[...].reshape(SWEEPS, pitch, across)
     far_planes = far_letter[far_at : far_at + size, :].reshape(SWEEPS, pitch, across)
     start = jnp.concatenate(
         [jnp.where(even, far_planes, near_planes), wide[...],
@@ -526,7 +533,7 @@
     return jax.ShapeDtypeStruct(shape, dtype)
 
 
-def call(kernel, name, outs, args, scratch=(), distant=0, flops=10**8):
+def call(kernel, outs, args, scratch=(), distant=0, flops=10**8):
     args = list(args)
     for k in range(distant):
         args[k] = pltpu.with_memory_space_constraint(args[k], pltpu.HBM)
@@ -541,7 +548,6 @@
         scratch_shapes=own,
         compiler_params=pltpu.CompilerParams(vmem_limit_bytes=GRANT),
         cost_estimate=pl.CostEstimate(flops=flops, bytes_accessed=10**6, transcendentals=0),
-        name=name,
     )(*args)
 
 
@@ -571,20 +577,21 @@
     return lax.ppermute(value, "energy", pairs)
 
 
-def body(energy_index, diag_blocks, couple, probes, orbital_cell, dopant_cells, initial_potential):
+def program(energy_index, diag_blocks, couple, probes, orbital_cell, dopant_cells, initial_potential):
     width = diag_blocks.shape[1]
     probe_count = probes.shape[1]
-    slab, slabs = lax.axis_index("slab"), lax.axis_size("slab")
-    energy, energies = lax.axis_index("energy"), lax.axis_size("energy")
+    slabs = lax.axis_size("slab")
+    energies = lax.axis_size("energy")
     half = slabs // 2
     square, column = like(width, width), like(width, probe_count)
     letter = like(2 * width, probe_count)
     sq, col = (width, width), (width, probe_count)
 
     even = slab_exchange(couple, False)
-    odd = lax.ppermute(couple, "slab", [(s + 1, s) for s in range(1, slabs - 1, 2)])
     paired = half == 2
-    probes_near = slab_exchange(probes, False) if paired else probes
+    odd = even
+    if not paired:
+        odd = lax.ppermute(couple, "slab", [(s + 1, s) for s in range(1, slabs - 1, 2)])
 
     message = None
     for t in range(half - 1):
@@ -596,7 +603,7 @@
             kept = message
             args += [message, even, odd]
         state = call(
-            functools.partial(stage_kernel, t), f"stage{t}",
+            functools.partial(stage_kernel, t),
             (square, column, square, square, column, square, column, letter),
             args, (sq, diag_blocks.shape, couple.shape, probes.shape), 3,
         )
@@ -614,49 +621,55 @@
     low, high = initial_potential[:, :halo], initial_potential[:, rows_here - halo :]
     got_even = energy_exchange(jnp.where(odd_e, low, high), False)
     got_odd = energy_exchange(jnp.where(odd_e, high, low), True)
-    packed = width + width // 2
-    near_at, far_at = packed + width, 2 * width
+    far_at = 2 * width
     cells = (depth + 2 * halo) * pitch
-
-    matrix, source, link, base, base_source, reach, second, wide, dopant_grid = call(
-        functools.partial(ready_kernel, rows_all), "ready",
-        (square, column, square, square, column, square, like(near_at + strip, probe_count),
-         like(depth, pitch, across), like(cells, across)),
-        [energy_index.reshape(1, 1), diag_blocks, couple, probes, probes_near, even, odd,
-         dopant_cells.reshape(1, -1), initial_potential, got_even, got_odd, *prepared[:5]],
-    )
-    second = slab_exchange(second, False)
+    matrix, source, link, base, base_source, reach, second = call(
+        ready_kernel,
+        (square, column, square, square, column, square,
+         like(width + width // 2 + width, probe_count)),
+        [energy_index.reshape(1, 1), diag_blocks, couple, probes, *prepared[:5]],
+    )
+    if paired:
+        probes_near = slab_exchange(probes, False)
+        second = slab_exchange(second, False)
+    wide, dopant_grid, planes = call(
+        functools.partial(halo_kernel, rows_all),
+        (like(depth, pitch, across), like(cells, across), like(strip, across)),
+        [dopant_cells.reshape(1, -1), initial_potential, got_even, got_odd],
+    )
     factor, value, total, total_source, sent = call(
-        centre_kernel, "centre",
+        centre_kernel,
         (square, column, square, column, like(far_at + strip, probe_count)),
         [couple, even, odd, message, matrix, source, link, base, base_source, wide],
         (sq, sq, col),
     )
     across_middle = slab_exchange(sent, half % 2 == 0)
+    planes, _ = lax.optimization_barrier((planes, sent))
+    near_planes = slab_exchange(planes, False)
     far_letter = across_middle if paired else slab_exchange(sent, True)
     if paired:
         slope, offset, weights = call(
-            expand_kernel, "expand",
+            expand_kernel,
             (like(4 * width, width), like(4 * width, probe_count), like(4 * width, probe_count)),
             [couple, even, odd, probes, probes_near, message, second, factor, value,
              prepared[0], prepared[1], reach],
         )
         dens = call(
-            join_pair_kernel, "join", like(1, 4 * width),
+            join_pair_kernel, like(1, 4 * width),
             [across_middle, total, total_source, slope, offset, weights], (sq,),
         )
     else:
         first, middle = call(
-            join_kernel, "join", (column, column),
+            join_kernel, (column, column),
             [across_middle, total, total_source, factor, value], (sq,),
         )
-        centred = lax.axis_index("slab") == half - 1
+        centred = lax.axis_index("slab") == half
         factor_p = jnp.where(centred, prepared[0], factor_p)
         value_p = jnp.where(centred, prepared[1], value_p)
         known_p, known_q = first, middle
         for t in range(half - 2, -1, -1):
             known_p, known_q, dens = call(
-                functools.partial(back_kernel, t), f"back{t}",
+                functools.partial(back_kernel, t),
                 (column, column, like(1, 2 * width)),
                 [couple, even, odd, probes, slab_exchange(known_p, t % 2 == 1), first, middle,
                  known_p, known_q, factor_p, value_p, inverse_q, value_q, reach],
@@ -666,7 +679,7 @@
         for k in range(1, energies)
     ]
     packet = call(
-        functools.partial(total_kernel, 1.0 / (probe_count * energies)), "total",
+        functools.partial(total_kernel, 1.0 / (probe_count * energies)),
         like(2, dens.shape[1]), [orbital_cell.reshape(1, -1), *parts],
     )
     near = slab_exchange(packet, False)
@@ -674,11 +687,11 @@
 
     def poisson(packet, near, far, dopant_grid, wide, near_letter, far_letter, out, density):
         poisson_kernel(rows_all, depth * slabs, paired, packet, near, far, dopant_grid, wide,
-                       near_letter, near_at, far_letter, far_at, out, density)
+                       near_letter, far_letter, far_at, out, density)
 
     potential, density = call(
-        poisson, "poisson", (like(depth, rows_here, across), like(2 * width)),
-        [packet, near, far, dopant_grid, wide, second, far_letter],
+        poisson, (like(depth, rows_here, across), like(2 * width)),
+        [packet, near, far, dopant_grid, wide, near_planes, far_letter],
     )
     return (potential, density)
 
@@ -694,7 +707,7 @@
         P(("cfg", "slab"), "energy", None),
     )
     return jax.shard_map(
-        body,
+        program,
         mesh=mesh,
         in_specs=placed,
         out_specs=(P(("cfg", "slab"), "energy", None), P(("cfg", "slab"))),

time: 46.4 us -> 44.3 us (0.955)
  waiting for transfers between devices: 14.8 us -> 11.6 us
  starting transfers between devices: 19.4 us -> 22.1 us
  other arithmetic: 0.78 us -> 0.01 us
  local copies, waits for them, and re-layouts: 0.67 us -> 0.03 us
    ppermute x7 -> x8, starting transfers between devices: 15.2 us -> 18.6 us  [slab_exchange(): return lax.ppermute(value, ('slab', 'energy'), whole)]
    ppermute x2, waiting for transfers between devices: 2.97 us -> 1.55 us  [energy_exchange(): return lax.ppermute(value, 'energy', pairs)]
    ppermute x7 -> x8, waiting for transfers between devices: 8.69 us -> 7.34 us  [slab_exchange(): return lax.ppermute(value, ('slab', 'energy'), whole)]
    ppermute x4 -> x3, starting transfers between devices: 2.88 us -> 1.92 us  [program(): lax.ppermute(dens, 'energy', [(e, e ^ k) for e in range(energies)])]
    select_n x1, other arithmetic: 0.78 us -> 0.01 us  [program(): got_odd = energy_exchange(jnp.where(odd_e, high, low), True)]
    unnamed x12, local copies, waits for them, and re-layouts: 0.66 us -> 0.03 us
    ppermute x4 -> x3, waiting for transfers between devices: 3.13 us -> 2.71 us  [program(): lax.ppermute(dens, 'energy', [(e, e ^ k) for e in range(energies)])]
    pallas_call x7 -> x8, Pallas kernels: 9.06 us -> 8.93 us  [call(): pl.pallas_call(kernel, out_shape=outs, in_specs=[FAR] * distant + [VM] *...]
  transfers between devices with their start and end apart: 13 -> 13, of which waited for: 6 -> 6; matrix products, arithmetic and copies ran while one was open for 2% -> 0% of each run, Pallas kernels for 16% -> 16%
where the time goes in v6:
time: 44.3 us; the launch traced here: 44.2 us
  starting transfers between devices  22.1 us (50%)
  waiting for transfers between devices  11.6 us (26%)
  Pallas kernels  8.93 us (20%)
  between operations  1.44 us (3%)
    ppermute x8, starting transfers between devices, slab_exchange(): return lax.ppermute(value, ('slab', 'energy'), whole)  18.6 us
    pallas_call x8, Pallas kernels, call(): pl.pallas_call(kernel, out_shape=outs, in_specs=[FAR] * distant + [VM] *...  8.93 us
    ppermute x8, waiting for transfers between devices, slab_exchange(): return lax.ppermute(value, ('slab', 'energy'), whole)  7.34 us
    ppermute x3, waiting for transfers between devices, program(): lax.ppermute(dens, 'energy', [(e, e ^ k) for e in range(energies)])  2.71 us
    ppermute x3, starting transfers between devices, program(): lax.ppermute(dens, 'energy', [(e, e ^ k) for e in range(energies)])  1.92 us
    ppermute x2, starting transfers between devices, energy_exchange(): return lax.ppermute(value, 'energy', pairs)  1.66 us
    ppermute x2, waiting for transfers between devices, energy_exchange(): return lax.ppermute(value, 'energy', pairs)  1.55 us
  transfers between devices with their start and end apart: 13, of which 6 were waited for; matrix products, arithmetic and copies ran while one was open for 0% of the time, Pallas kernels for 16%

profile of v6, /device:TPU:0, one launch (start us, length us, event | category | flops | bytes accessed | tf_op | source)
XLA Modules:
  0.0 44.2 jit_solution(17256331808965921150)
XLA Ops:
  0.6 3.1 %collective-permute-start = (f32[2,192,192]{2,1,0:T(8,128)}, f32[2,192,192]{2,1,0:T(8,128)S(1)}, u32[]{:S(2)}, u32[]{:S(2)}) collective-permute-start(f32[2,192,192]{2,1,0:T(8,128)} %couple.5), channel_id=1, source_target_pairs={{0,4},{1,5},{2,6},{3,7},{4,0},{5,1},{6,2},{7,3},{8,12},{9,13},{10,... | collective-permute-start | bytes 884744 | tf_op jit(solution)/shard_map/ppermute | solution.py:569
  4.4 6.8 %shard_map.86 = (f32[192,192]{1,0:T(8,128)S(1)}, f32[192,128]{1,0:T(8,128)S(1)}, f32[192,192]{1,0:T(8,128)S(1)}, f32[192,192]{1,0:T(8,128)S(1)}, f32[192,128]{1,...) custom-call(f32[2,192,192]{2,1,0:T(8,128)} %diag.1, f32[2,192,192]{2,1,0:T(8,128)} %couple.5, ...), custom_call_target="tpu_custom_call" | custom-call | flops 100000000 | bytes 1000000 | tf_op jit(solution)/shard_map/pallas_call | solution.py:543
  11.2 0.1 collective-permute-start.1
  11.3 0.0 copy-start.3
  11.3 0.1 shard_map.87
  11.4 2.1 %collective-permute-start.6 = (f32[480,128]{1,0:T(8,128)S(1)}, f32[480,128]{1,0:T(8,128)S(1)}, u32[]{:S(2)}, u32[]{:S(2)}) collective-permute-start(f32[480,128]{1,0:T(8,128)S(1)} %get-tuple-element.42), channel_id=1, source_target_pairs={{0,4},{1,5},{2,6},{3,7},{4,0},{5,1},{6,2},{7,3},{8,12},{9,13},{10,... | collective-permute-start | bytes 737288 | tf_op jit(solution)/shard_map/ppermute | solution.py:569
  13.6 0.0 copy-start.4
  13.6 0.1 collective-permute-start.2
  13.7 1.6 %collective-permute-start.3 = (f32[8,2,128]{2,1,0:T(2,128)S(1)}, f32[8,2,128]{2,1,0:T(2,128)S(1)}, u32[]{:S(2)}, u32[]{:S(2)}) collective-permute-start(f32[8,2,128]{2,1,0:T(2,128)S(1)} %get-tuple-element.52), channel_id=1, source_target_pairs={{1,2},{2,1},{3,0},{0,3},{5,6},{6,5},{7,4},{4,7},{9,10},{10,9},{11,... | collective-permute-start | bytes 24584 | tf_op jit(solution)/shard_map/ppermute | solution.py:577
  15.3 0.0 collective-permute-done.2.got_even
  15.3 1.5 %collective-permute-done.3.got_odd = f32[8,2,128]{2,1,0:T(2,128)S(1)} collective-permute-done((f32[8,2,128]{2,1,0:T(2,128)S(1)}, f32[8,2,128]{2,1,0:T(2,128)S(1)}, u32[]{:S(2)}, u32[]{:S(2)}) %collective-permute-start.3) | collective-permute-done | bytes 8224 | tf_op jit(solution)/shard_map/ppermute | solution.py:577
  16.8 0.3 shard_map.88
  17.2 1.9 %collective-permute-done.1.message.letter = f32[384,128]{1,0:T(8,128)S(1)} collective-permute-done((f32[384,128]{1,0:T(8,128)S(1)}, f32[384,128]{1,0:T(8,128)S(1)}, u32[]{:S(2)}, u32[]{:S(2)}) %collective-permute-start.1) | collective-permute-done | bytes 196640 | tf_op jit(solution)/shard_map/ppermute | solution.py:569
  19.1 0.0 collective-permute-done.even.odd
  19.1 0.1 collective-permute-start.4
  19.1 6.6 %collective-permute-start.5 = (f32[384,128]{1,0:T(8,128)S(1)}, f32[384,128]{1,0:T(8,128)S(1)}, u32[]{:S(2)}, u32[]{:S(2)}) collective-permute-start(f32[384,128]{1,0:T(8,128)S(1)} %copy-done.1), channel_id=1, source_target_pairs={{0,4},{1,5},{2,6},{3,7},{4,0},{5,1},{6,2},{7,3},{8,12},{9,13},{10,... | collective-permute-start | bytes 589832 | tf_op jit(solution)/shard_map/ppermute | solution.py:569
  25.7 0.0 collective-permute-start.12
  25.8 3.8 %collective-permute-done.5.probes_near = f32[384,128]{1,0:T(8,128)S(1)} collective-permute-done((f32[384,128]{1,0:T(8,128)S(1)}, f32[384,128]{1,0:T(8,128)S(1)}, u32[]{:S(2)}, u32[]{:S(2)}) %collective-permute-start.5) | collective-permute-done | bytes 196640 | tf_op jit(solution)/shard_map/ppermute | solution.py:569
  29.6 0.0 collective-permute-done.6.second
  29.6 0.0 collective-permute-done.4.message.far_letter
  29.6 0.0 copy-start.5
  29.6 0.1 collective-permute-start.7
  29.7 1.6 %collective-permute-start.8 = (f32[1,768]{1,0:T(1,128)S(1)}, f32[1,768]{1,0:T(1,128)S(1)}, u32[]{:S(2)}, u32[]{:S(2)}) collective-permute-start(f32[1,768]{1,0:T(1,128)S(1)} %shard_map.91.rest_0_), channel_id=1, source_target_pairs={{0,2},{1,3},{2,0},{3,1},{4,6},{5,7},{6,4},{7,5},{8,10},{9,11},{10,... | collective-permute-start | bytes 9224 | tf_op jit(solution)/shard_map/ppermute | solution.py:678
  31.3 0.3 collective-permute-start.9
  31.6 0.0 collective-permute-done.7.rest_1_
  31.6 1.8 %collective-permute-done.8.rest_2_ = f32[1,768]{1,0:T(1,128)S(1)} collective-permute-done((f32[1,768]{1,0:T(1,128)S(1)}, f32[1,768]{1,0:T(1,128)S(1)}, u32[]{:S(2)}, u32[]{:S(2)}) %collective-permute-start.8) | collective-permute-done | bytes 3104 | tf_op jit(solution)/shard_map/ppermute | solution.py:678
  33.4 0.9 %collective-permute-done.9.rest_3_ = f32[1,768]{1,0:T(1,128)S(1)} collective-permute-done((f32[1,768]{1,0:T(1,128)S(1)}, f32[1,768]{1,0:T(1,128)S(1)}, u32[]{:S(2)}, u32[]{:S(2)}) %collective-permute-start.9) | collective-permute-done | bytes 3104 | tf_op jit(solution)/shard_map/ppermute | solution.py:678
  34.3 6.6 %collective-permute-start.10 = (f32[2,768]{1,0:T(2,128)S(1)}, f32[2,768]{1,0:T(2,128)S(1)}, u32[]{:S(2)}, u32[]{:S(2)}) collective-permute-start(f32[2,768]{1,0:T(2,128)S(1)} %shard_map.92.packet), channel_id=1, source_target_pairs={{0,4},{1,5},{2,6},{3,7},{4,0},{5,1},{6,2},{7,3},{8,12},{9,13},{10,... | collective-permute-start | bytes 18440 | tf_op jit(solution)/shard_map/ppermute | solution.py:569
  40.9 0.0 collective-permute-start.11
  40.9 1.6 %collective-permute-done.10.near = f32[2,768]{1,0:T(2,128)S(1)} collective-permute-done((f32[2,768]{1,0:T(2,128)S(1)}, f32[2,768]{1,0:T(2,128)S(1)}, u32[]{:S(2)}, u32[]{:S(2)}) %collective-permute-start.10) | collective-permute-done | bytes 6176 | tf_op jit(solution)/shard_map/ppermute | solution.py:569
  42.5 0.0 collective-permute-done.11.far
  42.5 1.7 %shard_map.93 = (f32[8,16,128]{2,1,0:T(8,128)}, f32[384]{0:T(512)}) custom-call(f32[2,768]{1,0:T(2,128)S(1)} %shard_map.92.packet, f32[2,768]{1,0:T(2,128)S(1)} %collective-permute-done.10.near, f32[2,768]{1,0:T(2,128)S(1)} %collective-permute-done.11.far, f32[288,128]{1,0:T(8,128)S(1)} %get-tuple-element.49.dopant_grid, ...), custom_call_target="tpu_custom_call" | custom-call | flops 100000000 | bytes 1000000 | tf_op jit(solution)/shard_map/pallas_call | solution.py:543
  (16 shorter events, 0.1 us)
Async XLA Ops:
  0.6 18.4 %collective-permute-start = (f32[2,192,192]{2,1,0:T(8,128)}, f32[2,192,192]{2,1,0:T(8,128)S(1)}, u32[]{:S(2)}, u32[]{:S(2)}) collective-permute-start(f32[2,192,192]{2,1,0:T(8,128)} %couple.5), channel_id=1, source_target_pairs={{0,4},{1,5},{2,6},{3,7},{4,0},{5,1},{6,2},{7,3},{8,12},{9,13},{10,... | collective-permute-start | bytes 884744 | tf_op jit(solution)/shard_map/ppermute | solution.py:569
  4.4 6.9 %copy-start = (f32[2,192,192]{2,1,0:T(8,128)S(1)}, f32[2,192,192]{2,1,0:T(8,128)}, u32[]{:S(2)}) copy-start(f32[2,192,192]{2,1,0:T(8,128)} %couple.5) | copy-start | bytes 884740
  4.4 6.9 %copy-start.1 = (f32[384,128]{1,0:T(8,128)S(1)}, f32[384,128]{1,0:T(8,128)}, u32[]{:S(2)}) copy-start(f32[384,128]{1,0:T(8,128)} %probes.3) | copy-start | bytes 589828
  4.4 6.9 %copy-start.2 = (f32[2,192,192]{2,1,0:T(8,128)S(1)}, f32[2,192,192]{2,1,0:T(8,128)}, u32[]{:S(2)}) copy-start(f32[2,192,192]{2,1,0:T(8,128)} %diag.1) | copy-start | bytes 884740
  11.2 7.8 %collective-permute-start.1 = (f32[384,128]{1,0:T(8,128)S(1)}, f32[384,128]{1,0:T(8,128)S(1)}, u32[]{:S(2)}, u32[]{:S(2)}) collective-permute-start(f32[384,128]{1,0:T(8,128)S(1)} %get-tuple-element.27), channel_id=1, source_target_pairs={{0,4},{1,5},{2,6},{3,7},{4,0},{5,1},{6,2},{7,3},{8,12},{9,13},{10,... | collective-permute-start | bytes 589832 | tf_op jit(solution)/shard_map/ppermute | solution.py:569
  11.3 2.2 %copy-start.3 = (f32[8,16,128]{2,1,0:T(8,128)S(1)}, f32[8,16,128]{2,1,0:T(8,128)}, u32[]{:S(2)}) copy-start(f32[8,16,128]{2,1,0:T(8,128)} %potential.1) | copy-start | bytes 196612
  11.4 18.1 %collective-permute-start.6 = (f32[480,128]{1,0:T(8,128)S(1)}, f32[480,128]{1,0:T(8,128)S(1)}, u32[]{:S(2)}, u32[]{:S(2)}) collective-permute-start(f32[480,128]{1,0:T(8,128)S(1)} %get-tuple-element.42), channel_id=1, source_target_pairs={{0,4},{1,5},{2,6},{3,7},{4,0},{5,1},{6,2},{7,3},{8,12},{9,13},{10,... | collective-permute-start | bytes 737288 | tf_op jit(solution)/shard_map/ppermute | solution.py:569
  13.6 3.2 %copy-start.4 = (s32[1024]{0:T(1024)S(1)}, s32[1024]{0:T(1024)}, u32[]{:S(2)}) copy-start(s32[1024]{0:T(1024)} %param.12) | copy-start | bytes 12292
  13.6 1.7 %collective-permute-start.2 = (f32[8,2,128]{2,1,0:T(2,128)S(1)}, f32[8,2,128]{2,1,0:T(2,128)S(1)}, u32[]{:S(2)}, u32[]{:S(2)}) collective-permute-start(f32[8,2,128]{2,1,0:T(2,128)S(1)} %get-tuple-element.53), channel_id=1, source_target_pairs={{0,1},{1,0},{2,3},{3,2},{4,5},{5,4},{6,7},{7,6},{8,9},{9,8},{10,11... | collective-permute-start | bytes 24584 | tf_op jit(solution)/shard_map/ppermute | solution.py:577
  13.7 3.1 %collective-permute-start.3 = (f32[8,2,128]{2,1,0:T(2,128)S(1)}, f32[8,2,128]{2,1,0:T(2,128)S(1)}, u32[]{:S(2)}, u32[]{:S(2)}) collective-permute-start(f32[8,2,128]{2,1,0:T(2,128)S(1)} %get-tuple-element.52), channel_id=1, source_target_pairs={{1,2},{2,1},{3,0},{0,3},{5,6},{6,5},{7,4},{4,7},{9,10},{10,9},{11,... | collective-permute-start | bytes 24584 | tf_op jit(solution)/shard_map/ppermute | solution.py:577
  19.1 10.5 %collective-permute-start.4 = (f32[432,128]{1,0:T(8,128)S(1)}, f32[432,128]{1,0:T(8,128)S(1)}, u32[]{:S(2)}, u32[]{:S(2)}) collective-permute-start(f32[432,128]{1,0:T(8,128)S(1)} %get-tuple-element.39), channel_id=1, source_target_pairs={{4,8},{5,9},{6,10},{7,11},{8,4},{9,5},{10,6},{11,7},{0,1},{1,0},{2... | collective-permute-start | bytes 663560 | tf_op jit(solution)/shard_map/ppermute | solution.py:569
  19.1 10.4 %collective-permute-start.5 = (f32[384,128]{1,0:T(8,128)S(1)}, f32[384,128]{1,0:T(8,128)S(1)}, u32[]{:S(2)}, u32[]{:S(2)}) collective-permute-start(f32[384,128]{1,0:T(8,128)S(1)} %copy-done.1), channel_id=1, source_target_pairs={{0,4},{1,5},{2,6},{3,7},{4,0},{5,1},{6,2},{7,3},{8,12},{9,13},{10,... | collective-permute-start | bytes 589832 | tf_op jit(solution)/shard_map/ppermute | solution.py:569
  25.7 15.2 %collective-permute-start.12 = (f32[48,128]{1,0:T(8,128)S(1)}, f32[48,128]{1,0:T(8,128)S(1)}, u32[]{:S(2)}, u32[]{:S(2)}) collective-permute-start(f32[48,128]{1,0:T(8,128)S(1)} %get-tuple-element.51), channel_id=1, source_target_pairs={{0,4},{1,5},{2,6},{3,7},{4,0},{5,1},{6,2},{7,3},{8,12},{9,13},{10,... | collective-permute-start | bytes 73736 | tf_op jit(solution)/shard_map/ppermute | solution.py:569
  29.6 2.0 %copy-start.5 = (s32[384]{0:T(512)S(1)}, s32[384]{0:T(512)}, u32[]{:S(2)}) copy-start(s32[384]{0:T(512)} %param.11) | copy-start | bytes 4612
  29.6 1.9 %collective-permute-start.7 = (f32[1,768]{1,0:T(1,128)S(1)}, f32[1,768]{1,0:T(1,128)S(1)}, u32[]{:S(2)}, u32[]{:S(2)}) collective-permute-start(f32[1,768]{1,0:T(1,128)S(1)} %shard_map.91.rest_0_), channel_id=1, source_target_pairs={{0,1},{1,0},{2,3},{3,2},{4,5},{5,4},{6,7},{7,6},{8,9},{9,8},{10,11... | collective-permute-start | bytes 9224 | tf_op jit(solution)/shard_map/ppermute | solution.py:678
  29.7 3.7 %collective-permute-start.8 = (f32[1,768]{1,0:T(1,128)S(1)}, f32[1,768]{1,0:T(1,128)S(1)}, u32[]{:S(2)}, u32[]{:S(2)}) collective-permute-start(f32[1,768]{1,0:T(1,128)S(1)} %shard_map.91.rest_0_), channel_id=1, source_target_pairs={{0,2},{1,3},{2,0},{3,1},{4,6},{5,7},{6,4},{7,5},{8,10},{9,11},{10,... | collective-permute-start | bytes 9224 | tf_op jit(solution)/shard_map/ppermute | solution.py:678
  31.3 3.0 %collective-permute-start.9 = (f32[1,768]{1,0:T(1,128)S(1)}, f32[1,768]{1,0:T(1,128)S(1)}, u32[]{:S(2)}, u32[]{:S(2)}) collective-permute-start(f32[1,768]{1,0:T(1,128)S(1)} %shard_map.91.rest_0_), channel_id=1, source_target_pairs={{0,3},{1,2},{2,1},{3,0},{4,7},{5,6},{6,5},{7,4},{8,11},{9,10},{10,... | collective-permute-start | bytes 9224 | tf_op jit(solution)/shard_map/ppermute | solution.py:678
  34.3 8.2 %collective-permute-start.10 = (f32[2,768]{1,0:T(2,128)S(1)}, f32[2,768]{1,0:T(2,128)S(1)}, u32[]{:S(2)}, u32[]{:S(2)}) collective-permute-start(f32[2,768]{1,0:T(2,128)S(1)} %shard_map.92.packet), channel_id=1, source_target_pairs={{0,4},{1,5},{2,6},{3,7},{4,0},{5,1},{6,2},{7,3},{8,12},{9,13},{10,... | collective-permute-start | bytes 18440 | tf_op jit(solution)/shard_map/ppermute | solution.py:569
  40.9 1.6 %collective-permute-start.11 = (f32[2,768]{1,0:T(2,128)S(1)}, f32[2,768]{1,0:T(2,128)S(1)}, u32[]{:S(2)}, u32[]{:S(2)}) collective-permute-start(f32[2,768]{1,0:T(2,128)S(1)} %shard_map.92.packet), channel_id=1, source_target_pairs={{4,8},{5,9},{6,10},{7,11},{8,4},{9,5},{10,6},{11,7},{0,1},{1,0},{2... | collective-permute-start | bytes 18440 | tf_op jit(solution)/shard_map/ppermute | solution.py:569

commit v7 on v6

--- a/solution.py
+++ b/solution.py
@@ -147,17 +147,19 @@
     return jnp.where(lax.axis_index("slab") % 2 == 0, even[0], odd[0])
 
 
-def take_message(message, couple, ahead, left, block, column):
-    width = block.shape[0]
+def take_block(message, couple, ahead, left):
     link_t = jnp.where(left, couple[0].T, following(ahead))
     link = jnp.where(left, couple[0], following(ahead).T)
-    block[...] = dot3(link, dot3(unpack_symmetric(message[0:width, :]), link_t))
-    column[...] = dot3(link, message[width : 2 * width, :])
+    return dot3(link, dot3(unpack_symmetric(message[...]), link_t))
+
+
+def take_column(message, couple, ahead, left):
+    return dot3(jnp.where(left, couple[0], following(ahead).T), message[...])
 
 
 def stage_kernel(step, diag_far, couple_far, probes_far, energy, *rest):
     if step > 0:
-        message, even, odd, rest = rest[0], rest[1], rest[2], rest[3:]
+        message, sources, even, odd, rest = rest[0], rest[1], rest[2], rest[3], rest[4:]
     factor_p, value_p, inverse_p, matrix_q, source_q, inverse_q, value_q, out = rest[:8]
     hold, diag, couple, probes, sems = rest[8:]
     _, left, distance = place()
@@ -180,9 +182,9 @@
     sp = diag[0] + shifted
     if step > 0:
         taken = jnp.logical_and(distance >= 1, distance <= step)
-        take_message(message, couple, (even, odd), left, matrix_q, source_q)
-        sp = sp - jnp.where(taken, matrix_q[...], 0.0)
-        extra = jnp.where(taken, source_q[...], 0.0)
+        ahead = (even, odd)
+        sp = sp - jnp.where(taken, take_block(message, couple, ahead, left), 0.0)
+        extra = jnp.where(taken, take_column(sources, couple, ahead, left), 0.0)
 
     def run(invert):
         xp, size_p = invert(sp, hold, 1 / 12, 4)
@@ -211,7 +213,6 @@
         inverse_q[...] = xq
         value_q[...] = yq
         pack_symmetric(xq, out)
-        out[width : 2 * width, :] = yq
         return jnp.maximum(size_p, size_q)
 
     guarded(run)
@@ -286,7 +287,14 @@
         out[packed : packed + width, :] = value_p[...]
 
 
-def halo_kernel(rows_all, dopants, potential, got_even, got_odd, wide, dopant, planes):
+def deposit_kernel(rows_all, pitch, depth, rows_here, dopants, dopant):
+    first_z, first_x = region_start(depth, rows_here)
+    rows, ys = spots(dopants[...], rows_all, depth + 2 * SWEEPS, pitch, dopant.shape[1], first_z,
+                     first_x)
+    dopant[...] = dopant_charge * one_pass(rows, ys.astype(BF16), NT)
+
+
+def halo_kernel(potential, got_even, got_odd, wide, near_planes, far_planes):
     depth, rows_here, across = potential.shape
     even_e = lax.axis_index("energy") % 2 == 0
     below = jnp.where(even_e, got_odd[...], got_even[...])
@@ -296,11 +304,9 @@
     if spare > 0:
         parts.append(jnp.zeros((depth, spare, across), F32))
     wide[...] = jnp.concatenate(parts, axis=1)
-    put_planes(planes, 0, wide, lax.axis_index("slab") % 2 == 0)
-    first_z, first_x = region_start(depth, rows_here)
-    rows, ys = spots(dopants[...], rows_all, depth + 2 * SWEEPS, wide.shape[1], across, first_z,
-                     first_x)
-    dopant[...] = dopant_charge * one_pass(rows, ys.astype(BF16), NT)
+    even = lax.axis_index("slab") % 2 == 0
+    put_planes(near_planes, 0, wide, even)
+    put_planes(far_planes, 0, wide, jnp.logical_not(even))
 
 
 def put_planes(out, start, wide, high):
@@ -311,40 +317,49 @@
         out[start + k * pitch : start + (k + 1) * pitch, :] = plane
 
 
-def centre_kernel(couple, even, odd, message, matrix, source, link, base, base_source, wide,
-                  factor, value, total, total_source, out, hold, block, column):
+def middle_slab():
     slab, left, _ = place()
     half = lax.axis_size("slab") // 2
-    width = matrix.shape[0]
-    put_planes(out, 2 * width, wide, slab % 2 == 1)
-
-    @pl.when(jnp.logical_or(slab == half - 1, slab == half))
-    def _():
-        take_message(message, couple, (even, odd), left, block, column)
-        right_side = source[...] - column[...]
+    return jnp.logical_or(slab == half - 1, slab == half), left
+
+
+def centre_kernel(couple, even, odd, message, matrix, link, base, solved, factor, total, out,
+                  hold):
+    here, left = middle_slab()
+
+    @pl.when(here)
+    def _():
+        block = matrix[...] - take_block(message, couple, (even, odd), left)
         near = link[...]
         near_t = near.T
         sign = jnp.where(left, -1.0, 1.0)
 
         def run(invert):
-            solved, size = invert(matrix[...] - block[...], hold, 1 / 12, 4)
-            reach = dot3(solved, near)
-            found = dot3(solved, right_side)
+            found, size = invert(block, hold, 1 / 12, 4)
+            reach = dot3(found, near)
+            both = base[...] + sign * dot3(near_t, reach)
+            pack_symmetric(both, out)
+            solved[...] = found
             factor[...] = reach
-            value[...] = found
-            both = base[...] + sign * dot3(near_t, reach)
-            both_source = base_source[...] - dot3(near_t, found)
             total[...] = both
-            total_source[...] = both_source
-            pack_symmetric(both, out)
-            out[width : 2 * width, :] = both_source
             return size
 
         guarded(run)
 
 
-def expand_kernel(couple, even, odd, probes, probes_near, letter, second, factor, value, factor_p,
-                  value_p, reach, slope, offset, weights):
+def source_kernel(couple, even, odd, message, source, link, base_source, solved, value, total):
+    here, left = middle_slab()
+
+    @pl.when(here)
+    def _():
+        right_side = source[...] - take_column(message, couple, (even, odd), left)
+        found = dot3(solved[...], right_side)
+        value[...] = found
+        total[...] = base_source[...] - dot3(link[...].T, found)
+
+
+def expand_kernel(couple, even, odd, letter, sources, second, factor, value, factor_p, value_p,
+                  reach, slope, offset):
     slab, left, _ = place()
     half = lax.axis_size("slab") // 2
     width = value.shape[0]
@@ -371,55 +386,57 @@
             put(0, -(dot3(factor_p[...], m1) + reach[...]), value_p[...] - dot3(factor_p[...], v1))
 
         link = jnp.where(left, couple[0].T, following((even, odd)))
-        carry = dot3(unpack_symmetric(letter[0:width, :]), link)
+        carry = dot3(unpack_symmetric(letter[...]), link)
         mq = -dot3(carry, m1)
-        vq = letter[width : 2 * width, :] - dot3(carry, v1)
+        vq = sources[...] - dot3(carry, v1)
         put(jnp.where(left, 3, 2), mq, vq)
         outer = unpack_full(second[0:packed, :], width)
         put(jnp.where(left, 2, 3), -dot3(outer, mq),
             second[packed : packed + width, :] - dot3(outer, vq))
-        weights[0 : 2 * width, :] = probes[...]
-        weights[2 * width :, :] = probes_near[...]
-
-
-def join_middle(invert, message, total, total_source, hold, left):
-    width = total.shape[0]
+
+
+def join_kernel(message, total, inverse, hold):
+    here, left = middle_slab()
+
+    @pl.when(here)
+    def _():
+        sign = jnp.where(left, -1.0, 1.0)
+        matrix = sign * (unpack_symmetric(message[...]) - total[...])
+
+        def run(invert):
+            found, size = invert(matrix, hold, 1 / 48, 5)
+            inverse[...] = found
+            return size
+
+        guarded(run)
+
+
+def join_solution(message, inverse, total, left):
     sign = jnp.where(left, -1.0, 1.0)
-    matrix = sign * (unpack_symmetric(message[0:width, :]) - total[...])
-    right_side = sign * (message[width : 2 * width, :] - total_source[...])
-    inverse, size = invert(matrix, hold, 1 / 48, 5)
-    return dot3(inverse, right_side), size
-
-
-def join_pair_kernel(message, total, total_source, slope, offset, weights, dens, hold):
-    slab, left, _ = place()
-    half = lax.axis_size("slab") // 2
-
-    @pl.when(jnp.logical_or(slab == half - 1, slab == half))
-    def _():
-        def run(invert):
-            middle, size = join_middle(invert, message, total, total_source, hold, left)
-            terms = weights[...] * (offset[...] + dot3(slope[...], middle))
-            dens[...] = dot6(jnp.ones((8, terms.shape[1]), F32), terms, NT)[0:1]
-            return size
-
-        guarded(run)
-
-
-def join_kernel(message, total, total_source, factor, value, out_first, out_middle, hold):
-    slab, left, _ = place()
-    half = lax.axis_size("slab") // 2
-
-    @pl.when(jnp.logical_or(slab == half - 1, slab == half))
-    def _():
-        def run(invert):
-            middle, size = join_middle(invert, message, total, total_source, hold, left)
-            sign = jnp.where(left, -1.0, 1.0)
-            out_first[...] = value[...] + sign * dot3(factor[...], middle)
-            out_middle[...] = middle
-            return size
-
-        guarded(run)
+    return dot3(inverse[...], sign * (message[...] - total[...]))
+
+
+def density_kernel(message, inverse, total, slope, offset, probes, probes_near, dens):
+    here, left = middle_slab()
+
+    @pl.when(here)
+    def _():
+        middle = join_solution(message, inverse, total, left)
+        values = offset[...] + dot3(slope[...], middle)
+        n = probes.shape[0]
+        terms = jnp.concatenate([probes[...] * values[:n], probes_near[...] * values[n:]], axis=0)
+        dens[...] = dot6(jnp.ones((8, terms.shape[1]), F32), terms, NT)[0:1]
+
+
+def middle_kernel(message, inverse, total, factor, value, out_first, out_middle):
+    here, left = middle_slab()
+
+    @pl.when(here)
+    def _():
+        middle = join_solution(message, inverse, total, left)
+        sign = jnp.where(left, -1.0, 1.0)
+        out_first[...] = value[...] + sign * dot3(factor[...], middle)
+        out_middle[...] = middle
 
 
 def back_kernel(step, couple, even, odd, probes, message, first, middle, known_p, known_q,
@@ -469,7 +486,7 @@
 
 
 def poisson_kernel(rows_all, planes, paired, packet, near, far, dopant_grid, wide, near_letter,
-                   far_letter, far_at, out, density):
+                   far_letter, out, density):
     slab, slabs = lax.axis_index("slab"), lax.axis_size("slab")
     depth, pitch, across = wide.shape
     depth = depth + 2 * SWEEPS
@@ -494,9 +511,8 @@
     electron = one_pass(rows, h, NT) + (one_pass(rows, m, NT) + one_pass(rows, low, NT))
     electron = electron.reshape(depth, pitch, across)
     dopant = dopant_grid[...].reshape(depth, pitch, across)
-    size = SWEEPS * pitch
     near_planes = near_letter[...].reshape(SWEEPS, pitch, across)
-    far_planes = far_letter[far_at : far_at + size, :].reshape(SWEEPS, pitch, across)
+    far_planes = far_letter[...].reshape(SWEEPS, pitch, across)
     start = jnp.concatenate(
         [jnp.where(even, far_planes, near_planes), wide[...],
          jnp.where(even, near_planes, far_planes)],
@@ -584,8 +600,8 @@
     energies = lax.axis_size("energy")
     half = slabs // 2
     square, column = like(width, width), like(width, probe_count)
-    letter = like(2 * width, probe_count)
-    sq, col = (width, width), (width, probe_count)
+    letter = like(width, probe_count)
+    sq = (width, width)
 
     even = slab_exchange(couple, False)
     paired = half == 2
@@ -599,9 +615,10 @@
         if t > 0:
             if t > 1:
                 _, _, distance = place()
-                message = jnp.where(distance == t, message, kept)
-            kept = message
-            args += [message, even, odd]
+                message = jnp.where(distance == t, message, kept[0])
+                sources = jnp.where(distance == t, sources, kept[1])
+            kept = message, sources
+            args += [message, sources, even, odd]
         state = call(
             functools.partial(stage_kernel, t),
             (square, column, square, square, column, square, column, letter),
@@ -610,6 +627,7 @@
         if t == 0:
             prepared = state
         message = slab_exchange(state[-1], t % 2 == 1)
+        sources = slab_exchange(state[-2], t % 2 == 1)
     factor_p, value_p, _, _, _, inverse_q, value_q, _ = state
 
     depth, rows_here, across = initial_potential.shape
@@ -621,7 +639,6 @@
     low, high = initial_potential[:, :halo], initial_potential[:, rows_here - halo :]
     got_even = energy_exchange(jnp.where(odd_e, low, high), False)
     got_odd = energy_exchange(jnp.where(odd_e, high, low), True)
-    far_at = 2 * width
     cells = (depth + 2 * halo) * pitch
     matrix, source, link, base, base_source, reach, second = call(
         ready_kernel,
@@ -632,36 +649,42 @@
     if paired:
         probes_near = slab_exchange(probes, False)
         second = slab_exchange(second, False)
-    wide, dopant_grid, planes = call(
-        functools.partial(halo_kernel, rows_all),
-        (like(depth, pitch, across), like(cells, across), like(strip, across)),
-        [dopant_cells.reshape(1, -1), initial_potential, got_even, got_odd],
-    )
-    factor, value, total, total_source, sent = call(
-        centre_kernel,
-        (square, column, square, column, like(far_at + strip, probe_count)),
-        [couple, even, odd, message, matrix, source, link, base, base_source, wide],
-        (sq, sq, col),
+    dopant_grid = call(
+        functools.partial(deposit_kernel, rows_all, pitch, depth, rows_here),
+        like(cells, across), [dopant_cells.reshape(1, -1)],
+    )
+    solved, factor, total, sent = call(
+        centre_kernel, (square, square, square, letter),
+        [couple, even, odd, message, matrix, link, base], (sq,),
     )
     across_middle = slab_exchange(sent, half % 2 == 0)
-    planes, _ = lax.optimization_barrier((planes, sent))
-    near_planes = slab_exchange(planes, False)
-    far_letter = across_middle if paired else slab_exchange(sent, True)
+    value, total_source = call(
+        source_kernel, (column, column),
+        [couple, even, odd, sources, source, link, base_source, solved],
+    )
+    sources_middle = slab_exchange(total_source, half % 2 == 0)
+    wide, near_planes, far_planes = call(
+        halo_kernel,
+        (like(depth, pitch, across), like(strip, across), like(strip, across)),
+        [initial_potential, *lax.optimization_barrier((got_even, got_odd, sent))[:2]],
+    )
+    near_planes = slab_exchange(near_planes, False)
+    far_planes = slab_exchange(far_planes, True)
+    inverse = call(join_kernel, square, [across_middle, total], (sq,))
     if paired:
-        slope, offset, weights = call(
-            expand_kernel,
-            (like(4 * width, width), like(4 * width, probe_count), like(4 * width, probe_count)),
-            [couple, even, odd, probes, probes_near, message, second, factor, value,
-             prepared[0], prepared[1], reach],
+        slope, offset = call(
+            expand_kernel, (like(4 * width, width), like(4 * width, probe_count)),
+            [couple, even, odd, message, sources, second, factor, value, prepared[0],
+             prepared[1], reach],
         )
         dens = call(
-            join_pair_kernel, like(1, 4 * width),
-            [across_middle, total, total_source, slope, offset, weights], (sq,),
+            density_kernel, like(1, 4 * width),
+            [sources_middle, inverse, total_source, slope, offset, probes, probes_near],
         )
     else:
         first, middle = call(
-            join_kernel, (column, column),
-            [across_middle, total, total_source, factor, value], (sq,),
+            middle_kernel, (column, column),
+            [sources_middle, inverse, total_source, factor, value],
         )
         centred = lax.axis_index("slab") == half
         factor_p = jnp.where(centred, prepared[0], factor_p)
@@ -687,11 +710,11 @@
 
     def poisson(packet, near, far, dopant_grid, wide, near_letter, far_letter, out, density):
         poisson_kernel(rows_all, depth * slabs, paired, packet, near, far, dopant_grid, wide,
-                       near_letter, far_letter, far_at, out, density)
+                       near_letter, far_letter, out, density)
 
     potential, density = call(
         poisson, (like(depth, rows_here, across), like(2 * width)),
-        [packet, near, far, dopant_grid, wide, near_planes, far_letter],
+        [packet, near, far, dopant_grid, wide, near_planes, far_planes],
     )
     return (potential, density)
 

time: 44.3 us -> 43.9 us (level)
  waiting for transfers between devices: 11.6 us -> 10.7 us
    ppermute x8 -> x11, waiting for transfers between devices: 7.34 us -> 4.75 us  [slab_exchange(): return lax.ppermute(value, ('slab', 'energy'), whole)]
    ppermute x2, waiting for transfers between devices: 1.55 us -> 2.99 us  [energy_exchange(): return lax.ppermute(value, 'energy', pairs)]
    ppermute x8 -> x11, starting transfers between devices: 18.6 us -> 19 us  [slab_exchange(): return lax.ppermute(value, ('slab', 'energy'), whole)]
    pallas_call x8 -> x11, Pallas kernels: 8.93 us -> 9.05 us  [call(): pl.pallas_call(kernel, out_shape=outs, in_specs=[FAR] * distant + [VM] *...]
  transfers between devices with their start and end apart: 13 -> 16, of which waited for: 6 -> 7; matrix products, arithmetic and copies ran while one was open for 0% -> 0% of each run, Pallas kernels for 16% -> 17%
where the time goes in v7:
time: 43.9 us; the launch traced here: 43.8 us
  starting transfers between devices  22.3 us (51%)
  waiting for transfers between devices  10.7 us (24%)
  Pallas kernels  9.05 us (21%)
  between operations  1.42 us (3%)
    ppermute x11, starting transfers between devices, slab_exchange(): return lax.ppermute(value, ('slab', 'energy'), whole)  19 us
    pallas_call x11, Pallas kernels, call(): pl.pallas_call(kernel, out_shape=outs, in_specs=[FAR] * distant + [VM] *...  9.05 us
    ppermute x11, waiting for transfers between devices, slab_exchange(): return lax.ppermute(value, ('slab', 'energy'), whole)  4.75 us
    ppermute x2, waiting for transfers between devices, energy_exchange(): return lax.ppermute(value, 'energy', pairs)  2.99 us
    ppermute x3, waiting for transfers between devices, program(): lax.ppermute(dens, 'energy', [(e, e ^ k) for e in range(energies)])  2.93 us
    ppermute x3, starting transfers between devices, program(): lax.ppermute(dens, 'energy', [(e, e ^ k) for e in range(energies)])  1.93 us
    ppermute x2, starting transfers between devices, energy_exchange(): return lax.ppermute(value, 'energy', pairs)  1.32 us
  transfers between devices with their start and end apart: 16, of which 7 were waited for; matrix products, arithmetic and copies ran while one was open for 0% of the time, Pallas kernels for 17%

profile of v7, /device:TPU:0, one launch (start us, length us, event | category | flops | bytes accessed | tf_op | source)
XLA Modules:
  0.0 43.8 jit_solution(18261944665748025157)
XLA Ops:
  0.6 3.1 %collective-permute-start = (f32[2,192,192]{2,1,0:T(8,128)}, f32[2,192,192]{2,1,0:T(8,128)S(1)}, u32[]{:S(2)}, u32[]{:S(2)}) collective-permute-start(f32[2,192,192]{2,1,0:T(8,128)} %couple.7), channel_id=1, source_target_pairs={{0,4},{1,5},{2,6},{3,7},{4,0},{5,1},{6,2},{7,3},{8,12},{9,13},{10,... | collective-permute-start | bytes 884744 | tf_op jit(solution)/shard_map/ppermute | solution.py:585
  4.4 6.8 %shard_map.86 = (f32[192,192]{1,0:T(8,128)S(1)}, f32[192,128]{1,0:T(8,128)S(1)}, f32[192,192]{1,0:T(8,128)S(1)}, f32[192,192]{1,0:T(8,128)S(1)}, f32[192,128]{1,...) custom-call(f32[2,192,192]{2,1,0:T(8,128)} %diag.1, f32[2,192,192]{2,1,0:T(8,128)} %couple.7, ...), custom_call_target="tpu_custom_call" | custom-call | flops 100000000 | bytes 1000000 | tf_op jit(solution)/shard_map/pallas_call | solution.py:559
  11.2 0.1 collective-permute-start.2
  11.3 2.0 %collective-permute-start.1 = (f32[192,128]{1,0:T(8,128)S(1)}, f32[192,128]{1,0:T(8,128)S(1)}, u32[]{:S(2)}, u32[]{:S(2)}) collective-permute-start(f32[192,128]{1,0:T(8,128)S(1)} %get-tuple-element.29), channel_id=1, source_target_pairs={{0,4},{1,5},{2,6},{3,7},{4,0},{5,1},{6,2},{7,3},{8,12},{9,13},{10,... | collective-permute-start | bytes 294920 | tf_op jit(solution)/shard_map/ppermute | solution.py:585
  13.3 0.1 collective-permute-start.6
  13.4 0.1 shard_map.87
  13.5 2.1 %collective-permute-start.5 = (f32[480,128]{1,0:T(8,128)S(1)}, f32[480,128]{1,0:T(8,128)S(1)}, u32[]{:S(2)}, u32[]{:S(2)}) collective-permute-start(f32[480,128]{1,0:T(8,128)S(1)} %get-tuple-element.45), channel_id=1, source_target_pairs={{0,4},{1,5},{2,6},{3,7},{4,0},{5,1},{6,2},{7,3},{8,12},{9,13},{10,... | collective-permute-start | bytes 737288 | tf_op jit(solution)/shard_map/ppermute | solution.py:585
  15.5 1.4 %collective-permute-done.2.message.letter = f32[192,128]{1,0:T(8,128)S(1)} collective-permute-done((f32[192,128]{1,0:T(8,128)S(1)}, f32[192,128]{1,0:T(8,128)S(1)}, u32[]{:S(2)}, u32[]{:S(2)}) %collective-permute-start.2) | collective-permute-done | bytes 98336 | tf_op jit(solution)/shard_map/ppermute | solution.py:585
  16.9 0.0 collective-permute-done.even.odd
  16.9 2.1 %collective-permute-done.1.message.sources = f32[192,128]{1,0:T(8,128)S(1)} collective-permute-done((f32[192,128]{1,0:T(8,128)S(1)}, f32[192,128]{1,0:T(8,128)S(1)}, u32[]{:S(2)}, u32[]{:S(2)}) %collective-permute-start.1) | collective-permute-done | bytes 98336 | tf_op jit(solution)/shard_map/ppermute | solution.py:585
  19.0 0.0 collective-permute-start.3
  19.0 0.5 %collective-permute-start.4 = (f32[192,128]{1,0:T(8,128)S(1)}, f32[192,128]{1,0:T(8,128)S(1)}, u32[]{:S(2)}, u32[]{:S(2)}) collective-permute-start(f32[192,128]{1,0:T(8,128)S(1)} %get-tuple-element.43), channel_id=1, source_target_pairs={{4,8},{5,9},{6,10},{7,11},{8,4},{9,5},{10,6},{11,7},{0,1},{1,0},{2... | collective-permute-start | bytes 294920 | tf_op jit(solution)/shard_map/ppermute | solution.py:585
  19.5 0.3 copy-done.3
  19.9 0.1 collective-permute-start.12
  20.0 1.2 %collective-permute-done.12.got_even = f32[8,2,128]{2,1,0:T(2,128)S(1)} collective-permute-done((f32[8,2,128]{2,1,0:T(2,128)S(1)}, f32[8,2,128]{2,1,0:T(2,128)S(1)}, u32[]{:S(2)}, u32[]{:S(2)}) %collective-permute-start.12) | collective-permute-done | bytes 8224 | tf_op jit(solution)/shard_map/ppermute | solution.py:593
  21.1 1.2 %collective-permute-start.13 = (f32[8,2,128]{2,1,0:T(2,128)S(1)}, f32[8,2,128]{2,1,0:T(2,128)S(1)}, u32[]{:S(2)}, u32[]{:S(2)}) collective-permute-start(f32[8,2,128]{2,1,0:T(2,128)S(1)} %get-tuple-element.56), channel_id=1, source_target_pairs={{1,2},{2,1},{3,0},{0,3},{5,6},{6,5},{7,4},{4,7},{9,10},{10,9},{11,... | collective-permute-start | bytes 24584 | tf_op jit(solution)/shard_map/ppermute | solution.py:593
  22.4 1.8 %collective-permute-done.13.got_odd = f32[8,2,128]{2,1,0:T(2,128)S(1)} collective-permute-done((f32[8,2,128]{2,1,0:T(2,128)S(1)}, f32[8,2,128]{2,1,0:T(2,128)S(1)}, u32[]{:S(2)}, u32[]{:S(2)}) %collective-permute-start.13) | collective-permute-done | bytes 8224 | tf_op jit(solution)/shard_map/ppermute | solution.py:593
  24.2 4.6 %collective-permute-start.14 = (f32[48,128]{1,0:T(8,128)S(1)}, f32[48,128]{1,0:T(8,128)S(1)}, u32[]{:S(2)}, u32[]{:S(2)}) collective-permute-start(f32[48,128]{1,0:T(8,128)S(1)} %get-tuple-element.54), channel_id=1, source_target_pairs={{0,4},{1,5},{2,6},{3,7},{4,0},{5,1},{6,2},{7,3},{8,12},{9,13},{10,... | collective-permute-start | bytes 73736 | tf_op jit(solution)/shard_map/ppermute | solution.py:585
  28.8 0.0 collective-permute-done.5.second
  28.8 0.0 collective-permute-start.15
  28.9 0.2 shard_map.90.inverse
  29.1 0.0 copy-start.5
  29.1 0.4 collective-permute-start.7
  29.5 1.5 %collective-permute-start.8 = (f32[1,768]{1,0:T(1,128)S(1)}, f32[1,768]{1,0:T(1,128)S(1)}, u32[]{:S(2)}, u32[]{:S(2)}) collective-permute-start(f32[1,768]{1,0:T(1,128)S(1)} %shard_map.92.rest_0_), channel_id=1, source_target_pairs={{0,2},{1,3},{2,0},{3,1},{4,6},{5,7},{6,4},{7,5},{8,10},{9,11},{10,... | collective-permute-start | bytes 9224 | tf_op jit(solution)/shard_map/ppermute | solution.py:701
  31.0 0.1 collective-permute-start.9
  31.1 0.0 collective-permute-done.7.rest_1_
  31.1 2.0 %collective-permute-done.8.rest_2_ = f32[1,768]{1,0:T(1,128)S(1)} collective-permute-done((f32[1,768]{1,0:T(1,128)S(1)}, f32[1,768]{1,0:T(1,128)S(1)}, u32[]{:S(2)}, u32[]{:S(2)}) %collective-permute-start.8) | collective-permute-done | bytes 3104 | tf_op jit(solution)/shard_map/ppermute | solution.py:701
  33.1 0.9 %collective-permute-done.9.rest_3_ = f32[1,768]{1,0:T(1,128)S(1)} collective-permute-done((f32[1,768]{1,0:T(1,128)S(1)}, f32[1,768]{1,0:T(1,128)S(1)}, u32[]{:S(2)}, u32[]{:S(2)}) %collective-permute-start.9) | collective-permute-done | bytes 3104 | tf_op jit(solution)/shard_map/ppermute | solution.py:701
  34.0 6.5 %collective-permute-start.10 = (f32[2,768]{1,0:T(2,128)S(1)}, f32[2,768]{1,0:T(2,128)S(1)}, u32[]{:S(2)}, u32[]{:S(2)}) collective-permute-start(f32[2,768]{1,0:T(2,128)S(1)} %shard_map.93.packet), channel_id=1, source_target_pairs={{0,4},{1,5},{2,6},{3,7},{4,0},{5,1},{6,2},{7,3},{8,12},{9,13},{10,... | collective-permute-start | bytes 18440 | tf_op jit(solution)/shard_map/ppermute | solution.py:585
  40.5 0.3 shard_map.94.dopant_grid
  40.9 1.2 %collective-permute-done.10.near = f32[2,768]{1,0:T(2,128)S(1)} collective-permute-done((f32[2,768]{1,0:T(2,128)S(1)}, f32[2,768]{1,0:T(2,128)S(1)}, u32[]{:S(2)}, u32[]{:S(2)}) %collective-permute-start.10) | collective-permute-done | bytes 6176 | tf_op jit(solution)/shard_map/ppermute | solution.py:585
  42.1 1.7 %shard_map.96 = (f32[8,16,128]{2,1,0:T(8,128)}, f32[384]{0:T(512)}) custom-call(f32[2,768]{1,0:T(2,128)S(1)} %shard_map.93.packet, f32[2,768]{1,0:T(2,128)S(1)} %collective-permute-done.10.near, f32[2,768]{1,0:T(2,128)S(1)} %collective-permute-done.11.far, f32[288,128]{1,0:T(8,128)S(1)} %shard_map.94.dopant_grid, f32[8,24,128]{2,1,0:T(8,128)S(1)} %get-tuple-element.53.wide, ...), custom_call_target="tpu_custom_call" | custom-call | flops 100000000 | bytes 1000000 | tf_op jit(solution)/shard_map/pallas_call | solution.py:559
  (25 shorter events, 0.1 us)
Async XLA Ops:
  0.6 16.3 %collective-permute-start = (f32[2,192,192]{2,1,0:T(8,128)}, f32[2,192,192]{2,1,0:T(8,128)S(1)}, u32[]{:S(2)}, u32[]{:S(2)}) collective-permute-start(f32[2,192,192]{2,1,0:T(8,128)} %couple.7), channel_id=1, source_target_pairs={{0,4},{1,5},{2,6},{3,7},{4,0},{5,1},{6,2},{7,3},{8,12},{9,13},{10,... | collective-permute-start | bytes 884744 | tf_op jit(solution)/shard_map/ppermute | solution.py:585
  4.4 8.9 %copy-start.1 = (f32[384,128]{1,0:T(8,128)S(1)}, f32[384,128]{1,0:T(8,128)}, u32[]{:S(2)}) copy-start(f32[384,128]{1,0:T(8,128)} %probes.3) | copy-start | bytes 589828
  4.4 9.0 %copy-start = (f32[2,192,192]{2,1,0:T(8,128)S(1)}, f32[2,192,192]{2,1,0:T(8,128)}, u32[]{:S(2)}) copy-start(f32[2,192,192]{2,1,0:T(8,128)} %couple.7) | copy-start | bytes 884740
  4.4 9.0 %copy-start.2 = (f32[2,192,192]{2,1,0:T(8,128)S(1)}, f32[2,192,192]{2,1,0:T(8,128)}, u32[]{:S(2)}) copy-start(f32[2,192,192]{2,1,0:T(8,128)} %diag.1) | copy-start | bytes 884740
  11.2 5.7 %collective-permute-start.2 = (f32[192,128]{1,0:T(8,128)S(1)}, f32[192,128]{1,0:T(8,128)S(1)}, u32[]{:S(2)}, u32[]{:S(2)}) collective-permute-start(f32[192,128]{1,0:T(8,128)S(1)} %get-tuple-element.38), channel_id=1, source_target_pairs={{0,4},{1,5},{2,6},{3,7},{4,0},{5,1},{6,2},{7,3},{8,12},{9,13},{10,... | collective-permute-start | bytes 294920 | tf_op jit(solution)/shard_map/ppermute | solution.py:585
  11.3 7.8 %collective-permute-start.1 = (f32[192,128]{1,0:T(8,128)S(1)}, f32[192,128]{1,0:T(8,128)S(1)}, u32[]{:S(2)}, u32[]{:S(2)}) collective-permute-start(f32[192,128]{1,0:T(8,128)S(1)} %get-tuple-element.29), channel_id=1, source_target_pairs={{0,4},{1,5},{2,6},{3,7},{4,0},{5,1},{6,2},{7,3},{8,12},{9,13},{10,... | collective-permute-start | bytes 294920 | tf_op jit(solution)/shard_map/ppermute | solution.py:585
  13.3 15.8 %collective-permute-start.6 = (f32[384,128]{1,0:T(8,128)S(1)}, f32[384,128]{1,0:T(8,128)S(1)}, u32[]{:S(2)}, u32[]{:S(2)}) collective-permute-start(f32[384,128]{1,0:T(8,128)S(1)} %copy-done.1), channel_id=1, source_target_pairs={{0,4},{1,5},{2,6},{3,7},{4,0},{5,1},{6,2},{7,3},{8,12},{9,13},{10,... | collective-permute-start | bytes 589832 | tf_op jit(solution)/shard_map/ppermute | solution.py:585
  13.5 15.4 %collective-permute-start.5 = (f32[480,128]{1,0:T(8,128)S(1)}, f32[480,128]{1,0:T(8,128)S(1)}, u32[]{:S(2)}, u32[]{:S(2)}) collective-permute-start(f32[480,128]{1,0:T(8,128)S(1)} %get-tuple-element.45), channel_id=1, source_target_pairs={{0,4},{1,5},{2,6},{3,7},{4,0},{5,1},{6,2},{7,3},{8,12},{9,13},{10,... | collective-permute-start | bytes 737288 | tf_op jit(solution)/shard_map/ppermute | solution.py:585
  19.0 0.8 %copy-start.3 = (f32[8,16,128]{2,1,0:T(8,128)S(1)}, f32[8,16,128]{2,1,0:T(8,128)}, u32[]{:S(2)}) copy-start(f32[8,16,128]{2,1,0:T(8,128)} %potential.1) | copy-start | bytes 196612
  19.0 10.0 %collective-permute-start.3 = (f32[192,128]{1,0:T(8,128)S(1)}, f32[192,128]{1,0:T(8,128)S(1)}, u32[]{:S(2)}, u32[]{:S(2)}) collective-permute-start(f32[192,128]{1,0:T(8,128)S(1)} %get-tuple-element.42.total), channel_id=1, source_target_pairs={{4,8},{5,9},{6,10},{7,11},{8,4},{9,5},{10,6},{11,7},{0,1},{1,0},{2... | collective-permute-start | bytes 294920 | tf_op jit(solution)/shard_map/ppermute | solution.py:585
  19.0 9.9 %collective-permute-start.4 = (f32[192,128]{1,0:T(8,128)S(1)}, f32[192,128]{1,0:T(8,128)S(1)}, u32[]{:S(2)}, u32[]{:S(2)}) collective-permute-start(f32[192,128]{1,0:T(8,128)S(1)} %get-tuple-element.43), channel_id=1, source_target_pairs={{4,8},{5,9},{6,10},{7,11},{8,4},{9,5},{10,6},{11,7},{0,1},{1,0},{2... | collective-permute-start | bytes 294920 | tf_op jit(solution)/shard_map/ppermute | solution.py:585
  19.9 1.2 %collective-permute-start.12 = (f32[8,2,128]{2,1,0:T(2,128)S(1)}, f32[8,2,128]{2,1,0:T(2,128)S(1)}, u32[]{:S(2)}, u32[]{:S(2)}) collective-permute-start(f32[8,2,128]{2,1,0:T(2,128)S(1)} %get-tuple-element.57), channel_id=1, source_target_pairs={{0,1},{1,0},{2,3},{3,2},{4,5},{5,4},{6,7},{7,6},{8,9},{9,8},{10,11... | collective-permute-start | bytes 24584 | tf_op jit(solution)/shard_map/ppermute | solution.py:593
  21.1 3.1 %collective-permute-start.13 = (f32[8,2,128]{2,1,0:T(2,128)S(1)}, f32[8,2,128]{2,1,0:T(2,128)S(1)}, u32[]{:S(2)}, u32[]{:S(2)}) collective-permute-start(f32[8,2,128]{2,1,0:T(2,128)S(1)} %get-tuple-element.56), channel_id=1, source_target_pairs={{1,2},{2,1},{3,0},{0,3},{5,6},{6,5},{7,4},{4,7},{9,10},{10,9},{11,... | collective-permute-start | bytes 24584 | tf_op jit(solution)/shard_map/ppermute | solution.py:593
  24.2 16.6 %collective-permute-start.14 = (f32[48,128]{1,0:T(8,128)S(1)}, f32[48,128]{1,0:T(8,128)S(1)}, u32[]{:S(2)}, u32[]{:S(2)}) collective-permute-start(f32[48,128]{1,0:T(8,128)S(1)} %get-tuple-element.54), channel_id=1, source_target_pairs={{0,4},{1,5},{2,6},{3,7},{4,0},{5,1},{6,2},{7,3},{8,12},{9,13},{10,... | collective-permute-start | bytes 73736 | tf_op jit(solution)/shard_map/ppermute | solution.py:585
  28.8 12.0 %collective-permute-start.15 = (f32[48,128]{1,0:T(8,128)S(1)}, f32[48,128]{1,0:T(8,128)S(1)}, u32[]{:S(2)}, u32[]{:S(2)}) collective-permute-start(f32[48,128]{1,0:T(8,128)S(1)} %get-tuple-element.55), channel_id=1, source_target_pairs={{4,8},{5,9},{6,10},{7,11},{8,4},{9,5},{10,6},{11,7},{0,1},{1,0},{2... | collective-permute-start | bytes 73736 | tf_op jit(solution)/shard_map/ppermute | solution.py:585
  29.1 2.0 %copy-start.5 = (s32[384]{0:T(512)S(1)}, s32[384]{0:T(512)}, u32[]{:S(2)}) copy-start(s32[384]{0:T(512)} %param.11) | copy-start | bytes 4612
  29.1 1.9 %collective-permute-start.7 = (f32[1,768]{1,0:T(1,128)S(1)}, f32[1,768]{1,0:T(1,128)S(1)}, u32[]{:S(2)}, u32[]{:S(2)}) collective-permute-start(f32[1,768]{1,0:T(1,128)S(1)} %shard_map.92.rest_0_), channel_id=1, source_target_pairs={{0,1},{1,0},{2,3},{3,2},{4,5},{5,4},{6,7},{7,6},{8,9},{9,8},{10,11... | collective-permute-start | bytes 9224 | tf_op jit(solution)/shard_map/ppermute | solution.py:701
  29.5 3.6 %collective-permute-start.8 = (f32[1,768]{1,0:T(1,128)S(1)}, f32[1,768]{1,0:T(1,128)S(1)}, u32[]{:S(2)}, u32[]{:S(2)}) collective-permute-start(f32[1,768]{1,0:T(1,128)S(1)} %shard_map.92.rest_0_), channel_id=1, source_target_pairs={{0,2},{1,3},{2,0},{3,1},{4,6},{5,7},{6,4},{7,5},{8,10},{9,11},{10,... | collective-permute-start | bytes 9224 | tf_op jit(solution)/shard_map/ppermute | solution.py:701
  31.0 3.0 %collective-permute-start.9 = (f32[1,768]{1,0:T(1,128)S(1)}, f32[1,768]{1,0:T(1,128)S(1)}, u32[]{:S(2)}, u32[]{:S(2)}) collective-permute-start(f32[1,768]{1,0:T(1,128)S(1)} %shard_map.92.rest_0_), channel_id=1, source_target_pairs={{0,3},{1,2},{2,1},{3,0},{4,7},{5,6},{6,5},{7,4},{8,11},{9,10},{10,... | collective-permute-start | bytes 9224 | tf_op jit(solution)/shard_map/ppermute | solution.py:701
  31.1 9.4 %copy-start.4 = (s32[1024]{0:T(1024)S(1)}, s32[1024]{0:T(1024)}, u32[]{:S(2)}) copy-start(s32[1024]{0:T(1024)} %param.12) | copy-start | bytes 12292
  34.0 8.1 %collective-permute-start.10 = (f32[2,768]{1,0:T(2,128)S(1)}, f32[2,768]{1,0:T(2,128)S(1)}, u32[]{:S(2)}, u32[]{:S(2)}) collective-permute-start(f32[2,768]{1,0:T(2,128)S(1)} %shard_map.93.packet), channel_id=1, source_target_pairs={{0,4},{1,5},{2,6},{3,7},{4,0},{5,1},{6,2},{7,3},{8,12},{9,13},{10,... | collective-permute-start | bytes 18440 | tf_op jit(solution)/shard_map/ppermute | solution.py:585
  40.5 1.6 %collective-permute-start.11 = (f32[2,768]{1,0:T(2,128)S(1)}, f32[2,768]{1,0:T(2,128)S(1)}, u32[]{:S(2)}, u32[]{:S(2)}) collective-permute-start(f32[2,768]{1,0:T(2,128)S(1)} %shard_map.93.packet), channel_id=1, source_target_pairs={{4,8},{5,9},{6,10},{7,11},{8,4},{9,5},{10,6},{11,7},{0,1},{1,0},{2... | collective-permute-start | bytes 18440 | tf_op jit(solution)/shard_map/ppermute | solution.py:585

commit v8 on v7

--- a/solution.py
+++ b/solution.py
@@ -294,7 +294,7 @@
     dopant[...] = dopant_charge * one_pass(rows, ys.astype(BF16), NT)
 
 
-def halo_kernel(potential, got_even, got_odd, wide, near_planes, far_planes):
+def halo_kernel(potential, got_even, got_odd, wide):
     depth, rows_here, across = potential.shape
     even_e = lax.axis_index("energy") % 2 == 0
     below = jnp.where(even_e, got_odd[...], got_even[...])
@@ -304,9 +304,6 @@
     if spare > 0:
         parts.append(jnp.zeros((depth, spare, across), F32))
     wide[...] = jnp.concatenate(parts, axis=1)
-    even = lax.axis_index("slab") % 2 == 0
-    put_planes(near_planes, 0, wide, even)
-    put_planes(far_planes, 0, wide, jnp.logical_not(even))
 
 
 def put_planes(out, start, wide, high):
@@ -476,17 +473,33 @@
     dens[...] = dot6(jnp.ones((8, terms.shape[1]), F32), terms, NT)[0:1]
 
 
-def total_kernel(scale, cells, *rest):
-    parts, out = rest[:-1], rest[-1]
-    total = parts[0][0:1, :]
+def total_kernel(scale, cells, wide, *rest):
+    parts, outs = rest[:-2], rest[-2:]
+    total = parts[0][...]
     for part in parts[1:]:
-        total = total + part[0:1, :]
-    out[0:1, :] = total * scale
-    out[1:2, 0 : cells.shape[1]] = cells[...].astype(F32)
-
-
-def poisson_kernel(rows_all, planes, paired, packet, near, far, dopant_grid, wide, near_letter,
-                   far_letter, out, density):
+        total = total + part[...]
+    total = total * scale
+    place_of = cells[...].astype(F32)
+    lanes = wide.shape[2]
+    values = total.shape[1] // lanes
+    even = lax.axis_index("slab") % 2 == 0
+    for out, high in zip(outs, (even, jnp.logical_not(even))):
+        for k in range(values):
+            out[k : k + 1, :] = total[:, k * lanes : (k + 1) * lanes]
+        for k in range(cells.shape[1] // lanes):
+            out[values + k : values + k + 1, :] = place_of[:, k * lanes : (k + 1) * lanes]
+        put_planes(out, packet_planes(values, cells.shape[1] // lanes), wide, high)
+
+
+def packet_planes(values, cells):
+    return -(-(values + cells) // 8) * 8
+
+
+def packet_row(packet, first, count):
+    return jnp.concatenate([packet[first + k : first + k + 1, :] for k in range(count)], axis=1)
+
+
+def poisson_kernel(rows_all, planes, paired, packet, near, far, dopant_grid, wide, out, density):
     slab, slabs = lax.axis_index("slab"), lax.axis_size("slab")
     depth, pitch, across = wide.shape
     depth = depth + 2 * SWEEPS
@@ -494,13 +507,15 @@
     n = density.shape[0]
     even = slab % 2 == 0
     alone = jnp.logical_or(slab == 0, slab == slabs - 1)
-    own, beside, beyond = packet[0:1, 0:n], near[0:1, 0:n], far[0:1, 0:n]
+    count = n // across
+    values = 2 * count if paired else count
+    own, beside, beyond = [packet_row(p, 0, count) for p in (packet, near, far)]
     if paired:
-        own = jnp.where(alone, near[0:1, n : 2 * n], own)
-        beside = jnp.where(alone, beside, packet[0:1, n : 2 * n])
+        own = jnp.where(alone, packet_row(near, count, count), own)
+        beside = jnp.where(alone, beside, packet_row(packet, count, count))
     density[...] = own.reshape(n)
     weights = jnp.concatenate([own, beside, jnp.where(alone, 0.0, beyond)], axis=1)
-    orbitals = jnp.concatenate([packet[1:2, 0:n], near[1:2, 0:n], far[1:2, 0:n]], axis=1)
+    orbitals = jnp.concatenate([packet_row(p, values, count) for p in (packet, near, far)], axis=1)
     orbitals = jnp.where(jnp.abs(orbitals) < 2.0**30, orbitals, -1.0).astype(jnp.int32)
     rows, ys = spots(orbitals, rows_all, depth, pitch, across, first_z, first_x)
     spread = ys * weights
@@ -511,8 +526,8 @@
     electron = one_pass(rows, h, NT) + (one_pass(rows, m, NT) + one_pass(rows, low, NT))
     electron = electron.reshape(depth, pitch, across)
     dopant = dopant_grid[...].reshape(depth, pitch, across)
-    near_planes = near_letter[...].reshape(SWEEPS, pitch, across)
-    far_planes = far_letter[...].reshape(SWEEPS, pitch, across)
+    near_planes = near[packet_planes(values, count) :, :].reshape(SWEEPS, pitch, across)
+    far_planes = far[packet_planes(values, count) :, :].reshape(SWEEPS, pitch, across)
     start = jnp.concatenate(
         [jnp.where(even, far_planes, near_planes), wide[...],
          jnp.where(even, near_planes, far_planes)],
@@ -663,13 +678,10 @@
         [couple, even, odd, sources, source, link, base_source, solved],
     )
     sources_middle = slab_exchange(total_source, half % 2 == 0)
-    wide, near_planes, far_planes = call(
-        halo_kernel,
-        (like(depth, pitch, across), like(strip, across), like(strip, across)),
+    wide = call(
+        halo_kernel, like(depth, pitch, across),
         [initial_potential, *lax.optimization_barrier((got_even, got_odd, sent))[:2]],
     )
-    near_planes = slab_exchange(near_planes, False)
-    far_planes = slab_exchange(far_planes, True)
     inverse = call(join_kernel, square, [across_middle, total], (sq,))
     if paired:
         slope, offset = call(
@@ -701,20 +713,20 @@
         lax.ppermute(dens, "energy", [(e, e ^ k) for e in range(energies)])
         for k in range(1, energies)
     ]
-    packet = call(
+    spare = packet_planes(dens.shape[1] // across, orbital_cell.shape[0] // across)
+    packet, packet_far = call(
         functools.partial(total_kernel, 1.0 / (probe_count * energies)),
-        like(2, dens.shape[1]), [orbital_cell.reshape(1, -1), *parts],
+        (like(spare + strip, across),) * 2, [orbital_cell.reshape(1, -1), wide, *parts],
     )
     near = slab_exchange(packet, False)
-    far = slab_exchange(packet, True)
-
-    def poisson(packet, near, far, dopant_grid, wide, near_letter, far_letter, out, density):
-        poisson_kernel(rows_all, depth * slabs, paired, packet, near, far, dopant_grid, wide,
-                       near_letter, far_letter, out, density)
+    far = slab_exchange(packet_far, True)
+
+    def poisson(*refs):
+        poisson_kernel(rows_all, depth * slabs, paired, *refs)
 
     potential, density = call(
         poisson, (like(depth, rows_here, across), like(2 * width)),
-        [packet, near, far, dopant_grid, wide, near_planes, far_planes],
+        [packet, near, far, dopant_grid, wide],
     )
     return (potential, density)
 

time: 43.9 us -> 42.2 us (0.961)
  starting transfers between devices: 22.3 us -> 17.6 us
  waiting for transfers between devices: 10.7 us -> 13.3 us
  local copies, waits for them, and re-layouts: 0.35 us -> 0.86 us
    ppermute x11 -> x9, starting transfers between devices: 19 us -> 14 us  [slab_exchange(): return lax.ppermute(value, ('slab', 'energy'), whole)]
    ppermute x11 -> x9, waiting for transfers between devices: 4.75 us -> 7.93 us  [slab_exchange(): return lax.ppermute(value, ('slab', 'energy'), whole)]
    ppermute x3, waiting for transfers between devices: 2.93 us -> 2.35 us  [program(): lax.ppermute(dens, 'energy', [(e, e ^ k) for e in range(energies)])]
    unnamed x12, local copies, waits for them, and re-layouts: 0.35 us -> 0.86 us
  transfers between devices with their start and end apart: 16 -> 14, of which waited for: 7 -> 8; matrix products, arithmetic and copies ran while one was open for 0% -> 0% of each run, Pallas kernels for 17% -> 17%
where the time goes in v8:
time: 42.2 us; the launch traced here: 42 us
  starting transfers between devices  17.6 us (42%)
  waiting for transfers between devices  13.3 us (32%)
  Pallas kernels  8.88 us (21%)
  between operations  1.41 us (3%)
  local copies, waits for them, and re-layouts  0.86 us (2%)
    ppermute x9, starting transfers between devices, slab_exchange(): return lax.ppermute(value, ('slab', 'energy'), whole)  14 us
    pallas_call x11, Pallas kernels, call(): pl.pallas_call(kernel, out_shape=outs, in_specs=[FAR] * distant + [VM] *...  8.88 us
    ppermute x9, waiting for transfers between devices, slab_exchange(): return lax.ppermute(value, ('slab', 'energy'), whole)  7.93 us
    ppermute x2, waiting for transfers between devices, energy_exchange(): return lax.ppermute(value, 'energy', pairs)  2.98 us
    ppermute x3, waiting for transfers between devices, program(): lax.ppermute(dens, 'energy', [(e, e ^ k) for e in range(energies)])  2.35 us
    ppermute x3, starting transfers between devices, program(): lax.ppermute(dens, 'energy', [(e, e ^ k) for e in range(energies)])  2.21 us
    ppermute x2, starting transfers between devices, energy_exchange(): return lax.ppermute(value, 'energy', pairs)  1.32 us
    unnamed x12, local copies, waits for them, and re-layouts  0.86 us
  transfers between devices with their start and end apart: 14, of which 8 were waited for; matrix products, arithmetic and copies ran while one was open for 0% of the time, Pallas kernels for 17%

profile of v8, /device:TPU:0, one launch (start us, length us, event | category | flops | bytes accessed | tf_op | source)
XLA Modules:
  0.0 42.0 jit_solution(6833000653066912736)
XLA Ops:
  0.6 3.1 %collective-permute-start.2 = (f32[2,192,192]{2,1,0:T(8,128)}, f32[2,192,192]{2,1,0:T(8,128)S(1)}, u32[]{:S(2)}, u32[]{:S(2)}) collective-permute-start(f32[2,192,192]{2,1,0:T(8,128)} %couple.7), channel_id=1, source_target_pairs={{0,4},{1,5},{2,6},{3,7},{4,0},{5,1},{6,2},{7,3},{8,12},{9,13},{10,... | collective-permute-start | bytes 884744 | tf_op jit(solution)/shard_map/ppermute | solution.py:600
  4.4 6.7 %shard_map.86 = (f32[192,192]{1,0:T(8,128)S(1)}, f32[192,128]{1,0:T(8,128)S(1)}, f32[192,192]{1,0:T(8,128)S(1)}, f32[192,192]{1,0:T(8,128)S(1)}, f32[192,128]{1,...) custom-call(f32[2,192,192]{2,1,0:T(8,128)} %diag.1, f32[2,192,192]{2,1,0:T(8,128)} %couple.7, ...), custom_call_target="tpu_custom_call" | custom-call | flops 100000000 | bytes 1000000 | tf_op jit(solution)/shard_map/pallas_call | solution.py:574
  11.2 0.1 collective-permute-start.3
  11.3 2.0 %collective-permute-start.4 = (f32[192,128]{1,0:T(8,128)S(1)}, f32[192,128]{1,0:T(8,128)S(1)}, u32[]{:S(2)}, u32[]{:S(2)}) collective-permute-start(f32[192,128]{1,0:T(8,128)S(1)} %get-tuple-element.40), channel_id=1, source_target_pairs={{0,4},{1,5},{2,6},{3,7},{4,0},{5,1},{6,2},{7,3},{8,12},{9,13},{10,... | collective-permute-start | bytes 294920 | tf_op jit(solution)/shard_map/ppermute | solution.py:600
  13.3 0.1 collective-permute-start.8
  13.4 0.1 shard_map.87
  13.4 2.1 %collective-permute-start.7 = (f32[480,128]{1,0:T(8,128)S(1)}, f32[480,128]{1,0:T(8,128)S(1)}, u32[]{:S(2)}, u32[]{:S(2)}) collective-permute-start(f32[480,128]{1,0:T(8,128)S(1)} %get-tuple-element.46), channel_id=1, source_target_pairs={{0,4},{1,5},{2,6},{3,7},{4,0},{5,1},{6,2},{7,3},{8,12},{9,13},{10,... | collective-permute-start | bytes 737288 | tf_op jit(solution)/shard_map/ppermute | solution.py:600
  15.5 1.4 %collective-permute-done.3.message.letter = f32[192,128]{1,0:T(8,128)S(1)} collective-permute-done((f32[192,128]{1,0:T(8,128)S(1)}, f32[192,128]{1,0:T(8,128)S(1)}, u32[]{:S(2)}, u32[]{:S(2)}) %collective-permute-start.3) | collective-permute-done | bytes 98336 | tf_op jit(solution)/shard_map/ppermute | solution.py:600
  16.9 0.0 collective-permute-done.2.even.odd
  16.9 2.1 %collective-permute-done.4.message.sources = f32[192,128]{1,0:T(8,128)S(1)} collective-permute-done((f32[192,128]{1,0:T(8,128)S(1)}, f32[192,128]{1,0:T(8,128)S(1)}, u32[]{:S(2)}, u32[]{:S(2)}) %collective-permute-start.4) | collective-permute-done | bytes 98336 | tf_op jit(solution)/shard_map/ppermute | solution.py:600
  19.0 0.0 collective-permute-start.5
  19.0 0.8 %copy-done.3 = f32[8,16,128]{2,1,0:T(8,128)S(1)} copy-done((f32[8,16,128]{2,1,0:T(8,128)S(1)}, f32[8,16,128]{2,1,0:T(8,128)}, u32[]{:S(2)}) %copy-start.3) | copy-done | bytes 65560
  19.9 0.0 copy-start.5
  19.9 0.1 collective-permute-start
  20.0 1.2 %collective-permute-done.got_even = f32[8,2,128]{2,1,0:T(2,128)S(1)} collective-permute-done((f32[8,2,128]{2,1,0:T(2,128)S(1)}, f32[8,2,128]{2,1,0:T(2,128)S(1)}, u32[]{:S(2)}, u32[]{:S(2)}) %collective-permute-start) | collective-permute-done | bytes 8224 | tf_op jit(solution)/shard_map/ppermute | solution.py:608
  21.1 1.2 %collective-permute-start.1 = (f32[8,2,128]{2,1,0:T(2,128)S(1)}, f32[8,2,128]{2,1,0:T(2,128)S(1)}, u32[]{:S(2)}, u32[]{:S(2)}) collective-permute-start(f32[8,2,128]{2,1,0:T(2,128)S(1)} %get-tuple-element.54), channel_id=1, source_target_pairs={{1,2},{2,1},{3,0},{0,3},{5,6},{6,5},{7,4},{4,7},{9,10},{10,9},{11,... | collective-permute-start | bytes 24584 | tf_op jit(solution)/shard_map/ppermute | solution.py:608
  22.4 1.8 %collective-permute-done.1.got_odd = f32[8,2,128]{2,1,0:T(2,128)S(1)} collective-permute-done((f32[8,2,128]{2,1,0:T(2,128)S(1)}, f32[8,2,128]{2,1,0:T(2,128)S(1)}, u32[]{:S(2)}, u32[]{:S(2)}) %collective-permute-start.1) | collective-permute-done | bytes 8224 | tf_op jit(solution)/shard_map/ppermute | solution.py:608
  24.2 2.9 %collective-permute-done.7.second = f32[480,128]{1,0:T(8,128)S(1)} collective-permute-done((f32[480,128]{1,0:T(8,128)S(1)}, f32[480,128]{1,0:T(8,128)S(1)}, u32[]{:S(2)}, u32[]{:S(2)}) %collective-permute-start.7) | collective-permute-done | bytes 245792 | tf_op jit(solution)/shard_map/ppermute | solution.py:600
  27.1 0.0 collective-permute-done.6.message
  27.1 0.0 collective-permute-done.8.probes_near
  27.1 0.0 collective-permute-done.5.message
  27.1 1.6 %collective-permute-start.10 = (f32[1,768]{1,0:T(1,128)S(1)}, f32[1,768]{1,0:T(1,128)S(1)}, u32[]{:S(2)}, u32[]{:S(2)}) collective-permute-start(f32[1,768]{1,0:T(1,128)S(1)} %shard_map.93.rest_0_), channel_id=1, source_target_pairs={{0,2},{1,3},{2,0},{3,1},{4,6},{5,7},{6,4},{7,5},{8,10},{9,11},{10,... | collective-permute-start | bytes 9224 | tf_op jit(solution)/shard_map/ppermute | solution.py:713
  28.7 0.0 collective-permute-start.11
  28.7 0.6 %collective-permute-start.9 = (f32[1,768]{1,0:T(1,128)S(1)}, f32[1,768]{1,0:T(1,128)S(1)}, u32[]{:S(2)}, u32[]{:S(2)}) collective-permute-start(f32[1,768]{1,0:T(1,128)S(1)} %shard_map.93.rest_0_), channel_id=1, source_target_pairs={{0,1},{1,0},{2,3},{3,2},{4,5},{5,4},{6,7},{7,6},{8,9},{9,8},{10,11... | collective-permute-start | bytes 9224 | tf_op jit(solution)/shard_map/ppermute | solution.py:713
  29.4 1.4 %collective-permute-done.10.rest_2_ = f32[1,768]{1,0:T(1,128)S(1)} collective-permute-done((f32[1,768]{1,0:T(1,128)S(1)}, f32[1,768]{1,0:T(1,128)S(1)}, u32[]{:S(2)}, u32[]{:S(2)}) %collective-permute-start.10) | collective-permute-done | bytes 3104 | tf_op jit(solution)/shard_map/ppermute | solution.py:713
  30.8 0.9 %collective-permute-done.11.rest_3_ = f32[1,768]{1,0:T(1,128)S(1)} collective-permute-done((f32[1,768]{1,0:T(1,128)S(1)}, f32[1,768]{1,0:T(1,128)S(1)}, u32[]{:S(2)}, u32[]{:S(2)}) %collective-permute-start.11) | collective-permute-done | bytes 3104 | tf_op jit(solution)/shard_map/ppermute | solution.py:713
  31.7 0.0 collective-permute-done.9.rest_1_
  31.7 0.0 copy-start.4
  31.8 6.7 %collective-permute-start.12 = (f32[64,128]{1,0:T(8,128)S(1)}, f32[64,128]{1,0:T(8,128)S(1)}, u32[]{:S(2)}, u32[]{:S(2)}) collective-permute-start(f32[64,128]{1,0:T(8,128)S(1)} %get-tuple-element.52.refs_0_), channel_id=1, source_target_pairs={{0,4},{1,5},{2,6},{3,7},{4,0},{5,1},{6,2},{7,3},{8,12},{9,13},{10,... | collective-permute-start | bytes 98312 | tf_op jit(solution)/shard_map/ppermute | solution.py:600
  38.4 0.3 shard_map.95.refs_3_
  38.8 1.5 %collective-permute-done.12.refs_1_ = f32[64,128]{1,0:T(8,128)S(1)} collective-permute-done((f32[64,128]{1,0:T(8,128)S(1)}, f32[64,128]{1,0:T(8,128)S(1)}, u32[]{:S(2)}, u32[]{:S(2)}) %collective-permute-start.12) | collective-permute-done | bytes 32800 | tf_op jit(solution)/shard_map/ppermute | solution.py:600
  40.3 1.7 %shard_map.96 = (f32[8,16,128]{2,1,0:T(8,128)}, f32[384]{0:T(512)}) custom-call(f32[64,128]{1,0:T(8,128)S(1)} %get-tuple-element.52.refs_0_, f32[64,128]{1,0:T(8,128)S(1)} %collective-permute-done.12.refs_1_, f32[64,128]{1,0:T(8,128)S(1)} %collective-permute-done.13.refs_2_, f32[288,128]{1,0:T(8,128)S(1)} %shard_map.95.refs_3_, ...), custom_call_target="tpu_custom_call" | custom-call | flops 100000000 | bytes 1000000 | tf_op jit(solution)/shard_map/pallas_call | solution.py:574
  (21 shorter events, 0.1 us)
Async XLA Ops:
  0.6 16.3 %collective-permute-start.2 = (f32[2,192,192]{2,1,0:T(8,128)}, f32[2,192,192]{2,1,0:T(8,128)S(1)}, u32[]{:S(2)}, u32[]{:S(2)}) collective-permute-start(f32[2,192,192]{2,1,0:T(8,128)} %couple.7), channel_id=1, source_target_pairs={{0,4},{1,5},{2,6},{3,7},{4,0},{5,1},{6,2},{7,3},{8,12},{9,13},{10,... | collective-permute-start | bytes 884744 | tf_op jit(solution)/shard_map/ppermute | solution.py:600
  4.4 8.9 %copy-start.1 = (f32[384,128]{1,0:T(8,128)S(1)}, f32[384,128]{1,0:T(8,128)}, u32[]{:S(2)}) copy-start(f32[384,128]{1,0:T(8,128)} %probes.3) | copy-start | bytes 589828
  4.4 8.9 %copy-start = (f32[2,192,192]{2,1,0:T(8,128)S(1)}, f32[2,192,192]{2,1,0:T(8,128)}, u32[]{:S(2)}) copy-start(f32[2,192,192]{2,1,0:T(8,128)} %couple.7) | copy-start | bytes 884740
  4.4 8.9 %copy-start.2 = (f32[2,192,192]{2,1,0:T(8,128)S(1)}, f32[2,192,192]{2,1,0:T(8,128)}, u32[]{:S(2)}) copy-start(f32[2,192,192]{2,1,0:T(8,128)} %diag.1) | copy-start | bytes 884740
  11.2 5.7 %collective-permute-start.3 = (f32[192,128]{1,0:T(8,128)S(1)}, f32[192,128]{1,0:T(8,128)S(1)}, u32[]{:S(2)}, u32[]{:S(2)}) collective-permute-start(f32[192,128]{1,0:T(8,128)S(1)} %get-tuple-element.28), channel_id=1, source_target_pairs={{0,4},{1,5},{2,6},{3,7},{4,0},{5,1},{6,2},{7,3},{8,12},{9,13},{10,... | collective-permute-start | bytes 294920 | tf_op jit(solution)/shard_map/ppermute | solution.py:600
  11.3 7.8 %collective-permute-start.4 = (f32[192,128]{1,0:T(8,128)S(1)}, f32[192,128]{1,0:T(8,128)S(1)}, u32[]{:S(2)}, u32[]{:S(2)}) collective-permute-start(f32[192,128]{1,0:T(8,128)S(1)} %get-tuple-element.40), channel_id=1, source_target_pairs={{0,4},{1,5},{2,6},{3,7},{4,0},{5,1},{6,2},{7,3},{8,12},{9,13},{10,... | collective-permute-start | bytes 294920 | tf_op jit(solution)/shard_map/ppermute | solution.py:600
  13.3 13.8 %collective-permute-start.8 = (f32[384,128]{1,0:T(8,128)S(1)}, f32[384,128]{1,0:T(8,128)S(1)}, u32[]{:S(2)}, u32[]{:S(2)}) collective-permute-start(f32[384,128]{1,0:T(8,128)S(1)} %copy-done.1), channel_id=1, source_target_pairs={{0,4},{1,5},{2,6},{3,7},{4,0},{5,1},{6,2},{7,3},{8,12},{9,13},{10,... | collective-permute-start | bytes 589832 | tf_op jit(solution)/shard_map/ppermute | solution.py:600
  13.4 13.6 %collective-permute-start.7 = (f32[480,128]{1,0:T(8,128)S(1)}, f32[480,128]{1,0:T(8,128)S(1)}, u32[]{:S(2)}, u32[]{:S(2)}) collective-permute-start(f32[480,128]{1,0:T(8,128)S(1)} %get-tuple-element.46), channel_id=1, source_target_pairs={{0,4},{1,5},{2,6},{3,7},{4,0},{5,1},{6,2},{7,3},{8,12},{9,13},{10,... | collective-permute-start | bytes 737288 | tf_op jit(solution)/shard_map/ppermute | solution.py:600
  16.9 10.2 %collective-permute-start.6 = (f32[192,128]{1,0:T(8,128)S(1)}, f32[192,128]{1,0:T(8,128)S(1)}, u32[]{:S(2)}, u32[]{:S(2)}) collective-permute-start(f32[192,128]{1,0:T(8,128)S(1)} %get-tuple-element.37), channel_id=1, source_target_pairs={{4,8},{5,9},{6,10},{7,11},{8,4},{9,5},{10,6},{11,7},{0,1},{1,0},{2... | collective-permute-start | bytes 294920 | tf_op jit(solution)/shard_map/ppermute | solution.py:600
  19.0 0.8 %copy-start.3 = (f32[8,16,128]{2,1,0:T(8,128)S(1)}, f32[8,16,128]{2,1,0:T(8,128)}, u32[]{:S(2)}) copy-start(f32[8,16,128]{2,1,0:T(8,128)} %potential.1) | copy-start | bytes 196612
  19.0 8.1 %collective-permute-start.5 = (f32[192,128]{1,0:T(8,128)S(1)}, f32[192,128]{1,0:T(8,128)S(1)}, u32[]{:S(2)}, u32[]{:S(2)}) collective-permute-start(f32[192,128]{1,0:T(8,128)S(1)} %get-tuple-element.44.total), channel_id=1, source_target_pairs={{4,8},{5,9},{6,10},{7,11},{8,4},{9,5},{10,6},{11,7},{0,1},{1,0},{2... | collective-permute-start | bytes 294920 | tf_op jit(solution)/shard_map/ppermute | solution.py:600
  19.9 2.5 %copy-start.5 = (s32[384]{0:T(512)S(1)}, s32[384]{0:T(512)}, u32[]{:S(2)}) copy-start(s32[384]{0:T(512)} %param.11) | copy-start | bytes 4612
  19.9 1.2 %collective-permute-start = (f32[8,2,128]{2,1,0:T(2,128)S(1)}, f32[8,2,128]{2,1,0:T(2,128)S(1)}, u32[]{:S(2)}, u32[]{:S(2)}) collective-permute-start(f32[8,2,128]{2,1,0:T(2,128)S(1)} %get-tuple-element.55), channel_id=1, source_target_pairs={{0,1},{1,0},{2,3},{3,2},{4,5},{5,4},{6,7},{7,6},{8,9},{9,8},{10,11... | collective-permute-start | bytes 24584 | tf_op jit(solution)/shard_map/ppermute | solution.py:608
  21.1 3.1 %collective-permute-start.1 = (f32[8,2,128]{2,1,0:T(2,128)S(1)}, f32[8,2,128]{2,1,0:T(2,128)S(1)}, u32[]{:S(2)}, u32[]{:S(2)}) collective-permute-start(f32[8,2,128]{2,1,0:T(2,128)S(1)} %get-tuple-element.54), channel_id=1, source_target_pairs={{1,2},{2,1},{3,0},{0,3},{5,6},{6,5},{7,4},{4,7},{9,10},{10,9},{11,... | collective-permute-start | bytes 24584 | tf_op jit(solution)/shard_map/ppermute | solution.py:608
  27.1 3.7 %collective-permute-start.10 = (f32[1,768]{1,0:T(1,128)S(1)}, f32[1,768]{1,0:T(1,128)S(1)}, u32[]{:S(2)}, u32[]{:S(2)}) collective-permute-start(f32[1,768]{1,0:T(1,128)S(1)} %shard_map.93.rest_0_), channel_id=1, source_target_pairs={{0,2},{1,3},{2,0},{3,1},{4,6},{5,7},{6,4},{7,5},{8,10},{9,11},{10,... | collective-permute-start | bytes 9224 | tf_op jit(solution)/shard_map/ppermute | solution.py:713
  28.7 3.0 %collective-permute-start.11 = (f32[1,768]{1,0:T(1,128)S(1)}, f32[1,768]{1,0:T(1,128)S(1)}, u32[]{:S(2)}, u32[]{:S(2)}) collective-permute-start(f32[1,768]{1,0:T(1,128)S(1)} %shard_map.93.rest_0_), channel_id=1, source_target_pairs={{0,3},{1,2},{2,1},{3,0},{4,7},{5,6},{6,5},{7,4},{8,11},{9,10},{10,... | collective-permute-start | bytes 9224 | tf_op jit(solution)/shard_map/ppermute | solution.py:713
  28.7 3.0 %collective-permute-start.9 = (f32[1,768]{1,0:T(1,128)S(1)}, f32[1,768]{1,0:T(1,128)S(1)}, u32[]{:S(2)}, u32[]{:S(2)}) collective-permute-start(f32[1,768]{1,0:T(1,128)S(1)} %shard_map.93.rest_0_), channel_id=1, source_target_pairs={{0,1},{1,0},{2,3},{3,2},{4,5},{5,4},{6,7},{7,6},{8,9},{9,8},{10,11... | collective-permute-start | bytes 9224 | tf_op jit(solution)/shard_map/ppermute | solution.py:713
  31.7 6.7 %copy-start.4 = (s32[1024]{0:T(1024)S(1)}, s32[1024]{0:T(1024)}, u32[]{:S(2)}) copy-start(s32[1024]{0:T(1024)} %param.12) | copy-start | bytes 12292
  31.8 8.6 %collective-permute-start.12 = (f32[64,128]{1,0:T(8,128)S(1)}, f32[64,128]{1,0:T(8,128)S(1)}, u32[]{:S(2)}, u32[]{:S(2)}) collective-permute-start(f32[64,128]{1,0:T(8,128)S(1)} %get-tuple-element.52.refs_0_), channel_id=1, source_target_pairs={{0,4},{1,5},{2,6},{3,7},{4,0},{5,1},{6,2},{7,3},{8,12},{9,13},{10,... | collective-permute-start | bytes 98312 | tf_op jit(solution)/shard_map/ppermute | solution.py:600
  38.4 1.9 %collective-permute-start.13 = (f32[64,128]{1,0:T(8,128)S(1)}, f32[64,128]{1,0:T(8,128)S(1)}, u32[]{:S(2)}, u32[]{:S(2)}) collective-permute-start(f32[64,128]{1,0:T(8,128)S(1)} %get-tuple-element.53), channel_id=1, source_target_pairs={{4,8},{5,9},{6,10},{7,11},{8,4},{9,5},{10,6},{11,7},{0,1},{1,0},{2... | collective-permute-start | bytes 98312 | tf_op jit(solution)/shard_map/ppermute | solution.py:600

commit v9 on v8

--- a/solution.py
+++ b/solution.py
@@ -69,7 +69,8 @@
             error = scale * squared - (scale - 1.0) * unit
         tau = after
     residual = unit - dot6(matrix, guess)
-    return guess + dot3(guess, residual), jnp.sum(residual * residual), first
+    step = one_pass(guess.astype(BF16), residual.astype(BF16))
+    return guess + step, jnp.sum(residual * residual), first
 
 
 def fast(matrix, hold, ratio, doublings):
@@ -157,11 +158,15 @@
     return dot3(jnp.where(left, couple[0], following(ahead).T), message[...])
 
 
-def stage_kernel(step, diag_far, couple_far, probes_far, energy, *rest):
+def stage_kernel(step, inner_too, diag_far, couple_far, probes_far, energy, *rest):
     if step > 0:
         message, sources, even, odd, rest = rest[0], rest[1], rest[2], rest[3], rest[4:]
-    factor_p, value_p, inverse_p, matrix_q, source_q, inverse_q, value_q, out = rest[:8]
-    hold, diag, couple, probes, sems = rest[8:]
+    factor_p, value_p, inverse_p, matrix_q, source_q, out = rest[:6]
+    rest = rest[6:]
+    if inner_too:
+        inverse_q, value_q, out_inverse = rest[:3]
+        rest = rest[3:]
+    hold, diag, couple, probes, sems = rest
     _, left, distance = place()
     forward = lax.axis_index("slab") <= lax.axis_size("slab") // 2
     first = jnp.where(forward, 0, 1)
@@ -186,12 +191,14 @@
         sp = sp - jnp.where(taken, take_block(message, couple, ahead, left), 0.0)
         extra = jnp.where(taken, take_column(sources, couple, ahead, left), 0.0)
 
-    def run(invert):
-        xp, size_p = invert(sp, hold, 1 / 12, 4)
-        inverse_p[...] = xp
+    def await_loads():
+        for load in loads[2 if step > 0 else 1 :]:
+            load.wait()
+
+    def outer_block(invert):
+        xp, size = invert(sp, hold, 1 / 12, 4)
         if invert is fast:
-            for load in loads[2 if step > 0 else 1 :]:
-                load.wait()
+            await_loads()
         rp = probes[pl.ds(pl.multiple_of(first * width, width), width), :]
         rq = probes[pl.ds(pl.multiple_of((1 - first) * width, width), width), :]
         if step > 0:
@@ -205,15 +212,21 @@
         factor_p[...] = fp
         value_p[...] = yp
         sq = diag[1] + shifted - dot3(aqp, fp)
-        source = rq - dot3(aqp, yp)
+        return xp, yp, sq, rq - dot3(aqp, yp), size
+
+    def run(invert):
+        xp, _, sq, reduced, size = outer_block(invert)
+        inverse_p[...] = xp
         matrix_q[...] = sq
-        source_q[...] = source
-        xq, size_q = invert(sq, hold, 1 / 12, 4)
-        yq = dot3(xq, source)
-        inverse_q[...] = xq
-        value_q[...] = yq
-        pack_symmetric(xq, out)
-        return jnp.maximum(size_p, size_q)
+        source_q[...] = reduced
+        pack_symmetric(sq, out)
+        if inner_too:
+            xq, size_q = invert(sq, hold, 1 / 12, 4)
+            inverse_q[...] = xq
+            value_q[...] = dot3(xq, reduced)
+            pack_symmetric(xq, out_inverse)
+            size = jnp.maximum(size, size_q)
+        return size
 
     guarded(run)
 
@@ -252,39 +265,71 @@
     return first_z, lax.axis_index("energy") * rows_here - SWEEPS
 
 
-def ready_kernel(energy, diag, couple, probes, factor_p, value_p, inverse_p, matrix_q, source_q,
-                 matrix, source, link, base, base_source, reach, out):
-    slab, _, distance = place()
+def pack_kernel(factor_p, value_p, out):
+    _, _, distance = place()
+    width = value_p.shape[0]
+    packed = width + width // 2
+
+    @pl.when(distance < lax.axis_size("slab") // 2 - 1)
+    def _():
+        pack_full(factor_p[...], out)
+        out[packed : packed + width, :] = value_p[...]
+
+
+def ready_kernel(couple, even, odd, factor_p, value_p, inverse_p, matrix_q, source_q, matrix,
+                 source, link, base, base_source, near, far, inner, reach, hold):
+    slab, _, _ = place()
     half = lax.axis_size("slab") // 2
-    width = diag.shape[1]
-    packed = width + width // 2
-
-    @pl.when(slab == half)
+
+    @pl.when(slab == half - 1)
     def _():
         behind = couple[0]
         behind_t = behind.T
         across = dot3(inverse_p[...], behind)
-        reach[...] = across
-        matrix[...] = matrix_q[...]
-        source[...] = source_q[...]
-        link[...] = dot3(couple[1], across)
-        base[...] = dot3(behind_t, across)
-        base_source[...] = dot3(behind_t, value_p[...])
-
-    @pl.when(slab == half - 1)
-    def _():
-        shift = sigma_base + sigma_step * energy[...].astype(F32)
-        shifted = shift * eye(width)
-        matrix[...] = diag[0] + shifted
-        source[...] = probes[0:width, :]
-        link[...] = couple[1].T
-        base[...] = diag[1] + shifted
-        base_source[...] = probes[width : 2 * width, :]
-
-    @pl.when(distance < half - 1)
-    def _():
-        pack_full(factor_p[...], out)
-        out[packed : packed + width, :] = value_p[...]
+        near[...] = across
+        far[...] = factor_p[...]
+        inner[...] = value_p[...]
+        matrix[...] = dot3(behind_t, across)
+        source[...] = dot3(behind_t, value_p[...])
+        link[...] = -dot3(behind_t, factor_p[...])
+        base[...] = matrix_q[...]
+        base_source[...] = source_q[...]
+
+    @pl.when(slab == half)
+    def _():
+        behind = couple[0]
+        behind_t = behind.T
+        ahead = following((even, odd))
+        ahead_t = ahead.T
+        back = dot3(inverse_p[...], behind)
+        reach[...] = back
+        side = dot3(couple[1], back)
+        side_t = side.T
+
+        def run(invert):
+            solved, size = invert(matrix_q[...], hold, 1 / 12, 4)
+            found = dot3(solved, source_q[...])
+            across = dot3(solved, ahead_t)
+            aside = dot3(solved, side)
+            near[...] = across
+            far[...] = -aside
+            inner[...] = found
+            matrix[...] = dot3(ahead, across)
+            source[...] = dot3(ahead, found)
+            link[...] = -dot3(ahead, aside)
+            base[...] = dot3(behind_t, back) + dot3(side_t, aside)
+            base_source[...] = dot3(behind_t, value_p[...]) - dot3(side_t, found)
+            return size
+
+        guarded(run)
+
+
+def rows_kernel(potential, even_out, odd_out):
+    halo = even_out.shape[1]
+    low, high = potential[:, :halo], potential[:, potential.shape[1] - halo :]
+    odd = lax.axis_index("energy") % 2 == 1
+    even_out[...] = jnp.where(odd, low, high)
+    odd_out[...] = jnp.where(odd, high, low)
 
 
 def deposit_kernel(rows_all, pitch, depth, rows_here, dopants, dopant):
@@ -320,13 +365,12 @@
     return jnp.logical_or(slab == half - 1, slab == half), left
 
 
-def centre_kernel(couple, even, odd, message, matrix, link, base, solved, factor, total, out,
-                  hold):
+def centre_kernel(message, matrix, link, base, solved, factor, total, out, hold):
     here, left = middle_slab()
 
     @pl.when(here)
     def _():
-        block = matrix[...] - take_block(message, couple, (even, odd), left)
+        block = unpack_symmetric(message[...]) - matrix[...]
         near = link[...]
         near_t = near.T
         sign = jnp.where(left, -1.0, 1.0)
@@ -344,21 +388,19 @@
         guarded(run)
 
 
-def source_kernel(couple, even, odd, message, source, link, base_source, solved, value, total):
-    here, left = middle_slab()
+def source_kernel(message, source, link, base_source, solved, value, total):
+    here, _ = middle_slab()
 
     @pl.when(here)
     def _():
-        right_side = source[...] - take_column(message, couple, (even, odd), left)
-        found = dot3(solved[...], right_side)
+        found = dot3(solved[...], message[...] - source[...])
         value[...] = found
         total[...] = base_source[...] - dot3(link[...].T, found)
 
 
-def expand_kernel(couple, even, odd, letter, sources, second, factor, value, factor_p, value_p,
-                  reach, slope, offset):
-    slab, left, _ = place()
-    half = lax.axis_size("slab") // 2
+def expand_kernel(second, factor, value, factor_p, value_p, near, far, inner, reach, slope,
+                  offset):
+    here, left = middle_slab()
     width = value.shape[0]
     packed = width + width // 2
 
@@ -367,12 +409,14 @@
         slope[at, :] = m
         offset[at, :] = v
 
-    @pl.when(jnp.logical_or(slab == half - 1, slab == half))
-    def _():
-        own = jnp.where(left, 0, 1)
+    @pl.when(here)
+    def _():
         m1 = jnp.where(left, -1.0, 1.0) * factor[...]
         v1 = value[...]
-        put(own, m1, v1)
+        put(jnp.where(left, 3, 2), m1, v1)
+        m2 = -(dot3(near[...], m1) + far[...])
+        v2 = inner[...] - dot3(near[...], v1)
+        put(jnp.where(left, 0, 1), m2, v2)
 
         @pl.when(left)
         def _():
@@ -380,16 +424,11 @@
 
         @pl.when(jnp.logical_not(left))
         def _():
-            put(0, -(dot3(factor_p[...], m1) + reach[...]), value_p[...] - dot3(factor_p[...], v1))
-
-        link = jnp.where(left, couple[0].T, following((even, odd)))
-        carry = dot3(unpack_symmetric(letter[...]), link)
-        mq = -dot3(carry, m1)
-        vq = sources[...] - dot3(carry, v1)
-        put(jnp.where(left, 3, 2), mq, vq)
+            put(0, -(dot3(factor_p[...], m2) + reach[...]), value_p[...] - dot3(factor_p[...], v2))
+
         outer = unpack_full(second[0:packed, :], width)
-        put(jnp.where(left, 2, 3), -dot3(outer, mq),
-            second[packed : packed + width, :] - dot3(outer, vq))
+        put(jnp.where(left, 2, 3), -dot3(outer, m1),
+            second[packed : packed + width, :] - dot3(outer, v1))
 
 
 def join_kernel(message, total, inverse, hold):
@@ -413,15 +452,24 @@
     return dot3(inverse[...], sign * (message[...] - total[...]))
 
 
-def density_kernel(message, inverse, total, slope, offset, probes, probes_near, dens):
+def values_kernel(message, inverse, total, slope, offset, values):
     here, left = middle_slab()
 
     @pl.when(here)
     def _():
         middle = join_solution(message, inverse, total, left)
-        values = offset[...] + dot3(slope[...], middle)
+        values[...] = offset[...] + dot3(slope[...], middle)
+
+
+def density_kernel(values, probes, probes_near, dens):
+    here, _ = middle_slab()
+
+    @pl.when(here)
+    def _():
         n = probes.shape[0]
-        terms = jnp.concatenate([probes[...] * values[:n], probes_near[...] * values[n:]], axis=0)
+        terms = jnp.concatenate(
+            [probes[...] * values[0:n, :], probes_near[...] * values[n:, :]], axis=0
+        )
         dens[...] = dot6(jnp.ones((8, terms.shape[1]), F32), terms, NT)[0:1]
 
 
@@ -437,7 +485,8 @@
 
 
 def back_kernel(step, couple, even, odd, probes, message, first, middle, known_p, known_q,
-                factor_p, value_p, inverse_q, value_q, reach, out_p, out_q, dens):
+                factor_p, value_p, inverse_q, value_q, near, far, inner, reach, out_p, out_q,
+                dens):
     _, left, distance = place()
     centre = lax.axis_size("slab") // 2 - 1
     width = couple.shape[1]
@@ -447,23 +496,28 @@
         out_p[...] = known_p[...]
         out_q[...] = known_q[...]
 
-    @pl.when(distance == step)
+    @pl.when(jnp.logical_and(distance == step, step == centre - 1))
+    def _():
+        xq = message[...]
+        out_q[...] = xq
+        out_p[...] = value_p[...] - dot3(factor_p[...], xq)
+
+    @pl.when(jnp.logical_and(distance == step, step < centre - 1))
     def _():
         link = jnp.where(left, following((even, odd)).T, couple[0])
         xq = value_q[...] - dot3(inverse_q[...], dot3(link, message[...]))
         out_q[...] = xq
         out_p[...] = value_p[...] - dot3(factor_p[...], xq)
 
-    @pl.when(jnp.logical_and(distance == centre, left))
-    def _():
-        out_p[...] = first[...]
+    @pl.when(distance == centre)
+    def _():
+        xi = inner[...] - dot3(near[...], first[...]) - dot3(far[...], middle[...])
+        out_p[...] = xi
         out_q[...] = middle[...]
 
-    @pl.when(jnp.logical_and(distance == centre, jnp.logical_not(left)))
-    def _():
-        xb = first[...]
-        out_p[...] = xb
-        out_q[...] = value_p[...] - dot3(factor_p[...], xb) - dot3(reach[...], middle[...])
+        @pl.when(jnp.logical_not(left))
+        def _():
+            out_q[...] = value_p[...] - dot3(factor_p[...], xi) - dot3(reach[...], middle[...])
 
     xp = out_p[...]
     xq = out_q[...]
@@ -634,32 +688,40 @@
                 sources = jnp.where(distance == t, sources, kept[1])
             kept = message, sources
             args += [message, sources, even, odd]
+        outs = (square, column, square, square, column, letter)
+        if not paired:
+            outs += (square, column, letter)
         state = call(
-            functools.partial(stage_kernel, t),
-            (square, column, square, square, column, square, column, letter),
+            functools.partial(stage_kernel, t, not paired), outs,
             args, (sq, diag_blocks.shape, couple.shape, probes.shape), 3,
         )
         if t == 0:
             prepared = state
-        message = slab_exchange(state[-1], t % 2 == 1)
-        sources = slab_exchange(state[-2], t % 2 == 1)
-    factor_p, value_p, _, _, _, inverse_q, value_q, _ = state
+        last = t == half - 2
+        message = slab_exchange(state[5] if last else state[8], t % 2 == 1)
+        if not last:
+            sources = slab_exchange(state[7], t % 2 == 1)
+    factor_p, value_p = state[:2]
+    matrix, source, link, base, base_source, near_map, far_map, inner, reach = call(
+        ready_kernel,
+        (square, column, square, square, column, square, square, column, square),
+        [couple, even, odd, *prepared[:5]], (sq,),
+    )
+    reduced, first_factor, reach = lax.optimization_barrier((state[4], prepared[0], reach))
+    sources = slab_exchange(reduced, half % 2 == 1)
 
     depth, rows_here, across = initial_potential.shape
     halo = SWEEPS
     rows_all = rows_here * energies
     pitch = -(-(rows_here + 2 * halo) // 8) * 8
     strip = halo * pitch
-    odd_e = lax.axis_index("energy") % 2 == 1
-    low, high = initial_potential[:, :halo], initial_potential[:, rows_here - halo :]
-    got_even = energy_exchange(jnp.where(odd_e, low, high), False)
-    got_odd = energy_exchange(jnp.where(odd_e, high, low), True)
+    even_rows, odd_rows = call(rows_kernel, (like(depth, halo, across),) * 2, [initial_potential])
+    got_even = energy_exchange(even_rows, False)
+    got_odd = energy_exchange(odd_rows, True)
     cells = (depth + 2 * halo) * pitch
-    matrix, source, link, base, base_source, reach, second = call(
-        ready_kernel,
-        (square, column, square, square, column, square,
-         like(width + width // 2 + width, probe_count)),
-        [energy_index.reshape(1, 1), diag_blocks, couple, probes, *prepared[:5]],
+    second = call(
+        pack_kernel, like(width + width // 2 + width, probe_count),
+        [first_factor, prepared[1]],
     )
     if paired:
         probes_near = slab_exchange(probes, False)
@@ -670,12 +732,12 @@
     )
     solved, factor, total, sent = call(
         centre_kernel, (square, square, square, letter),
-        [couple, even, odd, message, matrix, link, base], (sq,),
+        [message, matrix, link, base], (sq,),
     )
     across_middle = slab_exchange(sent, half % 2 == 0)
     value, total_source = call(
         source_kernel, (column, column),
-        [couple, even, odd, sources, source, link, base_source, solved],
+        [sources, source, link, base_source, solved],
     )
     sources_middle = slab_exchange(total_source, half % 2 == 0)
     wide = call(
@@ -686,19 +748,19 @@
     if paired:
         slope, offset = call(
             expand_kernel, (like(4 * width, width), like(4 * width, probe_count)),
-            [couple, even, odd, message, sources, second, factor, value, prepared[0],
-             prepared[1], reach],
+            [second, factor, value, *prepared[:2], near_map, far_map, inner, reach],
         )
-        dens = call(
-            density_kernel, like(1, 4 * width),
-            [sources_middle, inverse, total_source, slope, offset, probes, probes_near],
+        values = call(
+            values_kernel, like(4 * width, probe_count),
+            [sources_middle, inverse, total_source, slope, offset],
         )
+        dens = call(density_kernel, like(1, 4 * width), [values, probes, probes_near])
     else:
         first, middle = call(
             middle_kernel, (column, column),
             [sources_middle, inverse, total_source, factor, value],
         )
-        centred = lax.axis_index("slab") == half
+        centred = (lax.axis_index("slab") == half) | (lax.axis_index("slab") == half - 1)
         factor_p = jnp.where(centred, prepared[0], factor_p)
         value_p = jnp.where(centred, prepared[1], value_p)
         known_p, known_q = first, middle
@@ -706,8 +768,10 @@
             known_p, known_q, dens = call(
                 functools.partial(back_kernel, t),
                 (column, column, like(1, 2 * width)),
-                [couple, even, odd, probes, slab_exchange(known_p, t % 2 == 1), first, middle,
-                 known_p, known_q, factor_p, value_p, inverse_q, value_q, reach],
+                [couple, even, odd, probes, slab_exchange(first if t == half - 2 else known_p, t % 2 == 1),
+                 first, middle,
+                 known_p, known_q, factor_p, value_p, state[6], state[7], near_map, far_map, inner,
+                 reach],
             )
     parts = [dens] + [
         lax.ppermute(dens, "energy", [(e, e ^ k) for e in range(energies)])

time: 42.2 us -> 53.3 us (1.26)
  waiting for transfers between devices: 13.3 us -> 20.5 us
  starting transfers between devices: 17.6 us -> 24.3 us
  Pallas kernels: 8.88 us -> 6.08 us
    ppermute x9, waiting for transfers between devices: 7.93 us -> 15.2 us  [slab_exchange(): return lax.ppermute(value, ('slab', 'energy'), whole)]
    ppermute x9, starting transfers between devices: 14 us -> 20.7 us  [slab_exchange(): return lax.ppermute(value, ('slab', 'energy'), whole)]
    pallas_call x11 -> x14, Pallas kernels: 8.88 us -> 6.08 us  [call(): pl.pallas_call(kernel, out_shape=outs, in_specs=[FAR] * distant + [VM] *...]
  transfers between devices with their start and end apart: 14 -> 14, of which waited for: 8 -> 8; matrix products, arithmetic and copies ran while one was open for 0% -> 0% of each run, Pallas kernels for 17% -> 8%
where the time goes in v9:
time: 53.3 us; the launch traced here: 53.2 us
  starting transfers between devices  24.3 us (46%)
  waiting for transfers between devices  20.5 us (38%)
  Pallas kernels  6.08 us (11%)
  between operations  1.41 us (3%)
  local copies, waits for them, and re-layouts  0.86 us (2%)
    ppermute x9, starting transfers between devices, slab_exchange(): return lax.ppermute(value, ('slab', 'energy'), whole)  20.7 us
    ppermute x9, waiting for transfers between devices, slab_exchange(): return lax.ppermute(value, ('slab', 'energy'), whole)  15.2 us
    pallas_call x14, Pallas kernels, call(): pl.pallas_call(kernel, out_shape=outs, in_specs=[FAR] * distant + [VM] *...  6.08 us
    ppermute x2, waiting for transfers between devices, energy_exchange(): return lax.ppermute(value, 'energy', pairs)  2.97 us
    ppermute x3, waiting for transfers between devices, program(): lax.ppermute(dens, 'energy', [(e, e ^ k) for e in range(energies)])  2.35 us
    ppermute x3, starting transfers between devices, program(): lax.ppermute(dens, 'energy', [(e, e ^ k) for e in range(energies)])  2.21 us
    ppermute x2, starting transfers between devices, energy_exchange(): return lax.ppermute(value, 'energy', pairs)  1.33 us
  transfers between devices with their start and end apart: 14, of which 8 were waited for; matrix products, arithmetic and copies ran while one was open for 0% of the time, Pallas kernels for 8%

profile of v9, /device:TPU:0, one launch (start us, length us, event | category | flops | bytes accessed | tf_op | source)
XLA Modules:
  0.0 53.2 jit_solution(6702480449118741623)
XLA Ops:
  0.6 3.1 %collective-permute-start.3 = (f32[2,192,192]{2,1,0:T(8,128)}, f32[2,192,192]{2,1,0:T(8,128)S(1)}, u32[]{:S(2)}, u32[]{:S(2)}) collective-permute-start(f32[2,192,192]{2,1,0:T(8,128)} %couple.1), channel_id=1, source_target_pairs={{0,4},{1,5},{2,6},{3,7},{4,0},{5,1},{6,2},{7,3},{8,12},{9,13},{10,... | collective-permute-start | bytes 884744 | tf_op jit(solution)/shard_map/ppermute | solution.py:654
  4.4 3.9 %shard_map.87 = (f32[192,192]{1,0:T(8,128)S(1)}, f32[192,128]{1,0:T(8,128)S(1)}, f32[192,192]{1,0:T(8,128)S(1)}, f32[192,192]{1,0:T(8,128)S(1)}, f32[192,128]{1,0:T(8,128)S(1)}, /*index=5*/f32[192,128]{1,0:T(8,128)S(1)}) custom-call(f32[2,192,192]{2,1,0:T(8,128)} %diag_far.1, f32[2,192,192]{2,1,0:T(8,128)} %couple.1, f32[384,128]{1,0:T(8,128)} %probes.1, ...), custom_call_target="tpu_custom_call" | custom-call | flops 100000000 | bytes 1000000 | tf_op jit(solution)/shard_map/pallas_call | solution.py:628
  8.3 4.8 %collective-permute-done.3.even.odd = f32[2,192,192]{2,1,0:T(8,128)S(1)} collective-permute-done((f32[2,192,192]{2,1,0:T(8,128)}, f32[2,192,192]{2,1,0:T(8,128)S(1)}, u32[]{:S(2)}, u32[]{:S(2)}) %collective-permute-start.3) | collective-permute-done | bytes 294944 | tf_op jit(solution)/shard_map/ppermute | solution.py:654
  13.1 0.1 shard_map.93
  13.2 2.5 %collective-permute-start.7 = (f32[480,128]{1,0:T(8,128)S(1)}, f32[480,128]{1,0:T(8,128)S(1)}, u32[]{:S(2)}, u32[]{:S(2)}) collective-permute-start(f32[480,128]{1,0:T(8,128)S(1)} %shard_map.93), channel_id=1, source_target_pairs={{0,4},{1,5},{2,6},{3,7},{4,0},{5,1},{6,2},{7,3},{8,12},{9,13},{10,... | collective-permute-start | bytes 737288 | tf_op jit(solution)/shard_map/ppermute | solution.py:654
  15.7 0.1 collective-permute-start.2
  15.7 1.9 %collective-permute-start.4 = (f32[192,128]{1,0:T(8,128)S(1)}, f32[192,128]{1,0:T(8,128)S(1)}, u32[]{:S(2)}, u32[]{:S(2)}) collective-permute-start(f32[192,128]{1,0:T(8,128)S(1)} %get-tuple-element.49.source_q), channel_id=1, source_target_pairs={{0,4},{1,5},{2,6},{3,7},{4,0},{5,1},{6,2},{7,3},{8,12},{9,13},{10,... | collective-permute-start | bytes 294920 | tf_op jit(solution)/shard_map/ppermute | solution.py:654
  17.7 0.1 collective-permute-start.8
  17.8 6.8 %collective-permute-done.2.message = f32[192,128]{1,0:T(8,128)S(1)} collective-permute-done((f32[192,128]{1,0:T(8,128)S(1)}, f32[192,128]{1,0:T(8,128)S(1)}, u32[]{:S(2)}, u32[]{:S(2)}) %collective-permute-start.2) | collective-permute-done | bytes 98336 | tf_op jit(solution)/shard_map/ppermute | solution.py:654
  24.6 0.0 collective-permute-start.6
  24.6 2.1 %collective-permute-done.4.message = f32[192,128]{1,0:T(8,128)S(1)} collective-permute-done((f32[192,128]{1,0:T(8,128)S(1)}, f32[192,128]{1,0:T(8,128)S(1)}, u32[]{:S(2)}, u32[]{:S(2)}) %collective-permute-start.4) | collective-permute-done | bytes 98336 | tf_op jit(solution)/shard_map/ppermute | solution.py:654
  26.7 0.0 collective-permute-start.5
  26.7 0.8 %copy-done.2 = f32[8,16,128]{2,1,0:T(8,128)S(1)} copy-done((f32[8,16,128]{2,1,0:T(8,128)S(1)}, f32[8,16,128]{2,1,0:T(8,128)}, u32[]{:S(2)}) %copy-start.2) | copy-done | bytes 65560
  27.5 0.0 copy-start.4
  27.5 0.1 collective-permute-start
  27.6 1.2 %collective-permute-done.got_even = f32[8,2,128]{2,1,0:T(2,128)S(1)} collective-permute-done((f32[8,2,128]{2,1,0:T(2,128)S(1)}, f32[8,2,128]{2,1,0:T(2,128)S(1)}, u32[]{:S(2)}, u32[]{:S(2)}) %collective-permute-start) | collective-permute-done | bytes 8224 | tf_op jit(solution)/shard_map/ppermute | solution.py:662
  28.8 1.3 %collective-permute-start.1 = (f32[8,2,128]{2,1,0:T(2,128)S(1)}, f32[8,2,128]{2,1,0:T(2,128)S(1)}, u32[]{:S(2)}, u32[]{:S(2)}) collective-permute-start(f32[8,2,128]{2,1,0:T(2,128)S(1)} %get-tuple-element.35), channel_id=1, source_target_pairs={{1,2},{2,1},{3,0},{0,3},{5,6},{6,5},{7,4},{4,7},{9,10},{10,9},{11,... | collective-permute-start | bytes 24584 | tf_op jit(solution)/shard_map/ppermute | solution.py:662
  30.0 1.8 %collective-permute-done.1.got_odd = f32[8,2,128]{2,1,0:T(2,128)S(1)} collective-permute-done((f32[8,2,128]{2,1,0:T(2,128)S(1)}, f32[8,2,128]{2,1,0:T(2,128)S(1)}, u32[]{:S(2)}, u32[]{:S(2)}) %collective-permute-start.1) | collective-permute-done | bytes 8224 | tf_op jit(solution)/shard_map/ppermute | solution.py:662
  31.9 0.0 collective-permute-done.6.message
  31.9 0.0 collective-permute-done.7.second
  32.0 1.6 %collective-permute-start.10 = (f32[1,768]{1,0:T(1,128)S(1)}, f32[1,768]{1,0:T(1,128)S(1)}, u32[]{:S(2)}, u32[]{:S(2)}) collective-permute-start(f32[1,768]{1,0:T(1,128)S(1)} %shard_map.96.rest_0_), channel_id=1, source_target_pairs={{0,2},{1,3},{2,0},{3,1},{4,6},{5,7},{6,4},{7,5},{8,10},{9,11},{10,... | collective-permute-start | bytes 9224 | tf_op jit(solution)/shard_map/ppermute | solution.py:777
  33.5 0.0 collective-permute-start.11
  33.5 0.6 %collective-permute-start.9 = (f32[1,768]{1,0:T(1,128)S(1)}, f32[1,768]{1,0:T(1,128)S(1)}, u32[]{:S(2)}, u32[]{:S(2)}) collective-permute-start(f32[1,768]{1,0:T(1,128)S(1)} %shard_map.96.rest_0_), channel_id=1, source_target_pairs={{0,1},{1,0},{2,3},{3,2},{4,5},{5,4},{6,7},{7,6},{8,9},{9,8},{10,11... | collective-permute-start | bytes 9224 | tf_op jit(solution)/shard_map/ppermute | solution.py:777
  34.2 1.4 %collective-permute-done.10.rest_2_ = f32[1,768]{1,0:T(1,128)S(1)} collective-permute-done((f32[1,768]{1,0:T(1,128)S(1)}, f32[1,768]{1,0:T(1,128)S(1)}, u32[]{:S(2)}, u32[]{:S(2)}) %collective-permute-start.10) | collective-permute-done | bytes 3104 | tf_op jit(solution)/shard_map/ppermute | solution.py:777
  35.6 0.9 %collective-permute-done.11.rest_3_ = f32[1,768]{1,0:T(1,128)S(1)} collective-permute-done((f32[1,768]{1,0:T(1,128)S(1)}, f32[1,768]{1,0:T(1,128)S(1)}, u32[]{:S(2)}, u32[]{:S(2)}) %collective-permute-start.11) | collective-permute-done | bytes 3104 | tf_op jit(solution)/shard_map/ppermute | solution.py:777
  36.6 0.0 copy-start.3
  36.6 13.0 %collective-permute-start.12 = (f32[64,128]{1,0:T(8,128)S(1)}, f32[64,128]{1,0:T(8,128)S(1)}, u32[]{:S(2)}, u32[]{:S(2)}) collective-permute-start(f32[64,128]{1,0:T(8,128)S(1)} %get-tuple-element.64.refs_0_), channel_id=1, source_target_pairs={{0,4},{1,5},{2,6},{3,7},{4,0},{5,1},{6,2},{7,3},{8,12},{9,13},{10,... | collective-permute-start | bytes 98312 | tf_op jit(solution)/shard_map/ppermute | solution.py:654
  49.6 0.0 collective-permute-start.13
  49.6 0.3 shard_map.98.refs_3_
  49.9 1.5 %collective-permute-done.12.refs_1_ = f32[64,128]{1,0:T(8,128)S(1)} collective-permute-done((f32[64,128]{1,0:T(8,128)S(1)}, f32[64,128]{1,0:T(8,128)S(1)}, u32[]{:S(2)}, u32[]{:S(2)}) %collective-permute-start.12) | collective-permute-done | bytes 32800 | tf_op jit(solution)/shard_map/ppermute | solution.py:654
  51.5 0.0 collective-permute-done.13.refs_2_
  51.5 1.7 %shard_map.99 = (f32[8,16,128]{2,1,0:T(8,128)}, f32[384]{0:T(512)}) custom-call(f32[64,128]{1,0:T(8,128)S(1)} %get-tuple-element.64.refs_0_, f32[64,128]{1,0:T(8,128)S(1)} %collective-permute-done.12.refs_1_, f32[64,128]{1,0:T(8,128)S(1)} %collective-permute-done.13.refs_2_, f32[288,128]{1,0:T(8,128)S(1)} %shard_map.98.refs_3_, ...), custom_call_target="tpu_custom_call" | custom-call | flops 100000000 | bytes 1000000 | tf_op jit(solution)/shard_map/pallas_call | solution.py:628
  (21 shorter events, 0.1 us)
Async XLA Ops:
  0.6 12.4 %collective-permute-start.3 = (f32[2,192,192]{2,1,0:T(8,128)}, f32[2,192,192]{2,1,0:T(8,128)S(1)}, u32[]{:S(2)}, u32[]{:S(2)}) collective-permute-start(f32[2,192,192]{2,1,0:T(8,128)} %couple.1), channel_id=1, source_target_pairs={{0,4},{1,5},{2,6},{3,7},{4,0},{5,1},{6,2},{7,3},{8,12},{9,13},{10,... | collective-permute-start | bytes 884744 | tf_op jit(solution)/shard_map/ppermute | solution.py:654
  4.4 8.7 %copy-start = (f32[2,192,192]{2,1,0:T(8,128)S(1)}, f32[2,192,192]{2,1,0:T(8,128)}, u32[]{:S(2)}) copy-start(f32[2,192,192]{2,1,0:T(8,128)} %couple.1) | copy-start | bytes 884740
  13.1 4.6 %copy-start.1 = (f32[384,128]{1,0:T(8,128)S(1)}, f32[384,128]{1,0:T(8,128)}, u32[]{:S(2)}) copy-start(f32[384,128]{1,0:T(8,128)} %probes.1) | copy-start | bytes 589828
  13.2 18.7 %collective-permute-start.7 = (f32[480,128]{1,0:T(8,128)S(1)}, f32[480,128]{1,0:T(8,128)S(1)}, u32[]{:S(2)}, u32[]{:S(2)}) collective-permute-start(f32[480,128]{1,0:T(8,128)S(1)} %shard_map.93), channel_id=1, source_target_pairs={{0,4},{1,5},{2,6},{3,7},{4,0},{5,1},{6,2},{7,3},{8,12},{9,13},{10,... | collective-permute-start | bytes 737288 | tf_op jit(solution)/shard_map/ppermute | solution.py:654
  15.7 8.9 %collective-permute-start.2 = (f32[192,128]{1,0:T(8,128)S(1)}, f32[192,128]{1,0:T(8,128)S(1)}, u32[]{:S(2)}, u32[]{:S(2)}) collective-permute-start(f32[192,128]{1,0:T(8,128)S(1)} %get-tuple-element.36), channel_id=1, source_target_pairs={{0,4},{1,5},{2,6},{3,7},{4,0},{5,1},{6,2},{7,3},{8,12},{9,13},{10,... | collective-permute-start | bytes 294920 | tf_op jit(solution)/shard_map/ppermute | solution.py:654
  15.7 10.9 %collective-permute-start.4 = (f32[192,128]{1,0:T(8,128)S(1)}, f32[192,128]{1,0:T(8,128)S(1)}, u32[]{:S(2)}, u32[]{:S(2)}) collective-permute-start(f32[192,128]{1,0:T(8,128)S(1)} %get-tuple-element.49.source_q), channel_id=1, source_target_pairs={{0,4},{1,5},{2,6},{3,7},{4,0},{5,1},{6,2},{7,3},{8,12},{9,13},{10,... | collective-permute-start | bytes 294920 | tf_op jit(solution)/shard_map/ppermute | solution.py:654
  17.7 14.2 %collective-permute-start.8 = (f32[384,128]{1,0:T(8,128)S(1)}, f32[384,128]{1,0:T(8,128)S(1)}, u32[]{:S(2)}, u32[]{:S(2)}) collective-permute-start(f32[384,128]{1,0:T(8,128)S(1)} %copy-done.1), channel_id=1, source_target_pairs={{0,4},{1,5},{2,6},{3,7},{4,0},{5,1},{6,2},{7,3},{8,12},{9,13},{10,... | collective-permute-start | bytes 589832 | tf_op jit(solution)/shard_map/ppermute | solution.py:654
  24.6 7.3 %collective-permute-start.6 = (f32[192,128]{1,0:T(8,128)S(1)}, f32[192,128]{1,0:T(8,128)S(1)}, u32[]{:S(2)}, u32[]{:S(2)}) collective-permute-start(f32[192,128]{1,0:T(8,128)S(1)} %get-tuple-element.45), channel_id=1, source_target_pairs={{4,8},{5,9},{6,10},{7,11},{8,4},{9,5},{10,6},{11,7},{0,1},{1,0},{2... | collective-permute-start | bytes 294920 | tf_op jit(solution)/shard_map/ppermute | solution.py:654
  26.7 0.8 %copy-start.2 = (f32[8,16,128]{2,1,0:T(8,128)S(1)}, f32[8,16,128]{2,1,0:T(8,128)}, u32[]{:S(2)}) copy-start(f32[8,16,128]{2,1,0:T(8,128)} %potential.3) | copy-start | bytes 196612
  26.7 5.2 %collective-permute-start.5 = (f32[192,128]{1,0:T(8,128)S(1)}, f32[192,128]{1,0:T(8,128)S(1)}, u32[]{:S(2)}, u32[]{:S(2)}) collective-permute-start(f32[192,128]{1,0:T(8,128)S(1)} %get-tuple-element.53.total), channel_id=1, source_target_pairs={{4,8},{5,9},{6,10},{7,11},{8,4},{9,5},{10,6},{11,7},{0,1},{1,0},{2... | collective-permute-start | bytes 294920 | tf_op jit(solution)/shard_map/ppermute | solution.py:654
  27.5 2.5 %copy-start.4 = (s32[384]{0:T(512)S(1)}, s32[384]{0:T(512)}, u32[]{:S(2)}) copy-start(s32[384]{0:T(512)} %param.11) | copy-start | bytes 4612
  27.5 1.2 %collective-permute-start = (f32[8,2,128]{2,1,0:T(2,128)S(1)}, f32[8,2,128]{2,1,0:T(2,128)S(1)}, u32[]{:S(2)}, u32[]{:S(2)}) collective-permute-start(f32[8,2,128]{2,1,0:T(2,128)S(1)} %get-tuple-element.34), channel_id=1, source_target_pairs={{0,1},{1,0},{2,3},{3,2},{4,5},{5,4},{6,7},{7,6},{8,9},{9,8},{10,11... | collective-permute-start | bytes 24584 | tf_op jit(solution)/shard_map/ppermute | solution.py:662
  28.8 3.1 %collective-permute-start.1 = (f32[8,2,128]{2,1,0:T(2,128)S(1)}, f32[8,2,128]{2,1,0:T(2,128)S(1)}, u32[]{:S(2)}, u32[]{:S(2)}) collective-permute-start(f32[8,2,128]{2,1,0:T(2,128)S(1)} %get-tuple-element.35), channel_id=1, source_target_pairs={{1,2},{2,1},{3,0},{0,3},{5,6},{6,5},{7,4},{4,7},{9,10},{10,9},{11,... | collective-permute-start | bytes 24584 | tf_op jit(solution)/shard_map/ppermute | solution.py:662
  32.0 3.7 %collective-permute-start.10 = (f32[1,768]{1,0:T(1,128)S(1)}, f32[1,768]{1,0:T(1,128)S(1)}, u32[]{:S(2)}, u32[]{:S(2)}) collective-permute-start(f32[1,768]{1,0:T(1,128)S(1)} %shard_map.96.rest_0_), channel_id=1, source_target_pairs={{0,2},{1,3},{2,0},{3,1},{4,6},{5,7},{6,4},{7,5},{8,10},{9,11},{10,... | collective-permute-start | bytes 9224 | tf_op jit(solution)/shard_map/ppermute | solution.py:777
  33.5 3.0 %collective-permute-start.11 = (f32[1,768]{1,0:T(1,128)S(1)}, f32[1,768]{1,0:T(1,128)S(1)}, u32[]{:S(2)}, u32[]{:S(2)}) collective-permute-start(f32[1,768]{1,0:T(1,128)S(1)} %shard_map.96.rest_0_), channel_id=1, source_target_pairs={{0,3},{1,2},{2,1},{3,0},{4,7},{5,6},{6,5},{7,4},{8,11},{9,10},{10,... | collective-permute-start | bytes 9224 | tf_op jit(solution)/shard_map/ppermute | solution.py:777
  33.5 3.0 %collective-permute-start.9 = (f32[1,768]{1,0:T(1,128)S(1)}, f32[1,768]{1,0:T(1,128)S(1)}, u32[]{:S(2)}, u32[]{:S(2)}) collective-permute-start(f32[1,768]{1,0:T(1,128)S(1)} %shard_map.96.rest_0_), channel_id=1, source_target_pairs={{0,1},{1,0},{2,3},{3,2},{4,5},{5,4},{6,7},{7,6},{8,9},{9,8},{10,11... | collective-permute-start | bytes 9224 | tf_op jit(solution)/shard_map/ppermute | solution.py:777
  36.6 13.0 %copy-start.3 = (s32[1024]{0:T(1024)S(1)}, s32[1024]{0:T(1024)}, u32[]{:S(2)}) copy-start(s32[1024]{0:T(1024)} %param.12) | copy-start | bytes 12292
  36.6 14.9 %collective-permute-start.12 = (f32[64,128]{1,0:T(8,128)S(1)}, f32[64,128]{1,0:T(8,128)S(1)}, u32[]{:S(2)}, u32[]{:S(2)}) collective-permute-start(f32[64,128]{1,0:T(8,128)S(1)} %get-tuple-element.64.refs_0_), channel_id=1, source_target_pairs={{0,4},{1,5},{2,6},{3,7},{4,0},{5,1},{6,2},{7,3},{8,12},{9,13},{10,... | collective-permute-start | bytes 98312 | tf_op jit(solution)/shard_map/ppermute | solution.py:654
  49.6 1.9 %collective-permute-start.13 = (f32[64,128]{1,0:T(8,128)S(1)}, f32[64,128]{1,0:T(8,128)S(1)}, u32[]{:S(2)}, u32[]{:S(2)}) collective-permute-start(f32[64,128]{1,0:T(8,128)S(1)} %get-tuple-element.65), channel_id=1, source_target_pairs={{4,8},{5,9},{6,10},{7,11},{8,4},{9,5},{10,6},{11,7},{0,1},{1,0},{2... | collective-permute-start | bytes 98312 | tf_op jit(solution)/shard_map/ppermute | solution.py:654

commit v10 on v9

--- a/solution.py
+++ b/solution.py
@@ -145,7 +145,7 @@
 
 def following(ahead):
     even, odd = ahead
-    return jnp.where(lax.axis_index("slab") % 2 == 0, even[0], odd[0])
+    return jnp.where(lax.axis_index("slab") % 2 == 0, even[...], odd[...])
 
 
 def take_block(message, couple, ahead, left):
@@ -672,11 +672,11 @@
     letter = like(width, probe_count)
     sq = (width, width)
 
-    even = slab_exchange(couple, False)
+    even = slab_exchange(couple[0], False)
     paired = half == 2
     odd = even
     if not paired:
-        odd = lax.ppermute(couple, "slab", [(s + 1, s) for s in range(1, slabs - 1, 2)])
+        odd = lax.ppermute(couple[0], "slab", [(s + 1, s) for s in range(1, slabs - 1, 2)])
 
     message = None
     for t in range(half - 1):

time: 53.3 us -> 49.9 us (0.936)
  waiting for transfers between devices: 20.5 us -> 16.1 us
  local copies, waits for them, and re-layouts: 0.86 us -> 1.8 us
    ppermute x9, waiting for transfers between devices: 15.2 us -> 10.8 us  [slab_exchange(): return lax.ppermute(value, ('slab', 'energy'), whole)]
    squeeze x0 -> x1, local copies, waits for them, and re-layouts: none -> 0.94 us  [program(): even = slab_exchange(couple[0], False)]
  transfers between devices with their start and end apart: 14 -> 14, of which waited for: 8 -> 8; matrix products, arithmetic and copies ran while one was open for 0% -> 0% of each run, Pallas kernels for 8% -> 9%
where the time goes in v10:
time: 49.9 us; the launch traced here: 49.7 us
  starting transfers between devices  24.3 us (49%)
  waiting for transfers between devices  16.1 us (32%)
  Pallas kernels  6.08 us (12%)
  local copies, waits for them, and re-layouts  1.8 us (4%)
  between operations  1.41 us (3%)
    ppermute x9, starting transfers between devices, slab_exchange(): return lax.ppermute(value, ('slab', 'energy'), whole)  20.7 us
    ppermute x9, waiting for transfers between devices, slab_exchange(): return lax.ppermute(value, ('slab', 'energy'), whole)  10.8 us
    pallas_call x14, Pallas kernels, call(): pl.pallas_call(kernel, out_shape=outs, in_specs=[FAR] * distant + [VM] *...  6.08 us
    ppermute x2, waiting for transfers between devices, energy_exchange(): return lax.ppermute(value, 'energy', pairs)  2.97 us
    ppermute x3, waiting for transfers between devices, program(): lax.ppermute(dens, 'energy', [(e, e ^ k) for e in range(energies)])  2.35 us
    ppermute x3, starting transfers between devices, program(): lax.ppermute(dens, 'energy', [(e, e ^ k) for e in range(energies)])  2.21 us
    ppermute x2, starting transfers between devices, energy_exchange(): return lax.ppermute(value, 'energy', pairs)  1.33 us
  transfers between devices with their start and end apart: 14, of which 8 were waited for; matrix products, arithmetic and copies ran while one was open for 0% of the time, Pallas kernels for 9%

profile of v10, /device:TPU:0, one launch (start us, length us, event | category | flops | bytes accessed | tf_op | source)
XLA Modules:
  0.0 49.7 jit_solution(5757918628883180377)
XLA Ops:
  0.6 0.9 %slice_bitcast_fusion = f32[192,192]{1,0:T(8,128)S(1)} fusion(f32[2,192,192]{2,1,0:T(8,128)} %couple.1), kind=kLoop, calls=%fused_computation | loop fusion | bytes 294912 | tf_op jit(solution)/shard_map/squeeze | solution.py:675
  1.6 3.1 %collective-permute-start.3 = (f32[192,192]{1,0:T(8,128)S(1)}, f32[192,192]{1,0:T(8,128)S(1)}, u32[]{:S(2)}, u32[]{:S(2)}) collective-permute-start(f32[192,192]{1,0:T(8,128)S(1)} %slice_bitcast_fusion), channel_id=1, source_target_pairs={{0,4},{1,5},{2,6},{3,7},{4,0},{5,1},{6,2},{7,3},{8,12},{9,13},{10,... | collective-permute-start | bytes 442376 | tf_op jit(solution)/shard_map/ppermute | solution.py:654
  5.3 0.0 copy-start
  5.4 3.9 %shard_map.87 = (f32[192,192]{1,0:T(8,128)S(1)}, f32[192,128]{1,0:T(8,128)S(1)}, f32[192,192]{1,0:T(8,128)S(1)}, f32[192,192]{1,0:T(8,128)S(1)}, f32[192,128]{1,0:T(8,128)S(1)}, /*index=5*/f32[192,128]{1,0:T(8,128)S(1)}) custom-call(f32[2,192,192]{2,1,0:T(8,128)} %diag_far.1, f32[2,192,192]{2,1,0:T(8,128)} %couple.1, f32[384,128]{1,0:T(8,128)} %probes.1, ...), custom_call_target="tpu_custom_call" | custom-call | flops 100000000 | bytes 1000000 | tf_op jit(solution)/shard_map/pallas_call | solution.py:628
  9.3 0.3 collective-permute-done.3.even.odd
  9.6 0.1 shard_map.93
  9.7 2.5 %collective-permute-start.7 = (f32[480,128]{1,0:T(8,128)S(1)}, f32[480,128]{1,0:T(8,128)S(1)}, u32[]{:S(2)}, u32[]{:S(2)}) collective-permute-start(f32[480,128]{1,0:T(8,128)S(1)} %shard_map.93), channel_id=1, source_target_pairs={{0,4},{1,5},{2,6},{3,7},{4,0},{5,1},{6,2},{7,3},{8,12},{9,13},{10,... | collective-permute-start | bytes 737288 | tf_op jit(solution)/shard_map/ppermute | solution.py:654
  12.2 0.1 collective-permute-start.2
  12.3 1.9 %collective-permute-start.4 = (f32[192,128]{1,0:T(8,128)S(1)}, f32[192,128]{1,0:T(8,128)S(1)}, u32[]{:S(2)}, u32[]{:S(2)}) collective-permute-start(f32[192,128]{1,0:T(8,128)S(1)} %get-tuple-element.49.source_q), channel_id=1, source_target_pairs={{0,4},{1,5},{2,6},{3,7},{4,0},{5,1},{6,2},{7,3},{8,12},{9,13},{10,... | collective-permute-start | bytes 294920 | tf_op jit(solution)/shard_map/ppermute | solution.py:654
  14.2 0.1 collective-permute-start.8
  14.3 6.8 %collective-permute-done.2.message = f32[192,128]{1,0:T(8,128)S(1)} collective-permute-done((f32[192,128]{1,0:T(8,128)S(1)}, f32[192,128]{1,0:T(8,128)S(1)}, u32[]{:S(2)}, u32[]{:S(2)}) %collective-permute-start.2) | collective-permute-done | bytes 98336 | tf_op jit(solution)/shard_map/ppermute | solution.py:654
  21.1 2.1 %collective-permute-done.4.message = f32[192,128]{1,0:T(8,128)S(1)} collective-permute-done((f32[192,128]{1,0:T(8,128)S(1)}, f32[192,128]{1,0:T(8,128)S(1)}, u32[]{:S(2)}, u32[]{:S(2)}) %collective-permute-start.4) | collective-permute-done | bytes 98336 | tf_op jit(solution)/shard_map/ppermute | solution.py:654
  23.2 0.0 collective-permute-start.5
  23.2 0.8 %copy-done.2 = f32[8,16,128]{2,1,0:T(8,128)S(1)} copy-done((f32[8,16,128]{2,1,0:T(8,128)S(1)}, f32[8,16,128]{2,1,0:T(8,128)}, u32[]{:S(2)}) %copy-start.2) | copy-done | bytes 65560
  24.0 0.0 copy-start.4
  24.1 0.1 collective-permute-start
  24.1 1.2 %collective-permute-done.got_even = f32[8,2,128]{2,1,0:T(2,128)S(1)} collective-permute-done((f32[8,2,128]{2,1,0:T(2,128)S(1)}, f32[8,2,128]{2,1,0:T(2,128)S(1)}, u32[]{:S(2)}, u32[]{:S(2)}) %collective-permute-start) | collective-permute-done | bytes 8224 | tf_op jit(solution)/shard_map/ppermute | solution.py:662
  25.3 1.3 %collective-permute-start.1 = (f32[8,2,128]{2,1,0:T(2,128)S(1)}, f32[8,2,128]{2,1,0:T(2,128)S(1)}, u32[]{:S(2)}, u32[]{:S(2)}) collective-permute-start(f32[8,2,128]{2,1,0:T(2,128)S(1)} %get-tuple-element.35), channel_id=1, source_target_pairs={{1,2},{2,1},{3,0},{0,3},{5,6},{6,5},{7,4},{4,7},{9,10},{10,9},{11,... | collective-permute-start | bytes 24584 | tf_op jit(solution)/shard_map/ppermute | solution.py:662
  26.6 1.8 %collective-permute-done.1.got_odd = f32[8,2,128]{2,1,0:T(2,128)S(1)} collective-permute-done((f32[8,2,128]{2,1,0:T(2,128)S(1)}, f32[8,2,128]{2,1,0:T(2,128)S(1)}, u32[]{:S(2)}, u32[]{:S(2)}) %collective-permute-start.1) | collective-permute-done | bytes 8224 | tf_op jit(solution)/shard_map/ppermute | solution.py:662
  28.4 0.0 collective-permute-done.5.message
  28.4 0.0 collective-permute-done.8.probes_near
  28.5 1.6 %collective-permute-start.10 = (f32[1,768]{1,0:T(1,128)S(1)}, f32[1,768]{1,0:T(1,128)S(1)}, u32[]{:S(2)}, u32[]{:S(2)}) collective-permute-start(f32[1,768]{1,0:T(1,128)S(1)} %shard_map.96.rest_0_), channel_id=1, source_target_pairs={{0,2},{1,3},{2,0},{3,1},{4,6},{5,7},{6,4},{7,5},{8,10},{9,11},{10,... | collective-permute-start | bytes 9224 | tf_op jit(solution)/shard_map/ppermute | solution.py:777
  30.0 0.0 collective-permute-start.11
  30.1 0.6 %collective-permute-start.9 = (f32[1,768]{1,0:T(1,128)S(1)}, f32[1,768]{1,0:T(1,128)S(1)}, u32[]{:S(2)}, u32[]{:S(2)}) collective-permute-start(f32[1,768]{1,0:T(1,128)S(1)} %shard_map.96.rest_0_), channel_id=1, source_target_pairs={{0,1},{1,0},{2,3},{3,2},{4,5},{5,4},{6,7},{7,6},{8,9},{9,8},{10,11... | collective-permute-start | bytes 9224 | tf_op jit(solution)/shard_map/ppermute | solution.py:777
  30.7 1.4 %collective-permute-done.10.rest_2_ = f32[1,768]{1,0:T(1,128)S(1)} collective-permute-done((f32[1,768]{1,0:T(1,128)S(1)}, f32[1,768]{1,0:T(1,128)S(1)}, u32[]{:S(2)}, u32[]{:S(2)}) %collective-permute-start.10) | collective-permute-done | bytes 3104 | tf_op jit(solution)/shard_map/ppermute | solution.py:777
  32.1 0.9 %collective-permute-done.11.rest_3_ = f32[1,768]{1,0:T(1,128)S(1)} collective-permute-done((f32[1,768]{1,0:T(1,128)S(1)}, f32[1,768]{1,0:T(1,128)S(1)}, u32[]{:S(2)}, u32[]{:S(2)}) %collective-permute-start.11) | collective-permute-done | bytes 3104 | tf_op jit(solution)/shard_map/ppermute | solution.py:777
  33.1 0.0 collective-permute-done.9.rest_1_
  33.1 0.0 copy-start.3
  33.1 13.0 %collective-permute-start.12 = (f32[64,128]{1,0:T(8,128)S(1)}, f32[64,128]{1,0:T(8,128)S(1)}, u32[]{:S(2)}, u32[]{:S(2)}) collective-permute-start(f32[64,128]{1,0:T(8,128)S(1)} %get-tuple-element.64.refs_0_), channel_id=1, source_target_pairs={{0,4},{1,5},{2,6},{3,7},{4,0},{5,1},{6,2},{7,3},{8,12},{9,13},{10,... | collective-permute-start | bytes 98312 | tf_op jit(solution)/shard_map/ppermute | solution.py:654
  46.1 0.3 shard_map.98.refs_3_
  46.4 1.5 %collective-permute-done.12.refs_1_ = f32[64,128]{1,0:T(8,128)S(1)} collective-permute-done((f32[64,128]{1,0:T(8,128)S(1)}, f32[64,128]{1,0:T(8,128)S(1)}, u32[]{:S(2)}, u32[]{:S(2)}) %collective-permute-start.12) | collective-permute-done | bytes 32800 | tf_op jit(solution)/shard_map/ppermute | solution.py:654
  48.0 1.7 %shard_map.99 = (f32[8,16,128]{2,1,0:T(8,128)}, f32[384]{0:T(512)}) custom-call(f32[64,128]{1,0:T(8,128)S(1)} %get-tuple-element.64.refs_0_, f32[64,128]{1,0:T(8,128)S(1)} %collective-permute-done.12.refs_1_, f32[64,128]{1,0:T(8,128)S(1)} %collective-permute-done.13.refs_2_, f32[288,128]{1,0:T(8,128)S(1)} %shard_map.98.refs_3_, ...), custom_call_target="tpu_custom_call" | custom-call | flops 100000000 | bytes 1000000 | tf_op jit(solution)/shard_map/pallas_call | solution.py:628
  (22 shorter events, 0.1 us)
Async XLA Ops:
  1.6 8.0 %collective-permute-start.3 = (f32[192,192]{1,0:T(8,128)S(1)}, f32[192,192]{1,0:T(8,128)S(1)}, u32[]{:S(2)}, u32[]{:S(2)}) collective-permute-start(f32[192,192]{1,0:T(8,128)S(1)} %slice_bitcast_fusion), channel_id=1, source_target_pairs={{0,4},{1,5},{2,6},{3,7},{4,0},{5,1},{6,2},{7,3},{8,12},{9,13},{10,... | collective-permute-start | bytes 442376 | tf_op jit(solution)/shard_map/ppermute | solution.py:654
  5.3 4.3 %copy-start = (f32[2,192,192]{2,1,0:T(8,128)S(1)}, f32[2,192,192]{2,1,0:T(8,128)}, u32[]{:S(2)}) copy-start(f32[2,192,192]{2,1,0:T(8,128)} %couple.1) | copy-start | bytes 884740
  9.6 4.6 %copy-start.1 = (f32[384,128]{1,0:T(8,128)S(1)}, f32[384,128]{1,0:T(8,128)}, u32[]{:S(2)}) copy-start(f32[384,128]{1,0:T(8,128)} %probes.1) | copy-start | bytes 589828
  9.7 18.7 %collective-permute-start.7 = (f32[480,128]{1,0:T(8,128)S(1)}, f32[480,128]{1,0:T(8,128)S(1)}, u32[]{:S(2)}, u32[]{:S(2)}) collective-permute-start(f32[480,128]{1,0:T(8,128)S(1)} %shard_map.93), channel_id=1, source_target_pairs={{0,4},{1,5},{2,6},{3,7},{4,0},{5,1},{6,2},{7,3},{8,12},{9,13},{10,... | collective-permute-start | bytes 737288 | tf_op jit(solution)/shard_map/ppermute | solution.py:654
  12.2 8.9 %collective-permute-start.2 = (f32[192,128]{1,0:T(8,128)S(1)}, f32[192,128]{1,0:T(8,128)S(1)}, u32[]{:S(2)}, u32[]{:S(2)}) collective-permute-start(f32[192,128]{1,0:T(8,128)S(1)} %get-tuple-element.36), channel_id=1, source_target_pairs={{0,4},{1,5},{2,6},{3,7},{4,0},{5,1},{6,2},{7,3},{8,12},{9,13},{10,... | collective-permute-start | bytes 294920 | tf_op jit(solution)/shard_map/ppermute | solution.py:654
  12.3 10.9 %collective-permute-start.4 = (f32[192,128]{1,0:T(8,128)S(1)}, f32[192,128]{1,0:T(8,128)S(1)}, u32[]{:S(2)}, u32[]{:S(2)}) collective-permute-start(f32[192,128]{1,0:T(8,128)S(1)} %get-tuple-element.49.source_q), channel_id=1, source_target_pairs={{0,4},{1,5},{2,6},{3,7},{4,0},{5,1},{6,2},{7,3},{8,12},{9,13},{10,... | collective-permute-start | bytes 294920 | tf_op jit(solution)/shard_map/ppermute | solution.py:654
  14.2 14.2 %collective-permute-start.8 = (f32[384,128]{1,0:T(8,128)S(1)}, f32[384,128]{1,0:T(8,128)S(1)}, u32[]{:S(2)}, u32[]{:S(2)}) collective-permute-start(f32[384,128]{1,0:T(8,128)S(1)} %copy-done.1), channel_id=1, source_target_pairs={{0,4},{1,5},{2,6},{3,7},{4,0},{5,1},{6,2},{7,3},{8,12},{9,13},{10,... | collective-permute-start | bytes 589832 | tf_op jit(solution)/shard_map/ppermute | solution.py:654
  21.1 7.3 %collective-permute-start.6 = (f32[192,128]{1,0:T(8,128)S(1)}, f32[192,128]{1,0:T(8,128)S(1)}, u32[]{:S(2)}, u32[]{:S(2)}) collective-permute-start(f32[192,128]{1,0:T(8,128)S(1)} %get-tuple-element.45), channel_id=1, source_target_pairs={{4,8},{5,9},{6,10},{7,11},{8,4},{9,5},{10,6},{11,7},{0,1},{1,0},{2... | collective-permute-start | bytes 294920 | tf_op jit(solution)/shard_map/ppermute | solution.py:654
  23.2 0.8 %copy-start.2 = (f32[8,16,128]{2,1,0:T(8,128)S(1)}, f32[8,16,128]{2,1,0:T(8,128)}, u32[]{:S(2)}) copy-start(f32[8,16,128]{2,1,0:T(8,128)} %potential.3) | copy-start | bytes 196612
  23.2 5.2 %collective-permute-start.5 = (f32[192,128]{1,0:T(8,128)S(1)}, f32[192,128]{1,0:T(8,128)S(1)}, u32[]{:S(2)}, u32[]{:S(2)}) collective-permute-start(f32[192,128]{1,0:T(8,128)S(1)} %get-tuple-element.53.total), channel_id=1, source_target_pairs={{4,8},{5,9},{6,10},{7,11},{8,4},{9,5},{10,6},{11,7},{0,1},{1,0},{2... | collective-permute-start | bytes 294920 | tf_op jit(solution)/shard_map/ppermute | solution.py:654
  24.0 2.5 %copy-start.4 = (s32[384]{0:T(512)S(1)}, s32[384]{0:T(512)}, u32[]{:S(2)}) copy-start(s32[384]{0:T(512)} %param.11) | copy-start | bytes 4612
  24.1 1.2 %collective-permute-start = (f32[8,2,128]{2,1,0:T(2,128)S(1)}, f32[8,2,128]{2,1,0:T(2,128)S(1)}, u32[]{:S(2)}, u32[]{:S(2)}) collective-permute-start(f32[8,2,128]{2,1,0:T(2,128)S(1)} %get-tuple-element.34), channel_id=1, source_target_pairs={{0,1},{1,0},{2,3},{3,2},{4,5},{5,4},{6,7},{7,6},{8,9},{9,8},{10,11... | collective-permute-start | bytes 24584 | tf_op jit(solution)/shard_map/ppermute | solution.py:662
  25.3 3.1 %collective-permute-start.1 = (f32[8,2,128]{2,1,0:T(2,128)S(1)}, f32[8,2,128]{2,1,0:T(2,128)S(1)}, u32[]{:S(2)}, u32[]{:S(2)}) collective-permute-start(f32[8,2,128]{2,1,0:T(2,128)S(1)} %get-tuple-element.35), channel_id=1, source_target_pairs={{1,2},{2,1},{3,0},{0,3},{5,6},{6,5},{7,4},{4,7},{9,10},{10,9},{11,... | collective-permute-start | bytes 24584 | tf_op jit(solution)/shard_map/ppermute | solution.py:662
  28.5 3.7 %collective-permute-start.10 = (f32[1,768]{1,0:T(1,128)S(1)}, f32[1,768]{1,0:T(1,128)S(1)}, u32[]{:S(2)}, u32[]{:S(2)}) collective-permute-start(f32[1,768]{1,0:T(1,128)S(1)} %shard_map.96.rest_0_), channel_id=1, source_target_pairs={{0,2},{1,3},{2,0},{3,1},{4,6},{5,7},{6,4},{7,5},{8,10},{9,11},{10,... | collective-permute-start | bytes 9224 | tf_op jit(solution)/shard_map/ppermute | solution.py:777
  30.0 3.0 %collective-permute-start.11 = (f32[1,768]{1,0:T(1,128)S(1)}, f32[1,768]{1,0:T(1,128)S(1)}, u32[]{:S(2)}, u32[]{:S(2)}) collective-permute-start(f32[1,768]{1,0:T(1,128)S(1)} %shard_map.96.rest_0_), channel_id=1, source_target_pairs={{0,3},{1,2},{2,1},{3,0},{4,7},{5,6},{6,5},{7,4},{8,11},{9,10},{10,... | collective-permute-start | bytes 9224 | tf_op jit(solution)/shard_map/ppermute | solution.py:777
  30.1 3.0 %collective-permute-start.9 = (f32[1,768]{1,0:T(1,128)S(1)}, f32[1,768]{1,0:T(1,128)S(1)}, u32[]{:S(2)}, u32[]{:S(2)}) collective-permute-start(f32[1,768]{1,0:T(1,128)S(1)} %shard_map.96.rest_0_), channel_id=1, source_target_pairs={{0,1},{1,0},{2,3},{3,2},{4,5},{5,4},{6,7},{7,6},{8,9},{9,8},{10,11... | collective-permute-start | bytes 9224 | tf_op jit(solution)/shard_map/ppermute | solution.py:777
  33.1 13.0 %copy-start.3 = (s32[1024]{0:T(1024)S(1)}, s32[1024]{0:T(1024)}, u32[]{:S(2)}) copy-start(s32[1024]{0:T(1024)} %param.12) | copy-start | bytes 12292
  33.1 14.9 %collective-permute-start.12 = (f32[64,128]{1,0:T(8,128)S(1)}, f32[64,128]{1,0:T(8,128)S(1)}, u32[]{:S(2)}, u32[]{:S(2)}) collective-permute-start(f32[64,128]{1,0:T(8,128)S(1)} %get-tuple-element.64.refs_0_), channel_id=1, source_target_pairs={{0,4},{1,5},{2,6},{3,7},{4,0},{5,1},{6,2},{7,3},{8,12},{9,13},{10,... | collective-permute-start | bytes 98312 | tf_op jit(solution)/shard_map/ppermute | solution.py:654
  46.1 1.9 %collective-permute-start.13 = (f32[64,128]{1,0:T(8,128)S(1)}, f32[64,128]{1,0:T(8,128)S(1)}, u32[]{:S(2)}, u32[]{:S(2)}) collective-permute-start(f32[64,128]{1,0:T(8,128)S(1)} %get-tuple-element.65), channel_id=1, source_target_pairs={{4,8},{5,9},{6,10},{7,11},{8,4},{9,5},{10,6},{11,7},{0,1},{1,0},{2... | collective-permute-start | bytes 98312 | tf_op jit(solution)/shard_map/ppermute | solution.py:654

commit v11 on v10

--- a/solution.py
+++ b/solution.py
@@ -265,7 +265,7 @@
     return first_z, lax.axis_index("energy") * rows_here - SWEEPS
 
 
-def pack_kernel(factor_p, value_p, out):
+def pack_kernel(factor_p, value_p, probes, out):
     _, _, distance = place()
     width = value_p.shape[0]
     packed = width + width // 2
@@ -274,6 +274,7 @@
     def _():
         pack_full(factor_p[...], out)
         out[packed : packed + width, :] = value_p[...]
+        out[packed + width :, :] = probes[...]
 
 
 def ready_kernel(couple, even, odd, factor_p, value_p, inverse_p, matrix_q, source_q, matrix,
@@ -324,12 +325,27 @@
         guarded(run)
 
 
-def rows_kernel(potential, even_out, odd_out):
-    halo = even_out.shape[1]
-    low, high = potential[:, :halo], potential[:, potential.shape[1] - halo :]
+ROWS_AT = 8
+
+
+def put_message(out, total, potential, high):
+    depth, rows_here, lanes = potential.shape
+    for k in range(total.shape[1] // lanes):
+        out[k : k + 1, :] = total[:, k * lanes : (k + 1) * lanes]
+    for k in range(depth):
+        at = ROWS_AT + k * SWEEPS
+        low, top = potential[k, 0:SWEEPS, :], potential[k, rows_here - SWEEPS :, :]
+        out[at : at + SWEEPS, :] = jnp.where(high, top, low)
+
+
+def put_messages(total, potential, even_out, odd_out):
     odd = lax.axis_index("energy") % 2 == 1
-    even_out[...] = jnp.where(odd, low, high)
-    odd_out[...] = jnp.where(odd, high, low)
+    put_message(even_out, total, potential, jnp.logical_not(odd))
+    put_message(odd_out, total, potential, odd)
+
+
+def message_kernel(dens, potential, even_out, odd_out):
+    put_messages(dens[...], potential, even_out, odd_out)
 
 
 def deposit_kernel(rows_all, pitch, depth, rows_here, dopants, dopant):
@@ -339,16 +355,17 @@
     dopant[...] = dopant_charge * one_pass(rows, ys.astype(BF16), NT)
 
 
-def halo_kernel(potential, got_even, got_odd, wide):
+def put_wide(potential, got_even, got_odd, wide):
     depth, rows_here, across = potential.shape
-    even_e = lax.axis_index("energy") % 2 == 0
-    below = jnp.where(even_e, got_odd[...], got_even[...])
-    above = jnp.where(even_e, got_even[...], got_odd[...])
+    even = lax.axis_index("energy") % 2 == 0
     spare = wide.shape[1] - rows_here - 2 * SWEEPS
-    parts = [below, potential[...], above]
-    if spare > 0:
-        parts.append(jnp.zeros((depth, spare, across), F32))
-    wide[...] = jnp.concatenate(parts, axis=1)
+    for k in range(depth):
+        at = ROWS_AT + k * SWEEPS
+        one, two = got_even[at : at + SWEEPS, :], got_odd[at : at + SWEEPS, :]
+        parts = [jnp.where(even, two, one), potential[k], jnp.where(even, one, two)]
+        if spare > 0:
+            parts.append(jnp.zeros((spare, across), F32))
+        wide[k] = jnp.concatenate(parts, axis=0)
 
 
 def put_planes(out, start, wide, high):
@@ -461,16 +478,17 @@
         values[...] = offset[...] + dot3(slope[...], middle)
 
 
-def density_kernel(values, probes, probes_near, dens):
+def density_kernel(values, probes, second, potential, even_out, odd_out, dens):
     here, _ = middle_slab()
 
     @pl.when(here)
     def _():
         n = probes.shape[0]
-        terms = jnp.concatenate(
-            [probes[...] * values[0:n, :], probes_near[...] * values[n:, :]], axis=0
-        )
-        dens[...] = dot6(jnp.ones((8, terms.shape[1]), F32), terms, NT)[0:1]
+        outer = second[second.shape[0] - n :, :]
+        terms = jnp.concatenate([probes[...] * values[0:n, :], outer * values[n:, :]], axis=0)
+        dens[...] = dot6(jnp.ones((8, terms.shape[1]), F32), terms, NT)
+
+    put_messages(dens[0:1, :], potential, even_out, odd_out)
 
 
 def middle_kernel(message, inverse, total, factor, value, out_first, out_middle):
@@ -527,19 +545,18 @@
     dens[...] = dot6(jnp.ones((8, terms.shape[1]), F32), terms, NT)[0:1]
 
 
-def total_kernel(scale, cells, wide, *rest):
-    parts, outs = rest[:-2], rest[-2:]
-    total = parts[0][...]
+def total_kernel(scale, values, cells, potential, got_odd, *rest):
+    parts, wide, outs = rest[:-3], rest[-3], rest[-2:]
+    total = parts[0][0:values, :]
     for part in parts[1:]:
-        total = total + part[...]
+        total = total + part[0:values, :]
     total = total * scale
     place_of = cells[...].astype(F32)
     lanes = wide.shape[2]
-    values = total.shape[1] // lanes
+    put_wide(potential, parts[1], got_odd, wide)
     even = lax.axis_index("slab") % 2 == 0
     for out, high in zip(outs, (even, jnp.logical_not(even))):
-        for k in range(values):
-            out[k : k + 1, :] = total[:, k * lanes : (k + 1) * lanes]
+        out[0:values, :] = total
         for k in range(cells.shape[1] // lanes):
             out[values + k : values + k + 1, :] = place_of[:, k * lanes : (k + 1) * lanes]
         put_planes(out, packet_planes(values, cells.shape[1] // lanes), wide, high)
@@ -715,16 +732,12 @@
     rows_all = rows_here * energies
     pitch = -(-(rows_here + 2 * halo) // 8) * 8
     strip = halo * pitch
-    even_rows, odd_rows = call(rows_kernel, (like(depth, halo, across),) * 2, [initial_potential])
-    got_even = energy_exchange(even_rows, False)
-    got_odd = energy_exchange(odd_rows, True)
     cells = (depth + 2 * halo) * pitch
     second = call(
-        pack_kernel, like(width + width // 2 + width, probe_count),
-        [first_factor, prepared[1]],
+        pack_kernel, like(width + width // 2 + 3 * width, probe_count),
+        [first_factor, prepared[1], probes],
     )
     if paired:
-        probes_near = slab_exchange(probes, False)
         second = slab_exchange(second, False)
     dopant_grid = call(
         functools.partial(deposit_kernel, rows_all, pitch, depth, rows_here),
@@ -740,10 +753,6 @@
         [sources, source, link, base_source, solved],
     )
     sources_middle = slab_exchange(total_source, half % 2 == 0)
-    wide = call(
-        halo_kernel, like(depth, pitch, across),
-        [initial_potential, *lax.optimization_barrier((got_even, got_odd, sent))[:2]],
-    )
     inverse = call(join_kernel, square, [across_middle, total], (sq,))
     if paired:
         slope, offset = call(
@@ -754,7 +763,10 @@
             values_kernel, like(4 * width, probe_count),
             [sources_middle, inverse, total_source, slope, offset],
         )
-        dens = call(density_kernel, like(1, 4 * width), [values, probes, probes_near])
+        even_message, odd_message = call(
+            density_kernel, (like(ROWS_AT + depth * halo, across),) * 2,
+            [values, probes, second, initial_potential], ((8, 4 * width),),
+        )
     else:
         first, middle = call(
             middle_kernel, (column, column),
@@ -773,14 +785,26 @@
                  known_p, known_q, factor_p, value_p, state[6], state[7], near_map, far_map, inner,
                  reach],
             )
-    parts = [dens] + [
-        lax.ppermute(dens, "energy", [(e, e ^ k) for e in range(energies)])
-        for k in range(1, energies)
-    ]
-    spare = packet_planes(dens.shape[1] // across, orbital_cell.shape[0] // across)
-    packet, packet_far = call(
-        functools.partial(total_kernel, 1.0 / (probe_count * energies)),
-        (like(spare + strip, across),) * 2, [orbital_cell.reshape(1, -1), wide, *parts],
+    if not paired:
+        even_message, odd_message = call(
+            message_kernel, (like(ROWS_AT + depth * halo, across),) * 2,
+            [dens, initial_potential],
+        )
+    got_even = energy_exchange(even_message, False)
+    got_odd = energy_exchange(odd_message, True)
+    parts = [even_message, got_even]
+    for k in range(2, energies):
+        if energies == 4 and k == 3:
+            parts.append(got_odd)
+        else:
+            partners = [(e, e ^ k) for e in range(energies)]
+            parts.append(lax.ppermute(even_message, "energy", partners))
+    values_rows = (4 if paired else 2) * width // across
+    spare = packet_planes(values_rows, orbital_cell.shape[0] // across)
+    wide, packet, packet_far = call(
+        functools.partial(total_kernel, 1.0 / (probe_count * energies), values_rows),
+        (like(depth, pitch, across),) + (like(spare + strip, across),) * 2,
+        [orbital_cell.reshape(1, -1), initial_potential, got_odd, *parts],
     )
     near = slab_exchange(packet, False)
     far = slab_exchange(packet_far, True)

time: 49.9 us -> 53.9 us (1.080)
  waiting for transfers between devices: 16.1 us -> 18.2 us
  starting transfers between devices: 24.3 us -> 25.3 us
  local copies, waits for them, and re-layouts: 1.8 us -> 2.73 us
    ppermute x9 -> x8, waiting for transfers between devices: 10.8 us -> 15.1 us  [slab_exchange(): return lax.ppermute(value, ('slab', 'energy'), whole)]
    ppermute x9 -> x8, starting transfers between devices: 20.7 us -> 23.1 us  [slab_exchange(): return lax.ppermute(value, ('slab', 'energy'), whole)]
    ppermute x2, waiting for transfers between devices: 2.97 us -> 0.98 us  [energy_exchange(): return lax.ppermute(value, 'energy', pairs)]
    ppermute x3 -> x1, starting transfers between devices: 2.21 us -> 0.54 us  [program(): parts.append(lax.ppermute(even_message, 'energy', partners))]
    unnamed x10, local copies, waits for them, and re-layouts: 0.86 us -> 1.78 us
    ppermute x3 -> x1, waiting for transfers between devices: 2.35 us -> 2.17 us  [program(): parts.append(lax.ppermute(even_message, 'energy', partners))]
    pallas_call x14 -> x12, Pallas kernels: 6.08 us -> 6.02 us  [call(): pl.pallas_call(kernel, out_shape=outs, in_specs=[FAR] * distant + [VM] *...]
  transfers between devices with their start and end apart: 14 -> 11, of which waited for: 8 -> 8; matrix products, arithmetic and copies ran while one was open for 0% -> 0% of each run, Pallas kernels for 9% -> 8%
where the time goes in v11:
time: 53.9 us; the launch traced here: 53.7 us
  starting transfers between devices  25.3 us (47%)
  waiting for transfers between devices  18.2 us (34%)
  Pallas kernels  6.02 us (11%)
  local copies, waits for them, and re-layouts  2.73 us (5%)
  between operations  1.37 us (3%)
    ppermute x8, starting transfers between devices, slab_exchange(): return lax.ppermute(value, ('slab', 'energy'), whole)  23.1 us
    ppermute x8, waiting for transfers between devices, slab_exchange(): return lax.ppermute(value, ('slab', 'energy'), whole)  15.1 us
    pallas_call x12, Pallas kernels, call(): pl.pallas_call(kernel, out_shape=outs, in_specs=[FAR] * distant + [VM] *...  6.02 us
    ppermute x1, waiting for transfers between devices, program(): parts.append(lax.ppermute(even_message, 'energy', partners))  2.17 us
    unnamed x10, local copies, waits for them, and re-layouts  1.78 us
    ppermute x2, starting transfers between devices, energy_exchange(): return lax.ppermute(value, 'energy', pairs)  1.67 us
  transfers between devices with their start and end apart: 11, of which 8 were waited for; matrix products, arithmetic and copies ran while one was open for 0% of the time, Pallas kernels for 8%

profile of v11, /device:TPU:0, one launch (start us, length us, event | category | flops | bytes accessed | tf_op | source)
XLA Modules:
  0.0 53.7 jit_solution(16695979828079000372)
XLA Ops:
  0.6 0.9 %slice_bitcast_fusion = f32[192,192]{1,0:T(8,128)S(1)} fusion(f32[2,192,192]{2,1,0:T(8,128)} %couple.1), kind=kLoop, calls=%fused_computation | loop fusion | bytes 294912 | tf_op jit(solution)/shard_map/squeeze | solution.py:692
  1.6 3.1 %collective-permute-start = (f32[192,192]{1,0:T(8,128)S(1)}, f32[192,192]{1,0:T(8,128)S(1)}, u32[]{:S(2)}, u32[]{:S(2)}) collective-permute-start(f32[192,192]{1,0:T(8,128)S(1)} %slice_bitcast_fusion), channel_id=1, source_target_pairs={{0,4},{1,5},{2,6},{3,7},{4,0},{5,1},{6,2},{7,3},{8,12},{9,13},{10,... | collective-permute-start | bytes 442376 | tf_op jit(solution)/shard_map/ppermute | solution.py:671
  5.3 0.0 copy-start
  5.4 3.9 %shard_map.86 = (f32[192,192]{1,0:T(8,128)S(1)}, f32[192,128]{1,0:T(8,128)S(1)}, f32[192,192]{1,0:T(8,128)S(1)}, f32[192,192]{1,0:T(8,128)S(1)}, f32[192,128]{1,0:T(8,128)S(1)}, /*index=5*/f32[192,128]{1,0:T(8,128)S(1)}) custom-call(f32[2,192,192]{2,1,0:T(8,128)} %diag_far.1, f32[2,192,192]{2,1,0:T(8,128)} %couple.1, f32[384,128]{1,0:T(8,128)} %probes.3, ...), custom_call_target="tpu_custom_call" | custom-call | flops 100000000 | bytes 1000000 | tf_op jit(solution)/shard_map/pallas_call | solution.py:645
  9.3 0.3 collective-permute-done.even.odd
  9.6 0.9 %copy-done.1 = f32[384,128]{1,0:T(8,128)S(1)} copy-done((f32[384,128]{1,0:T(8,128)S(1)}, f32[384,128]{1,0:T(8,128)}, u32[]{:S(2)}) %copy-start.1) | copy-done | bytes 196632
  10.5 0.1 shard_map.91
  10.6 1.7 %collective-permute-start.5 = (f32[864,128]{1,0:T(8,128)S(1)}, f32[864,128]{1,0:T(8,128)S(1)}, u32[]{:S(2)}, u32[]{:S(2)}) collective-permute-start(f32[864,128]{1,0:T(8,128)S(1)} %shard_map.91), channel_id=1, source_target_pairs={{0,4},{1,5},{2,6},{3,7},{4,0},{5,1},{6,2},{7,3},{8,12},{9,13},{10,... | collective-permute-start | bytes 1327112 | tf_op jit(solution)/shard_map/ppermute | solution.py:671
  12.3 0.4 collective-permute-start.2
  12.7 1.6 %collective-permute-start.1 = (f32[192,128]{1,0:T(8,128)S(1)}, f32[192,128]{1,0:T(8,128)S(1)}, u32[]{:S(2)}, u32[]{:S(2)}) collective-permute-start(f32[192,128]{1,0:T(8,128)S(1)} %get-tuple-element.39.source_q), channel_id=1, source_target_pairs={{0,4},{1,5},{2,6},{3,7},{4,0},{5,1},{6,2},{7,3},{8,12},{9,13},{10,... | collective-permute-start | bytes 294920 | tf_op jit(solution)/shard_map/ppermute | solution.py:671
  14.3 10.9 %collective-permute-done.2.message = f32[192,128]{1,0:T(8,128)S(1)} collective-permute-done((f32[192,128]{1,0:T(8,128)S(1)}, f32[192,128]{1,0:T(8,128)S(1)}, u32[]{:S(2)}, u32[]{:S(2)}) %collective-permute-start.2) | collective-permute-done | bytes 98336 | tf_op jit(solution)/shard_map/ppermute | solution.py:671
  25.2 0.0 collective-permute-start.4
  25.2 1.0 %collective-permute-done.1.message = f32[192,128]{1,0:T(8,128)S(1)} collective-permute-done((f32[192,128]{1,0:T(8,128)S(1)}, f32[192,128]{1,0:T(8,128)S(1)}, u32[]{:S(2)}, u32[]{:S(2)}) %collective-permute-start.1) | collective-permute-done | bytes 98336 | tf_op jit(solution)/shard_map/ppermute | solution.py:671
  26.2 0.0 collective-permute-start.3
  26.2 0.2 collective-permute-done.4.message
  26.5 0.0 collective-permute-done.5.second
  26.5 1.0 %collective-permute-done.3.message = f32[192,128]{1,0:T(8,128)S(1)} collective-permute-done((f32[192,128]{1,0:T(8,128)S(1)}, f32[192,128]{1,0:T(8,128)S(1)}, u32[]{:S(2)}, u32[]{:S(2)}) %collective-permute-start.3) | collective-permute-done | bytes 98336 | tf_op jit(solution)/shard_map/ppermute | solution.py:671
  27.5 0.8 %copy-done.2 = f32[8,16,128]{2,1,0:T(8,128)S(1)} copy-done((f32[8,16,128]{2,1,0:T(8,128)S(1)}, f32[8,16,128]{2,1,0:T(8,128)}, u32[]{:S(2)}) %copy-start.2) | copy-done | bytes 65560
  28.4 0.0 copy-start.4
  28.4 1.3 %collective-permute-start.6 = (f32[24,128]{1,0:T(8,128)S(1)}, f32[24,128]{1,0:T(8,128)S(1)}, u32[]{:S(2)}, u32[]{:S(2)}) collective-permute-start(f32[24,128]{1,0:T(8,128)S(1)} %get-tuple-element.59), channel_id=1, source_target_pairs={{1,2},{2,1},{3,0},{0,3},{5,6},{6,5},{7,4},{4,7},{9,10},{10,9},{11,... | collective-permute-start | bytes 36872 | tf_op jit(solution)/shard_map/ppermute | solution.py:679
  29.7 0.4 collective-permute-start.7
  30.1 0.5 %collective-permute-start.8 = (f32[24,128]{1,0:T(8,128)S(1)}, f32[24,128]{1,0:T(8,128)S(1)}, u32[]{:S(2)}, u32[]{:S(2)}) collective-permute-start(f32[24,128]{1,0:T(8,128)S(1)} %get-tuple-element.60.rest_0_), channel_id=1, source_target_pairs={{0,2},{1,3},{2,0},{3,1},{4,6},{5,7},{6,4},{7,5},{8,10},{9,11},{10,... | collective-permute-start | bytes 36872 | tf_op jit(solution)/shard_map/ppermute | solution.py:801
  30.6 1.0 %collective-permute-done.6.got_odd.rest_3_ = f32[24,128]{1,0:T(8,128)S(1)} collective-permute-done((f32[24,128]{1,0:T(8,128)S(1)}, f32[24,128]{1,0:T(8,128)S(1)}, u32[]{:S(2)}, u32[]{:S(2)}) %collective-permute-start.6) | collective-permute-done | bytes 12320 | tf_op jit(solution)/shard_map/ppermute | solution.py:679
  31.6 0.0 collective-permute-done.7.rest_1_
  31.6 2.2 %collective-permute-done.8.rest_2_ = f32[24,128]{1,0:T(8,128)S(1)} collective-permute-done((f32[24,128]{1,0:T(8,128)S(1)}, f32[24,128]{1,0:T(8,128)S(1)}, u32[]{:S(2)}, u32[]{:S(2)}) %collective-permute-start.8) | collective-permute-done | bytes 12320 | tf_op jit(solution)/shard_map/ppermute | solution.py:801
  33.8 0.0 copy-start.3
  33.8 0.1 collective-permute-start.10
  33.9 16.3 %collective-permute-start.9 = (f32[64,128]{1,0:T(8,128)S(1)}, f32[64,128]{1,0:T(8,128)S(1)}, u32[]{:S(2)}, u32[]{:S(2)}) collective-permute-start(f32[64,128]{1,0:T(8,128)S(1)} %get-tuple-element.61.refs_0_), channel_id=1, source_target_pairs={{0,4},{1,5},{2,6},{3,7},{4,0},{5,1},{6,2},{7,3},{8,12},{9,13},{10,... | collective-permute-start | bytes 98312 | tf_op jit(solution)/shard_map/ppermute | solution.py:671
  50.1 0.3 shard_map.96.refs_3_
  50.5 0.0 collective-permute-done.10.refs_2_
  50.5 1.5 %collective-permute-done.9.refs_1_ = f32[64,128]{1,0:T(8,128)S(1)} collective-permute-done((f32[64,128]{1,0:T(8,128)S(1)}, f32[64,128]{1,0:T(8,128)S(1)}, u32[]{:S(2)}, u32[]{:S(2)}) %collective-permute-start.9) | collective-permute-done | bytes 32800 | tf_op jit(solution)/shard_map/ppermute | solution.py:671
  52.0 1.7 %shard_map.97 = (f32[8,16,128]{2,1,0:T(8,128)}, f32[384]{0:T(512)}) custom-call(f32[64,128]{1,0:T(8,128)S(1)} %get-tuple-element.61.refs_0_, f32[64,128]{1,0:T(8,128)S(1)} %collective-permute-done.9.refs_1_, f32[64,128]{1,0:T(8,128)S(1)} %collective-permute-done.10.refs_2_, f32[288,128]{1,0:T(8,128)S(1)} %shard_map.96.refs_3_, ...), custom_call_target="tpu_custom_call" | custom-call | flops 100000000 | bytes 1000000 | tf_op jit(solution)/shard_map/pallas_call | solution.py:645
  (14 shorter events, 0.1 us)
Async XLA Ops:
  1.6 8.0 %collective-permute-start = (f32[192,192]{1,0:T(8,128)S(1)}, f32[192,192]{1,0:T(8,128)S(1)}, u32[]{:S(2)}, u32[]{:S(2)}) collective-permute-start(f32[192,192]{1,0:T(8,128)S(1)} %slice_bitcast_fusion), channel_id=1, source_target_pairs={{0,4},{1,5},{2,6},{3,7},{4,0},{5,1},{6,2},{7,3},{8,12},{9,13},{10,... | collective-permute-start | bytes 442376 | tf_op jit(solution)/shard_map/ppermute | solution.py:671
  5.3 4.3 %copy-start = (f32[2,192,192]{2,1,0:T(8,128)S(1)}, f32[2,192,192]{2,1,0:T(8,128)}, u32[]{:S(2)}) copy-start(f32[2,192,192]{2,1,0:T(8,128)} %couple.1) | copy-start | bytes 884740
  9.6 0.9 %copy-start.1 = (f32[384,128]{1,0:T(8,128)S(1)}, f32[384,128]{1,0:T(8,128)}, u32[]{:S(2)}) copy-start(f32[384,128]{1,0:T(8,128)} %probes.3) | copy-start | bytes 589828
  10.6 15.9 %collective-permute-start.5 = (f32[864,128]{1,0:T(8,128)S(1)}, f32[864,128]{1,0:T(8,128)S(1)}, u32[]{:S(2)}, u32[]{:S(2)}) collective-permute-start(f32[864,128]{1,0:T(8,128)S(1)} %shard_map.91), channel_id=1, source_target_pairs={{0,4},{1,5},{2,6},{3,7},{4,0},{5,1},{6,2},{7,3},{8,12},{9,13},{10,... | collective-permute-start | bytes 1327112 | tf_op jit(solution)/shard_map/ppermute | solution.py:671
  12.3 12.9 %collective-permute-start.2 = (f32[192,128]{1,0:T(8,128)S(1)}, f32[192,128]{1,0:T(8,128)S(1)}, u32[]{:S(2)}, u32[]{:S(2)}) collective-permute-start(f32[192,128]{1,0:T(8,128)S(1)} %get-tuple-element.43), channel_id=1, source_target_pairs={{0,4},{1,5},{2,6},{3,7},{4,0},{5,1},{6,2},{7,3},{8,12},{9,13},{10,... | collective-permute-start | bytes 294920 | tf_op jit(solution)/shard_map/ppermute | solution.py:671
  12.7 13.5 %collective-permute-start.1 = (f32[192,128]{1,0:T(8,128)S(1)}, f32[192,128]{1,0:T(8,128)S(1)}, u32[]{:S(2)}, u32[]{:S(2)}) collective-permute-start(f32[192,128]{1,0:T(8,128)S(1)} %get-tuple-element.39.source_q), channel_id=1, source_target_pairs={{0,4},{1,5},{2,6},{3,7},{4,0},{5,1},{6,2},{7,3},{8,12},{9,13},{10,... | collective-permute-start | bytes 294920 | tf_op jit(solution)/shard_map/ppermute | solution.py:671
  25.2 1.3 %collective-permute-start.4 = (f32[192,128]{1,0:T(8,128)S(1)}, f32[192,128]{1,0:T(8,128)S(1)}, u32[]{:S(2)}, u32[]{:S(2)}) collective-permute-start(f32[192,128]{1,0:T(8,128)S(1)} %get-tuple-element.48), channel_id=1, source_target_pairs={{4,8},{5,9},{6,10},{7,11},{8,4},{9,5},{10,6},{11,7},{0,1},{1,0},{2... | collective-permute-start | bytes 294920 | tf_op jit(solution)/shard_map/ppermute | solution.py:671
  26.2 1.3 %collective-permute-start.3 = (f32[192,128]{1,0:T(8,128)S(1)}, f32[192,128]{1,0:T(8,128)S(1)}, u32[]{:S(2)}, u32[]{:S(2)}) collective-permute-start(f32[192,128]{1,0:T(8,128)S(1)} %get-tuple-element.47.total), channel_id=1, source_target_pairs={{4,8},{5,9},{6,10},{7,11},{8,4},{9,5},{10,6},{11,7},{0,1},{1,0},{2... | collective-permute-start | bytes 294920 | tf_op jit(solution)/shard_map/ppermute | solution.py:671
  27.5 0.8 %copy-start.2 = (f32[8,16,128]{2,1,0:T(8,128)S(1)}, f32[8,16,128]{2,1,0:T(8,128)}, u32[]{:S(2)}) copy-start(f32[8,16,128]{2,1,0:T(8,128)} %potential.3) | copy-start | bytes 196612
  28.4 2.2 %copy-start.4 = (s32[384]{0:T(512)S(1)}, s32[384]{0:T(512)}, u32[]{:S(2)}) copy-start(s32[384]{0:T(512)} %param.11) | copy-start | bytes 4612
  28.4 3.2 %collective-permute-start.6 = (f32[24,128]{1,0:T(8,128)S(1)}, f32[24,128]{1,0:T(8,128)S(1)}, u32[]{:S(2)}, u32[]{:S(2)}) collective-permute-start(f32[24,128]{1,0:T(8,128)S(1)} %get-tuple-element.59), channel_id=1, source_target_pairs={{1,2},{2,1},{3,0},{0,3},{5,6},{6,5},{7,4},{4,7},{9,10},{10,9},{11,... | collective-permute-start | bytes 36872 | tf_op jit(solution)/shard_map/ppermute | solution.py:679
  29.7 1.9 %collective-permute-start.7 = (f32[24,128]{1,0:T(8,128)S(1)}, f32[24,128]{1,0:T(8,128)S(1)}, u32[]{:S(2)}, u32[]{:S(2)}) collective-permute-start(f32[24,128]{1,0:T(8,128)S(1)} %get-tuple-element.60.rest_0_), channel_id=1, source_target_pairs={{0,1},{1,0},{2,3},{3,2},{4,5},{5,4},{6,7},{7,6},{8,9},{9,8},{10,11... | collective-permute-start | bytes 36872 | tf_op jit(solution)/shard_map/ppermute | solution.py:679
  30.1 3.7 %collective-permute-start.8 = (f32[24,128]{1,0:T(8,128)S(1)}, f32[24,128]{1,0:T(8,128)S(1)}, u32[]{:S(2)}, u32[]{:S(2)}) collective-permute-start(f32[24,128]{1,0:T(8,128)S(1)} %get-tuple-element.60.rest_0_), channel_id=1, source_target_pairs={{0,2},{1,3},{2,0},{3,1},{4,6},{5,7},{6,4},{7,5},{8,10},{9,11},{10,... | collective-permute-start | bytes 36872 | tf_op jit(solution)/shard_map/ppermute | solution.py:801
  33.8 16.4 %copy-start.3 = (s32[1024]{0:T(1024)S(1)}, s32[1024]{0:T(1024)}, u32[]{:S(2)}) copy-start(s32[1024]{0:T(1024)} %param.12) | copy-start | bytes 12292
  33.8 16.7 %collective-permute-start.10 = (f32[64,128]{1,0:T(8,128)S(1)}, f32[64,128]{1,0:T(8,128)S(1)}, u32[]{:S(2)}, u32[]{:S(2)}) collective-permute-start(f32[64,128]{1,0:T(8,128)S(1)} %get-tuple-element.62), channel_id=1, source_target_pairs={{4,8},{5,9},{6,10},{7,11},{8,4},{9,5},{10,6},{11,7},{0,1},{1,0},{2... | collective-permute-start | bytes 98312 | tf_op jit(solution)/shard_map/ppermute | solution.py:671
  33.9 18.2 %collective-permute-start.9 = (f32[64,128]{1,0:T(8,128)S(1)}, f32[64,128]{1,0:T(8,128)S(1)}, u32[]{:S(2)}, u32[]{:S(2)}) collective-permute-start(f32[64,128]{1,0:T(8,128)S(1)} %get-tuple-element.61.refs_0_), channel_id=1, source_target_pairs={{0,4},{1,5},{2,6},{3,7},{4,0},{5,1},{6,2},{7,3},{8,12},{9,13},{10,... | collective-permute-start | bytes 98312 | tf_op jit(solution)/shard_map/ppermute | solution.py:671

commit v12 on v10

--- a/solution.py
+++ b/solution.py
@@ -105,7 +105,7 @@
 def guarded(run):
     worst = run(fast)
 
-    @pl.when(jnp.logical_not(worst < 4e-5))
+    @pl.when(jnp.logical_not(worst < 1e-4))
     def _():
         run(careful)
 
@@ -196,7 +196,7 @@
             load.wait()
 
     def outer_block(invert):
-        xp, size = invert(sp, hold, 1 / 12, 4)
+        xp, size = invert(sp, hold, 1 / 16, 4)
         if invert is fast:
             await_loads()
         rp = probes[pl.ds(pl.multiple_of(first * width, width), width), :]
@@ -221,7 +221,7 @@
         source_q[...] = reduced
         pack_symmetric(sq, out)
         if inner_too:
-            xq, size_q = invert(sq, hold, 1 / 12, 4)
+            xq, size_q = invert(sq, hold, 1 / 16, 4)
             inverse_q[...] = xq
             value_q[...] = dot3(xq, reduced)
             pack_symmetric(xq, out_inverse)
@@ -307,7 +307,7 @@
         side_t = side.T
 
         def run(invert):
-            solved, size = invert(matrix_q[...], hold, 1 / 12, 4)
+            solved, size = invert(matrix_q[...], hold, 1 / 16, 4)
             found = dot3(solved, source_q[...])
             across = dot3(solved, ahead_t)
             aside = dot3(solved, side)
@@ -376,7 +376,7 @@
         sign = jnp.where(left, -1.0, 1.0)
 
         def run(invert):
-            found, size = invert(block, hold, 1 / 12, 4)
+            found, size = invert(block, hold, 1 / 16, 4)
             reach = dot3(found, near)
             both = base[...] + sign * dot3(near_t, reach)
             pack_symmetric(both, out)
@@ -774,7 +774,7 @@
                  reach],
             )
     parts = [dens] + [
-        lax.ppermute(dens, "energy", [(e, e ^ k) for e in range(energies)])
+        lax.ppermute(dens, "energy", [(e, (e + k) % energies) for e in range(energies)])
         for k in range(1, energies)
     ]
     spare = packet_planes(dens.shape[1] // across, orbital_cell.shape[0] // across)

time: 49.9 us -> 49.5 us (level)
  the two profiles are of different devices: /device:TPU:0 before, /device:TPU:22 now
where the time goes in v12:
time: 49.5 us; the launch traced here: 49.3 us
  Pallas kernels  19 us (38%)
  waiting for transfers between devices  17.6 us (36%)
  starting transfers between devices  9.62 us (19%)
  local copies, waits for them, and re-layouts  1.49 us (3%)
  between operations  1.49 us (3%)
    pallas_call x14, Pallas kernels, call(): pl.pallas_call(kernel, out_shape=outs, in_specs=[FAR] * distant + [VM] *...  19 us
    ppermute x9, waiting for transfers between devices, slab_exchange(): return lax.ppermute(value, ('slab', 'energy'), whole)  10.4 us
    ppermute x9, starting transfers between devices, slab_exchange(): return lax.ppermute(value, ('slab', 'energy'), whole)  8.01 us
    ppermute x2, waiting for transfers between devices, energy_exchange(): return lax.ppermute(value, 'energy', pairs)  4.22 us
    ppermute x3, waiting for transfers between devices, program(): lax.ppermute(dens, 'energy', [(e, (e + k) % energies) for e in range(ener...  2.99 us
    ppermute x3, starting transfers between devices, program(): lax.ppermute(dens, 'energy', [(e, (e + k) % energies) for e in range(ener...  1.53 us
  transfers between devices with their start and end apart: 14, of which 8 were waited for; matrix products, arithmetic and copies ran while one was open for 0% of the time, Pallas kernels for 27%

profile of v12, /device:TPU:22, one launch (start us, length us, event | category | flops | bytes accessed | tf_op | source)
XLA Modules:
  0.0 49.3 jit_solution(7929484462966986744)
XLA Ops:
  0.6 0.9 %slice_bitcast_fusion = f32[192,192]{1,0:T(8,128)S(1)} fusion(f32[2,192,192]{2,1,0:T(8,128)} %couple.1), kind=kLoop, calls=%fused_computation | loop fusion | bytes 294912 | tf_op jit(solution)/shard_map/squeeze | solution.py:675
  1.6 1.6 %collective-permute-start.3 = (f32[192,192]{1,0:T(8,128)S(1)}, f32[192,192]{1,0:T(8,128)S(1)}, u32[]{:S(2)}, u32[]{:S(2)}) collective-permute-start(f32[192,192]{1,0:T(8,128)S(1)} %slice_bitcast_fusion), channel_id=1, source_target_pairs={{0,4},{1,5},{2,6},{3,7},{4,0},{5,1},{6,2},{7,3},{8,12},{9,13},{10,... | collective-permute-start | bytes 442376 | tf_op jit(solution)/shard_map/ppermute | solution.py:654
  3.9 3.9 %shard_map.87 = (f32[192,192]{1,0:T(8,128)S(1)}, f32[192,128]{1,0:T(8,128)S(1)}, f32[192,192]{1,0:T(8,128)S(1)}, f32[192,192]{1,0:T(8,128)S(1)}, f32[192,128]{1,0:T(8,128)S(1)}, /*index=5*/f32[192,128]{1,0:T(8,128)S(1)}) custom-call(f32[2,192,192]{2,1,0:T(8,128)} %diag_far.1, f32[2,192,192]{2,1,0:T(8,128)} %couple.1, f32[384,128]{1,0:T(8,128)} %probes.1, ...), custom_call_target="tpu_custom_call" | custom-call | flops 100000000 | bytes 1000000 | tf_op jit(solution)/shard_map/pallas_call | solution.py:628
  7.8 0.5 %collective-permute-done.3.even.odd = f32[192,192]{1,0:T(8,128)S(1)} collective-permute-done((f32[192,192]{1,0:T(8,128)S(1)}, f32[192,192]{1,0:T(8,128)S(1)}, u32[]{:S(2)}, u32[]{:S(2)}) %collective-permute-start.3) | collective-permute-done | bytes 147488 | tf_op jit(solution)/shard_map/ppermute | solution.py:654
  8.3 3.4 %shard_map.88 = (f32[192,192]{1,0:T(8,128)S(1)}, f32[192,128]{1,0:T(8,128)S(1)}, f32[192,192]{1,0:T(8,128)S(1)}, f32[192,192]{1,0:T(8,128)S(1)}, f32[192,128]{1,...) custom-call(f32[2,192,192]{2,1,0:T(8,128)S(1)} %copy-done, ...), custom_call_target="tpu_custom_call" | custom-call | flops 100000000 | bytes 1000000 | tf_op jit(solution)/shard_map/pallas_call | solution.py:628
  11.7 0.1 collective-permute-start.7
  11.8 2.0 %collective-permute-start.2 = (f32[192,128]{1,0:T(8,128)S(1)}, f32[192,128]{1,0:T(8,128)S(1)}, u32[]{:S(2)}, u32[]{:S(2)}) collective-permute-start(f32[192,128]{1,0:T(8,128)S(1)} %get-tuple-element.36), channel_id=1, source_target_pairs={{0,4},{1,5},{2,6},{3,7},{4,0},{5,1},{6,2},{7,3},{8,12},{9,13},{10,... | collective-permute-start | bytes 294920 | tf_op jit(solution)/shard_map/ppermute | solution.py:654
  13.8 0.1 collective-permute-start.4
  13.9 1.9 %collective-permute-start.8 = (f32[384,128]{1,0:T(8,128)S(1)}, f32[384,128]{1,0:T(8,128)S(1)}, u32[]{:S(2)}, u32[]{:S(2)}) collective-permute-start(f32[384,128]{1,0:T(8,128)S(1)} %copy-done.1), channel_id=1, source_target_pairs={{0,4},{1,5},{2,6},{3,7},{4,0},{5,1},{6,2},{7,3},{8,12},{9,13},{10,... | collective-permute-start | bytes 589832 | tf_op jit(solution)/shard_map/ppermute | solution.py:654
  15.9 6.9 %collective-permute-done.2.message = f32[192,128]{1,0:T(8,128)S(1)} collective-permute-done((f32[192,128]{1,0:T(8,128)S(1)}, f32[192,128]{1,0:T(8,128)S(1)}, u32[]{:S(2)}, u32[]{:S(2)}) %collective-permute-start.2) | collective-permute-done | bytes 98336 | tf_op jit(solution)/shard_map/ppermute | solution.py:654
  22.7 4.2 %shard_map.89 = (f32[192,192]{1,0:T(8,128)S(1)}, f32[192,192]{1,0:T(8,128)S(1)}, f32[192,192]{1,0:T(8,128)S(1)}, f32[192,128]{1,0:T(8,128)S(1)}) custom-call(f32[192,128]{1,0:T(8,128)S(1)} %collective-permute-done.2.message, f32[192,192]{1,0:T(8,128)S(1)} %get-tuple-element.42.matrix, f32[192,192]{1,0:T(8,128)S(1)} %get-tuple-element.43.link, ...), custom_call_target="tpu_custom_call" | custom-call | flops 100000000 | bytes 1000000 | tf_op jit(solution)/shard_map/pallas_call | solution.py:628
  27.0 0.1 collective-permute-start.6
  27.1 0.6 %shard_map.91 = (f32[192,128]{1,0:T(8,128)S(1)}, f32[192,128]{1,0:T(8,128)S(1)}) custom-call(f32[192,128]{1,0:T(8,128)S(1)} %collective-permute-done.4.message, f32[192,128]{1,0:T(8,128)S(1)} %get-tuple-element.50.source, f32[192,192]{1,0:T(8,128)S(1)} %get-tuple-element.43.link, f32[192,128]{1,0:T(8,128)S(1)} %get-tuple-element.51.base_source, ...), custom_call_target="tpu_custom_call" | custom-call | flops 100000000 | bytes 1000000 | tf_op jit(solution)/shard_map/pallas_call | solution.py:628
  27.7 2.0 %collective-permute-start.5 = (f32[192,128]{1,0:T(8,128)S(1)}, f32[192,128]{1,0:T(8,128)S(1)}, u32[]{:S(2)}, u32[]{:S(2)}) collective-permute-start(f32[192,128]{1,0:T(8,128)S(1)} %get-tuple-element.53.total), channel_id=1, source_target_pairs={{4,8},{5,9},{6,10},{7,11},{8,4},{9,5},{10,6},{11,7},{0,1},{1,0},{2... | collective-permute-start | bytes 294920 | tf_op jit(solution)/shard_map/ppermute | solution.py:654
  29.7 0.1 collective-permute-start
  29.8 1.2 %collective-permute-done.got_even = f32[8,2,128]{2,1,0:T(2,128)S(1)} collective-permute-done((f32[8,2,128]{2,1,0:T(2,128)S(1)}, f32[8,2,128]{2,1,0:T(2,128)S(1)}, u32[]{:S(2)}, u32[]{:S(2)}) %collective-permute-start) | collective-permute-done | bytes 8224 | tf_op jit(solution)/shard_map/ppermute | solution.py:662
  31.0 3.1 %collective-permute-done.1.got_odd = f32[8,2,128]{2,1,0:T(2,128)S(1)} collective-permute-done((f32[8,2,128]{2,1,0:T(2,128)S(1)}, f32[8,2,128]{2,1,0:T(2,128)S(1)}, u32[]{:S(2)}, u32[]{:S(2)}) %collective-permute-start.1) | collective-permute-done | bytes 8224 | tf_op jit(solution)/shard_map/ppermute | solution.py:662
  34.1 2.6 %shard_map.92.inverse = f32[192,192]{1,0:T(8,128)S(1)} custom-call(f32[192,128]{1,0:T(8,128)S(1)} %collective-permute-done.6.message, f32[192,192]{1,0:T(8,128)S(1)} %get-tuple-element.54.total), custom_call_target="tpu_custom_call" | custom-call | flops 100000000 | bytes 1000000 | tf_op jit(solution)/shard_map/pallas_call | solution.py:628
  36.7 1.0 %shard_map.94 = (f32[768,192]{1,0:T(8,128)S(1)}, f32[768,128]{1,0:T(8,128)S(1)}) custom-call(f32[480,128]{1,0:T(8,128)S(1)} %collective-permute-done.7.second, f32[192,192]{1,0:T(8,128)S(1)} %get-tuple-element.56.factor, f32[192,128]{1,0:T(8,128)S(1)} %get-tuple-element.57.value, f32[192,192]{1,0:T(8,128)S(1)} %get-tuple-element.55.factor_p, ...), custom_call_target="tpu_custom_call" | custom-call | flops 100000000 | bytes 1000000 | tf_op jit(solution)/shard_map/pallas_call | solution.py:628
  37.7 0.8 %shard_map.95.values = f32[768,128]{1,0:T(8,128)S(1)} custom-call(f32[192,128]{1,0:T(8,128)S(1)} %collective-permute-done.5.message, f32[192,192]{1,0:T(8,128)S(1)} %shard_map.92.inverse, f32[192,128]{1,0:T(8,128)S(1)} %get-tuple-element.53.total, f32[768,192]{1,0:T(8,128)S(1)} %get-tuple-element.62.slope, f32[768,128]{1,0:T(8,128)S(1)} %get-tuple-element.63.offset), custom_call_target="tpu_custom_call" | custom-call | flops 100000000 | bytes 1000000 | tf_op jit(solution)/shard_map/pallas_call | solution.py:628
  38.5 0.4 shard_map.96.rest_0_
  39.0 0.1 collective-permute-start.10
  39.1 1.4 %collective-permute-start.11 = (f32[1,768]{1,0:T(1,128)S(1)}, f32[1,768]{1,0:T(1,128)S(1)}, u32[]{:S(2)}, u32[]{:S(2)}) collective-permute-start(f32[1,768]{1,0:T(1,128)S(1)} %shard_map.96.rest_0_), channel_id=1, source_target_pairs={{0,3},{1,0},{2,1},{3,2},{4,7},{5,4},{6,5},{7,6},{8,11},{9,8},{10,9... | collective-permute-start | bytes 9224 | tf_op jit(solution)/shard_map/ppermute | solution.py:777
  40.5 2.1 %collective-permute-done.10.rest_2_ = f32[1,768]{1,0:T(1,128)S(1)} collective-permute-done((f32[1,768]{1,0:T(1,128)S(1)}, f32[1,768]{1,0:T(1,128)S(1)}, u32[]{:S(2)}, u32[]{:S(2)}) %collective-permute-start.10) | collective-permute-done | bytes 3104 | tf_op jit(solution)/shard_map/ppermute | solution.py:777
  42.6 0.9 %collective-permute-done.9.rest_1_ = f32[1,768]{1,0:T(1,128)S(1)} collective-permute-done((f32[1,768]{1,0:T(1,128)S(1)}, f32[1,768]{1,0:T(1,128)S(1)}, u32[]{:S(2)}, u32[]{:S(2)}) %collective-permute-start.9) | collective-permute-done | bytes 3104 | tf_op jit(solution)/shard_map/ppermute | solution.py:777
  43.6 0.1 collective-permute-start.12
  43.6 0.1 collective-permute-start.13
  43.7 0.5 %copy-done.3 = s32[1024]{0:T(1024)S(1)} copy-done((s32[1024]{0:T(1024)S(1)}, s32[1024]{0:T(1024)}, u32[]{:S(2)}) %copy-start.3) | copy-done | bytes 4120
  44.2 0.3 shard_map.98.refs_3_
  44.6 3.0 %collective-permute-done.12.refs_1_ = f32[64,128]{1,0:T(8,128)S(1)} collective-permute-done((f32[64,128]{1,0:T(8,128)S(1)}, f32[64,128]{1,0:T(8,128)S(1)}, u32[]{:S(2)}, u32[]{:S(2)}) %collective-permute-start.12) | collective-permute-done | bytes 32800 | tf_op jit(solution)/shard_map/ppermute | solution.py:654
  47.5 0.1 collective-permute-done.13.refs_2_
  47.6 1.7 %shard_map.99 = (f32[8,16,128]{2,1,0:T(8,128)}, f32[384]{0:T(512)}) custom-call(f32[64,128]{1,0:T(8,128)S(1)} %get-tuple-element.64.refs_0_, f32[64,128]{1,0:T(8,128)S(1)} %collective-permute-done.12.refs_1_, f32[64,128]{1,0:T(8,128)S(1)} %collective-permute-done.13.refs_2_, f32[288,128]{1,0:T(8,128)S(1)} %shard_map.98.refs_3_, ...), custom_call_target="tpu_custom_call" | custom-call | flops 100000000 | bytes 1000000 | tf_op jit(solution)/shard_map/pallas_call | solution.py:628
  (22 shorter events, 0.1 us)
Async XLA Ops:
  1.6 6.7 %collective-permute-start.3 = (f32[192,192]{1,0:T(8,128)S(1)}, f32[192,192]{1,0:T(8,128)S(1)}, u32[]{:S(2)}, u32[]{:S(2)}) collective-permute-start(f32[192,192]{1,0:T(8,128)S(1)} %slice_bitcast_fusion), channel_id=1, source_target_pairs={{0,4},{1,5},{2,6},{3,7},{4,0},{5,1},{6,2},{7,3},{8,12},{9,13},{10,... | collective-permute-start | bytes 442376 | tf_op jit(solution)/shard_map/ppermute | solution.py:654
  3.9 4.4 %copy-start = (f32[2,192,192]{2,1,0:T(8,128)S(1)}, f32[2,192,192]{2,1,0:T(8,128)}, u32[]{:S(2)}) copy-start(f32[2,192,192]{2,1,0:T(8,128)} %couple.1) | copy-start | bytes 884740
  11.7 2.2 %copy-start.1 = (f32[384,128]{1,0:T(8,128)S(1)}, f32[384,128]{1,0:T(8,128)}, u32[]{:S(2)}) copy-start(f32[384,128]{1,0:T(8,128)} %probes.1) | copy-start | bytes 589828
  11.7 24.9 %collective-permute-start.7 = (f32[480,128]{1,0:T(8,128)S(1)}, f32[480,128]{1,0:T(8,128)S(1)}, u32[]{:S(2)}, u32[]{:S(2)}) collective-permute-start(f32[480,128]{1,0:T(8,128)S(1)} %shard_map.93), channel_id=1, source_target_pairs={{0,4},{1,5},{2,6},{3,7},{4,0},{5,1},{6,2},{7,3},{8,12},{9,13},{10,... | collective-permute-start | bytes 737288 | tf_op jit(solution)/shard_map/ppermute | solution.py:654
  11.8 10.9 %collective-permute-start.2 = (f32[192,128]{1,0:T(8,128)S(1)}, f32[192,128]{1,0:T(8,128)S(1)}, u32[]{:S(2)}, u32[]{:S(2)}) collective-permute-start(f32[192,128]{1,0:T(8,128)S(1)} %get-tuple-element.36), channel_id=1, source_target_pairs={{0,4},{1,5},{2,6},{3,7},{4,0},{5,1},{6,2},{7,3},{8,12},{9,13},{10,... | collective-permute-start | bytes 294920 | tf_op jit(solution)/shard_map/ppermute | solution.py:654
  13.8 13.2 %collective-permute-start.4 = (f32[192,128]{1,0:T(8,128)S(1)}, f32[192,128]{1,0:T(8,128)S(1)}, u32[]{:S(2)}, u32[]{:S(2)}) collective-permute-start(f32[192,128]{1,0:T(8,128)S(1)} %get-tuple-element.49.source_q), channel_id=1, source_target_pairs={{0,4},{1,5},{2,6},{3,7},{4,0},{5,1},{6,2},{7,3},{8,12},{9,13},{10,... | collective-permute-start | bytes 294920 | tf_op jit(solution)/shard_map/ppermute | solution.py:654
  13.9 24.6 %collective-permute-start.8 = (f32[384,128]{1,0:T(8,128)S(1)}, f32[384,128]{1,0:T(8,128)S(1)}, u32[]{:S(2)}, u32[]{:S(2)}) collective-permute-start(f32[384,128]{1,0:T(8,128)S(1)} %copy-done.1), channel_id=1, source_target_pairs={{0,4},{1,5},{2,6},{3,7},{4,0},{5,1},{6,2},{7,3},{8,12},{9,13},{10,... | collective-permute-start | bytes 589832 | tf_op jit(solution)/shard_map/ppermute | solution.py:654
  27.0 7.1 %collective-permute-start.6 = (f32[192,128]{1,0:T(8,128)S(1)}, f32[192,128]{1,0:T(8,128)S(1)}, u32[]{:S(2)}, u32[]{:S(2)}) collective-permute-start(f32[192,128]{1,0:T(8,128)S(1)} %get-tuple-element.45), channel_id=1, source_target_pairs={{4,8},{5,9},{6,10},{7,11},{8,4},{9,5},{10,6},{11,7},{0,1},{1,0},{2... | collective-permute-start | bytes 294920 | tf_op jit(solution)/shard_map/ppermute | solution.py:654
  27.1 2.6 %copy-start.2 = (f32[8,16,128]{2,1,0:T(8,128)S(1)}, f32[8,16,128]{2,1,0:T(8,128)}, u32[]{:S(2)}) copy-start(f32[8,16,128]{2,1,0:T(8,128)} %potential.3) | copy-start | bytes 196612
  27.7 10.0 %collective-permute-start.5 = (f32[192,128]{1,0:T(8,128)S(1)}, f32[192,128]{1,0:T(8,128)S(1)}, u32[]{:S(2)}, u32[]{:S(2)}) collective-permute-start(f32[192,128]{1,0:T(8,128)S(1)} %get-tuple-element.53.total), channel_id=1, source_target_pairs={{4,8},{5,9},{6,10},{7,11},{8,4},{9,5},{10,6},{11,7},{0,1},{1,0},{2... | collective-permute-start | bytes 294920 | tf_op jit(solution)/shard_map/ppermute | solution.py:654
  29.7 1.3 %copy-start.4 = (s32[384]{0:T(512)S(1)}, s32[384]{0:T(512)}, u32[]{:S(2)}) copy-start(s32[384]{0:T(512)} %param.11) | copy-start | bytes 4612
  29.7 1.2 %collective-permute-start = (f32[8,2,128]{2,1,0:T(2,128)S(1)}, f32[8,2,128]{2,1,0:T(2,128)S(1)}, u32[]{:S(2)}, u32[]{:S(2)}) collective-permute-start(f32[8,2,128]{2,1,0:T(2,128)S(1)} %get-tuple-element.34), channel_id=1, source_target_pairs={{0,1},{1,0},{2,3},{3,2},{4,5},{5,4},{6,7},{7,6},{8,9},{9,8},{10,11... | collective-permute-start | bytes 24584 | tf_op jit(solution)/shard_map/ppermute | solution.py:662
  31.0 3.1 %collective-permute-start.1 = (f32[8,2,128]{2,1,0:T(2,128)S(1)}, f32[8,2,128]{2,1,0:T(2,128)S(1)}, u32[]{:S(2)}, u32[]{:S(2)}) collective-permute-start(f32[8,2,128]{2,1,0:T(2,128)S(1)} %get-tuple-element.35), channel_id=1, source_target_pairs={{1,2},{2,1},{3,0},{0,3},{5,6},{6,5},{7,4},{4,7},{9,10},{10,9},{11,... | collective-permute-start | bytes 24584 | tf_op jit(solution)/shard_map/ppermute | solution.py:662
  39.0 3.6 %collective-permute-start.10 = (f32[1,768]{1,0:T(1,128)S(1)}, f32[1,768]{1,0:T(1,128)S(1)}, u32[]{:S(2)}, u32[]{:S(2)}) collective-permute-start(f32[1,768]{1,0:T(1,128)S(1)} %shard_map.96.rest_0_), channel_id=1, source_target_pairs={{0,2},{1,3},{2,0},{3,1},{4,6},{5,7},{6,4},{7,5},{8,10},{9,11},{10,... | collective-permute-start | bytes 9224 | tf_op jit(solution)/shard_map/ppermute | solution.py:777
  39.1 3.5 %collective-permute-start.11 = (f32[1,768]{1,0:T(1,128)S(1)}, f32[1,768]{1,0:T(1,128)S(1)}, u32[]{:S(2)}, u32[]{:S(2)}) collective-permute-start(f32[1,768]{1,0:T(1,128)S(1)} %shard_map.96.rest_0_), channel_id=1, source_target_pairs={{0,3},{1,0},{2,1},{3,2},{4,7},{5,4},{6,5},{7,6},{8,11},{9,8},{10,9... | collective-permute-start | bytes 9224 | tf_op jit(solution)/shard_map/ppermute | solution.py:777
  40.5 3.0 %collective-permute-start.9 = (f32[1,768]{1,0:T(1,128)S(1)}, f32[1,768]{1,0:T(1,128)S(1)}, u32[]{:S(2)}, u32[]{:S(2)}) collective-permute-start(f32[1,768]{1,0:T(1,128)S(1)} %shard_map.96.rest_0_), channel_id=1, source_target_pairs={{0,1},{1,2},{2,3},{3,0},{4,5},{5,6},{6,7},{7,4},{8,9},{9,10},{10,1... | collective-permute-start | bytes 9224 | tf_op jit(solution)/shard_map/ppermute | solution.py:777
  43.5 0.7 %copy-start.3 = (s32[1024]{0:T(1024)S(1)}, s32[1024]{0:T(1024)}, u32[]{:S(2)}) copy-start(s32[1024]{0:T(1024)} %param.12) | copy-start | bytes 12292
  43.6 4.0 %collective-permute-start.12 = (f32[64,128]{1,0:T(8,128)S(1)}, f32[64,128]{1,0:T(8,128)S(1)}, u32[]{:S(2)}, u32[]{:S(2)}) collective-permute-start(f32[64,128]{1,0:T(8,128)S(1)} %get-tuple-element.64.refs_0_), channel_id=1, source_target_pairs={{0,4},{1,5},{2,6},{3,7},{4,0},{5,1},{6,2},{7,3},{8,12},{9,13},{10,... | collective-permute-start | bytes 98312 | tf_op jit(solution)/shard_map/ppermute | solution.py:654
  43.6 4.0 %collective-permute-start.13 = (f32[64,128]{1,0:T(8,128)S(1)}, f32[64,128]{1,0:T(8,128)S(1)}, u32[]{:S(2)}, u32[]{:S(2)}) collective-permute-start(f32[64,128]{1,0:T(8,128)S(1)} %get-tuple-element.65), channel_id=1, source_target_pairs={{4,8},{5,9},{6,10},{7,11},{8,4},{9,5},{10,6},{11,7},{0,1},{1,0},{2... | collective-permute-start | bytes 98312 | tf_op jit(solution)/shard_map/ppermute | solution.py:654

commit v13 on v12

--- a/solution.py
+++ b/solution.py
@@ -572,11 +572,11 @@
     orbitals = jnp.concatenate([packet_row(p, values, count) for p in (packet, near, far)], axis=1)
     orbitals = jnp.where(jnp.abs(orbitals) < 2.0**30, orbitals, -1.0).astype(jnp.int32)
     rows, ys = spots(orbitals, rows_all, depth, pitch, across, first_z, first_x)
-    spread = ys * weights
-    h = spread.astype(BF16)
-    rest = spread - h.astype(F32)
-    m = rest.astype(BF16)
-    low = (rest - m.astype(F32)).astype(BF16)
+    high = weights.astype(BF16).astype(F32)
+    middle = (weights - high).astype(BF16).astype(F32)
+    h = (ys * high).astype(BF16)
+    m = (ys * middle).astype(BF16)
+    low = (ys * (weights - high - middle)).astype(BF16)
     electron = one_pass(rows, h, NT) + (one_pass(rows, m, NT) + one_pass(rows, low, NT))
     electron = electron.reshape(depth, pitch, across)
     dopant = dopant_grid[...].reshape(depth, pitch, across)
@@ -774,7 +774,7 @@
                  reach],
             )
     parts = [dens] + [
-        lax.ppermute(dens, "energy", [(e, (e + k) % energies) for e in range(energies)])
+        lax.ppermute(dens, "energy", [(e, e ^ k) for e in range(energies)])
         for k in range(1, energies)
     ]
     spare = packet_planes(dens.shape[1] // across, orbital_cell.shape[0] // across)

time: 49.5 us -> 49.4 us (level)
  the two profiles are of different devices: /device:TPU:22 before, /device:TPU:20 now
where the time goes in v13:
time: 49.4 us; the launch traced here: 49.2 us
  Pallas kernels  17.4 us (35%)
  waiting for transfers between devices  15.7 us (32%)
  starting transfers between devices  13 us (26%)
  local copies, waits for them, and re-layouts  1.49 us (3%)
  between operations  1.49 us (3%)
    pallas_call x14, Pallas kernels, call(): pl.pallas_call(kernel, out_shape=outs, in_specs=[FAR] * distant + [VM] *...  17.4 us
    ppermute x9, waiting for transfers between devices, slab_exchange(): return lax.ppermute(value, ('slab', 'energy'), whole)  10.4 us
    ppermute x9, starting transfers between devices, slab_exchange(): return lax.ppermute(value, ('slab', 'energy'), whole)  8.01 us
    ppermute x2, starting transfers between devices, energy_exchange(): return lax.ppermute(value, 'energy', pairs)  2.86 us
    ppermute x3, waiting for transfers between devices, program(): lax.ppermute(dens, 'energy', [(e, e ^ k) for e in range(energies)])  2.8 us
    ppermute x2, waiting for transfers between devices, energy_exchange(): return lax.ppermute(value, 'energy', pairs)  2.52 us
    ppermute x3, starting transfers between devices, program(): lax.ppermute(dens, 'energy', [(e, e ^ k) for e in range(energies)])  2.16 us
  transfers between devices with their start and end apart: 14, of which 8 were waited for; matrix products, arithmetic and copies ran while one was open for 0% of the time, Pallas kernels for 24%

profile of v13, /device:TPU:20, one launch (start us, length us, event | category | flops | bytes accessed | tf_op | source)
XLA Modules:
  0.0 49.2 jit_solution(8881939728210281138)
XLA Ops:
  0.6 0.9 %slice_bitcast_fusion = f32[192,192]{1,0:T(8,128)S(1)} fusion(f32[2,192,192]{2,1,0:T(8,128)} %couple.1), kind=kLoop, calls=%fused_computation | loop fusion | bytes 294912 | tf_op jit(solution)/shard_map/squeeze | solution.py:675
  1.6 1.6 %collective-permute-start.3 = (f32[192,192]{1,0:T(8,128)S(1)}, f32[192,192]{1,0:T(8,128)S(1)}, u32[]{:S(2)}, u32[]{:S(2)}) collective-permute-start(f32[192,192]{1,0:T(8,128)S(1)} %slice_bitcast_fusion), channel_id=1, source_target_pairs={{0,4},{1,5},{2,6},{3,7},{4,0},{5,1},{6,2},{7,3},{8,12},{9,13},{10,... | collective-permute-start | bytes 442376 | tf_op jit(solution)/shard_map/ppermute | solution.py:654
  3.9 3.9 %shard_map.87 = (f32[192,192]{1,0:T(8,128)S(1)}, f32[192,128]{1,0:T(8,128)S(1)}, f32[192,192]{1,0:T(8,128)S(1)}, f32[192,192]{1,0:T(8,128)S(1)}, f32[192,128]{1,0:T(8,128)S(1)}, /*index=5*/f32[192,128]{1,0:T(8,128)S(1)}) custom-call(f32[2,192,192]{2,1,0:T(8,128)} %diag_far.1, f32[2,192,192]{2,1,0:T(8,128)} %couple.1, f32[384,128]{1,0:T(8,128)} %probes.1, ...), custom_call_target="tpu_custom_call" | custom-call | flops 100000000 | bytes 1000000 | tf_op jit(solution)/shard_map/pallas_call | solution.py:628
  7.8 0.5 collective-permute-done.3.even.odd
  8.3 3.4 %shard_map.88 = (f32[192,192]{1,0:T(8,128)S(1)}, f32[192,128]{1,0:T(8,128)S(1)}, f32[192,192]{1,0:T(8,128)S(1)}, f32[192,192]{1,0:T(8,128)S(1)}, f32[192,128]{1,...) custom-call(f32[2,192,192]{2,1,0:T(8,128)S(1)} %copy-done, ...), custom_call_target="tpu_custom_call" | custom-call | flops 100000000 | bytes 1000000 | tf_op jit(solution)/shard_map/pallas_call | solution.py:628
  11.7 0.1 collective-permute-start.7
  11.8 2.0 %collective-permute-start.2 = (f32[192,128]{1,0:T(8,128)S(1)}, f32[192,128]{1,0:T(8,128)S(1)}, u32[]{:S(2)}, u32[]{:S(2)}) collective-permute-start(f32[192,128]{1,0:T(8,128)S(1)} %get-tuple-element.36), channel_id=1, source_target_pairs={{0,4},{1,5},{2,6},{3,7},{4,0},{5,1},{6,2},{7,3},{8,12},{9,13},{10,... | collective-permute-start | bytes 294920 | tf_op jit(solution)/shard_map/ppermute | solution.py:654
  13.8 0.1 collective-permute-start.4
  13.9 1.9 %collective-permute-start.8 = (f32[384,128]{1,0:T(8,128)S(1)}, f32[384,128]{1,0:T(8,128)S(1)}, u32[]{:S(2)}, u32[]{:S(2)}) collective-permute-start(f32[384,128]{1,0:T(8,128)S(1)} %copy-done.1), channel_id=1, source_target_pairs={{0,4},{1,5},{2,6},{3,7},{4,0},{5,1},{6,2},{7,3},{8,12},{9,13},{10,... | collective-permute-start | bytes 589832 | tf_op jit(solution)/shard_map/ppermute | solution.py:654
  15.8 6.9 %collective-permute-done.2.message = f32[192,128]{1,0:T(8,128)S(1)} collective-permute-done((f32[192,128]{1,0:T(8,128)S(1)}, f32[192,128]{1,0:T(8,128)S(1)}, u32[]{:S(2)}, u32[]{:S(2)}) %collective-permute-start.2) | collective-permute-done | bytes 98336 | tf_op jit(solution)/shard_map/ppermute | solution.py:654
  22.7 2.7 %shard_map.89 = (f32[192,192]{1,0:T(8,128)S(1)}, f32[192,192]{1,0:T(8,128)S(1)}, f32[192,192]{1,0:T(8,128)S(1)}, f32[192,128]{1,0:T(8,128)S(1)}) custom-call(f32[192,128]{1,0:T(8,128)S(1)} %collective-permute-done.2.message, f32[192,192]{1,0:T(8,128)S(1)} %get-tuple-element.42.matrix, f32[192,192]{1,0:T(8,128)S(1)} %get-tuple-element.43.link, ...), custom_call_target="tpu_custom_call" | custom-call | flops 100000000 | bytes 1000000 | tf_op jit(solution)/shard_map/pallas_call | solution.py:628
  25.5 0.1 collective-permute-start.6
  25.6 0.6 %shard_map.91 = (f32[192,128]{1,0:T(8,128)S(1)}, f32[192,128]{1,0:T(8,128)S(1)}) custom-call(f32[192,128]{1,0:T(8,128)S(1)} %collective-permute-done.4.message, f32[192,128]{1,0:T(8,128)S(1)} %get-tuple-element.50.source, f32[192,192]{1,0:T(8,128)S(1)} %get-tuple-element.43.link, f32[192,128]{1,0:T(8,128)S(1)} %get-tuple-element.51.base_source, ...), custom_call_target="tpu_custom_call" | custom-call | flops 100000000 | bytes 1000000 | tf_op jit(solution)/shard_map/pallas_call | solution.py:628
  26.1 2.0 %collective-permute-start.5 = (f32[192,128]{1,0:T(8,128)S(1)}, f32[192,128]{1,0:T(8,128)S(1)}, u32[]{:S(2)}, u32[]{:S(2)}) collective-permute-start(f32[192,128]{1,0:T(8,128)S(1)} %get-tuple-element.53.total), channel_id=1, source_target_pairs={{4,8},{5,9},{6,10},{7,11},{8,4},{9,5},{10,6},{11,7},{0,1},{1,0},{2... | collective-permute-start | bytes 294920 | tf_op jit(solution)/shard_map/ppermute | solution.py:654
  28.2 0.1 collective-permute-start
  28.3 1.2 %collective-permute-done.got_even = f32[8,2,128]{2,1,0:T(2,128)S(1)} collective-permute-done((f32[8,2,128]{2,1,0:T(2,128)S(1)}, f32[8,2,128]{2,1,0:T(2,128)S(1)}, u32[]{:S(2)}, u32[]{:S(2)}) %collective-permute-start) | collective-permute-done | bytes 8224 | tf_op jit(solution)/shard_map/ppermute | solution.py:662
  29.4 2.8 %collective-permute-start.1 = (f32[8,2,128]{2,1,0:T(2,128)S(1)}, f32[8,2,128]{2,1,0:T(2,128)S(1)}, u32[]{:S(2)}, u32[]{:S(2)}) collective-permute-start(f32[8,2,128]{2,1,0:T(2,128)S(1)} %get-tuple-element.35), channel_id=1, source_target_pairs={{1,2},{2,1},{3,0},{0,3},{5,6},{6,5},{7,4},{4,7},{9,10},{10,9},{11,... | collective-permute-start | bytes 24584 | tf_op jit(solution)/shard_map/ppermute | solution.py:662
  32.2 1.4 %collective-permute-done.1.got_odd = f32[8,2,128]{2,1,0:T(2,128)S(1)} collective-permute-done((f32[8,2,128]{2,1,0:T(2,128)S(1)}, f32[8,2,128]{2,1,0:T(2,128)S(1)}, u32[]{:S(2)}, u32[]{:S(2)}) %collective-permute-start.1) | collective-permute-done | bytes 8224 | tf_op jit(solution)/shard_map/ppermute | solution.py:662
  33.6 2.6 %shard_map.92.inverse = f32[192,192]{1,0:T(8,128)S(1)} custom-call(f32[192,128]{1,0:T(8,128)S(1)} %collective-permute-done.6.message, f32[192,192]{1,0:T(8,128)S(1)} %get-tuple-element.54.total), custom_call_target="tpu_custom_call" | custom-call | flops 100000000 | bytes 1000000 | tf_op jit(solution)/shard_map/pallas_call | solution.py:628
  36.2 1.0 %shard_map.94 = (f32[768,192]{1,0:T(8,128)S(1)}, f32[768,128]{1,0:T(8,128)S(1)}) custom-call(f32[480,128]{1,0:T(8,128)S(1)} %collective-permute-done.7.second, f32[192,192]{1,0:T(8,128)S(1)} %get-tuple-element.56.factor, f32[192,128]{1,0:T(8,128)S(1)} %get-tuple-element.57.value, f32[192,192]{1,0:T(8,128)S(1)} %get-tuple-element.55.factor_p, ...), custom_call_target="tpu_custom_call" | custom-call | flops 100000000 | bytes 1000000 | tf_op jit(solution)/shard_map/pallas_call | solution.py:628
  37.2 0.8 %shard_map.95.values = f32[768,128]{1,0:T(8,128)S(1)} custom-call(f32[192,128]{1,0:T(8,128)S(1)} %collective-permute-done.5.message, f32[192,192]{1,0:T(8,128)S(1)} %shard_map.92.inverse, f32[192,128]{1,0:T(8,128)S(1)} %get-tuple-element.53.total, f32[768,192]{1,0:T(8,128)S(1)} %get-tuple-element.62.slope, f32[768,128]{1,0:T(8,128)S(1)} %get-tuple-element.63.offset), custom_call_target="tpu_custom_call" | custom-call | flops 100000000 | bytes 1000000 | tf_op jit(solution)/shard_map/pallas_call | solution.py:628
  38.1 0.4 shard_map.96.rest_0_
  38.5 2.0 %collective-permute-start.10 = (f32[1,768]{1,0:T(1,128)S(1)}, f32[1,768]{1,0:T(1,128)S(1)}, u32[]{:S(2)}, u32[]{:S(2)}) collective-permute-start(f32[1,768]{1,0:T(1,128)S(1)} %shard_map.96.rest_0_), channel_id=1, source_target_pairs={{0,2},{1,3},{2,0},{3,1},{4,6},{5,7},{6,4},{7,5},{8,10},{9,11},{10,... | collective-permute-start | bytes 9224 | tf_op jit(solution)/shard_map/ppermute | solution.py:777
  40.5 0.2 collective-permute-start.9
  40.7 1.4 %collective-permute-done.10.rest_2_ = f32[1,768]{1,0:T(1,128)S(1)} collective-permute-done((f32[1,768]{1,0:T(1,128)S(1)}, f32[1,768]{1,0:T(1,128)S(1)}, u32[]{:S(2)}, u32[]{:S(2)}) %collective-permute-start.10) | collective-permute-done | bytes 3104 | tf_op jit(solution)/shard_map/ppermute | solution.py:777
  42.1 1.4 %collective-permute-done.11.rest_3_ = f32[1,768]{1,0:T(1,128)S(1)} collective-permute-done((f32[1,768]{1,0:T(1,128)S(1)}, f32[1,768]{1,0:T(1,128)S(1)}, u32[]{:S(2)}, u32[]{:S(2)}) %collective-permute-start.11) | collective-permute-done | bytes 3104 | tf_op jit(solution)/shard_map/ppermute | solution.py:777
  43.6 0.1 collective-permute-start.13
  43.7 0.5 %copy-done.3 = s32[1024]{0:T(1024)S(1)} copy-done((s32[1024]{0:T(1024)S(1)}, s32[1024]{0:T(1024)}, u32[]{:S(2)}) %copy-start.3) | copy-done | bytes 4120
  44.2 0.3 shard_map.98.refs_3_
  44.6 3.0 %collective-permute-done.12.refs_1_ = f32[64,128]{1,0:T(8,128)S(1)} collective-permute-done((f32[64,128]{1,0:T(8,128)S(1)}, f32[64,128]{1,0:T(8,128)S(1)}, u32[]{:S(2)}, u32[]{:S(2)}) %collective-permute-start.12) | collective-permute-done | bytes 32800 | tf_op jit(solution)/shard_map/ppermute | solution.py:654
  47.5 0.1 collective-permute-done.13.refs_2_
  47.6 1.6 %shard_map.99 = (f32[8,16,128]{2,1,0:T(8,128)}, f32[384]{0:T(512)}) custom-call(f32[64,128]{1,0:T(8,128)S(1)} %get-tuple-element.64.refs_0_, f32[64,128]{1,0:T(8,128)S(1)} %collective-permute-done.12.refs_1_, f32[64,128]{1,0:T(8,128)S(1)} %collective-permute-done.13.refs_2_, f32[288,128]{1,0:T(8,128)S(1)} %shard_map.98.refs_3_, ...), custom_call_target="tpu_custom_call" | custom-call | flops 100000000 | bytes 1000000 | tf_op jit(solution)/shard_map/pallas_call | solution.py:628
  (22 shorter events, 0.2 us)
Async XLA Ops:
  1.6 6.7 %collective-permute-start.3 = (f32[192,192]{1,0:T(8,128)S(1)}, f32[192,192]{1,0:T(8,128)S(1)}, u32[]{:S(2)}, u32[]{:S(2)}) collective-permute-start(f32[192,192]{1,0:T(8,128)S(1)} %slice_bitcast_fusion), channel_id=1, source_target_pairs={{0,4},{1,5},{2,6},{3,7},{4,0},{5,1},{6,2},{7,3},{8,12},{9,13},{10,... | collective-permute-start | bytes 442376 | tf_op jit(solution)/shard_map/ppermute | solution.py:654
  3.9 4.4 %copy-start = (f32[2,192,192]{2,1,0:T(8,128)S(1)}, f32[2,192,192]{2,1,0:T(8,128)}, u32[]{:S(2)}) copy-start(f32[2,192,192]{2,1,0:T(8,128)} %couple.1) | copy-start | bytes 884740
  11.7 2.2 %copy-start.1 = (f32[384,128]{1,0:T(8,128)S(1)}, f32[384,128]{1,0:T(8,128)}, u32[]{:S(2)}) copy-start(f32[384,128]{1,0:T(8,128)} %probes.1) | copy-start | bytes 589828
  11.7 24.5 %collective-permute-start.7 = (f32[480,128]{1,0:T(8,128)S(1)}, f32[480,128]{1,0:T(8,128)S(1)}, u32[]{:S(2)}, u32[]{:S(2)}) collective-permute-start(f32[480,128]{1,0:T(8,128)S(1)} %shard_map.93), channel_id=1, source_target_pairs={{0,4},{1,5},{2,6},{3,7},{4,0},{5,1},{6,2},{7,3},{8,12},{9,13},{10,... | collective-permute-start | bytes 737288 | tf_op jit(solution)/shard_map/ppermute | solution.py:654
  11.8 10.9 %collective-permute-start.2 = (f32[192,128]{1,0:T(8,128)S(1)}, f32[192,128]{1,0:T(8,128)S(1)}, u32[]{:S(2)}, u32[]{:S(2)}) collective-permute-start(f32[192,128]{1,0:T(8,128)S(1)} %get-tuple-element.36), channel_id=1, source_target_pairs={{0,4},{1,5},{2,6},{3,7},{4,0},{5,1},{6,2},{7,3},{8,12},{9,13},{10,... | collective-permute-start | bytes 294920 | tf_op jit(solution)/shard_map/ppermute | solution.py:654
  13.8 11.7 %collective-permute-start.4 = (f32[192,128]{1,0:T(8,128)S(1)}, f32[192,128]{1,0:T(8,128)S(1)}, u32[]{:S(2)}, u32[]{:S(2)}) collective-permute-start(f32[192,128]{1,0:T(8,128)S(1)} %get-tuple-element.49.source_q), channel_id=1, source_target_pairs={{0,4},{1,5},{2,6},{3,7},{4,0},{5,1},{6,2},{7,3},{8,12},{9,13},{10,... | collective-permute-start | bytes 294920 | tf_op jit(solution)/shard_map/ppermute | solution.py:654
  13.9 24.2 %collective-permute-start.8 = (f32[384,128]{1,0:T(8,128)S(1)}, f32[384,128]{1,0:T(8,128)S(1)}, u32[]{:S(2)}, u32[]{:S(2)}) collective-permute-start(f32[384,128]{1,0:T(8,128)S(1)} %copy-done.1), channel_id=1, source_target_pairs={{0,4},{1,5},{2,6},{3,7},{4,0},{5,1},{6,2},{7,3},{8,12},{9,13},{10,... | collective-permute-start | bytes 589832 | tf_op jit(solution)/shard_map/ppermute | solution.py:654
  25.5 8.2 %collective-permute-start.6 = (f32[192,128]{1,0:T(8,128)S(1)}, f32[192,128]{1,0:T(8,128)S(1)}, u32[]{:S(2)}, u32[]{:S(2)}) collective-permute-start(f32[192,128]{1,0:T(8,128)S(1)} %get-tuple-element.45), channel_id=1, source_target_pairs={{4,8},{5,9},{6,10},{7,11},{8,4},{9,5},{10,6},{11,7},{0,1},{1,0},{2... | collective-permute-start | bytes 294920 | tf_op jit(solution)/shard_map/ppermute | solution.py:654
  25.5 2.6 %copy-start.2 = (f32[8,16,128]{2,1,0:T(8,128)S(1)}, f32[8,16,128]{2,1,0:T(8,128)}, u32[]{:S(2)}) copy-start(f32[8,16,128]{2,1,0:T(8,128)} %potential.3) | copy-start | bytes 196612
  26.1 11.1 %collective-permute-start.5 = (f32[192,128]{1,0:T(8,128)S(1)}, f32[192,128]{1,0:T(8,128)S(1)}, u32[]{:S(2)}, u32[]{:S(2)}) collective-permute-start(f32[192,128]{1,0:T(8,128)S(1)} %get-tuple-element.53.total), channel_id=1, source_target_pairs={{4,8},{5,9},{6,10},{7,11},{8,4},{9,5},{10,6},{11,7},{0,1},{1,0},{2... | collective-permute-start | bytes 294920 | tf_op jit(solution)/shard_map/ppermute | solution.py:654
  28.2 4.0 %copy-start.4 = (s32[384]{0:T(512)S(1)}, s32[384]{0:T(512)}, u32[]{:S(2)}) copy-start(s32[384]{0:T(512)} %param.11) | copy-start | bytes 4612
  28.2 1.2 %collective-permute-start = (f32[8,2,128]{2,1,0:T(2,128)S(1)}, f32[8,2,128]{2,1,0:T(2,128)S(1)}, u32[]{:S(2)}, u32[]{:S(2)}) collective-permute-start(f32[8,2,128]{2,1,0:T(2,128)S(1)} %get-tuple-element.34), channel_id=1, source_target_pairs={{0,1},{1,0},{2,3},{3,2},{4,5},{5,4},{6,7},{7,6},{8,9},{9,8},{10,11... | collective-permute-start | bytes 24584 | tf_op jit(solution)/shard_map/ppermute | solution.py:662
  29.4 4.2 %collective-permute-start.1 = (f32[8,2,128]{2,1,0:T(2,128)S(1)}, f32[8,2,128]{2,1,0:T(2,128)S(1)}, u32[]{:S(2)}, u32[]{:S(2)}) collective-permute-start(f32[8,2,128]{2,1,0:T(2,128)S(1)} %get-tuple-element.35), channel_id=1, source_target_pairs={{1,2},{2,1},{3,0},{0,3},{5,6},{6,5},{7,4},{4,7},{9,10},{10,9},{11,... | collective-permute-start | bytes 24584 | tf_op jit(solution)/shard_map/ppermute | solution.py:662
  38.5 3.6 %collective-permute-start.10 = (f32[1,768]{1,0:T(1,128)S(1)}, f32[1,768]{1,0:T(1,128)S(1)}, u32[]{:S(2)}, u32[]{:S(2)}) collective-permute-start(f32[1,768]{1,0:T(1,128)S(1)} %shard_map.96.rest_0_), channel_id=1, source_target_pairs={{0,2},{1,3},{2,0},{3,1},{4,6},{5,7},{6,4},{7,5},{8,10},{9,11},{10,... | collective-permute-start | bytes 9224 | tf_op jit(solution)/shard_map/ppermute | solution.py:777
  40.5 3.0 %collective-permute-start.11 = (f32[1,768]{1,0:T(1,128)S(1)}, f32[1,768]{1,0:T(1,128)S(1)}, u32[]{:S(2)}, u32[]{:S(2)}) collective-permute-start(f32[1,768]{1,0:T(1,128)S(1)} %shard_map.96.rest_0_), channel_id=1, source_target_pairs={{0,3},{1,2},{2,1},{3,0},{4,7},{5,6},{6,5},{7,4},{8,11},{9,10},{10,... | collective-permute-start | bytes 9224 | tf_op jit(solution)/shard_map/ppermute | solution.py:777
  40.5 3.0 %collective-permute-start.9 = (f32[1,768]{1,0:T(1,128)S(1)}, f32[1,768]{1,0:T(1,128)S(1)}, u32[]{:S(2)}, u32[]{:S(2)}) collective-permute-start(f32[1,768]{1,0:T(1,128)S(1)} %shard_map.96.rest_0_), channel_id=1, source_target_pairs={{0,1},{1,0},{2,3},{3,2},{4,5},{5,4},{6,7},{7,6},{8,9},{9,8},{10,11... | collective-permute-start | bytes 9224 | tf_op jit(solution)/shard_map/ppermute | solution.py:777
  43.5 0.7 %copy-start.3 = (s32[1024]{0:T(1024)S(1)}, s32[1024]{0:T(1024)}, u32[]{:S(2)}) copy-start(s32[1024]{0:T(1024)} %param.12) | copy-start | bytes 12292
  43.5 4.0 %collective-permute-start.12 = (f32[64,128]{1,0:T(8,128)S(1)}, f32[64,128]{1,0:T(8,128)S(1)}, u32[]{:S(2)}, u32[]{:S(2)}) collective-permute-start(f32[64,128]{1,0:T(8,128)S(1)} %get-tuple-element.64.refs_0_), channel_id=1, source_target_pairs={{0,4},{1,5},{2,6},{3,7},{4,0},{5,1},{6,2},{7,3},{8,12},{9,13},{10,... | collective-permute-start | bytes 98312 | tf_op jit(solution)/shard_map/ppermute | solution.py:654
  43.6 4.0 %collective-permute-start.13 = (f32[64,128]{1,0:T(8,128)S(1)}, f32[64,128]{1,0:T(8,128)S(1)}, u32[]{:S(2)}, u32[]{:S(2)}) collective-permute-start(f32[64,128]{1,0:T(8,128)S(1)} %get-tuple-element.65), channel_id=1, source_target_pairs={{4,8},{5,9},{6,10},{7,11},{8,4},{9,5},{10,6},{11,7},{0,1},{1,0},{2... | collective-permute-start | bytes 98312 | tf_op jit(solution)/shard_map/ppermute | solution.py:654
